TPU v7x, 128 devices: a whole 4x4x4 slice. The times are simulated.
128 devices in a mesh: grp: 8 (over z, x_hi), tile: 16 (over x_lo, y, core).
Axes of the slice: x: 4 (x_hi: 2, x_lo: 2; x = x_hi * 2 + x_lo), y: 4, z: 4, core: 2. Of those that a mesh axis runs over, the one named last changes fastest.
Arguments:
- ens_control: float32 [16, 32, 256, 128], P('grp', None, 'tile'), may hold values from -6 to 6
- static_control: float32 [8, 5, 32, 256, 128], P('grp', None, None, 'tile'), may hold values from -6 to 6
- member_perturb: bfloat16 [16, 5, 32, 256, 128], P('grp', None, None, 'tile'), may hold values from -5 to 5
- member_group: int32 [16], P('grp'), may hold values from 0 to 11
- localize_rate: float32 [12], replicated, may hold values from 0.04 to 0.24
- static_rate: float32 [8], P('grp'), may hold values from 0.04 to 0.24
- static_scale: float32 [8, 5, 32], P('grp'), may hold values from 0.2 to 2
- obs_index: int32 [65536], P('tile'), may hold values from 0 to 2047
- obs_frac: float32 [65536], P('tile'), may hold values from 0 to 1
- obs_layer: int32 [65536], P('tile'), may hold values from 0 to 159
- obs_kind: int32 [65536], P('tile'), may hold values from 0 to 7
- obs_precision: float32 [8], replicated, may hold values from 0.5 to 8
Outputs:
- hv_ensemble: float32 [16, 32, 256, 128], P('grp', None, 'tile')
- hv_static: float32 [8, 5, 32, 256, 128], P('grp', None, None, 'tile')
All inputs are finite; a program needn't handle non-finite values.
Results may differ from a plain program's by a relative error of at most 0.0003.
Values sent between devices are 32-bit elements; how exact they have to be, the bound alone decides.
No kernel may reach another device: no remote copies, remote signals or barrier semaphores. Data moves between devices by JAX's collectives and lax.ppermute only.
A program may use at most 64 MiB of HBM per device.

v0:
```python
import jax
import jax.numpy as jnp
from jax import lax
from jax.sharding import PartitionSpec as P

SWEEPS = 4


def extended(block, sides, width):
    for axis, dim in sides:
        count = lax.axis_size(axis)
        forward = [(i, i + 1) for i in range(count - 1)]
        backward = [(target, source) for source, target in forward]
        low = lax.ppermute(
            lax.slice_in_dim(block, block.shape[dim] - width, None, axis=dim), axis, forward
        )
        high = lax.ppermute(lax.slice_in_dim(block, 0, width, axis=dim), axis, backward)
        block = jnp.concatenate([low, block, high], axis=dim)
    return block


def diffuse_once(padded, rate_table):
    center = padded[:, :, 1:-1]
    ypadded = jnp.pad(center, ((0, 0), (0, 0), (0, 0), (1, 1)))
    beside = padded[:, :, 2:] + padded[:, :, :-2]
    beside = beside + ypadded[..., 2:] + ypadded[..., :-2]
    return center + rate_table * (beside - 4.0 * center)


def smooth(fields, rate_table):
    for number in range(SWEEPS):
        padded = extended(fields, (("tile", 2),), 1)
        fields = diffuse_once(padded, rate_table)
    return fields


def per_device(
    ens_control,
    static_control,
    member_perturb,
    member_group,
    localize_rate,
    static_rate,
    static_scale,
    obs_index,
    obs_frac,
    obs_layer,
    obs_kind,
    obs_precision,
):
    members = ens_control.shape[0]
    nvars = static_control.shape[1]
    group_ids = jnp.arange(localize_rate.shape[0], dtype=jnp.int32)
    member_rate = jnp.sum(
        jnp.where(member_group[:, None] == group_ids[None, :], localize_rate[None, :], 0.0), axis=1
    )
    rate_table = jnp.concatenate([member_rate, jnp.broadcast_to(static_rate, (nvars,))]).reshape(
        -1, 1, 1, 1
    )
    scales = static_scale[0][:, :, None, None]
    forward = smooth(jnp.concatenate([ens_control, static_control[0]], 0), rate_table)
    partial_value = jnp.sum(member_perturb.astype(jnp.float32) * forward[:members][:, None], axis=0)
    partial_value = partial_value + scales * forward[members:]
    kind_ids = jnp.arange(obs_precision.shape[0], dtype=jnp.int32)
    weight = jnp.sum(
        jnp.where(obs_kind[:, None] == kind_ids[None, :], obs_precision[None, :], 0.0), axis=1
    )
    ny_cells = partial_value.shape[3]
    plane = partial_value.shape[2] * ny_cells
    next_index = obs_index // ny_cells * ny_cells + (obs_index % ny_cells + 1) % ny_cells
    increment = lax.psum(partial_value, "grp")
    flat = increment.reshape(-1)
    base = obs_layer * plane
    first_spot = base + obs_index
    second_spot = base + next_index
    seen = (1.0 - obs_frac) * flat[first_spot] + obs_frac * flat[second_spot]
    valued = weight * seen
    placed = jnp.zeros_like(flat).at[first_spot].add((1.0 - obs_frac) * valued)
    placed = placed.at[second_spot].add(obs_frac * valued)
    gradient = placed.reshape(increment.shape)
    member_source = jnp.sum(member_perturb.astype(jnp.float32) * gradient[None], axis=1)
    adjoint = smooth(jnp.concatenate([member_source, scales * gradient], 0), rate_table)
    hv_ensemble = ens_control + adjoint[:members]
    hv_static = static_control + adjoint[members:][None]
    return (hv_ensemble, hv_static)


def solution(mesh):
    placed = (
        P("grp", None, "tile", None),
        P("grp", None, None, "tile", None),
        P("grp", None, None, "tile", None),
        P("grp"),
        P(),
        P("grp"),
        P("grp", None, None),
        P("tile"),
        P("tile"),
        P("tile"),
        P("tile"),
        P(),
    )
    return jax.shard_map(
        per_device,
        mesh=mesh,
        in_specs=placed,
        out_specs=(P("grp", None, "tile", None), P("grp", None, None, "tile", None)),
        check_vma=False,
    )
```

profile of v0, /device:TPU:6, one launch (start us, length us, event | category | flops | bytes accessed | tf_op | source)
XLA Modules:
  0.0 326.6 jit_solution(13083859683332948064)
XLA Ops:
  7.2 1.7 fusion.56
  9.0 4.6 %collective-permute-start = (f32[7,32,1,128]{3,2,1,0:T(1,128)S(1)}, f32[7,32,1,128]{3,2,1,0:T(1,128)S(1)}, u32[]{:S(2)}, u32[]{:S(2)}) collective-permute-start(f32[7,32,1,128]{3,2,1,0:T(1,128)S(1)} %get-tuple-element.20), channel_id=1, source_target_pairs={{1,0},{2,1},{3,2},{4,3},{5,4},{6,5},{7,6},{8,7},{9,8},{10,9},{11,1... | collective-permute-start | bytes 344072 | tf_op jit(solution)/shard_map/ppermute | solution.py:17
  13.6 1.9 collective-permute-start.1
  16.6 5.3 %collective-permute-done.1 = f32[7,32,1,128]{3,2,1,0:T(1,128)S(1)} collective-permute-done((f32[7,32,1,128]{3,2,1,0:T(1,128)S(1)}, f32[7,32,1,128]{3,2,1,0:T(1,128)S(1)}, u32[]{:S(2)}, u32[]{:S(2)}) %collective-permute-start.1) | collective-permute-done | bytes 114720 | tf_op jit(solution)/shard_map/ppermute | solution.py:14
  21.8 1.6 fusion.6
  23.4 0.2 fusion.72
  23.6 1.9 collective-permute-start.2
  25.5 2.4 collective-permute-start.3
  28.0 5.8 %collective-permute-done.3 = f32[7,32,1,128]{3,2,1,0:T(1,128)S(1)} collective-permute-done((f32[7,32,1,128]{3,2,1,0:T(1,128)S(1)}, f32[7,32,1,128]{3,2,1,0:T(1,128)S(1)}, u32[]{:S(2)}, u32[]{:S(2)}) %collective-permute-start.3) | collective-permute-done | bytes 114720 | tf_op jit(solution)/shard_map/ppermute | solution.py:14
  33.8 1.6 fusion.11
  35.5 1.9 collective-permute-start.4
  37.5 2.4 collective-permute-start.5
  39.9 5.8 %collective-permute-done.5 = f32[7,32,1,128]{3,2,1,0:T(1,128)S(1)} collective-permute-done((f32[7,32,1,128]{3,2,1,0:T(1,128)S(1)}, f32[7,32,1,128]{3,2,1,0:T(1,128)S(1)}, u32[]{:S(2)}, u32[]{:S(2)}) %collective-permute-start.5) | collective-permute-done | bytes 114720 | tf_op jit(solution)/shard_map/ppermute | solution.py:14
  45.7 1.6 fusion.16
  47.3 0.2 fusion.70
  47.5 1.9 collective-permute-start.6
  49.4 2.4 collective-permute-start.7
  51.9 5.8 %collective-permute-done.7 = f32[7,32,1,128]{3,2,1,0:T(1,128)S(1)} collective-permute-done((f32[7,32,1,128]{3,2,1,0:T(1,128)S(1)}, f32[7,32,1,128]{3,2,1,0:T(1,128)S(1)}, u32[]{:S(2)}, u32[]{:S(2)}) %collective-permute-start.7) | collective-permute-done | bytes 114720 | tf_op jit(solution)/shard_map/ppermute | solution.py:14
  57.6 1.6 fusion.21
  59.3 0.3 fusion
  59.6 1.3 fusion.51
  61.2 90.1 %all-reduce.11.cloned.1.call-done = f32[327680]{0:T(1024)} async-done(((f32[327680]{0:T(1024)}), f32[327680]{0:T(1024)}) %all-reduce.11.cloned.1.call-update) | async-done | bytes 1310736 | tf_op jit(solution)/shard_map/psum | solution.py:71
  151.3 48.4 %gather_fusion.1 = f32[4096]{0:T(1024)S(1)} fusion(f32[327680]{0:T(1024)} %all-reduce.11.cloned.1.call-done, s32[4096]{0:T(1024)S(1)} %get-tuple-element.4), kind=kCustom, calls=%fused_computation.1 | custom fusion | bytes 49152 | tf_op jit(solution)/shard_map/gather | solution.py:76
  199.7 23.0 %gather_fusion = f32[4096]{0:T(1024)S(1)} fusion(f32[327680]{0:T(1024)S(1)} %copy-done, s32[4096]{0:T(1024)S(1)} %get-tuple-element.24), kind=kCustom, calls=%fused_computation | custom fusion | bytes 49152 | tf_op jit(solution)/shard_map/gather | solution.py:76
  222.8 22.2 %scatter_custom_fusion = f32[327680]{0:T(1024)S(1)} fusion(s32[4096]{0:T(1024)S(1)} %get-tuple-element.25, f32[4096]{0:T(1024)S(1)} %get-tuple-element.23, f32[]{:T(128)} %constant.38.clone.1), kind=kCustom, calls=%fused_computation.107 | custom fusion | flops 4096 | bytes 1310724 | tf_op jit(solution)/shard_map/scatter-add | solution.py:78
  245.0 23.0 %scatter_fusion = f32[327680]{0:T(1024)S(1)} fusion(f32[327680]{0:T(1024)S(1)} %scatter_custom_fusion, s32[4096]{0:T(1024)S(1)} %get-tuple-element.5, f32[4096]{0:T(1024)S(1)} %get-tuple-element.22), kind=kCustom, calls=%fused_computation.3 | custom fusion | flops 4096 | bytes 65536 | tf_op jit(solution)/shard_map/scatter-add | solution.py:79
  268.1 1.7 fusion.1
  269.7 0.2 broadcast_multiply_fusion
  270.2 1.9 collective-permute-start.8
  272.1 2.4 collective-permute-start.9
  274.7 5.6 %collective-permute-done.9 = f32[7,32,1,128]{3,2,1,0:T(1,128)S(1)} collective-permute-done((f32[7,32,1,128]{3,2,1,0:T(1,128)S(1)}, f32[7,32,1,128]{3,2,1,0:T(1,128)S(1)}, u32[]{:S(2)}, u32[]{:S(2)}) %collective-permute-start.9) | collective-permute-done | bytes 114720 | tf_op jit(solution)/shard_map/ppermute | solution.py:14
  280.3 1.6 fusion.26
  281.9 0.2 fusion.69
  282.1 1.9 collective-permute-start.10
  284.0 2.4 collective-permute-start.11
  286.4 5.8 %collective-permute-done.11 = f32[7,32,1,128]{3,2,1,0:T(1,128)S(1)} collective-permute-done((f32[7,32,1,128]{3,2,1,0:T(1,128)S(1)}, f32[7,32,1,128]{3,2,1,0:T(1,128)S(1)}, u32[]{:S(2)}, u32[]{:S(2)}) %collective-permute-start.11) | collective-permute-done | bytes 114720 | tf_op jit(solution)/shard_map/ppermute | solution.py:14
  292.2 1.6 fusion.31
  294.0 1.9 collective-permute-start.12
  295.9 2.4 collective-permute-start.13
  298.4 5.8 %collective-permute-done.13 = f32[7,32,1,128]{3,2,1,0:T(1,128)S(1)} collective-permute-done((f32[7,32,1,128]{3,2,1,0:T(1,128)S(1)}, f32[7,32,1,128]{3,2,1,0:T(1,128)S(1)}, u32[]{:S(2)}, u32[]{:S(2)}) %collective-permute-start.13) | collective-permute-done | bytes 114720 | tf_op jit(solution)/shard_map/ppermute | solution.py:14
  304.2 1.6 fusion.36
  305.7 0.2 fusion.67
  305.9 1.9 collective-permute-start.14
  307.9 2.4 collective-permute-start.15
  310.3 5.8 %collective-permute-done.15 = f32[7,32,1,128]{3,2,1,0:T(1,128)S(1)} collective-permute-done((f32[7,32,1,128]{3,2,1,0:T(1,128)S(1)}, f32[7,32,1,128]{3,2,1,0:T(1,128)S(1)}, u32[]{:S(2)}, u32[]{:S(2)}) %collective-permute-start.15) | collective-permute-done | bytes 114720 | tf_op jit(solution)/shard_map/ppermute | solution.py:14
  316.1 1.6 fusion.41
  317.7 0.9 slice_add_fusion
  318.5 1.2 fusion.50
  (46 shorter events, 1.4 us)
Async XLA Ops:
  7.2 9.2 %copy-start.2 = (f32[2,32,16,128]{3,2,1,0:T(8,128)S(1)}, f32[2,32,16,128]{3,2,1,0:T(8,128)}, u32[]{:S(2)}) copy-start(f32[2,32,16,128]{3,2,1,0:T(8,128)} %param.12) | copy-start | bytes 1572868
  7.2 9.2 %copy-start.1 = (f32[1,5,32,16,128]{4,3,2,1,0:T(8,128)S(1)}, f32[1,5,32,16,128]{4,3,2,1,0:T(8,128)}, u32[]{:S(2)}) copy-start(f32[1,5,32,16,128]{4,3,2,1,0:T(8,128)} %param.13) | copy-start | bytes 3932164
  7.2 9.0 %copy-start.10 = (f32[12]{0:T(128)S(1)}, f32[12]{0:T(128)}, u32[]{:S(2)}) copy-start(f32[12]{0:T(128)} %param.16) | copy-start | bytes 148
  7.2 9.0 %copy-start.11 = (s32[2]{0:T(128)S(1)}, s32[2]{0:T(128)}, u32[]{:S(2)}) copy-start(s32[2]{0:T(128)} %param.15) | copy-start | bytes 28
  7.2 144.1 %all-reduce.11.cloned.1.call-start = ((), (), s32[]{:S(2)}) async-start(), calls=%async_computation | async-start | bytes 2621440 | tf_op jit(solution)/shard_map/psum | solution.py:71
  9.0 7.6 %collective-permute-start = (f32[7,32,1,128]{3,2,1,0:T(1,128)S(1)}, f32[7,32,1,128]{3,2,1,0:T(1,128)S(1)}, u32[]{:S(2)}, u32[]{:S(2)}) collective-permute-start(f32[7,32,1,128]{3,2,1,0:T(1,128)S(1)} %get-tuple-element.20), channel_id=1, source_target_pairs={{1,0},{2,1},{3,2},{4,3},{5,4},{6,5},{7,6},{8,7},{9,8},{10,9},{11,1... | collective-permute-start | bytes 344072 | tf_op jit(solution)/shard_map/ppermute | solution.py:17
  13.6 8.2 %collective-permute-start.1 = (f32[7,32,1,128]{3,2,1,0:T(1,128)S(1)}, f32[7,32,1,128]{3,2,1,0:T(1,128)S(1)}, u32[]{:S(2)}, u32[]{:S(2)}) collective-permute-start(f32[7,32,1,128]{3,2,1,0:T(1,128)S(1)} %get-tuple-element.21), channel_id=1, source_target_pairs={{0,1},{1,2},{2,3},{3,4},{4,5},{5,6},{6,7},{7,8},{8,9},{9,10},{10,1... | collective-permute-start | bytes 344072 | tf_op jit(solution)/shard_map/ppermute | solution.py:14
  23.6 4.3 %collective-permute-start.2 = (f32[7,32,1,128]{3,2,1,0:T(1,128)S(1)}, f32[7,32,1,128]{3,2,1,0:T(1,128)S(1)}, u32[]{:S(2)}, u32[]{:S(2)}) collective-permute-start(f32[7,32,1,128]{3,2,1,0:T(1,128)S(1)} %get-tuple-element.18), channel_id=1, source_target_pairs={{1,0},{2,1},{3,2},{4,3},{5,4},{6,5},{7,6},{8,7},{9,8},{10,9},{11,1... | collective-permute-start | bytes 344072 | tf_op jit(solution)/shard_map/ppermute | solution.py:17
  25.5 8.2 %collective-permute-start.3 = (f32[7,32,1,128]{3,2,1,0:T(1,128)S(1)}, f32[7,32,1,128]{3,2,1,0:T(1,128)S(1)}, u32[]{:S(2)}, u32[]{:S(2)}) collective-permute-start(f32[7,32,1,128]{3,2,1,0:T(1,128)S(1)} %get-tuple-element.19), channel_id=1, source_target_pairs={{0,1},{1,2},{2,3},{3,4},{4,5},{5,6},{6,7},{7,8},{8,9},{9,10},{10,1... | collective-permute-start | bytes 344072 | tf_op jit(solution)/shard_map/ppermute | solution.py:14
  35.5 4.4 %collective-permute-start.4 = (f32[7,32,1,128]{3,2,1,0:T(1,128)S(1)}, f32[7,32,1,128]{3,2,1,0:T(1,128)S(1)}, u32[]{:S(2)}, u32[]{:S(2)}) collective-permute-start(f32[7,32,1,128]{3,2,1,0:T(1,128)S(1)} %get-tuple-element.16), channel_id=1, source_target_pairs={{1,0},{2,1},{3,2},{4,3},{5,4},{6,5},{7,6},{8,7},{9,8},{10,9},{11,1... | collective-permute-start | bytes 344072 | tf_op jit(solution)/shard_map/ppermute | solution.py:17
  37.5 14.4 %copy-start.8 = (f32[1,5,32]{2,0,1:T(1,128)S(1)}, f32[1,5,32]{2,0,1:T(1,128)}, u32[]{:S(2)}) copy-start(f32[1,5,32]{2,0,1:T(1,128)} %param.18) | copy-start | bytes 1924
  37.5 8.2 %collective-permute-start.5 = (f32[7,32,1,128]{3,2,1,0:T(1,128)S(1)}, f32[7,32,1,128]{3,2,1,0:T(1,128)S(1)}, u32[]{:S(2)}, u32[]{:S(2)}) collective-permute-start(f32[7,32,1,128]{3,2,1,0:T(1,128)S(1)} %get-tuple-element.17), channel_id=1, source_target_pairs={{0,1},{1,2},{2,3},{3,4},{4,5},{5,6},{6,7},{7,8},{8,9},{9,10},{10,1... | collective-permute-start | bytes 344072 | tf_op jit(solution)/shard_map/ppermute | solution.py:14
  47.5 4.4 %collective-permute-start.6 = (f32[7,32,1,128]{3,2,1,0:T(1,128)S(1)}, f32[7,32,1,128]{3,2,1,0:T(1,128)S(1)}, u32[]{:S(2)}, u32[]{:S(2)}) collective-permute-start(f32[7,32,1,128]{3,2,1,0:T(1,128)S(1)} %get-tuple-element.14), channel_id=1, source_target_pairs={{1,0},{2,1},{3,2},{4,3},{5,4},{6,5},{7,6},{8,7},{9,8},{10,9},{11,1... | collective-permute-start | bytes 344072 | tf_op jit(solution)/shard_map/ppermute | solution.py:17
  49.4 8.2 %collective-permute-start.7 = (f32[7,32,1,128]{3,2,1,0:T(1,128)S(1)}, f32[7,32,1,128]{3,2,1,0:T(1,128)S(1)}, u32[]{:S(2)}, u32[]{:S(2)}) collective-permute-start(f32[7,32,1,128]{3,2,1,0:T(1,128)S(1)} %get-tuple-element.15), channel_id=1, source_target_pairs={{0,1},{1,2},{2,3},{3,4},{4,5},{5,6},{6,7},{7,8},{8,9},{9,10},{10,1... | collective-permute-start | bytes 344072 | tf_op jit(solution)/shard_map/ppermute | solution.py:14
  51.9 7.4 %copy-start.3 = (bf16[2,5,32,16,128]{4,3,2,1,0:T(8,128)(2,1)S(1)}, bf16[2,5,32,16,128]{4,3,2,1,0:T(8,128)(2,1)}, u32[]{:S(2)}) copy-start(bf16[2,5,32,16,128]{4,3,2,1,0:T(8,128)(2,1)} %param.14) | copy-start | bytes 3932164
  59.6 1.4 copy-start.4
  59.6 1.4 copy-start.9
  59.6 1.5 copy-start.5
  59.6 1.5 copy-start.6
  151.3 48.4 %copy-start = (f32[327680]{0:T(1024)S(1)}, f32[327680]{0:T(1024)}, u32[]{:S(2)}) copy-start(f32[327680]{0:T(1024)} %all-reduce.11.cloned.1.call-done) | copy-start | bytes 3932164
  199.7 23.1 %copy-start.7 = (f32[4096]{0:T(1024)S(1)}, f32[4096]{0:T(1024)}, u32[]{:S(2)}) copy-start(f32[4096]{0:T(1024)} %param.20) | copy-start | bytes 49156
  270.2 4.5 %collective-permute-start.8 = (f32[7,32,1,128]{3,2,1,0:T(1,128)S(1)}, f32[7,32,1,128]{3,2,1,0:T(1,128)S(1)}, u32[]{:S(2)}, u32[]{:S(2)}) collective-permute-start(f32[7,32,1,128]{3,2,1,0:T(1,128)S(1)} %get-tuple-element.12), channel_id=1, source_target_pairs={{1,0},{2,1},{3,2},{4,3},{5,4},{6,5},{7,6},{8,7},{9,8},{10,9},{11,1... | collective-permute-start | bytes 344072 | tf_op jit(solution)/shard_map/ppermute | solution.py:17
  272.1 8.2 %collective-permute-start.9 = (f32[7,32,1,128]{3,2,1,0:T(1,128)S(1)}, f32[7,32,1,128]{3,2,1,0:T(1,128)S(1)}, u32[]{:S(2)}, u32[]{:S(2)}) collective-permute-start(f32[7,32,1,128]{3,2,1,0:T(1,128)S(1)} %get-tuple-element.13), channel_id=1, source_target_pairs={{0,1},{1,2},{2,3},{3,4},{4,5},{5,6},{6,7},{7,8},{8,9},{9,10},{10,1... | collective-permute-start | bytes 344072 | tf_op jit(solution)/shard_map/ppermute | solution.py:14
  282.1 4.3 %collective-permute-start.10 = (f32[7,32,1,128]{3,2,1,0:T(1,128)S(1)}, f32[7,32,1,128]{3,2,1,0:T(1,128)S(1)}, u32[]{:S(2)}, u32[]{:S(2)}) collective-permute-start(f32[7,32,1,128]{3,2,1,0:T(1,128)S(1)} %get-tuple-element.10), channel_id=1, source_target_pairs={{1,0},{2,1},{3,2},{4,3},{5,4},{6,5},{7,6},{8,7},{9,8},{10,9},{11,1... | collective-permute-start | bytes 344072 | tf_op jit(solution)/shard_map/ppermute | solution.py:17
  284.0 8.2 %collective-permute-start.11 = (f32[7,32,1,128]{3,2,1,0:T(1,128)S(1)}, f32[7,32,1,128]{3,2,1,0:T(1,128)S(1)}, u32[]{:S(2)}, u32[]{:S(2)}) collective-permute-start(f32[7,32,1,128]{3,2,1,0:T(1,128)S(1)} %get-tuple-element.11), channel_id=1, source_target_pairs={{0,1},{1,2},{2,3},{3,4},{4,5},{5,6},{6,7},{7,8},{8,9},{9,10},{10,1... | collective-permute-start | bytes 344072 | tf_op jit(solution)/shard_map/ppermute | solution.py:14
  294.0 4.3 %collective-permute-start.12 = (f32[7,32,1,128]{3,2,1,0:T(1,128)S(1)}, f32[7,32,1,128]{3,2,1,0:T(1,128)S(1)}, u32[]{:S(2)}, u32[]{:S(2)}) collective-permute-start(f32[7,32,1,128]{3,2,1,0:T(1,128)S(1)} %get-tuple-element.8), channel_id=1, source_target_pairs={{1,0},{2,1},{3,2},{4,3},{5,4},{6,5},{7,6},{8,7},{9,8},{10,9},{11,1... | collective-permute-start | bytes 344072 | tf_op jit(solution)/shard_map/ppermute | solution.py:17
  295.9 8.2 %collective-permute-start.13 = (f32[7,32,1,128]{3,2,1,0:T(1,128)S(1)}, f32[7,32,1,128]{3,2,1,0:T(1,128)S(1)}, u32[]{:S(2)}, u32[]{:S(2)}) collective-permute-start(f32[7,32,1,128]{3,2,1,0:T(1,128)S(1)} %get-tuple-element.9), channel_id=1, source_target_pairs={{0,1},{1,2},{2,3},{3,4},{4,5},{5,6},{6,7},{7,8},{8,9},{9,10},{10,1... | collective-permute-start | bytes 344072 | tf_op jit(solution)/shard_map/ppermute | solution.py:14
  305.9 4.3 %collective-permute-start.14 = (f32[7,32,1,128]{3,2,1,0:T(1,128)S(1)}, f32[7,32,1,128]{3,2,1,0:T(1,128)S(1)}, u32[]{:S(2)}, u32[]{:S(2)}) collective-permute-start(f32[7,32,1,128]{3,2,1,0:T(1,128)S(1)} %get-tuple-element.6), channel_id=1, source_target_pairs={{1,0},{2,1},{3,2},{4,3},{5,4},{6,5},{7,6},{8,7},{9,8},{10,9},{11,1... | collective-permute-start | bytes 344072 | tf_op jit(solution)/shard_map/ppermute | solution.py:17
  307.9 8.2 %collective-permute-start.15 = (f32[7,32,1,128]{3,2,1,0:T(1,128)S(1)}, f32[7,32,1,128]{3,2,1,0:T(1,128)S(1)}, u32[]{:S(2)}, u32[]{:S(2)}) collective-permute-start(f32[7,32,1,128]{3,2,1,0:T(1,128)S(1)} %get-tuple-element.7), channel_id=1, source_target_pairs={{0,1},{1,2},{2,3},{3,4},{4,5},{5,6},{6,7},{7,8},{8,9},{9,10},{10,1... | collective-permute-start | bytes 344072 | tf_op jit(solution)/shard_map/ppermute | solution.py:14
Sparse Core Ops, SparseCore 0:
  61.1 90.1 all-reduce.10
where the time goes:
time: 332 us; the launch traced here: 327 us
  waiting for transfers between devices  136 us (41%)
  local copies, waits for them, and re-layouts  72.6 us (22%)
  other arithmetic  66 us (20%)
  starting transfers between devices  36.9 us (11%)
  between operations  15.3 us (5%)
    psum x1, waiting for transfers between devices, per_device(): increment = lax.psum(partial_value, 'grp')  90.1 us
    gather x2, local copies, waits for them, and re-layouts, per_device(): seen = (1.0 - obs_frac) * flat[first_spot] + obs_frac * flat[second_spot]  71.4 us
    ppermute x8, waiting for transfers between devices, extended(): lax.ppermute(lax.slice_in_dim(block, block.shape[dim] - width, None, axis...  45.6 us
    scatter-add x1, other arithmetic, per_device(): placed = placed.at[second_spot].add(obs_frac * valued)  23 us
    scatter-add x1, other arithmetic, per_device(): placed = jnp.zeros_like(flat).at[first_spot].add((1.0 - obs_frac) * valued)  22.2 us
    ppermute x8, starting transfers between devices, extended(): lax.ppermute(lax.slice_in_dim(block, block.shape[dim] - width, None, axis...  18.8 us
    ppermute x8, starting transfers between devices, extended(): lax.ppermute(lax.slice_in_dim(block, 0, width, axis=dim), axis, backward)  18.1 us
    add x8, other arithmetic, diffuse_once(): return center + rate_table * (beside - 4.0 * center)  12.6 us
  transfers between devices with their start and end apart: 17, of which 9 were waited for; matrix products, arithmetic and copies ran while one was open for 0% of the time, Pallas kernels for 0%

commit v1 on v0

v1 whole, which is shorter than its diff:
```python
import jax
import jax.numpy as jnp
from jax import lax
from jax.experimental import pallas as pl
from jax.experimental.pallas import tpu as pltpu
from jax.sharding import PartitionSpec as P

SWEEPS = 4
BLOCK = 256
ALIGN = 16


def sweep(planes, wanted, rows, rate, inside):
    shape = next(iter(planes.values())).shape
    cells = shape[1]
    lane = lax.broadcasted_iota(jnp.int32, shape, 1)
    factors = [(1.0 - 4.0 * rate, rate)] + [((1.0 - 4.0 * rate) * side, rate * side) for side in inside]
    swept = {}
    for x in wanted:
        keep, share = factors[1 if x < 0 else 2 if x >= rows else 0]
        here = planes.get(x)
        beside = [planes[near] for near in (x - 1, x + 1) if near in planes]
        if here is not None:
            beside.append(jnp.where(lane == 0, 0.0, pltpu.roll(here, 1, 1)))
            beside.append(jnp.where(lane == cells - 1, 0.0, pltpu.roll(here, cells - 1, 1)))
        if not beside:
            continue
        total = beside[0]
        for more in beside[1:]:
            total = total + more
        swept[x] = share * total if here is None else keep * here + share * total
    return swept


def spread(planes, first, last, rows, rate, inside):
    for left in range(SWEEPS - 1, -1, -1):
        planes = sweep(planes, range(first - left, last + left + 1), rows, rate, inside)
    return planes


def plane_rows(chunk, at, rows):
    return pl.ds(chunk * 8 * rows + at, 8, stride=rows)


def weights_of(key, frac, cells):
    cell = key & (cells - 1)
    second = (cell + 1) & (cells - 1)
    spot = lax.broadcasted_iota(jnp.int32, (cells, key.shape[1]), 0)
    return jnp.where(spot == cell, 1.0 - frac, jnp.where(spot == second, frac, 0.0))


def chosen_rows(key, start, shift):
    row = (key >> shift) - start
    spot = lax.broadcasted_iota(jnp.int32, (BLOCK, key.shape[1]), 0)
    return jnp.where(spot == row, 1.0, 0.0).astype(jnp.bfloat16)


def halves(value):
    high = value.astype(jnp.bfloat16)
    low = (value - high.astype(jnp.float32)).astype(jnp.bfloat16)
    return high, low


def further_windows(first_row, last_row, blocks, visit):
    def of_block(block, carry):
        start = first_row[block]
        count = (last_row[block] - start) // BLOCK + 1

        def of_window(window, inner):
            visit(block, start + window * BLOCK)
            return inner

        return lax.fori_loop(1, count, of_window, carry)

    lax.fori_loop(0, blocks, of_block, 0)


def forward_kernel(dims, ens, stat, perturb, scale, side_a, side_b, key, frac, rate, inside, parity, first_row, last_row, more, out, smooth, table):
    members, nvars, levels, rows, cells, blocks, copies = dims
    shift = cells.bit_length() - 1
    even = parity[0] == 1

    def halo(field, chunk, j):
        a = side_a[field, plane_rows(chunk, j, SWEEPS), :]
        b = side_b[field, plane_rows(chunk, j, SWEEPS), :]
        return jnp.where(even, b, a), jnp.where(even, a, b)

    def smooth_field(source, at, field, factor):
        def of_chunk(chunk, carry):
            planes = {x: source[at, plane_rows(chunk, x, rows), :] for x in range(rows)}
            for j in range(SWEEPS):
                planes[j - SWEEPS], planes[rows + j] = halo(field, chunk, j)
            planes = spread(planes, 0, rows - 1, rows, rate[field], (inside[0], inside[1]))
            for x in range(rows):
                value = planes[x]
                if factor:
                    value = value * scale[at, pl.ds(chunk * 8, 8), :]
                smooth[field, plane_rows(chunk, x, rows), :] = value
            return carry

        lax.fori_loop(0, levels // 8, of_chunk, 0)

    def of_member(m, carry):
        smooth_field(ens, m, m, False)
        return carry

    def of_group(v, carry):
        smooth_field(stat, v, members + v, True)
        return carry

    lax.fori_loop(0, members, of_member, 0)
    lax.fori_loop(0, nvars, of_group, 0)
    plane = levels * rows
    for v in range(nvars):
        total = smooth[members + v]
        for m in range(members):
            total = total + perturb[m, v].astype(jnp.float32) * smooth[m]
        high, low = halves(total)
        table[v * plane : (v + 1) * plane, :cells] = high
        table[v * plane : (v + 1) * plane, cells:] = low
    table[nvars * plane :, :] = jnp.zeros((BLOCK, 2 * cells), jnp.bfloat16)

    def seen_in(block, start):
        keys = key[pl.ds(block, 1), :]
        picked = lax.dot_general(
            table[pl.ds(pl.multiple_of(start, ALIGN), BLOCK), :],
            chosen_rows(keys, start, shift),
            (((0,), (0,)), ((), ())),
            preferred_element_type=jnp.float32,
        )
        picked = picked[:cells] + picked[cells:]
        return jnp.sum(picked * weights_of(keys, frac[pl.ds(block, 1), :], cells), axis=0, keepdims=True)

    for block in range(blocks):
        out[0, pl.ds(block, 1), :] = seen_in(block, first_row[block])

    @pl.when(more[0] != 0)
    def _():
        def visit(block, start):
            out[0, pl.ds(block, 1), :] = out[0, pl.ds(block, 1), :] + seen_in(block, start)

        further_windows(first_row, last_row, blocks, visit)

    for copy in range(1, copies):
        out[copy] = out[0]


def scatter_kernel(dims, parts, key, frac, weight, perturb, scale, parity, first_row, last_row, more, source, side_a, side_b, gradient, valued):
    members, nvars, levels, rows, cells, blocks, copies = dims
    shift = cells.bit_length() - 1
    seen = parts[0]
    for copy in range(1, copies):
        seen = seen + parts[copy]
    valued[...] = seen * weight[...]
    gradient[...] = jnp.zeros(gradient.shape, jnp.float32)

    def add_block(block, start):
        keys = key[pl.ds(block, 1), :]
        placed = weights_of(keys, frac[pl.ds(block, 1), :], cells) * valued[pl.ds(block, 1), :]
        high, low = halves(placed)
        both = lax.dot_general(
            chosen_rows(keys, start, shift),
            jnp.concatenate([high, low], axis=0),
            (((1,), (1,)), ((), ())),
            preferred_element_type=jnp.float32,
        )
        at = pl.ds(pl.multiple_of(start, ALIGN), BLOCK)
        gradient[at, :] = gradient[at, :] + (both[:, :cells] + both[:, cells:])

    for block in range(blocks):
        add_block(block, first_row[block])

    @pl.when(more[0] != 0)
    def _():
        further_windows(first_row, last_row, blocks, add_block)

    plane = levels * rows
    for m in range(members):
        total = perturb[m, 0].astype(jnp.float32) * gradient[:plane, :]
        for v in range(1, nvars):
            total = total + perturb[m, v].astype(jnp.float32) * gradient[v * plane : (v + 1) * plane, :]
        source[m] = total
    for v in range(nvars):
        for x in range(rows):
            at = pl.ds(x, levels, stride=rows)
            source[members + v, at, :] = gradient[pl.ds(v * plane + x, levels, stride=rows), :] * scale[v]
    even = parity[0] == 1
    begin_a = jnp.where(even, rows - SWEEPS, 0)
    begin_b = jnp.where(even, 0, rows - SWEEPS)
    for field in range(members + nvars):
        for j in range(SWEEPS):
            side_a[field, pl.ds(j, levels, stride=SWEEPS), :] = source[field, pl.ds(begin_a + j, levels, stride=rows), :]
            side_b[field, pl.ds(j, levels, stride=SWEEPS), :] = source[field, pl.ds(begin_b + j, levels, stride=rows), :]


def local_kernel(dims, source, ens, stat, rate, inside, hv_ens, hv_stat):
    members, nvars, levels, rows, cells, blocks, copies = dims

    def field_of(control, out, at, field):
        def of_chunk(chunk, carry):
            planes = {x: source[field, plane_rows(chunk, x, rows), :] for x in range(rows)}
            planes = spread(planes, 0, rows - 1, rows, rate[field], (inside[0], inside[1]))
            for x in range(rows):
                spot = plane_rows(chunk, x, rows)
                out[at, spot, :] = control[at, spot, :] + planes[x]
            return carry

        lax.fori_loop(0, levels // 8, of_chunk, 0)

    def of_member(m, carry):
        field_of(ens, hv_ens, m, m)
        return carry

    def of_group(v, carry):
        field_of(stat, hv_stat, v, members + v)
        return carry

    lax.fori_loop(0, members, of_member, 0)
    lax.fori_loop(0, nvars, of_group, 0)


def edge_kernel(dims, hv_ens_in, hv_stat_in, side_a, side_b, rate, parity, hv_ens, hv_stat):
    members, nvars, levels, rows, cells, blocks, copies = dims
    even = parity[0] == 1

    def field_of(before, out, at, field):
        def of_chunk(chunk, carry):
            lower, upper = {}, {}
            for j in range(SWEEPS):
                a = side_a[field, plane_rows(chunk, j, SWEEPS), :]
                b = side_b[field, plane_rows(chunk, j, SWEEPS), :]
                lower[j - SWEEPS] = jnp.where(even, b, a)
                upper[rows + j] = jnp.where(even, a, b)
            lower = spread(lower, 0, SWEEPS - 1, rows, rate[field], (1.0, 1.0))
            upper = spread(upper, rows - SWEEPS, rows - 1, rows, rate[field], (1.0, 1.0))
            for x in range(rows):
                spot = plane_rows(chunk, x, rows)
                value = before[at, spot, :]
                if x < SWEEPS:
                    value = value + lower[x]
                if x >= rows - SWEEPS:
                    value = value + upper[x]
                out[at, spot, :] = value
            return carry

        lax.fori_loop(0, levels // 8, of_chunk, 0)

    def of_member(m, carry):
        field_of(hv_ens_in, hv_ens, m, m)
        return carry

    def of_group(v, carry):
        field_of(hv_stat_in, hv_stat, v, members + v)
        return carry

    lax.fori_loop(0, members, of_member, 0)
    lax.fori_loop(0, nvars, of_group, 0)


def exchange(side_a, side_b):
    count = lax.axis_size("tile")
    pairs_a = [(i, i ^ 1) for i in range(count)]
    pairs_b = [(i, ((i + 1) ^ 1) - 1) for i in range(1, count - 1)]
    return lax.ppermute(side_a, "tile", pairs_a), lax.ppermute(side_b, "tile", pairs_b)


VMEM = pl.BlockSpec(memory_space=pltpu.VMEM)
SMEM = pl.BlockSpec(memory_space=pltpu.SMEM)


def call(kernel, dims, outs, ins, scalars, scratch=(), aliases={}, cost=2_000_000):
    def body(*refs):
        kernel(dims, *refs)

    return pl.pallas_call(
        body,
        out_shape=tuple(jax.ShapeDtypeStruct(shape, jnp.float32) for shape in outs),
        in_specs=[VMEM] * len(ins) + [SMEM] * len(scalars),
        out_specs=tuple([VMEM] * len(outs)),
        scratch_shapes=list(scratch),
        input_output_aliases=aliases,
        compiler_params=pltpu.CompilerParams(vmem_limit_bytes=48 * 1024 * 1024),
        cost_estimate=pl.CostEstimate(flops=cost * 10, bytes_accessed=cost, transcendentals=0),
        name=kernel.__name__,
    )(*ins, *scalars)


def per_device(
    ens_control,
    static_control,
    member_perturb,
    member_group,
    localize_rate,
    static_rate,
    static_scale,
    obs_index,
    obs_frac,
    obs_layer,
    obs_kind,
    obs_precision,
):
    members, levels, rows, cells = ens_control.shape
    nvars = static_control.shape[1]
    fields = members + nvars
    copies = lax.axis_size("grp")
    blocks = obs_index.shape[0] // BLOCK
    dims = (members, nvars, levels, rows, cells, blocks, copies)
    plane = levels * rows

    tile = lax.axis_index("tile")
    inside = jnp.stack([tile > 0, tile < lax.axis_size("tile") - 1]).astype(jnp.float32)
    even = tile % 2 == 0
    parity = even.astype(jnp.int32).reshape(1)
    begin_a = jnp.where(even, rows - SWEEPS, 0)
    begin_b = jnp.where(even, 0, rows - SWEEPS)

    def side(begin):
        parts = [
            lax.dynamic_slice_in_dim(ens_control, begin, SWEEPS, axis=2),
            lax.dynamic_slice_in_dim(static_control[0], begin, SWEEPS, axis=2),
        ]
        return jnp.concatenate(parts, 0).reshape(fields, levels * SWEEPS, cells)

    side_a, side_b = exchange(side(begin_a), side(begin_b))

    group_ids = jnp.arange(localize_rate.shape[0], dtype=jnp.int32)
    member_rate = jnp.sum(
        jnp.where(member_group[:, None] == group_ids[None, :], localize_rate[None, :], 0.0), axis=1
    )
    rate = jnp.concatenate([member_rate, jnp.broadcast_to(static_rate, (nvars,))])
    scale = jnp.broadcast_to(static_scale[0][:, :, None], (nvars, levels, cells))

    kind_ids = jnp.arange(obs_precision.shape[0], dtype=jnp.int32)
    weight = jnp.sum(
        jnp.where(obs_kind[:, None] == kind_ids[None, :], obs_precision[None, :], 0.0), axis=1
    )
    key = obs_layer * (rows * cells) + obs_index
    key, frac, weight = lax.sort((key, obs_frac, weight), num_keys=1, is_stable=False)
    key, frac, weight = (x.reshape(blocks, BLOCK) for x in (key, frac, weight))
    first_row = key[:, 0] // cells // ALIGN * ALIGN
    last_row = key[:, -1] // cells
    more = jnp.any(last_row - first_row >= BLOCK).astype(jnp.int32).reshape(1)

    ens = ens_control.reshape(members, plane, cells)
    stat = static_control.reshape(nvars, plane, cells)
    perturb = member_perturb.reshape(members, nvars, plane, cells)
    table_rows = nvars * plane + BLOCK
    (seen,) = call(
        forward_kernel,
        dims,
        [(copies, blocks, BLOCK)],
        [ens, stat, perturb, scale, side_a, side_b, key, frac],
        [rate, inside, parity, first_row, last_row, more],
        [pltpu.VMEM((fields, plane, cells), jnp.float32), pltpu.VMEM((table_rows, 2 * cells), jnp.bfloat16)],
    )
    parts = lax.all_to_all(seen, "grp", 0, 0)
    source, side_a, side_b = call(
        scatter_kernel,
        dims,
        [(fields, plane, cells), (fields, levels * SWEEPS, cells), (fields, levels * SWEEPS, cells)],
        [parts, key, frac, weight, perturb, scale],
        [parity, first_row, last_row, more],
        [pltpu.VMEM((table_rows, cells), jnp.float32), pltpu.VMEM((blocks, BLOCK), jnp.float32)],
    )
    side_a, side_b = exchange(side_a, side_b)
    shapes = [(members, plane, cells), (nvars, plane, cells)]
    hv_ens, hv_stat = call(local_kernel, dims, shapes, [source, ens, stat], [rate, inside])
    hv_ens, hv_stat = call(
        edge_kernel, dims, shapes, [hv_ens, hv_stat, side_a, side_b], [rate, parity], aliases={0: 0, 1: 1}
    )
    return hv_ens.reshape(ens_control.shape), hv_stat.reshape(static_control.shape)


def solution(mesh):
    placed = (
        P("grp", None, "tile", None),
        P("grp", None, None, "tile", None),
        P("grp", None, None, "tile", None),
        P("grp"),
        P(),
        P("grp"),
        P("grp", None, None),
        P("tile"),
        P("tile"),
        P("tile"),
        P("tile"),
        P(),
    )
    return jax.shard_map(
        per_device,
        mesh=mesh,
        in_specs=placed,
        out_specs=(P("grp", None, "tile", None), P("grp", None, None, "tile", None)),
        check_vma=False,
    )
```

time: 332 us -> 78 us (0.23)
  the two profiles are of different devices: /device:TPU:6 before, /device:TPU:2 now
where the time goes in v1:
time: 78 us; the launch traced here: 77.6 us
  Pallas kernels  40.7 us (52%)
  starting transfers between devices  16.1 us (21%)
  waiting for transfers between devices  8.2 us (11%)
  other arithmetic  7.6 us (10%)
  local copies, waits for them, and re-layouts  2.96 us (4%)
  between operations  2.15 us (3%)
    pallas_call x4, Pallas kernels, call(): pl.pallas_call(body, out_shape=tuple((jax.ShapeDtypeStruct(shape, jnp.flo...  40.7 us
    ppermute x2, starting transfers between devices, exchange(): lax.ppermute(side_b, 'tile', pairs_b)  8.82 us
    all_to_all x1, waiting for transfers between devices, per_device(): parts = lax.all_to_all(seen, 'grp', 0, 0)  8.19 us
    all_to_all x1, starting transfers between devices, per_device(): parts = lax.all_to_all(seen, 'grp', 0, 0)  7.16 us
    sort x1, other arithmetic, per_device(): lax.sort((key, obs_frac, weight), num_keys=1, is_stable=False)  4.98 us
    concatenate x2, other arithmetic, side(): return jnp.concatenate(parts, 0).reshape(fields, levels * SWEEPS, cells)  1.6 us
  transfers between devices with their start and end apart: 5, of which 1 were waited for; matrix products, arithmetic and copies ran while one was open for 9% of the time, Pallas kernels for 16%

profile of v1, /device:TPU:2, one launch (start us, length us, event | category | flops | bytes accessed | tf_op | source)
XLA Modules:
  0.0 77.6 jit_solution(12255027083688760427)
XLA Ops:
  0.6 1.1 %constant_dynamic-slice_fusion.1 = (f32[2,32,4,128]{3,2,1,0:T(4,128)S(1)}, f32[2,32,4,128]{3,2,1,0:T(4,128)S(1)}) fusion(f32[2,32,16,128]{3,2,1,0:T(8,128)} %param.12, s32[]{:T(128)S(6)} %select_n.39, s32[]{:T(128)S(6)} %select_n.38), kind=kLoop, calls=%fused_computation.25 | loop fusion | bytes 524296 | tf_op jit(solution)/shard_map/dynamic_slice | solution.py:319
  1.7 0.0 copy-start.3
  1.7 0.0 copy-start.4
  1.8 0.0 copy-start.6
  1.8 0.0 copy-start.8
  1.8 0.0 copy-start.5
  1.8 0.0 copy-start.1
  1.8 1.5 %constant_dynamic-slice_fusion = (f32[1,5,32,4,128]{4,3,2,1,0:T(4,128)S(1)}, f32[1,5,32,4,128]{4,3,2,1,0:T(4,128)S(1)}) fusion(f32[1,5,32,16,128]{4,3,2,1,0:T(8,128)} %param.13, s32[]{:T(128)S(6)} %select_n.39, s32[]{:T(128)S(6)} %select_n.38), kind=kLoop, calls=%fused_computation.24 | loop fusion | bytes 1310728 | tf_op jit(solution)/shard_map/dynamic_slice | solution.py:320
  3.3 0.0 copy-start.7
  3.4 0.0 copy-start.9
  3.4 0.0 copy-start.10
  3.4 0.0 copy-start
  3.4 0.0 copy-start.2
  3.4 0.8 %pad_maximum_fusion = f32[7,128,128]{2,1,0:T(8,128)} fusion(f32[5,128,128]{2,1,0:T(8,128)S(1)} %bitcast.26, f32[2,128,128]{2,1,0:T(8,128)S(1)} %bitcast.29), kind=kLoop, calls=%fused_computation | loop fusion | flops 114688 | bytes 917504 | tf_op jit(solution)/shard_map/concatenate | solution.py:322
  4.2 0.0 collective-permute-start
  4.2 0.8 %pad_maximum_fusion.1 = f32[7,128,128]{2,1,0:T(8,128)} fusion(f32[5,128,128]{2,1,0:T(8,128)S(1)} %bitcast.25, f32[2,128,128]{2,1,0:T(8,128)S(1)} %bitcast.28), kind=kLoop, calls=%fused_computation.1 | loop fusion | flops 114688 | bytes 917504 | tf_op jit(solution)/shard_map/concatenate | solution.py:322
  5.0 5.0 %collective-permute-start.1 = (f32[7,128,128]{2,1,0:T(8,128)}, f32[7,128,128]{2,1,0:T(8,128)}, u32[]{:S(2)}, u32[]{:S(2)}) collective-permute-start(f32[7,128,128]{2,1,0:T(8,128)} %pad_maximum_fusion.1), channel_id=1, source_target_pairs={{1,2},{2,1},{3,4},{4,3},{5,6},{6,5},{7,8},{8,7},{9,10},{10,9},{11,... | collective-permute-start | bytes 1376264 | tf_op jit(solution)/shard_map/ppermute | solution.py:264
  10.0 0.0 copy-done.3
  10.0 0.0 copy-done.4
  10.0 0.0 copy-done.6
  10.1 0.0 copy-done.8
  10.1 0.1 select_reduce_fusion
  10.2 0.0 copy-done.5
  10.2 5.0 %sort.21 = (s32[4096]{0:T(1024)S(1)}, f32[4096]{0:T(1024)S(1)}, f32[4096]{0:T(1024)S(1)}) sort(s32[4096]{0:T(1024)S(1)} %multiply_add_fusion, f32[4096]{0:T(1024)S(1)} %copy-done.5, f32[4096]{0:T(1024)S(1)} %select_reduce_fusion), dimensions={0}, to_apply=%region_1.2 | sort | flops 49152 | bytes 98304 | tf_op jit(solution)/shard_map/sort | solution.py:338
  15.2 0.2 slice_reduce_fusion
  16.0 0.0 copy-done.7
  16.0 0.7 compare_reduce_fusion
  17.3 0.0 copy-done.9
  17.3 0.0 copy-done.10
  17.3 0.2 fusion
  17.5 0.1 add_convert_fusion.refs_9_.refs_4_
  17.6 0.0 collective-permute-done.refs_4_
  17.6 0.0 collective-permute-done.1.refs_5_
  17.6 0.1 broadcast_in_dim.43.refs_3_.refs_5_
  17.6 0.0 copy-done.1
  17.7 0.0 copy-done
  17.7 0.0 copy-done.2
  17.7 15.1 %forward_kernel.1 = f32[8,16,256]{2,1,0:T(8,128)} custom-call(f32[2,512,128]{2,1,0:T(8,128)S(1)} %bitcast.22, f32[5,512,128]{2,1,0:T(8,128)S(1)} %bitcast.18, bf16[2,5,512,128]{3,2,1,0:T(8,128)(2,1)S(1)} %bitcast.20, f32[5,32,128]{2,1,0:T(8,128)S(1)} %broadcast_in_dim.43.refs_3_.refs_5_, f32[7,128,128]{2,1,0:T(8,128)} %collective-permute-done.refs_4_, ...), custom_call_target="tpu_custom_call" | custom-call | flops 20000000 | bytes 2000000 | tf_op jit(solution)/shard_map/forward_kernel/pallas_call | solution.py:275
  32.7 7.2 %all-to-all-start = ((f32[8,16,256]{2,1,0:T(8,128)}), f32[8,16,256]{2,1,0:T(8,128)S(1)}, u32[]{:S(2)}, u32[]{:S(2)}) async-start(f32[8,16,256]{2,1,0:T(8,128)} %forward_kernel.1), calls=%async_computation | async-start | bytes 262144 | tf_op jit(solution)/shard_map/all_to_all | solution.py:356
  39.9 8.2 %all-to-all-done.refs_0_ = f32[8,16,256]{2,1,0:T(8,128)S(1)} async-done(((f32[8,16,256]{2,1,0:T(8,128)}), f32[8,16,256]{2,1,0:T(8,128)S(1)}, u32[]{:S(2)}, u32[]{:S(2)}) %all-to-all-start) | async-done | bytes 131104 | tf_op jit(solution)/shard_map/all_to_all | solution.py:356
  48.1 3.5 %scatter_kernel.1 = (f32[7,512,128]{2,1,0:T(8,128)S(1)}, f32[7,128,128]{2,1,0:T(8,128)S(1)}, f32[7,128,128]{2,1,0:T(8,128)S(1)}) custom-call(f32[8,16,256]{2,1,0:T(8,128)S(1)} %all-to-all-done.refs_0_, s32[16,256]{1,0:T(8,128)S(1)} %reshape.56.refs_6_.refs_1_, f32[16,256]{1,0:T(8,128)S(1)} %reshape.57.refs_7_.refs_2_, f32[16,256]{1,0:T(8,128)S(1)} %reshape.62.refs_3_, ...), custom_call_target="tpu_custom_call" | custom-call | flops 20000000 | bytes 2000000 | tf_op jit(solution)/shard_map/scatter_kernel/pallas_call | solution.py:275
  51.6 0.1 collective-permute-start.2
  51.7 3.8 %collective-permute-start.3 = (f32[7,128,128]{2,1,0:T(8,128)S(1)}, f32[7,128,128]{2,1,0:T(8,128)S(1)}, u32[]{:S(2)}, u32[]{:S(2)}) collective-permute-start(f32[7,128,128]{2,1,0:T(8,128)S(1)} %get-tuple-element.19), channel_id=1, source_target_pairs={{1,2},{2,1},{3,4},{4,3},{5,6},{6,5},{7,8},{8,7},{9,10},{10,9},{11,... | collective-permute-start | bytes 1376264 | tf_op jit(solution)/shard_map/ppermute | solution.py:264
  55.5 12.5 %local_kernel.1 = (f32[2,512,128]{2,1,0:T(8,128)}, f32[5,512,128]{2,1,0:T(8,128)}) custom-call(f32[7,512,128]{2,1,0:T(8,128)S(1)} %get-tuple-element.15.refs_0_, f32[2,512,128]{2,1,0:T(8,128)S(1)} %bitcast.23, f32[5,512,128]{2,1,0:T(8,128)S(1)} %bitcast.19, f32[7]{0:T(128)S(1)} %concatenate.25.refs_8_.refs_3_.refs_4_, f32[2]{0:T(128)S(1)} %add_convert_fusion.refs_9_.refs_4_), custom_call_target="tpu_custom_call" | custom-call | flops 20000000 | bytes 2000000 | tf_op jit(solution)/shard_map/local_kernel/pallas_call | solution.py:275
  67.9 0.0 collective-permute-done.2.refs_2_
  67.9 0.0 collective-permute-done.3.refs_3_
  68.0 9.7 %edge_kernel.1 = (f32[2,512,128]{2,1,0:T(8,128)}, f32[5,512,128]{2,1,0:T(8,128)}) custom-call(f32[2,512,128]{2,1,0:T(8,128)} %get-tuple-element.16.refs_0_, f32[5,512,128]{2,1,0:T(8,128)} %get-tuple-element.17.refs_1_, f32[7,128,128]{2,1,0:T(8,128)S(1)} %collective-permute-done.2.refs_2_, ...), custom_call_target="tpu_custom_call", output_to_operand_aliasing={{0}: (0, {}), {1}: (1, {})} | custom-call | flops 20000000 | bytes 2000000 | tf_op jit(solution)/shard_map/edge_kernel/pallas_call | solution.py:275
  (6 shorter events, 0.0 us)
Async XLA Ops:
  1.7 8.3 %copy-start.3 = (s32[4096]{0:T(1024)S(1)}, s32[4096]{0:T(1024)}, u32[]{:S(2)}) copy-start(s32[4096]{0:T(1024)} %param.19) | copy-start | bytes 49156
  1.7 8.3 %copy-start.4 = (s32[4096]{0:T(1024)S(1)}, s32[4096]{0:T(1024)}, u32[]{:S(2)}) copy-start(s32[4096]{0:T(1024)} %param.21) | copy-start | bytes 49156
  1.8 8.3 %copy-start.6 = (s32[4096]{0:T(1024)S(1)}, s32[4096]{0:T(1024)}, u32[]{:S(2)}) copy-start(s32[4096]{0:T(1024)} %param.22) | copy-start | bytes 49156
  1.8 8.3 %copy-start.8 = (f32[8]{0:T(128)S(1)}, f32[8]{0:T(128)}, u32[]{:S(2)}) copy-start(f32[8]{0:T(128)} %param.23) | copy-start | bytes 100
  1.8 8.4 %copy-start.5 = (f32[4096]{0:T(1024)S(1)}, f32[4096]{0:T(1024)}, u32[]{:S(2)}) copy-start(f32[4096]{0:T(1024)} %param.20) | copy-start | bytes 49156
  1.8 15.9 %copy-start.1 = (bf16[2,5,32,16,128]{4,3,2,1,0:T(8,128)(2,1)S(1)}, bf16[2,5,32,16,128]{4,3,2,1,0:T(8,128)(2,1)}, u32[]{:S(2)}) copy-start(bf16[2,5,32,16,128]{4,3,2,1,0:T(8,128)(2,1)} %param.14) | copy-start | bytes 3932164
  3.3 12.7 %copy-start.7 = (f32[1,5,32]{2,0,1:T(1,128)S(1)}, f32[1,5,32]{2,0,1:T(1,128)}, u32[]{:S(2)}) copy-start(f32[1,5,32]{2,0,1:T(1,128)} %param.18) | copy-start | bytes 1924
  3.4 13.9 %copy-start.9 = (f32[12]{0:T(128)S(1)}, f32[12]{0:T(128)}, u32[]{:S(2)}) copy-start(f32[12]{0:T(128)} %param.16) | copy-start | bytes 148
  3.4 13.9 %copy-start.10 = (s32[2]{0:T(128)S(1)}, s32[2]{0:T(128)}, u32[]{:S(2)}) copy-start(s32[2]{0:T(128)} %param.15) | copy-start | bytes 28
  3.4 14.3 %copy-start = (f32[1,5,32,16,128]{4,3,2,1,0:T(8,128)S(1)}, f32[1,5,32,16,128]{4,3,2,1,0:T(8,128)}, u32[]{:S(2)}) copy-start(f32[1,5,32,16,128]{4,3,2,1,0:T(8,128)} %param.13) | copy-start | bytes 3932164
  3.4 14.3 %copy-start.2 = (f32[2,32,16,128]{3,2,1,0:T(8,128)S(1)}, f32[2,32,16,128]{3,2,1,0:T(8,128)}, u32[]{:S(2)}) copy-start(f32[2,32,16,128]{3,2,1,0:T(8,128)} %param.12) | copy-start | bytes 1572868
  4.2 13.4 %collective-permute-start = (f32[7,128,128]{2,1,0:T(8,128)}, f32[7,128,128]{2,1,0:T(8,128)}, u32[]{:S(2)}, u32[]{:S(2)}) collective-permute-start(f32[7,128,128]{2,1,0:T(8,128)} %pad_maximum_fusion), channel_id=1, source_target_pairs={{0,1},{1,0},{2,3},{3,2},{4,5},{5,4},{6,7},{7,6},{8,9},{9,8},{10,11... | collective-permute-start | bytes 1376264 | tf_op jit(solution)/shard_map/ppermute | solution.py:264
  5.0 12.6 %collective-permute-start.1 = (f32[7,128,128]{2,1,0:T(8,128)}, f32[7,128,128]{2,1,0:T(8,128)}, u32[]{:S(2)}, u32[]{:S(2)}) collective-permute-start(f32[7,128,128]{2,1,0:T(8,128)} %pad_maximum_fusion.1), channel_id=1, source_target_pairs={{1,2},{2,1},{3,4},{4,3},{5,6},{6,5},{7,8},{8,7},{9,10},{10,9},{11,... | collective-permute-start | bytes 1376264 | tf_op jit(solution)/shard_map/ppermute | solution.py:264
  32.7 15.4 %all-to-all-start = ((f32[8,16,256]{2,1,0:T(8,128)}), f32[8,16,256]{2,1,0:T(8,128)S(1)}, u32[]{:S(2)}, u32[]{:S(2)}) async-start(f32[8,16,256]{2,1,0:T(8,128)} %forward_kernel.1), calls=%async_computation | async-start | bytes 262144 | tf_op jit(solution)/shard_map/all_to_all | solution.py:356
  51.6 16.4 %collective-permute-start.2 = (f32[7,128,128]{2,1,0:T(8,128)S(1)}, f32[7,128,128]{2,1,0:T(8,128)S(1)}, u32[]{:S(2)}, u32[]{:S(2)}) collective-permute-start(f32[7,128,128]{2,1,0:T(8,128)S(1)} %get-tuple-element.18), channel_id=1, source_target_pairs={{0,1},{1,0},{2,3},{3,2},{4,5},{5,4},{6,7},{7,6},{8,9},{9,8},{10,11... | collective-permute-start | bytes 1376264 | tf_op jit(solution)/shard_map/ppermute | solution.py:264
  51.7 16.3 %collective-permute-start.3 = (f32[7,128,128]{2,1,0:T(8,128)S(1)}, f32[7,128,128]{2,1,0:T(8,128)S(1)}, u32[]{:S(2)}, u32[]{:S(2)}) collective-permute-start(f32[7,128,128]{2,1,0:T(8,128)S(1)} %get-tuple-element.19), channel_id=1, source_target_pairs={{1,2},{2,1},{3,4},{4,3},{5,6},{6,5},{7,8},{8,7},{9,10},{10,9},{11,... | collective-permute-start | bytes 1376264 | tf_op jit(solution)/shard_map/ppermute | solution.py:264

commit v2 on v1

v2 whole, which is shorter than its diff:
```python
import jax
import jax.numpy as jnp
from jax import lax
from jax.experimental import pallas as pl
from jax.experimental.pallas import tpu as pltpu
from jax.sharding import PartitionSpec as P

SWEEPS = 4
BLOCK = 256
ALIGN = 16


def sweep(planes, wanted, rows, rate, inside):
    shape = next(iter(planes.values())).shape
    cells = shape[1]
    lane = lax.broadcasted_iota(jnp.int32, shape, 1)
    factors = [(1.0 - 4.0 * rate, rate)] + [((1.0 - 4.0 * rate) * side, rate * side) for side in inside]
    swept = {}
    for x in wanted:
        keep, share = factors[1 if x < 0 else 2 if x >= rows else 0]
        here = planes.get(x)
        beside = [planes[near] for near in (x - 1, x + 1) if near in planes]
        if here is not None:
            beside.append(jnp.where(lane == 0, 0.0, pltpu.roll(here, 1, 1)))
            beside.append(jnp.where(lane == cells - 1, 0.0, pltpu.roll(here, cells - 1, 1)))
        if not beside:
            continue
        total = beside[0]
        for more in beside[1:]:
            total = total + more
        swept[x] = share * total if here is None else keep * here + share * total
    return swept


def spread(planes, first, last, rows, rate, inside):
    for left in range(SWEEPS - 1, -1, -1):
        planes = sweep(planes, range(first - left, last + left + 1), rows, rate, inside)
    return planes


def rate_of(field, members, group, localize, static):
    if field is None:
        return static[0]
    return localize[group[field]]


def neighbours():
    tile = lax.axis_index("tile")
    last = lax.axis_size("tile") - 1
    return jnp.where(tile > 0, 1.0, 0.0), jnp.where(tile < last, 1.0, 0.0)


def is_even():
    return lax.axis_index("tile") % 2 == 0


def begins(rows):
    even = is_even()
    return jnp.where(even, rows - SWEEPS, 0), jnp.where(even, 0, rows - SWEEPS)


def sides_of(side_a, side_b, field, levels):
    even = is_even()
    lower, upper = [], []
    for j in range(SWEEPS):
        a = side_a[field, pl.ds(j * levels, levels), :]
        b = side_b[field, pl.ds(j * levels, levels), :]
        lower.append(jnp.where(even, b, a))
        upper.append(jnp.where(even, a, b))
    return lower, upper


def block_of(ref, block):
    lanes = ref.shape[1]
    parts = BLOCK // lanes
    return jnp.concatenate([ref[pl.ds(block * parts + part, 1), :] for part in range(parts)], axis=1)


def weights_of(key, frac, cells):
    cell = key & (cells - 1)
    second = (cell + 1) & (cells - 1)
    spot = lax.broadcasted_iota(jnp.int32, (cells, key.shape[1]), 0)
    return jnp.where(spot == cell, 1.0 - frac, jnp.where(spot == second, frac, 0.0))


def chosen_rows(key, start, shift):
    row = (key >> shift) - start
    spot = lax.broadcasted_iota(jnp.int32, (BLOCK, key.shape[1]), 0)
    return jnp.where(spot == row, 1.0, 0.0).astype(jnp.bfloat16)


def halves(value):
    high = value.astype(jnp.bfloat16)
    low = (value - high.astype(jnp.float32)).astype(jnp.bfloat16)
    return high, low


def window_of(bound, block, cells):
    parts = BLOCK // bound.shape[1]
    shift = cells.bit_length() - 1
    start = ((bound[block * parts, 0] >> shift) // ALIGN) * ALIGN
    last = bound[block * parts + parts - 1, bound.shape[1] - 1] >> shift
    return start, (last - start) // BLOCK + 1


def every_window(bound, blocks, cells, visit, visit_again):
    most = 1
    for block in range(blocks):
        start, count = window_of(bound, block, cells)
        most = jnp.maximum(most, count)
        visit(block, start)

    @pl.when(most > 1)
    def _():
        def of_block(block, carry):
            start, count = window_of(bound, block, cells)

            def of_window(window, inner):
                visit_again(block, start + window * BLOCK)
                return inner

            return lax.fori_loop(1, count, of_window, carry)

        lax.fori_loop(0, blocks, of_block, 0)


def each_field(members, nvars, visit):
    def of_member(m, carry):
        visit(True, m, m)
        return carry

    def of_group(v, carry):
        visit(False, v, members + v)
        return carry

    lax.fori_loop(0, members, of_member, 0)
    lax.fori_loop(0, nvars, of_group, 0)


def pack_kernel(dims, ens, stat, side_a, side_b):
    members, nvars, levels, rows, cells, blocks, copies = dims
    for begin, side in zip(begins(rows), (side_a, side_b)):
        for field in range(members + nvars):
            for j in range(SWEEPS):
                source, at = (ens, field) if field < members else (stat, field - members)
                side[field, pl.ds(j * levels, levels), :] = source[at, pl.ds(begin + j, levels, stride=rows), :]


def forward_kernel(dims, ens, stat, perturb, scale, side_a, side_b, key, frac, bound, group, localize, static, out, smooth, table):
    members, nvars, levels, rows, cells, blocks, copies = dims
    shift = cells.bit_length() - 1
    inside = neighbours()

    def of_field(member, at, field):
        source = ens if member else stat
        planes = {x: source[at, pl.ds(x, levels, stride=rows), :] for x in range(rows)}
        lower, upper = sides_of(side_a, side_b, field, levels)
        for j in range(SWEEPS):
            planes[j - SWEEPS], planes[rows + j] = lower[j], upper[j]
        rate = rate_of(field if member else None, members, group, localize, static)
        planes = spread(planes, 0, rows - 1, rows, rate, inside)
        for x in range(rows):
            value = planes[x] if member else planes[x] * scale[at]
            smooth[field, pl.ds(x, levels, stride=rows), :] = value

    each_field(members, nvars, of_field)
    plane = levels * rows
    for v in range(nvars):
        total = smooth[members + v]
        for m in range(members):
            total = total + perturb[m, v].astype(jnp.float32) * smooth[m]
        high, low = halves(total)
        table[v * plane : (v + 1) * plane, :cells] = high
        table[v * plane : (v + 1) * plane, cells:] = low
    table[nvars * plane :, :] = jnp.zeros((BLOCK, 2 * cells), jnp.bfloat16)
    lanes = key.shape[1]
    parts = BLOCK // lanes

    def seen_in(block, start):
        keys = block_of(key, block)
        picked = lax.dot_general(
            table[pl.ds(pl.multiple_of(start, ALIGN), BLOCK), :],
            chosen_rows(keys, start, shift),
            (((0,), (0,)), ((), ())),
            preferred_element_type=jnp.float32,
        )
        picked = picked[:cells] + picked[cells:]
        return jnp.sum(picked * weights_of(keys, block_of(frac, block), cells), axis=0, keepdims=True)

    def visit(block, start):
        seen = seen_in(block, start)
        for part in range(parts):
            out[0, pl.ds(block * parts + part, 1), :] = seen[:, part * lanes : (part + 1) * lanes]

    def visit_again(block, start):
        seen = seen_in(block, start)
        for part in range(parts):
            at = pl.ds(block * parts + part, 1)
            out[0, at, :] = out[0, at, :] + seen[:, part * lanes : (part + 1) * lanes]

    every_window(bound, blocks, cells, visit, visit_again)
    for copy in range(1, copies):
        out[copy] = out[0]


def scatter_kernel(dims, parts, key, frac, weight, perturb, scale, bound, source, side_a, side_b, gradient, valued):
    members, nvars, levels, rows, cells, blocks, copies = dims
    shift = cells.bit_length() - 1
    seen = parts[0]
    for copy in range(1, copies):
        seen = seen + parts[copy]
    valued[...] = seen * weight[...]
    gradient[...] = jnp.zeros(gradient.shape, jnp.float32)

    def add_block(block, start):
        keys = block_of(key, block)
        placed = weights_of(keys, block_of(frac, block), cells) * block_of(valued, block)
        high, low = halves(placed)
        both = lax.dot_general(
            chosen_rows(keys, start, shift),
            jnp.concatenate([high, low], axis=0),
            (((1,), (1,)), ((), ())),
            preferred_element_type=jnp.float32,
        )
        at = pl.ds(pl.multiple_of(start, ALIGN), BLOCK)
        gradient[at, :] = gradient[at, :] + (both[:, :cells] + both[:, cells:])

    every_window(bound, blocks, cells, add_block, add_block)

    plane = levels * rows
    for m in range(members):
        total = perturb[m, 0].astype(jnp.float32) * gradient[:plane, :]
        for v in range(1, nvars):
            total = total + perturb[m, v].astype(jnp.float32) * gradient[v * plane : (v + 1) * plane, :]
        source[m] = total
    for v in range(nvars):
        for x in range(rows):
            at = pl.ds(x, levels, stride=rows)
            source[members + v, at, :] = gradient[pl.ds(v * plane + x, levels, stride=rows), :] * scale[v]
    for begin, side in zip(begins(rows), (side_a, side_b)):
        for field in range(members + nvars):
            for j in range(SWEEPS):
                side[field, pl.ds(j * levels, levels), :] = source[field, pl.ds(begin + j, levels, stride=rows), :]


def local_kernel(dims, source, ens, stat, group, localize, static, hv):
    members, nvars, levels, rows, cells, blocks, copies = dims
    inside = neighbours()

    def of_field(member, at, field):
        control = ens if member else stat
        planes = {x: source[field, pl.ds(x, levels, stride=rows), :] for x in range(rows)}
        rate = rate_of(field if member else None, members, group, localize, static)
        planes = spread(planes, 0, rows - 1, rows, rate, inside)
        for x in range(rows):
            spot = pl.ds(x, levels, stride=rows)
            hv[field, spot, :] = control[at, spot, :] + planes[x]

    each_field(members, nvars, of_field)


def edge_kernel(dims, before, side_a, side_b, group, localize, static, hv_ens, hv_stat, after, sems):
    members, nvars, levels, rows, cells, blocks, copies = dims

    def copy_of(member, at, field):
        out = hv_ens if member else hv_stat
        return pltpu.make_async_copy(after.at[field], out.at[at], sems.at[field])

    def of_field(member, at, field):
        rate = rate_of(field if member else None, members, group, localize, static)
        lower, upper = sides_of(side_a, side_b, field, levels)
        lower = spread({j - SWEEPS: lower[j] for j in range(SWEEPS)}, 0, SWEEPS - 1, rows, rate, (1.0, 1.0))
        upper = spread({rows + j: upper[j] for j in range(SWEEPS)}, rows - SWEEPS, rows - 1, rows, rate, (1.0, 1.0))
        for x in range(rows):
            spot = pl.ds(x, levels, stride=rows)
            value = before[field, spot, :]
            if x < SWEEPS:
                value = value + lower[x]
            if x >= rows - SWEEPS:
                value = value + upper[x]
            after[field, spot, :] = value
        copy_of(member, at, field).start()

    each_field(members, nvars, of_field)
    each_field(members, nvars, lambda member, at, field: copy_of(member, at, field).wait())


def exchange(side_a, side_b):
    count = lax.axis_size("tile")
    pairs_a = [(i, i ^ 1) for i in range(count)]
    pairs_b = [(i, ((i + 1) ^ 1) - 1) for i in range(1, count - 1)]
    return lax.ppermute(side_a, "tile", pairs_a), lax.ppermute(side_b, "tile", pairs_b)


VMEM = pl.BlockSpec(memory_space=pltpu.VMEM)
SMEM = pl.BlockSpec(memory_space=pltpu.SMEM)
ANY = pl.BlockSpec(memory_space=pl.ANY)


def call(kernel, dims, outs, ins, scalars=(), scratch=(), out_spec=VMEM, cost=2_000_000):
    def body(*refs):
        kernel(dims, *refs)

    return pl.pallas_call(
        body,
        out_shape=tuple(jax.ShapeDtypeStruct(shape, jnp.float32) for shape in outs),
        in_specs=[VMEM] * len(ins) + [SMEM] * len(scalars),
        out_specs=tuple([out_spec] * len(outs)),
        scratch_shapes=list(scratch),
        compiler_params=pltpu.CompilerParams(vmem_limit_bytes=40 * 1024 * 1024),
        cost_estimate=pl.CostEstimate(flops=cost * 10, bytes_accessed=cost, transcendentals=0),
        name=kernel.__name__,
    )(*ins, *scalars)


def per_device(
    ens_control,
    static_control,
    member_perturb,
    member_group,
    localize_rate,
    static_rate,
    static_scale,
    obs_index,
    obs_frac,
    obs_layer,
    obs_kind,
    obs_precision,
):
    members, levels, rows, cells = ens_control.shape
    nvars = static_control.shape[1]
    fields = members + nvars
    copies = lax.axis_size("grp")
    blocks = obs_index.shape[0] // BLOCK
    dims = (members, nvars, levels, rows, cells, blocks, copies)
    plane = levels * rows
    strip = (fields, SWEEPS * levels, cells)

    ens = ens_control.reshape(members, plane, cells)
    stat = static_control.reshape(nvars, plane, cells)
    perturb = member_perturb.reshape(members, nvars, plane, cells)
    rates = [member_group, localize_rate, static_rate]

    side_a, side_b = exchange(*call(pack_kernel, dims, [strip, strip], [ens, stat]))

    scale = jnp.broadcast_to(static_scale[0][:, :, None], (nvars, levels, cells))
    kind_ids = jnp.arange(obs_precision.shape[0], dtype=jnp.int32)
    weight = jnp.sum(
        jnp.where(obs_kind[:, None] == kind_ids[None, :], obs_precision[None, :], 0.0), axis=1
    )
    key = obs_layer * (rows * cells) + obs_index
    key, frac, weight = lax.sort((key, obs_frac, weight), num_keys=1, is_stable=False)
    key, frac, weight = (x.reshape(-1, cells) for x in (key, frac, weight))

    table_rows = nvars * plane + BLOCK
    (seen,) = call(
        forward_kernel,
        dims,
        [(copies,) + key.shape],
        [ens, stat, perturb, scale, side_a, side_b, key, frac],
        [key] + rates,
        [pltpu.VMEM((fields, plane, cells), jnp.float32), pltpu.VMEM((table_rows, 2 * cells), jnp.bfloat16)],
    )
    parts = lax.all_to_all(seen, "grp", 0, 0)
    source, side_a, side_b = call(
        scatter_kernel,
        dims,
        [(fields, plane, cells), strip, strip],
        [parts, key, frac, weight, perturb, scale],
        [key],
        [pltpu.VMEM((table_rows, cells), jnp.float32), pltpu.VMEM(key.shape, jnp.float32)],
    )
    side_a, side_b = exchange(side_a, side_b)
    (before,) = call(local_kernel, dims, [(fields, plane, cells)], [source, ens, stat], rates)
    hv_ens, hv_stat = call(
        edge_kernel,
        dims,
        [(members, plane, cells), (nvars, plane, cells)],
        [before, side_a, side_b],
        rates,
        [pltpu.VMEM((fields, plane, cells), jnp.float32), pltpu.SemaphoreType.DMA((fields,))],
        ANY,
    )
    return hv_ens.reshape(ens_control.shape), hv_stat.reshape(static_control.shape)


def solution(mesh):
    placed = (
        P("grp", None, "tile", None),
        P("grp", None, None, "tile", None),
        P("grp", None, None, "tile", None),
        P("grp"),
        P(),
        P("grp"),
        P("grp", None, None),
        P("tile"),
        P("tile"),
        P("tile"),
        P("tile"),
        P(),
    )
    return jax.shard_map(
        per_device,
        mesh=mesh,
        in_specs=placed,
        out_specs=(P("grp", None, "tile", None), P("grp", None, None, "tile", None)),
        check_vma=False,
    )
```

time: 78 us -> 60.9 us (0.78)
  the two profiles are of different devices: /device:TPU:2 before, /device:TPU:25 now
where the time goes in v2:
time: 60.9 us; the launch traced here: 60.5 us
  Pallas kernels  22.8 us (37%)
  blocking collectives  14.3 us (23%)
  starting transfers between devices  6.6 us (11%)
  other arithmetic  5.83 us (10%)
  waiting for transfers between devices  5.67 us (9%)
  local copies, waits for them, and re-layouts  3.79 us (6%)
  between operations  1.48 us (2%)
    pallas_call x5, Pallas kernels, call(): pl.pallas_call(body, out_shape=tuple((jax.ShapeDtypeStruct(shape, jnp.flo...  22.8 us
    all_to_all x1, blocking collectives, per_device(): parts = lax.all_to_all(seen, 'grp', 0, 0)  14.3 us
    ppermute x2, starting transfers between devices, exchange(): lax.ppermute(side_b, 'tile', pairs_b)  5.84 us
    ppermute x2, waiting for transfers between devices, exchange(): lax.ppermute(side_b, 'tile', pairs_b)  5.67 us
    sort x1, other arithmetic, per_device(): lax.sort((key, obs_frac, weight), num_keys=1, is_stable=False)  4.98 us
    unnamed x25, local copies, waits for them, and re-layouts  3.72 us
  transfers between devices with their start and end apart: 4, of which 2 were waited for; matrix products, arithmetic and copies ran while one was open for 10% of the time, Pallas kernels for 9%

profile of v2, /device:TPU:25, one launch (start us, length us, event | category | flops | bytes accessed | tf_op | source)
XLA Modules:
  0.0 60.5 jit_solution(15804352458437427628)
XLA Ops:
  0.6 0.0 copy-start.11
  0.6 0.0 copy-start.7
  0.7 0.0 copy-start.6
  0.7 0.0 copy-start
  0.7 1.3 %copy-done = f32[1,5,32,16,128]{4,3,2,1,0:T(8,128)S(1)} copy-done((f32[1,5,32,16,128]{4,3,2,1,0:T(8,128)S(1)}, f32[1,5,32,16,128]{4,3,2,1,0:T(8,128)}, u32[]{:S(2)}) %copy-start) | copy-done | bytes 1310744
  2.0 0.0 copy-start.4
  2.0 1.0 %copy-done.4 = f32[2,32,16,128]{3,2,1,0:T(8,128)S(1)} copy-done((f32[2,32,16,128]{3,2,1,0:T(8,128)S(1)}, f32[2,32,16,128]{3,2,1,0:T(8,128)}, u32[]{:S(2)}) %copy-start.4) | copy-done | bytes 524312
  3.0 0.0 copy-start.8
  3.0 0.0 copy-start.9
  3.0 0.0 copy-start.10
  3.0 0.0 copy-start.1
  3.1 0.0 copy-start.5
  3.1 1.1 %pack_kernel.1 = (f32[7,128,128]{2,1,0:T(8,128)}, f32[7,128,128]{2,1,0:T(8,128)S(1)}) custom-call(f32[2,512,128]{2,1,0:T(8,128)S(1)} %bitcast.16, f32[5,512,128]{2,1,0:T(8,128)S(1)} %bitcast.11), custom_call_target="tpu_custom_call" | custom-call | flops 20000000 | bytes 2000000 | tf_op jit(solution)/shard_map/pack_kernel/pallas_call | solution.py:304
  4.1 0.7 %collective-permute-start = (f32[7,128,128]{2,1,0:T(8,128)}, f32[7,128,128]{2,1,0:T(8,128)S(1)}, u32[]{:S(2)}, u32[]{:S(2)}) collective-permute-start(f32[7,128,128]{2,1,0:T(8,128)} %get-tuple-element.12), channel_id=1, source_target_pairs={{0,1},{1,0},{2,3},{3,2},{4,5},{5,4},{6,7},{7,6},{8,9},{9,8},{10,11... | collective-permute-start | bytes 1376264 | tf_op jit(solution)/shard_map/ppermute | solution.py:292
  4.8 2.7 %collective-permute-start.1 = (f32[7,128,128]{2,1,0:T(8,128)S(1)}, f32[7,128,128]{2,1,0:T(8,128)S(1)}, u32[]{:S(2)}, u32[]{:S(2)}) collective-permute-start(f32[7,128,128]{2,1,0:T(8,128)S(1)} %get-tuple-element.13), channel_id=1, source_target_pairs={{1,2},{2,1},{3,4},{4,3},{5,6},{6,5},{7,8},{8,7},{9,10},{10,9},{11,... | collective-permute-start | bytes 1376264 | tf_op jit(solution)/shard_map/ppermute | solution.py:292
  8.1 0.0 copy-done.11
  8.1 0.8 %select_reduce_fusion = f32[4096]{0:T(1024)S(1)} fusion(f32[8]{0:T(128)} %param.23, s32[4096]{0:T(1024)} %param.22), kind=kLoop, calls=%fused_computation | loop fusion | flops 94208 | bytes 32800 | tf_op jit(solution)/shard_map/reduce_sum | solution.py:348
  9.0 0.0 copy-done.8
  9.0 0.0 copy-done.9
  9.0 0.0 copy-done.10
  9.0 5.0 %sort.21 = (s32[4096]{0:T(1024)S(1)}, f32[4096]{0:T(1024)S(1)}, f32[4096]{0:T(1024)S(1)}) sort(s32[4096]{0:T(1024)S(1)} %multiply_add_fusion, f32[4096]{0:T(1024)S(1)} %copy-done.10, f32[4096]{0:T(1024)S(1)} %select_reduce_fusion), dimensions={0}, to_apply=%region_1.2 | sort | flops 49152 | bytes 98304 | tf_op jit(solution)/shard_map/sort | solution.py:352
  14.0 0.0 collective-permute-done.refs_4_
  14.0 2.7 %collective-permute-done.1.refs_5_ = f32[7,128,128]{2,1,0:T(8,128)S(1)} collective-permute-done((f32[7,128,128]{2,1,0:T(8,128)S(1)}, f32[7,128,128]{2,1,0:T(8,128)S(1)}, u32[]{:S(2)}, u32[]{:S(2)}) %collective-permute-start.1) | collective-permute-done | bytes 458784 | tf_op jit(solution)/shard_map/ppermute | solution.py:292
  16.7 0.1 broadcast_in_dim.23.refs_3_.refs_5_
  16.8 0.0 copy-done.7
  16.8 0.0 copy-done.6
  16.8 0.0 copy-done.1
  16.8 0.0 copy-done.5
  16.8 0.0 copy-start.2
  16.8 1.3 %copy-done.2 = bf16[2,5,32,16,128]{4,3,2,1,0:T(8,128)(2,1)S(1)} copy-done((bf16[2,5,32,16,128]{4,3,2,1,0:T(8,128)(2,1)S(1)}, bf16[2,5,32,16,128]{4,3,2,1,0:T(8,128)(2,1)}, u32[]{:S(2)}) %copy-start.2) | copy-done | bytes 1310744
  18.1 0.0 copy-start.3
  18.1 8.1 %forward_kernel.1 = f32[8,32,128]{2,1,0:T(8,128)S(1)} custom-call(f32[2,512,128]{2,1,0:T(8,128)S(1)} %bitcast.17, f32[5,512,128]{2,1,0:T(8,128)S(1)} %bitcast.12, bf16[2,5,512,128]{3,2,1,0:T(8,128)(2,1)S(1)} %bitcast.14, f32[5,32,128]{2,1,0:T(8,128)S(1)} %broadcast_in_dim.23.refs_3_.refs_5_, f32[7,128,128]{2,1,0:T(8,128)S(1)} %collective-permute-done.refs_4_, ...), custom_call_target="tpu_custom_call" | custom-call | flops 20000000 | bytes 2000000 | tf_op jit(solution)/shard_map/forward_kernel/pallas_call | solution.py:304
  26.3 14.3 %all_to_all.5.refs_0_ = f32[8,32,128]{2,1,0:T(8,128)S(1)} all-to-all(f32[8,32,128]{2,1,0:T(8,128)S(1)} %forward_kernel.1), channel_id=1, replica_groups=mesh['grp'=8,'tile'=16] {'grp'}, dimensions={0} | all-to-all | bytes 262144 | tf_op jit(solution)/shard_map/all_to_all | solution.py:364
  40.6 0.0 copy-done.3
  40.6 3.7 %scatter_kernel.1 = (f32[7,512,128]{2,1,0:T(8,128)S(1)}, f32[7,128,128]{2,1,0:T(8,128)S(1)}, f32[7,128,128]{2,1,0:T(8,128)S(1)}) custom-call(f32[8,32,128]{2,1,0:T(8,128)S(1)} %all_to_all.5.refs_0_, s32[32,128]{1,0:T(8,128)S(1)} %bitcast.21, f32[32,128]{1,0:T(8,128)S(1)} %bitcast.24, f32[32,128]{1,0:T(8,128)S(1)} %bitcast.25, ...), custom_call_target="tpu_custom_call" | custom-call | flops 20000000 | bytes 2000000 | tf_op jit(solution)/shard_map/scatter_kernel/pallas_call | solution.py:304
  44.4 0.1 collective-permute-start.2
  44.5 3.2 %collective-permute-start.3 = (f32[7,128,128]{2,1,0:T(8,128)S(1)}, f32[7,128,128]{2,1,0:T(8,128)S(1)}, u32[]{:S(2)}, u32[]{:S(2)}) collective-permute-start(f32[7,128,128]{2,1,0:T(8,128)S(1)} %get-tuple-element.19), channel_id=1, source_target_pairs={{1,2},{2,1},{3,4},{4,3},{5,6},{6,5},{7,8},{8,7},{9,10},{10,9},{11,... | collective-permute-start | bytes 1376264 | tf_op jit(solution)/shard_map/ppermute | solution.py:292
  47.6 5.7 %local_kernel.1.refs_0_ = f32[7,512,128]{2,1,0:T(8,128)S(1)} custom-call(f32[7,512,128]{2,1,0:T(8,128)S(1)} %get-tuple-element.17.refs_0_, f32[2,512,128]{2,1,0:T(8,128)S(1)} %bitcast.18, f32[5,512,128]{2,1,0:T(8,128)S(1)} %bitcast.13, s32[2]{0:T(128)S(1)} %copy-done.6, f32[12]{0:T(128)S(1)} %copy-done.7, f32[1]{0:T(128)S(6)} %copy.17.refs_11_.refs_5_), custom_call_target="tpu_custom_call" | custom-call | flops 20000000 | bytes 2000000 | tf_op jit(solution)/shard_map/local_kernel/pallas_call | solution.py:304
  53.4 0.0 collective-permute-done.2.refs_1_
  53.4 3.0 %collective-permute-done.3.refs_2_ = f32[7,128,128]{2,1,0:T(8,128)S(1)} collective-permute-done((f32[7,128,128]{2,1,0:T(8,128)S(1)}, f32[7,128,128]{2,1,0:T(8,128)S(1)}, u32[]{:S(2)}, u32[]{:S(2)}) %collective-permute-start.3) | collective-permute-done | bytes 458784 | tf_op jit(solution)/shard_map/ppermute | solution.py:292
  56.4 4.2 %edge_kernel.1 = (f32[2,512,128]{2,1,0:T(8,128)}, f32[5,512,128]{2,1,0:T(8,128)}) custom-call(f32[7,512,128]{2,1,0:T(8,128)S(1)} %local_kernel.1.refs_0_, f32[7,128,128]{2,1,0:T(8,128)S(1)} %collective-permute-done.2.refs_1_, f32[7,128,128]{2,1,0:T(8,128)S(1)} %collective-permute-done.3.refs_2_, s32[2]{0:T(128)S(1)} %copy-done.6, f32[12]{0:T(128)S(1)} %copy-done.7, ...), custom_call_target="tpu_custom_call" | custom-call | flops 20000000 | bytes 2000000 | tf_op jit(solution)/shard_map/edge_kernel/pallas_call | solution.py:304
  (2 shorter events, 0.0 us)
Async XLA Ops:
  0.6 7.5 %copy-start.11 = (f32[1,5,32]{2,0,1:T(1,128)S(1)}, f32[1,5,32]{2,0,1:T(1,128)}, u32[]{:S(2)}) copy-start(f32[1,5,32]{2,0,1:T(1,128)} %param.18) | copy-start | bytes 1924
  0.6 16.1 %copy-start.7 = (f32[12]{0:T(128)S(1)}, f32[12]{0:T(128)}, u32[]{:S(2)}) copy-start(f32[12]{0:T(128)} %refs_4_.3) | copy-start | bytes 148
  0.7 16.1 %copy-start.6 = (s32[2]{0:T(128)S(1)}, s32[2]{0:T(128)}, u32[]{:S(2)}) copy-start(s32[2]{0:T(128)} %refs_3_.3) | copy-start | bytes 28
  0.7 1.3 %copy-start = (f32[1,5,32,16,128]{4,3,2,1,0:T(8,128)S(1)}, f32[1,5,32,16,128]{4,3,2,1,0:T(8,128)}, u32[]{:S(2)}) copy-start(f32[1,5,32,16,128]{4,3,2,1,0:T(8,128)} %param.13) | copy-start | bytes 3932164
  2.0 1.0 %copy-start.4 = (f32[2,32,16,128]{3,2,1,0:T(8,128)S(1)}, f32[2,32,16,128]{3,2,1,0:T(8,128)}, u32[]{:S(2)}) copy-start(f32[2,32,16,128]{3,2,1,0:T(8,128)} %param.12) | copy-start | bytes 1572868
  3.0 5.9 %copy-start.8 = (s32[4096]{0:T(1024)S(1)}, s32[4096]{0:T(1024)}, u32[]{:S(2)}) copy-start(s32[4096]{0:T(1024)} %param.19) | copy-start | bytes 49156
  3.0 5.9 %copy-start.9 = (s32[4096]{0:T(1024)S(1)}, s32[4096]{0:T(1024)}, u32[]{:S(2)}) copy-start(s32[4096]{0:T(1024)} %param.21) | copy-start | bytes 49156
  3.0 6.0 %copy-start.10 = (f32[4096]{0:T(1024)S(1)}, f32[4096]{0:T(1024)}, u32[]{:S(2)}) copy-start(f32[4096]{0:T(1024)} %param.20) | copy-start | bytes 49156
  3.0 13.8 %copy-start.1 = (f32[1,5,32,16,128]{4,3,2,1,0:T(8,128)S(1)}, f32[1,5,32,16,128]{4,3,2,1,0:T(8,128)}, u32[]{:S(2)}) copy-start(f32[1,5,32,16,128]{4,3,2,1,0:T(8,128)} %param.13) | copy-start | bytes 3932164
  3.1 13.8 %copy-start.5 = (f32[2,32,16,128]{3,2,1,0:T(8,128)S(1)}, f32[2,32,16,128]{3,2,1,0:T(8,128)}, u32[]{:S(2)}) copy-start(f32[2,32,16,128]{3,2,1,0:T(8,128)} %param.12) | copy-start | bytes 1572868
  4.1 9.9 %collective-permute-start = (f32[7,128,128]{2,1,0:T(8,128)}, f32[7,128,128]{2,1,0:T(8,128)S(1)}, u32[]{:S(2)}, u32[]{:S(2)}) collective-permute-start(f32[7,128,128]{2,1,0:T(8,128)} %get-tuple-element.12), channel_id=1, source_target_pairs={{0,1},{1,0},{2,3},{3,2},{4,5},{5,4},{6,7},{7,6},{8,9},{9,8},{10,11... | collective-permute-start | bytes 1376264 | tf_op jit(solution)/shard_map/ppermute | solution.py:292
  4.8 11.9 %collective-permute-start.1 = (f32[7,128,128]{2,1,0:T(8,128)S(1)}, f32[7,128,128]{2,1,0:T(8,128)S(1)}, u32[]{:S(2)}, u32[]{:S(2)}) collective-permute-start(f32[7,128,128]{2,1,0:T(8,128)S(1)} %get-tuple-element.13), channel_id=1, source_target_pairs={{1,2},{2,1},{3,4},{4,3},{5,6},{6,5},{7,8},{8,7},{9,10},{10,9},{11,... | collective-permute-start | bytes 1376264 | tf_op jit(solution)/shard_map/ppermute | solution.py:292
  16.8 1.3 %copy-start.2 = (bf16[2,5,32,16,128]{4,3,2,1,0:T(8,128)(2,1)S(1)}, bf16[2,5,32,16,128]{4,3,2,1,0:T(8,128)(2,1)}, u32[]{:S(2)}) copy-start(bf16[2,5,32,16,128]{4,3,2,1,0:T(8,128)(2,1)} %param.14) | copy-start | bytes 3932164
  18.1 22.5 %copy-start.3 = (bf16[2,5,32,16,128]{4,3,2,1,0:T(8,128)(2,1)S(1)}, bf16[2,5,32,16,128]{4,3,2,1,0:T(8,128)(2,1)}, u32[]{:S(2)}) copy-start(bf16[2,5,32,16,128]{4,3,2,1,0:T(8,128)(2,1)} %param.14) | copy-start | bytes 3932164
  44.4 9.0 %collective-permute-start.2 = (f32[7,128,128]{2,1,0:T(8,128)S(1)}, f32[7,128,128]{2,1,0:T(8,128)S(1)}, u32[]{:S(2)}, u32[]{:S(2)}) collective-permute-start(f32[7,128,128]{2,1,0:T(8,128)S(1)} %get-tuple-element.18), channel_id=1, source_target_pairs={{0,1},{1,0},{2,3},{3,2},{4,5},{5,4},{6,7},{7,6},{8,9},{9,8},{10,11... | collective-permute-start | bytes 1376264 | tf_op jit(solution)/shard_map/ppermute | solution.py:292
  44.5 11.9 %collective-permute-start.3 = (f32[7,128,128]{2,1,0:T(8,128)S(1)}, f32[7,128,128]{2,1,0:T(8,128)S(1)}, u32[]{:S(2)}, u32[]{:S(2)}) collective-permute-start(f32[7,128,128]{2,1,0:T(8,128)S(1)} %get-tuple-element.19), channel_id=1, source_target_pairs={{1,2},{2,1},{3,4},{4,3},{5,6},{6,5},{7,8},{8,7},{9,10},{10,9},{11,... | collective-permute-start | bytes 1376264 | tf_op jit(solution)/shard_map/ppermute | solution.py:292

commit v3 on v2

--- a/solution.py
+++ b/solution.py
@@ -1,5 +1,8 @@
+import math
+
 import jax
 import jax.numpy as jnp
+import numpy as np
 from jax import lax
 from jax.experimental import pallas as pl
 from jax.experimental.pallas import tpu as pltpu
@@ -10,32 +13,91 @@
 ALIGN = 16
 
 
-def sweep(planes, wanted, rows, rate, inside):
-    shape = next(iter(planes.values())).shape
-    cells = shape[1]
-    lane = lax.broadcasted_iota(jnp.int32, shape, 1)
+def along_x(planes, wanted, rows, rate, inside):
     factors = [(1.0 - 4.0 * rate, rate)] + [((1.0 - 4.0 * rate) * side, rate * side) for side in inside]
-    swept = {}
+    result = {}
     for x in wanted:
         keep, share = factors[1 if x < 0 else 2 if x >= rows else 0]
-        here = planes.get(x)
-        beside = [planes[near] for near in (x - 1, x + 1) if near in planes]
-        if here is not None:
-            beside.append(jnp.where(lane == 0, 0.0, pltpu.roll(here, 1, 1)))
-            beside.append(jnp.where(lane == cells - 1, 0.0, pltpu.roll(here, cells - 1, 1)))
-        if not beside:
-            continue
-        total = beside[0]
-        for more in beside[1:]:
-            total = total + more
-        swept[x] = share * total if here is None else keep * here + share * total
-    return swept
-
-
-def spread(planes, first, last, rows, rate, inside):
+        total = None
+        for near in (x - 1, x + 1):
+            if near in planes:
+                total = planes[near] if total is None else total + planes[near]
+        if total is not None:
+            total = share * total
+        if x in planes:
+            total = keep * planes[x] if total is None else keep * planes[x] + total
+        if total is not None:
+            result[x] = total
+    return result
+
+
+def powers_along_x(planes, first, last, rows, rate, inside):
+    stages = [planes]
     for left in range(SWEEPS - 1, -1, -1):
-        planes = sweep(planes, range(first - left, last + left + 1), rows, rate, inside)
-    return planes
+        stages.append(along_x(stages[-1], range(first - left, last + left + 1), rows, rate, inside))
+    return stages
+
+
+def binomial(j, rate):
+    factor = float(math.comb(SWEEPS, j))
+    for number in range(j):
+        factor = factor * rate
+    return factor
+
+
+def along_y(value):
+    cells = value.shape[1]
+    lane = lax.broadcasted_iota(jnp.int32, value.shape, 1)
+    below = jnp.where(lane == 0, 0.0, pltpu.roll(value, 1, 1))
+    return below + jnp.where(lane == cells - 1, 0.0, pltpu.roll(value, cells - 1, 1))
+
+
+def spread_rolled(planes, first, last, rows, rate, inside):
+    stages = powers_along_x(planes, first, last, rows, rate, inside)
+    result = {}
+    for x in range(first, last + 1):
+        total = None
+        for j in range(SWEEPS, -1, -1):
+            if total is not None:
+                total = along_y(total)
+            term = stages[SWEEPS - j].get(x)
+            if term is not None:
+                term = term if j == 0 else binomial(j, rate) * term
+                total = term if total is None else total + term
+        result[x] = total
+    return result
+
+
+def halves(value):
+    high = value.astype(jnp.bfloat16)
+    low = (value - high.astype(jnp.float32)).astype(jnp.bfloat16)
+    return high, low
+
+
+def y_powers(cells):
+    once = np.eye(cells, k=1) + np.eye(cells, k=-1)
+    stack = []
+    for j in range(1, SWEEPS + 1):
+        stack += [np.linalg.matrix_power(once, j)] * 2
+    return jnp.asarray(np.concatenate(stack), jnp.bfloat16)
+
+
+GROUP = 4
+
+
+def spread_product(planes, rows, rate, inside, powers):
+    stages = powers_along_x(planes, 0, rows - 1, rows, rate, inside)
+    levels = planes[0].shape[0]
+    result = {}
+    for first in range(0, rows, GROUP):
+        columns = []
+        for j in range(1, SWEEPS + 1):
+            term = jnp.concatenate([stages[SWEEPS - j][x] for x in range(first, first + GROUP)], axis=0)
+            columns += halves(binomial(j, rate) * term)
+        product = jnp.dot(jnp.concatenate(columns, axis=1), powers[...], preferred_element_type=jnp.float32)
+        for at in range(GROUP):
+            result[first + at] = stages[SWEEPS][first + at] + product[at * levels : (at + 1) * levels]
+    return result
 
 
 def rate_of(field, members, group, localize, static):
@@ -89,12 +151,6 @@
     return jnp.where(spot == row, 1.0, 0.0).astype(jnp.bfloat16)
 
 
-def halves(value):
-    high = value.astype(jnp.bfloat16)
-    low = (value - high.astype(jnp.float32)).astype(jnp.bfloat16)
-    return high, low
-
-
 def window_of(bound, block, cells):
     parts = BLOCK // bound.shape[1]
     shift = cells.bit_length() - 1
@@ -137,33 +193,72 @@
     lax.fori_loop(0, nvars, of_group, 0)
 
 
-def pack_kernel(dims, ens, stat, side_a, side_b):
-    members, nvars, levels, rows, cells, blocks, copies = dims
-    for begin, side in zip(begins(rows), (side_a, side_b)):
-        for field in range(members + nvars):
+def fetches(dims, ens, stat, into, sems):
+    members, nvars = dims[:2]
+    parts = [ens.at[m] for m in range(members)] + [stat.at[v] for v in range(nvars)]
+    return [pltpu.make_async_copy(part, into.at[field], sems.at[field]) for field, part in enumerate(parts)]
+
+
+def pack_kernel(dims, ens, stat, side_a, side_b, held, sems):
+    members, nvars, levels, rows, cells, blocks, copies = dims
+    loads = fetches(dims, ens, stat, held, sems)
+    for load in loads:
+        load.start()
+    for field, load in enumerate(loads):
+        load.wait()
+        for begin, side in zip(begins(rows), (side_a, side_b)):
             for j in range(SWEEPS):
-                source, at = (ens, field) if field < members else (stat, field - members)
-                side[field, pl.ds(j * levels, levels), :] = source[at, pl.ds(begin + j, levels, stride=rows), :]
-
-
-def forward_kernel(dims, ens, stat, perturb, scale, side_a, side_b, key, frac, bound, group, localize, static, out, smooth, table):
+                side[field, pl.ds(j * levels, levels), :] = held[field, pl.ds(begin + j, levels, stride=rows), :]
+
+
+def own_kernel(dims, powers, ens, stat, group, localize, static, out, held, sems):
+    members, nvars, levels, rows, cells, blocks, copies = dims
+    inside = neighbours()
+    loads = fetches(dims, ens, stat, held, sems)
+    for load in loads:
+        load.start()
+    for load in loads:
+        load.wait()
+
+    def of_field(member, at, field):
+        planes = {x: held[field, pl.ds(x, levels, stride=rows), :] for x in range(rows)}
+        rate = rate_of(field if member else None, members, group, localize, static)
+        planes = spread_product(planes, rows, rate, inside, powers)
+        for x in range(rows):
+            out[field, pl.ds(x * levels, levels), :] = planes[x]
+
+    each_field(members, nvars, of_field)
+
+
+def with_sides(dims, own, side_a, side_b, field, rate):
+    members, nvars, levels, rows, cells, blocks, copies = dims
+    lower, upper = sides_of(side_a, side_b, field, levels)
+    lower = spread_rolled({j - SWEEPS: lower[j] for j in range(SWEEPS)}, 0, SWEEPS - 1, rows, rate, (1.0, 1.0))
+    upper = spread_rolled({rows + j: upper[j] for j in range(SWEEPS)}, rows - SWEEPS, rows - 1, rows, rate, (1.0, 1.0))
+    planes = {}
+    for x in range(rows):
+        planes[x] = own[field, pl.ds(x * levels, levels), :]
+        for extra in (lower, upper):
+            if x in extra:
+                planes[x] = planes[x] + extra[x]
+    return planes
+
+
+def forward_kernel(dims, own, scale, side_a, side_b, key, frac, perturb_far, bound, group, localize, static, out, smooth, table, perturb, sem):
     members, nvars, levels, rows, cells, blocks, copies = dims
     shift = cells.bit_length() - 1
-    inside = neighbours()
+    load = pltpu.make_async_copy(perturb_far, perturb, sem)
+    load.start()
 
     def of_field(member, at, field):
-        source = ens if member else stat
-        planes = {x: source[at, pl.ds(x, levels, stride=rows), :] for x in range(rows)}
-        lower, upper = sides_of(side_a, side_b, field, levels)
-        for j in range(SWEEPS):
-            planes[j - SWEEPS], planes[rows + j] = lower[j], upper[j]
         rate = rate_of(field if member else None, members, group, localize, static)
-        planes = spread(planes, 0, rows - 1, rows, rate, inside)
+        planes = with_sides(dims, own, side_a, side_b, field, rate)
         for x in range(rows):
             value = planes[x] if member else planes[x] * scale[at]
             smooth[field, pl.ds(x, levels, stride=rows), :] = value
 
     each_field(members, nvars, of_field)
+    load.wait()
     plane = levels * rows
     for v in range(nvars):
         total = smooth[members + v]
@@ -243,23 +338,26 @@
                 side[field, pl.ds(j * levels, levels), :] = source[field, pl.ds(begin + j, levels, stride=rows), :]
 
 
-def local_kernel(dims, source, ens, stat, group, localize, static, hv):
+def local_kernel(dims, powers, source, ens, stat, group, localize, static, out, held, sems):
     members, nvars, levels, rows, cells, blocks, copies = dims
     inside = neighbours()
+    loads = fetches(dims, ens, stat, held, sems)
+    for load in loads:
+        load.start()
+    for load in loads:
+        load.wait()
 
     def of_field(member, at, field):
-        control = ens if member else stat
         planes = {x: source[field, pl.ds(x, levels, stride=rows), :] for x in range(rows)}
         rate = rate_of(field if member else None, members, group, localize, static)
-        planes = spread(planes, 0, rows - 1, rows, rate, inside)
+        planes = spread_product(planes, rows, rate, inside, powers)
         for x in range(rows):
-            spot = pl.ds(x, levels, stride=rows)
-            hv[field, spot, :] = control[at, spot, :] + planes[x]
+            out[field, pl.ds(x * levels, levels), :] = held[field, pl.ds(x, levels, stride=rows), :] + planes[x]
 
     each_field(members, nvars, of_field)
 
 
-def edge_kernel(dims, before, side_a, side_b, group, localize, static, hv_ens, hv_stat, after, sems):
+def edge_kernel(dims, own, side_a, side_b, group, localize, static, hv_ens, hv_stat, after, sems):
     members, nvars, levels, rows, cells, blocks, copies = dims
 
     def copy_of(member, at, field):
@@ -268,17 +366,9 @@
 
     def of_field(member, at, field):
         rate = rate_of(field if member else None, members, group, localize, static)
-        lower, upper = sides_of(side_a, side_b, field, levels)
-        lower = spread({j - SWEEPS: lower[j] for j in range(SWEEPS)}, 0, SWEEPS - 1, rows, rate, (1.0, 1.0))
-        upper = spread({rows + j: upper[j] for j in range(SWEEPS)}, rows - SWEEPS, rows - 1, rows, rate, (1.0, 1.0))
+        planes = with_sides(dims, own, side_a, side_b, field, rate)
         for x in range(rows):
-            spot = pl.ds(x, levels, stride=rows)
-            value = before[field, spot, :]
-            if x < SWEEPS:
-                value = value + lower[x]
-            if x >= rows - SWEEPS:
-                value = value + upper[x]
-            after[field, spot, :] = value
+            after[field, pl.ds(x, levels, stride=rows), :] = planes[x]
         copy_of(member, at, field).start()
 
     each_field(members, nvars, of_field)
@@ -294,23 +384,24 @@
 
 VMEM = pl.BlockSpec(memory_space=pltpu.VMEM)
 SMEM = pl.BlockSpec(memory_space=pltpu.SMEM)
-ANY = pl.BlockSpec(memory_space=pl.ANY)
-
-
-def call(kernel, dims, outs, ins, scalars=(), scratch=(), out_spec=VMEM, cost=2_000_000):
+HBM = pl.BlockSpec(memory_space=pltpu.HBM)
+
+
+def call(kernel, dims, outs, ins, far=(), scalars=(), scratch=(), out_spec=VMEM, cost=2_000_000):
     def body(*refs):
         kernel(dims, *refs)
 
+    far = [pltpu.with_memory_space_constraint(x, pltpu.HBM) for x in far]
     return pl.pallas_call(
         body,
         out_shape=tuple(jax.ShapeDtypeStruct(shape, jnp.float32) for shape in outs),
-        in_specs=[VMEM] * len(ins) + [SMEM] * len(scalars),
+        in_specs=[VMEM] * len(ins) + [HBM] * len(far) + [SMEM] * len(scalars),
         out_specs=tuple([out_spec] * len(outs)),
         scratch_shapes=list(scratch),
         compiler_params=pltpu.CompilerParams(vmem_limit_bytes=40 * 1024 * 1024),
         cost_estimate=pl.CostEstimate(flops=cost * 10, bytes_accessed=cost, transcendentals=0),
         name=kernel.__name__,
-    )(*ins, *scalars)
+    )(*ins, *far, *scalars)
 
 
 def per_device(
@@ -341,7 +432,10 @@
     perturb = member_perturb.reshape(members, nvars, plane, cells)
     rates = [member_group, localize_rate, static_rate]
 
-    side_a, side_b = exchange(*call(pack_kernel, dims, [strip, strip], [ens, stat]))
+    fetched = [pltpu.VMEM((fields, plane, cells), jnp.float32), pltpu.SemaphoreType.DMA((fields,))]
+    powers = y_powers(cells)
+
+    side_a, side_b = exchange(*call(pack_kernel, dims, [strip, strip], [], [ens, stat], [], fetched))
 
     scale = jnp.broadcast_to(static_scale[0][:, :, None], (nvars, levels, cells))
     kind_ids = jnp.arange(obs_precision.shape[0], dtype=jnp.int32)
@@ -353,13 +447,20 @@
     key, frac, weight = (x.reshape(-1, cells) for x in (key, frac, weight))
 
     table_rows = nvars * plane + BLOCK
+    (own,) = call(own_kernel, dims, [(fields, plane, cells)], [powers], [ens, stat], rates, fetched)
     (seen,) = call(
         forward_kernel,
         dims,
         [(copies,) + key.shape],
-        [ens, stat, perturb, scale, side_a, side_b, key, frac],
+        [own, scale, side_a, side_b, key, frac],
+        [perturb],
         [key] + rates,
-        [pltpu.VMEM((fields, plane, cells), jnp.float32), pltpu.VMEM((table_rows, 2 * cells), jnp.bfloat16)],
+        [
+            pltpu.VMEM((fields, plane, cells), jnp.float32),
+            pltpu.VMEM((table_rows, 2 * cells), jnp.bfloat16),
+            pltpu.VMEM(perturb.shape, perturb.dtype),
+            pltpu.SemaphoreType.DMA(()),
+        ],
     )
     parts = lax.all_to_all(seen, "grp", 0, 0)
     source, side_a, side_b = call(
@@ -367,19 +468,21 @@
         dims,
         [(fields, plane, cells), strip, strip],
         [parts, key, frac, weight, perturb, scale],
+        [],
         [key],
         [pltpu.VMEM((table_rows, cells), jnp.float32), pltpu.VMEM(key.shape, jnp.float32)],
     )
     side_a, side_b = exchange(side_a, side_b)
-    (before,) = call(local_kernel, dims, [(fields, plane, cells)], [source, ens, stat], rates)
+    (own,) = call(local_kernel, dims, [(fields, plane, cells)], [powers, source], [ens, stat], rates, fetched)
     hv_ens, hv_stat = call(
         edge_kernel,
         dims,
         [(members, plane, cells), (nvars, plane, cells)],
-        [before, side_a, side_b],
+        [own, side_a, side_b],
+        [],
         rates,
         [pltpu.VMEM((fields, plane, cells), jnp.float32), pltpu.SemaphoreType.DMA((fields,))],
-        ANY,
+        HBM,
     )
     return hv_ens.reshape(ens_control.shape), hv_stat.reshape(static_control.shape)
 

time: 60.9 us -> 58.4 us (0.959)
  the two profiles are of different devices: /device:TPU:25 before, /device:TPU:2 now
where the time goes in v3:
time: 58.4 us; the launch traced here: 58.1 us
  Pallas kernels  24.9 us (43%)
  blocking collectives  15.2 us (26%)
  starting transfers between devices  8.5 us (15%)
  other arithmetic  5.1 us (9%)
  waiting for transfers between devices  2.82 us (5%)
  between operations  1.55 us (3%)
    pallas_call x6, Pallas kernels, call(): pl.pallas_call(body, out_shape=tuple((jax.ShapeDtypeStruct(shape, jnp.flo...  24.9 us
    all_to_all x1, blocking collectives, per_device(): parts = lax.all_to_all(seen, 'grp', 0, 0)  15.2 us
    ppermute x2, starting transfers between devices, exchange(): lax.ppermute(side_b, 'tile', pairs_b)  8.33 us
    sort x1, other arithmetic, per_device(): lax.sort((key, obs_frac, weight), num_keys=1, is_stable=False)  4.98 us
    ppermute x2, waiting for transfers between devices, exchange(): lax.ppermute(side_b, 'tile', pairs_b)  2.81 us
  transfers between devices with their start and end apart: 4, of which 1 were waited for; matrix products, arithmetic and copies ran while one was open for 9% of the time, Pallas kernels for 19%

profile of v3, /device:TPU:2, one launch (start us, length us, event | category | flops | bytes accessed | tf_op | source)
XLA Modules:
  0.0 58.1 jit_solution(2906171343836225460)
XLA Ops:
  0.6 0.0 copy-start.1
  0.6 0.0 copy-start.8
  0.7 0.0 copy-start.9
  0.7 0.0 copy-start.7
  0.7 0.0 copy-start.5
  0.7 0.0 copy-start.4
  0.7 0.0 copy-start.6
  0.7 0.0 copy-start.3
  0.7 0.0 copy-start.2
  0.7 1.6 %pack_kernel.1 = (f32[7,128,128]{2,1,0:T(8,128)S(1)}, f32[7,128,128]{2,1,0:T(8,128)S(1)}) custom-call(f32[2,512,128]{2,1,0:T(8,128)} %bitcast.23, f32[5,512,128]{2,1,0:T(8,128)} %bitcast.20), custom_call_target="tpu_custom_call" | custom-call | flops 20000000 | bytes 2000000 | tf_op jit(solution)/shard_map/pack_kernel/pallas_call | solution.py:395
  2.4 0.1 collective-permute-start
  2.5 5.0 %collective-permute-start.1 = (f32[7,128,128]{2,1,0:T(8,128)S(1)}, f32[7,128,128]{2,1,0:T(8,128)S(1)}, u32[]{:S(2)}, u32[]{:S(2)}) collective-permute-start(f32[7,128,128]{2,1,0:T(8,128)S(1)} %get-tuple-element.13), channel_id=1, source_target_pairs={{1,2},{2,1},{3,4},{4,3},{5,6},{6,5},{7,8},{8,7},{9,10},{10,9},{11,... | collective-permute-start | bytes 1376264 | tf_op jit(solution)/shard_map/ppermute | solution.py:382
  8.1 0.0 copy-done.8
  8.1 0.0 copy-done.9
  8.1 0.0 copy-done.7
  8.1 0.1 select_reduce_fusion
  8.3 0.0 copy-done.5
  8.3 0.0 copy-done.4
  8.3 0.0 copy-done.6
  8.3 5.0 %sort.21 = (s32[4096]{0:T(1024)S(1)}, f32[4096]{0:T(1024)S(1)}, f32[4096]{0:T(1024)S(1)}) sort(s32[4096]{0:T(1024)S(1)} %multiply_add_fusion, f32[4096]{0:T(1024)S(1)} %copy-done.6, f32[4096]{0:T(1024)S(1)} %select_reduce_fusion), dimensions={0}, to_apply=%region_1.2 | sort | flops 49152 | bytes 98304 | tf_op jit(solution)/shard_map/sort | solution.py:446
  13.3 0.0 copy-done.1
  13.3 0.0 copy-done.3
  13.3 0.0 copy-done.2
  13.3 5.6 %own_kernel.1.refs_0_ = f32[7,512,128]{2,1,0:T(8,128)S(1)} custom-call(bf16[1024,128]{1,0:T(8,128)(2,1)S(1)} %copy-done.1, f32[2,512,128]{2,1,0:T(8,128)} %bitcast.24, f32[5,512,128]{2,1,0:T(8,128)} %bitcast.21, s32[2]{0:T(128)S(1)} %copy-done.2, f32[12]{0:T(128)S(1)} %copy-done.3, f32[1]{0:T(128)S(6)} %copy.18.refs_5_.refs_10_.refs_6_), custom_call_target="tpu_custom_call" | custom-call | flops 20000000 | bytes 2000000 | tf_op jit(solution)/shard_map/own_kernel/pallas_call | solution.py:395
  18.9 0.0 collective-permute-done.refs_2_
  18.9 0.0 collective-permute-done.1.refs_3_
  18.9 0.1 broadcast_in_dim.23.refs_1_.refs_5_
  19.0 0.0 copy-start
  19.0 4.9 %forward_kernel.1 = f32[8,32,128]{2,1,0:T(8,128)S(1)} custom-call(f32[7,512,128]{2,1,0:T(8,128)S(1)} %own_kernel.1.refs_0_, f32[5,32,128]{2,1,0:T(8,128)S(1)} %broadcast_in_dim.23.refs_1_.refs_5_, f32[7,128,128]{2,1,0:T(8,128)S(1)} %collective-permute-done.refs_2_, f32[7,128,128]{2,1,0:T(8,128)S(1)} %collective-permute-done.1.refs_3_, ...), custom_call_target="tpu_custom_call" | custom-call | flops 20000000 | bytes 2000000 | tf_op jit(solution)/shard_map/forward_kernel/pallas_call | solution.py:395
  23.9 15.2 %all_to_all.5.refs_0_ = f32[8,32,128]{2,1,0:T(8,128)S(1)} all-to-all(f32[8,32,128]{2,1,0:T(8,128)S(1)} %forward_kernel.1), channel_id=1, replica_groups=mesh['grp'=8,'tile'=16] {'grp'}, dimensions={0} | all-to-all | bytes 262144 | tf_op jit(solution)/shard_map/all_to_all | solution.py:465
  39.1 0.0 copy-done
  39.1 3.7 %scatter_kernel.1 = (f32[7,512,128]{2,1,0:T(8,128)S(1)}, f32[7,128,128]{2,1,0:T(8,128)S(1)}, f32[7,128,128]{2,1,0:T(8,128)S(1)}) custom-call(f32[8,32,128]{2,1,0:T(8,128)S(1)} %all_to_all.5.refs_0_, s32[32,128]{1,0:T(8,128)S(1)} %bitcast.15, f32[32,128]{1,0:T(8,128)S(1)} %bitcast.18, f32[32,128]{1,0:T(8,128)S(1)} %bitcast.19, ...), custom_call_target="tpu_custom_call" | custom-call | flops 20000000 | bytes 2000000 | tf_op jit(solution)/shard_map/scatter_kernel/pallas_call | solution.py:395
  42.8 0.1 collective-permute-start.2
  42.9 3.3 %collective-permute-start.3 = (f32[7,128,128]{2,1,0:T(8,128)S(1)}, f32[7,128,128]{2,1,0:T(8,128)S(1)}, u32[]{:S(2)}, u32[]{:S(2)}) collective-permute-start(f32[7,128,128]{2,1,0:T(8,128)S(1)} %get-tuple-element.19), channel_id=1, source_target_pairs={{1,2},{2,1},{3,4},{4,3},{5,6},{6,5},{7,8},{8,7},{9,10},{10,9},{11,... | collective-permute-start | bytes 1376264 | tf_op jit(solution)/shard_map/ppermute | solution.py:382
  46.2 5.7 %local_kernel.1.refs_0_ = f32[7,512,128]{2,1,0:T(8,128)S(1)} custom-call(bf16[1024,128]{1,0:T(8,128)(2,1)S(1)} %copy-done.1, f32[7,512,128]{2,1,0:T(8,128)S(1)} %get-tuple-element.17.refs_1_, f32[2,512,128]{2,1,0:T(8,128)} %bitcast.25, f32[5,512,128]{2,1,0:T(8,128)} %bitcast.22, s32[2]{0:T(128)S(1)} %copy-done.2, f32[12]{0:T(128)S(1)} %copy-done.3, ...), custom_call_target="tpu_custom_call" | custom-call | flops 20000000 | bytes 2000000 | tf_op jit(solution)/shard_map/local_kernel/pallas_call | solution.py:395
  52.0 0.0 collective-permute-done.2.refs_1_
  52.0 2.8 %collective-permute-done.3.refs_2_ = f32[7,128,128]{2,1,0:T(8,128)S(1)} collective-permute-done((f32[7,128,128]{2,1,0:T(8,128)S(1)}, f32[7,128,128]{2,1,0:T(8,128)S(1)}, u32[]{:S(2)}, u32[]{:S(2)}) %collective-permute-start.3) | collective-permute-done | bytes 458784 | tf_op jit(solution)/shard_map/ppermute | solution.py:382
  54.8 3.3 %edge_kernel.1 = (f32[2,512,128]{2,1,0:T(8,128)}, f32[5,512,128]{2,1,0:T(8,128)}) custom-call(f32[7,512,128]{2,1,0:T(8,128)S(1)} %local_kernel.1.refs_0_, f32[7,128,128]{2,1,0:T(8,128)S(1)} %collective-permute-done.2.refs_1_, f32[7,128,128]{2,1,0:T(8,128)S(1)} %collective-permute-done.3.refs_2_, s32[2]{0:T(128)S(1)} %copy-done.2, f32[12]{0:T(128)S(1)} %copy-done.3, ...), custom_call_target="tpu_custom_call" | custom-call | flops 20000000 | bytes 2000000 | tf_op jit(solution)/shard_map/edge_kernel/pallas_call | solution.py:395
  (2 shorter events, 0.0 us)
Async XLA Ops:
  0.6 12.7 %copy-start.1 = (bf16[1024,128]{1,0:T(8,128)(2,1)S(1)}, bf16[1024,128]{1,0:T(8,128)(2,1)}, u32[]{:S(2)}) copy-start(bf16[1024,128]{1,0:T(8,128)(2,1)} %constant.6.clone.refs_0_) | copy-start | bytes 786436
  0.6 7.5 %copy-start.8 = (f32[1,5,32]{2,0,1:T(1,128)S(1)}, f32[1,5,32]{2,0,1:T(1,128)}, u32[]{:S(2)}) copy-start(f32[1,5,32]{2,0,1:T(1,128)} %param.19) | copy-start | bytes 1924
  0.7 7.5 %copy-start.9 = (f32[8]{0:T(128)S(1)}, f32[8]{0:T(128)}, u32[]{:S(2)}) copy-start(f32[8]{0:T(128)} %param.24) | copy-start | bytes 100
  0.7 7.5 %copy-start.7 = (s32[4096]{0:T(1024)S(1)}, s32[4096]{0:T(1024)}, u32[]{:S(2)}) copy-start(s32[4096]{0:T(1024)} %param.23) | copy-start | bytes 49156
  0.7 7.6 %copy-start.5 = (s32[4096]{0:T(1024)S(1)}, s32[4096]{0:T(1024)}, u32[]{:S(2)}) copy-start(s32[4096]{0:T(1024)} %param.22) | copy-start | bytes 49156
  0.7 7.6 %copy-start.4 = (s32[4096]{0:T(1024)S(1)}, s32[4096]{0:T(1024)}, u32[]{:S(2)}) copy-start(s32[4096]{0:T(1024)} %param.20) | copy-start | bytes 49156
  0.7 7.6 %copy-start.6 = (f32[4096]{0:T(1024)S(1)}, f32[4096]{0:T(1024)}, u32[]{:S(2)}) copy-start(f32[4096]{0:T(1024)} %param.21) | copy-start | bytes 49156
  0.7 12.6 %copy-start.3 = (f32[12]{0:T(128)S(1)}, f32[12]{0:T(128)}, u32[]{:S(2)}) copy-start(f32[12]{0:T(128)} %refs_4_.5) | copy-start | bytes 148
  0.7 12.6 %copy-start.2 = (s32[2]{0:T(128)S(1)}, s32[2]{0:T(128)}, u32[]{:S(2)}) copy-start(s32[2]{0:T(128)} %refs_3_.3) | copy-start | bytes 28
  2.4 16.5 %collective-permute-start = (f32[7,128,128]{2,1,0:T(8,128)S(1)}, f32[7,128,128]{2,1,0:T(8,128)S(1)}, u32[]{:S(2)}, u32[]{:S(2)}) collective-permute-start(f32[7,128,128]{2,1,0:T(8,128)S(1)} %get-tuple-element.12), channel_id=1, source_target_pairs={{0,1},{1,0},{2,3},{3,2},{4,5},{5,4},{6,7},{7,6},{8,9},{9,8},{10,11... | collective-permute-start | bytes 1376264 | tf_op jit(solution)/shard_map/ppermute | solution.py:382
  2.5 16.5 %collective-permute-start.1 = (f32[7,128,128]{2,1,0:T(8,128)S(1)}, f32[7,128,128]{2,1,0:T(8,128)S(1)}, u32[]{:S(2)}, u32[]{:S(2)}) collective-permute-start(f32[7,128,128]{2,1,0:T(8,128)S(1)} %get-tuple-element.13), channel_id=1, source_target_pairs={{1,2},{2,1},{3,4},{4,3},{5,6},{6,5},{7,8},{8,7},{9,10},{10,9},{11,... | collective-permute-start | bytes 1376264 | tf_op jit(solution)/shard_map/ppermute | solution.py:382
  19.0 20.0 %copy-start = (bf16[2,5,32,16,128]{4,3,2,1,0:T(8,128)(2,1)S(1)}, bf16[2,5,32,16,128]{4,3,2,1,0:T(8,128)(2,1)}, u32[]{:S(2)}) copy-start(bf16[2,5,32,16,128]{4,3,2,1,0:T(8,128)(2,1)} %param.15) | copy-start | bytes 3932164
  42.8 9.2 %collective-permute-start.2 = (f32[7,128,128]{2,1,0:T(8,128)S(1)}, f32[7,128,128]{2,1,0:T(8,128)S(1)}, u32[]{:S(2)}, u32[]{:S(2)}) collective-permute-start(f32[7,128,128]{2,1,0:T(8,128)S(1)} %get-tuple-element.18), channel_id=1, source_target_pairs={{0,1},{1,0},{2,3},{3,2},{4,5},{5,4},{6,7},{7,6},{8,9},{9,8},{10,11... | collective-permute-start | bytes 1376264 | tf_op jit(solution)/shard_map/ppermute | solution.py:382
  42.9 11.9 %collective-permute-start.3 = (f32[7,128,128]{2,1,0:T(8,128)S(1)}, f32[7,128,128]{2,1,0:T(8,128)S(1)}, u32[]{:S(2)}, u32[]{:S(2)}) collective-permute-start(f32[7,128,128]{2,1,0:T(8,128)S(1)} %get-tuple-element.19), channel_id=1, source_target_pairs={{1,2},{2,1},{3,4},{4,3},{5,6},{6,5},{7,8},{8,7},{9,10},{10,9},{11,... | collective-permute-start | bytes 1376264 | tf_op jit(solution)/shard_map/ppermute | solution.py:382

commit v4 on v3

--- a/solution.py
+++ b/solution.py
@@ -76,34 +76,35 @@
 
 def y_powers(cells):
     once = np.eye(cells, k=1) + np.eye(cells, k=-1)
-    stack = []
+    row = np.concatenate([np.linalg.matrix_power(once, j) for j in range(1, SWEEPS + 1)], axis=1)
+    return jnp.asarray(np.concatenate([row, row], axis=0), jnp.bfloat16)
+
+
+GROUP = 8
+
+
+def spread_product(planes, rows, rate, inside, powers):
+    levels, cells = planes[0].shape
+    terms = [{} for j in range(SWEEPS)]
+    for first in range(0, rows, GROUP):
+        both = jnp.concatenate(halves(jnp.concatenate([planes[x] for x in range(first, first + GROUP)], axis=0)), axis=1)
+        product = jnp.dot(both, powers[...], preferred_element_type=jnp.float32)
+        for at in range(GROUP):
+            for j in range(SWEEPS):
+                terms[j][first + at] = product[at * levels : (at + 1) * levels, j * cells : (j + 1) * cells]
+    result = planes
     for j in range(1, SWEEPS + 1):
-        stack += [np.linalg.matrix_power(once, j)] * 2
-    return jnp.asarray(np.concatenate(stack), jnp.bfloat16)
-
-
-GROUP = 4
-
-
-def spread_product(planes, rows, rate, inside, powers):
-    stages = powers_along_x(planes, 0, rows - 1, rows, rate, inside)
-    levels = planes[0].shape[0]
-    result = {}
-    for first in range(0, rows, GROUP):
-        columns = []
-        for j in range(1, SWEEPS + 1):
-            term = jnp.concatenate([stages[SWEEPS - j][x] for x in range(first, first + GROUP)], axis=0)
-            columns += halves(binomial(j, rate) * term)
-        product = jnp.dot(jnp.concatenate(columns, axis=1), powers[...], preferred_element_type=jnp.float32)
-        for at in range(GROUP):
-            result[first + at] = stages[SWEEPS][first + at] + product[at * levels : (at + 1) * levels]
+        left = SWEEPS - j
+        result = along_x(result, range(-left, rows + left), rows, rate, inside)
+        factor = binomial(j, rate)
+        for x in range(rows):
+            result[x] = result[x] + factor * terms[j - 1][x]
     return result
 
 
 def rate_of(field, members, group, localize, static):
-    if field is None:
-        return static[0]
-    return localize[group[field]]
+    member = jnp.minimum(field, members - 1)
+    return jnp.where(field < members, localize[group[member]], static[0])
 
 
 def neighbours():
@@ -180,28 +181,18 @@
         lax.fori_loop(0, blocks, of_block, 0)
 
 
-def each_field(members, nvars, visit):
-    def of_member(m, carry):
-        visit(True, m, m)
+def each_field(fields, visit):
+    def step(field, carry):
+        visit(field)
         return carry
 
-    def of_group(v, carry):
-        visit(False, v, members + v)
-        return carry
-
-    lax.fori_loop(0, members, of_member, 0)
-    lax.fori_loop(0, nvars, of_group, 0)
-
-
-def fetches(dims, ens, stat, into, sems):
-    members, nvars = dims[:2]
+    lax.fori_loop(0, fields, step, 0)
+
+
+def pack_kernel(dims, ens, stat, side_a, side_b, held, sems):
+    members, nvars, levels, rows, cells, blocks, copies = dims
     parts = [ens.at[m] for m in range(members)] + [stat.at[v] for v in range(nvars)]
-    return [pltpu.make_async_copy(part, into.at[field], sems.at[field]) for field, part in enumerate(parts)]
-
-
-def pack_kernel(dims, ens, stat, side_a, side_b, held, sems):
-    members, nvars, levels, rows, cells, blocks, copies = dims
-    loads = fetches(dims, ens, stat, held, sems)
+    loads = [pltpu.make_async_copy(part, held.at[field], sems.at[field]) for field, part in enumerate(parts)]
     for load in loads:
         load.start()
     for field, load in enumerate(loads):
@@ -211,23 +202,18 @@
                 side[field, pl.ds(j * levels, levels), :] = held[field, pl.ds(begin + j, levels, stride=rows), :]
 
 
-def own_kernel(dims, powers, ens, stat, group, localize, static, out, held, sems):
+def own_kernel(dims, powers, held, group, localize, static, out):
     members, nvars, levels, rows, cells, blocks, copies = dims
     inside = neighbours()
-    loads = fetches(dims, ens, stat, held, sems)
-    for load in loads:
-        load.start()
-    for load in loads:
-        load.wait()
-
-    def of_field(member, at, field):
+
+    def of_field(field):
         planes = {x: held[field, pl.ds(x, levels, stride=rows), :] for x in range(rows)}
-        rate = rate_of(field if member else None, members, group, localize, static)
+        rate = rate_of(field, members, group, localize, static)
         planes = spread_product(planes, rows, rate, inside, powers)
         for x in range(rows):
             out[field, pl.ds(x * levels, levels), :] = planes[x]
 
-    each_field(members, nvars, of_field)
+    each_field(members + nvars, of_field)
 
 
 def with_sides(dims, own, side_a, side_b, field, rate):
@@ -250,14 +236,13 @@
     load = pltpu.make_async_copy(perturb_far, perturb, sem)
     load.start()
 
-    def of_field(member, at, field):
-        rate = rate_of(field if member else None, members, group, localize, static)
+    def of_field(field):
+        rate = rate_of(field, members, group, localize, static)
         planes = with_sides(dims, own, side_a, side_b, field, rate)
         for x in range(rows):
-            value = planes[x] if member else planes[x] * scale[at]
-            smooth[field, pl.ds(x, levels, stride=rows), :] = value
-
-    each_field(members, nvars, of_field)
+            smooth[field, pl.ds(x, levels, stride=rows), :] = planes[x] * scale[field]
+
+    each_field(members + nvars, of_field)
     load.wait()
     plane = levels * rows
     for v in range(nvars):
@@ -328,51 +313,55 @@
         for v in range(1, nvars):
             total = total + perturb[m, v].astype(jnp.float32) * gradient[v * plane : (v + 1) * plane, :]
         source[m] = total
-    for v in range(nvars):
-        for x in range(rows):
-            at = pl.ds(x, levels, stride=rows)
-            source[members + v, at, :] = gradient[pl.ds(v * plane + x, levels, stride=rows), :] * scale[v]
     for begin, side in zip(begins(rows), (side_a, side_b)):
         for field in range(members + nvars):
             for j in range(SWEEPS):
-                side[field, pl.ds(j * levels, levels), :] = source[field, pl.ds(begin + j, levels, stride=rows), :]
-
-
-def local_kernel(dims, powers, source, ens, stat, group, localize, static, out, held, sems):
+                if field < members:
+                    strip = source[field, pl.ds(begin + j, levels, stride=rows), :]
+                else:
+                    at = (field - members) * plane + begin + j
+                    strip = gradient[pl.ds(at, levels, stride=rows), :] * scale[field]
+                side[field, pl.ds(j * levels, levels), :] = strip
+
+
+def local_kernel(dims, powers, source, gradient, scale, held, group, localize, static, out):
     members, nvars, levels, rows, cells, blocks, copies = dims
     inside = neighbours()
-    loads = fetches(dims, ens, stat, held, sems)
-    for load in loads:
-        load.start()
-    for load in loads:
-        load.wait()
-
-    def of_field(member, at, field):
-        planes = {x: source[field, pl.ds(x, levels, stride=rows), :] for x in range(rows)}
-        rate = rate_of(field if member else None, members, group, localize, static)
+    plane = levels * rows
+
+    def of_field(field, planes):
+        rate = rate_of(field, members, group, localize, static)
         planes = spread_product(planes, rows, rate, inside, powers)
         for x in range(rows):
             out[field, pl.ds(x * levels, levels), :] = held[field, pl.ds(x, levels, stride=rows), :] + planes[x]
 
-    each_field(members, nvars, of_field)
+    def of_member(m):
+        of_field(m, {x: source[m, pl.ds(x, levels, stride=rows), :] for x in range(rows)})
+
+    def of_group(v):
+        field = members + v
+        planes = {x: gradient[pl.ds(v * plane + x, levels, stride=rows), :] * scale[field] for x in range(rows)}
+        of_field(field, planes)
+
+    each_field(members, of_member)
+    each_field(nvars, of_group)
 
 
 def edge_kernel(dims, own, side_a, side_b, group, localize, static, hv_ens, hv_stat, after, sems):
     members, nvars, levels, rows, cells, blocks, copies = dims
 
-    def copy_of(member, at, field):
-        out = hv_ens if member else hv_stat
-        return pltpu.make_async_copy(after.at[field], out.at[at], sems.at[field])
-
-    def of_field(member, at, field):
-        rate = rate_of(field if member else None, members, group, localize, static)
+    writes = []
+    for field in range(members + nvars):
+        rate = rate_of(field, members, group, localize, static)
         planes = with_sides(dims, own, side_a, side_b, field, rate)
         for x in range(rows):
             after[field, pl.ds(x, levels, stride=rows), :] = planes[x]
-        copy_of(member, at, field).start()
-
-    each_field(members, nvars, of_field)
-    each_field(members, nvars, lambda member, at, field: copy_of(member, at, field).wait())
+        out = hv_ens.at[field] if field < members else hv_stat.at[field - members]
+        write = pltpu.make_async_copy(after.at[field], out, sems.at[field])
+        write.start()
+        writes.append(write)
+    for write in writes:
+        write.wait()
 
 
 def exchange(side_a, side_b):
@@ -432,12 +421,14 @@
     perturb = member_perturb.reshape(members, nvars, plane, cells)
     rates = [member_group, localize_rate, static_rate]
 
-    fetched = [pltpu.VMEM((fields, plane, cells), jnp.float32), pltpu.SemaphoreType.DMA((fields,))]
+    whole = (fields, plane, cells)
     powers = y_powers(cells)
-
-    side_a, side_b = exchange(*call(pack_kernel, dims, [strip, strip], [], [ens, stat], [], fetched))
-
-    scale = jnp.broadcast_to(static_scale[0][:, :, None], (nvars, levels, cells))
+    copying = [pltpu.SemaphoreType.DMA((fields,))]
+    side_a, side_b, held = call(pack_kernel, dims, [strip, strip, whole], [], [ens, stat], [], copying)
+    side_a, side_b = exchange(side_a, side_b)
+
+    scale = jnp.concatenate([jnp.ones((members, levels), jnp.float32), static_scale[0]])
+    scale = jnp.broadcast_to(scale[:, :, None], (fields, levels, cells))
     kind_ids = jnp.arange(obs_precision.shape[0], dtype=jnp.int32)
     weight = jnp.sum(
         jnp.where(obs_kind[:, None] == kind_ids[None, :], obs_precision[None, :], 0.0), axis=1
@@ -447,7 +438,7 @@
     key, frac, weight = (x.reshape(-1, cells) for x in (key, frac, weight))
 
     table_rows = nvars * plane + BLOCK
-    (own,) = call(own_kernel, dims, [(fields, plane, cells)], [powers], [ens, stat], rates, fetched)
+    (own,) = call(own_kernel, dims, [whole], [powers, held], [], rates)
     (seen,) = call(
         forward_kernel,
         dims,
@@ -456,24 +447,24 @@
         [perturb],
         [key] + rates,
         [
-            pltpu.VMEM((fields, plane, cells), jnp.float32),
+            pltpu.VMEM(whole, jnp.float32),
             pltpu.VMEM((table_rows, 2 * cells), jnp.bfloat16),
             pltpu.VMEM(perturb.shape, perturb.dtype),
             pltpu.SemaphoreType.DMA(()),
         ],
     )
     parts = lax.all_to_all(seen, "grp", 0, 0)
-    source, side_a, side_b = call(
+    source, side_a, side_b, gradient = call(
         scatter_kernel,
         dims,
-        [(fields, plane, cells), strip, strip],
+        [(members, plane, cells), strip, strip, (table_rows, cells)],
         [parts, key, frac, weight, perturb, scale],
         [],
         [key],
-        [pltpu.VMEM((table_rows, cells), jnp.float32), pltpu.VMEM(key.shape, jnp.float32)],
+        [pltpu.VMEM(key.shape, jnp.float32)],
     )
     side_a, side_b = exchange(side_a, side_b)
-    (own,) = call(local_kernel, dims, [(fields, plane, cells)], [powers, source], [ens, stat], rates, fetched)
+    (own,) = call(local_kernel, dims, [whole], [powers, source, gradient, scale, held], [], rates)
     hv_ens, hv_stat = call(
         edge_kernel,
         dims,
@@ -481,7 +472,7 @@
         [own, side_a, side_b],
         [],
         rates,
-        [pltpu.VMEM((fields, plane, cells), jnp.float32), pltpu.SemaphoreType.DMA((fields,))],
+        [pltpu.VMEM(whole, jnp.float32), pltpu.SemaphoreType.DMA((fields,))],
         HBM,
     )
     return hv_ens.reshape(ens_control.shape), hv_stat.reshape(static_control.shape)

time: 58.4 us -> 58.7 us (level)
  Pallas kernels: 24.9 us -> 21.6 us
  waiting for transfers between devices: 2.82 us -> 4.97 us
  other arithmetic: 5.1 us -> 6.44 us
    pallas_call x6, Pallas kernels: 24.9 us -> 21.6 us  [call(): pl.pallas_call(body, out_shape=tuple((jax.ShapeDtypeStruct(shape, jnp.flo...]
    ppermute x2, waiting for transfers between devices: 2.81 us -> 4.97 us  [exchange(): lax.ppermute(side_b, 'tile', pairs_b)]
    sort x1, other arithmetic: 4.98 us -> 5.72 us  [per_device(): lax.sort((key, obs_frac, weight), num_keys=1, is_stable=False)]
    reduce_sum x1, other arithmetic: 0.11 us -> 0.71 us  [per_device(): jnp.sum(jnp.where(obs_kind[:, None] == kind_ids[None, :], obs_precision[N...]
  transfers between devices with their start and end apart: 4 -> 4, of which waited for: 1 -> 1; matrix products, arithmetic and copies ran while one was open for 9% -> 11% of each run, Pallas kernels for 19% -> 12%
where the time goes in v4:
time: 58.7 us; the launch traced here: 58.3 us
  Pallas kernels  21.6 us (37%)
  blocking collectives  15.2 us (26%)
  starting transfers between devices  8.47 us (14%)
  other arithmetic  6.44 us (11%)
  waiting for transfers between devices  4.97 us (8%)
  between operations  1.52 us (3%)
    pallas_call x6, Pallas kernels, call(): pl.pallas_call(body, out_shape=tuple((jax.ShapeDtypeStruct(shape, jnp.flo...  21.6 us
    all_to_all x1, blocking collectives, per_device(): parts = lax.all_to_all(seen, 'grp', 0, 0)  15.2 us
    ppermute x2, starting transfers between devices, exchange(): lax.ppermute(side_b, 'tile', pairs_b)  8.3 us
    sort x1, other arithmetic, per_device(): lax.sort((key, obs_frac, weight), num_keys=1, is_stable=False)  5.72 us
    ppermute x2, waiting for transfers between devices, exchange(): lax.ppermute(side_b, 'tile', pairs_b)  4.97 us
  transfers between devices with their start and end apart: 4, of which 1 were waited for; matrix products, arithmetic and copies ran while one was open for 11% of the time, Pallas kernels for 12%

profile of v4, /device:TPU:2, one launch (start us, length us, event | category | flops | bytes accessed | tf_op | source)
XLA Modules:
  0.0 58.3 jit_solution(6902655695655797001)
XLA Ops:
  0.6 0.0 copy-start.1
  0.6 0.0 copy-start.7
  0.7 0.0 copy-start.8
  0.7 0.0 copy-start.6
  0.7 0.0 copy-start.5
  0.7 0.0 copy-start.4
  0.7 0.0 copy-start.3
  0.7 0.0 copy-start.2
  0.7 2.4 %pack_kernel.1 = (f32[7,128,128]{2,1,0:T(8,128)}, f32[7,128,128]{2,1,0:T(8,128)S(1)}, f32[7,512,128]{2,1,0:T(8,128)S(1)}) custom-call(f32[2,512,128]{2,1,0:T(8,128)} %bitcast.21, f32[5,512,128]{2,1,0:T(8,128)} %bitcast.20), custom_call_target="tpu_custom_call" | custom-call | flops 20000000 | bytes 2000000 | tf_op jit(solution)/shard_map/pack_kernel/pallas_call | solution.py:384
  3.1 0.1 collective-permute-start
  3.2 5.0 %collective-permute-start.1 = (f32[7,128,128]{2,1,0:T(8,128)S(1)}, f32[7,128,128]{2,1,0:T(8,128)S(1)}, u32[]{:S(2)}, u32[]{:S(2)}) collective-permute-start(f32[7,128,128]{2,1,0:T(8,128)S(1)} %get-tuple-element.16), channel_id=1, source_target_pairs={{1,2},{2,1},{3,4},{4,3},{5,6},{6,5},{7,8},{8,7},{9,10},{10,9},{11,... | collective-permute-start | bytes 1376264 | tf_op jit(solution)/shard_map/ppermute | solution.py:371
  8.9 0.0 copy-done.7
  8.9 0.0 copy-done.8
  8.9 0.0 copy-done.6
  8.9 0.7 %select_reduce_fusion = f32[4096]{0:T(1024)} fusion(f32[8]{0:T(128)S(1)} %copy-done.8, s32[4096]{0:T(1024)S(1)} %copy-done.6), kind=kLoop, calls=%fused_computation | loop fusion | flops 94208 | bytes 32800 | tf_op jit(solution)/shard_map/reduce_sum | solution.py:433
  9.6 0.0 copy-done.5
  9.6 0.0 copy-done.4
  9.6 5.7 %sort.21 = (s32[4096]{0:T(1024)S(1)}, f32[4096]{0:T(1024)S(1)}, f32[4096]{0:T(1024)S(1)}) sort(s32[4096]{0:T(1024)S(1)} %multiply_add_fusion, f32[4096]{0:T(1024)} %param.21, f32[4096]{0:T(1024)} %select_reduce_fusion), dimensions={0}, to_apply=%region_1.2 | sort | flops 49152 | bytes 98304 | tf_op jit(solution)/shard_map/sort | solution.py:437
  15.4 0.0 copy-done.1
  15.4 0.0 copy-done.3
  15.4 0.0 copy-done.2
  15.4 3.3 %own_kernel.1.refs_0_ = f32[7,512,128]{2,1,0:T(8,128)S(1)} custom-call(bf16[256,512]{1,0:T(8,128)(2,1)S(1)} %copy-done.1, f32[7,512,128]{2,1,0:T(8,128)S(1)} %get-tuple-element.14.refs_1_.refs_4_, s32[2]{0:T(128)S(1)} %copy-done.2, f32[12]{0:T(128)S(1)} %copy-done.3, f32[1]{0:T(128)S(6)} %copy.18.refs_4_.refs_10_.refs_7_.refs_5_), custom_call_target="tpu_custom_call" | custom-call | flops 20000000 | bytes 2000000 | tf_op jit(solution)/shard_map/own_kernel/pallas_call | solution.py:384
  18.7 0.0 collective-permute-done.refs_2_
  18.7 0.0 collective-permute-done.1.refs_3_
  18.7 0.1 broadcast_in_dim.10.refs_1_.refs_5_.refs_3_
  18.8 0.0 copy-start
  18.8 4.8 %forward_kernel.1 = f32[8,32,128]{2,1,0:T(8,128)S(1)} custom-call(f32[7,512,128]{2,1,0:T(8,128)S(1)} %own_kernel.1.refs_0_, f32[7,32,128]{2,1,0:T(8,128)S(1)} %broadcast_in_dim.10.refs_1_.refs_5_.refs_3_, f32[7,128,128]{2,1,0:T(8,128)S(1)} %collective-permute-done.refs_2_, f32[7,128,128]{2,1,0:T(8,128)S(1)} %collective-permute-done.1.refs_3_, ...), custom_call_target="tpu_custom_call" | custom-call | flops 20000000 | bytes 2000000 | tf_op jit(solution)/shard_map/forward_kernel/pallas_call | solution.py:384
  23.6 15.2 %all_to_all.5.refs_0_ = f32[8,32,128]{2,1,0:T(8,128)S(1)} all-to-all(f32[8,32,128]{2,1,0:T(8,128)S(1)} %forward_kernel.1), channel_id=1, replica_groups=mesh['grp'=8,'tile'=16] {'grp'}, dimensions={0} | all-to-all | bytes 262144 | tf_op jit(solution)/shard_map/all_to_all | solution.py:456
  38.8 0.0 copy-done
  38.8 3.0 %scatter_kernel.1 = (f32[2,512,128]{2,1,0:T(8,128)S(1)}, f32[7,128,128]{2,1,0:T(8,128)S(1)}, f32[7,128,128]{2,1,0:T(8,128)S(1)}, f32[2816,128]{1,0:T(8,128)S(1)}) custom-call(f32[8,32,128]{2,1,0:T(8,128)S(1)} %all_to_all.5.refs_0_, s32[32,128]{1,0:T(8,128)S(1)} %bitcast.15, f32[32,128]{1,0:T(8,128)S(1)} %bitcast.18, f32[32,128]{1,0:T(8,128)S(1)} %bitcast.19, ...), custom_call_target="tpu_custom_call" | custom-call | flops 20000000 | bytes 2000000 | tf_op jit(solution)/shard_map/scatter_kernel/pallas_call | solution.py:384
  41.8 0.1 collective-permute-start.2
  41.9 3.3 %collective-permute-start.3 = (f32[7,128,128]{2,1,0:T(8,128)S(1)}, f32[7,128,128]{2,1,0:T(8,128)S(1)}, u32[]{:S(2)}, u32[]{:S(2)}) collective-permute-start(f32[7,128,128]{2,1,0:T(8,128)S(1)} %get-tuple-element.23), channel_id=1, source_target_pairs={{1,2},{2,1},{3,4},{4,3},{5,6},{6,5},{7,8},{8,7},{9,10},{10,9},{11,... | collective-permute-start | bytes 1376264 | tf_op jit(solution)/shard_map/ppermute | solution.py:371
  45.2 3.6 %local_kernel.1.refs_0_ = f32[7,512,128]{2,1,0:T(8,128)S(1)} custom-call(bf16[256,512]{1,0:T(8,128)(2,1)S(1)} %copy-done.1, f32[2,512,128]{2,1,0:T(8,128)S(1)} %get-tuple-element.20.refs_1_, f32[2816,128]{1,0:T(8,128)S(1)} %get-tuple-element.21.refs_2_, f32[7,32,128]{2,1,0:T(8,128)S(1)} %broadcast_in_dim.10.refs_1_.refs_5_.refs_3_, ...), custom_call_target="tpu_custom_call" | custom-call | flops 20000000 | bytes 2000000 | tf_op jit(solution)/shard_map/local_kernel/pallas_call | solution.py:384
  48.8 0.0 collective-permute-done.2.refs_1_
  48.8 5.0 %collective-permute-done.3.refs_2_ = f32[7,128,128]{2,1,0:T(8,128)S(1)} collective-permute-done((f32[7,128,128]{2,1,0:T(8,128)S(1)}, f32[7,128,128]{2,1,0:T(8,128)S(1)}, u32[]{:S(2)}, u32[]{:S(2)}) %collective-permute-start.3) | collective-permute-done | bytes 458784 | tf_op jit(solution)/shard_map/ppermute | solution.py:371
  53.8 4.5 %edge_kernel.1 = (f32[2,512,128]{2,1,0:T(8,128)}, f32[5,512,128]{2,1,0:T(8,128)}) custom-call(f32[7,512,128]{2,1,0:T(8,128)S(1)} %local_kernel.1.refs_0_, f32[7,128,128]{2,1,0:T(8,128)S(1)} %collective-permute-done.2.refs_1_, f32[7,128,128]{2,1,0:T(8,128)S(1)} %collective-permute-done.3.refs_2_, s32[2]{0:T(128)S(1)} %copy-done.2, f32[12]{0:T(128)S(1)} %copy-done.3, ...), custom_call_target="tpu_custom_call" | custom-call | flops 20000000 | bytes 2000000 | tf_op jit(solution)/shard_map/edge_kernel/pallas_call | solution.py:384
  (3 shorter events, 0.0 us)
Async XLA Ops:
  0.6 14.7 %copy-start.1 = (bf16[256,512]{1,0:T(8,128)(2,1)S(1)}, bf16[256,512]{1,0:T(8,128)(2,1)}, u32[]{:S(2)}) copy-start(bf16[256,512]{1,0:T(8,128)(2,1)} %constant.8.clone.refs_0_) | copy-start | bytes 786436
  0.6 8.2 %copy-start.7 = (f32[1,5,32]{2,0,1:T(1,128)S(1)}, f32[1,5,32]{2,0,1:T(1,128)}, u32[]{:S(2)}) copy-start(f32[1,5,32]{2,0,1:T(1,128)} %param.19) | copy-start | bytes 1924
  0.7 8.2 %copy-start.8 = (f32[8]{0:T(128)S(1)}, f32[8]{0:T(128)}, u32[]{:S(2)}) copy-start(f32[8]{0:T(128)} %param.24) | copy-start | bytes 100
  0.7 8.2 %copy-start.6 = (s32[4096]{0:T(1024)S(1)}, s32[4096]{0:T(1024)}, u32[]{:S(2)}) copy-start(s32[4096]{0:T(1024)} %param.23) | copy-start | bytes 49156
  0.7 8.9 %copy-start.5 = (s32[4096]{0:T(1024)S(1)}, s32[4096]{0:T(1024)}, u32[]{:S(2)}) copy-start(s32[4096]{0:T(1024)} %param.22) | copy-start | bytes 49156
  0.7 8.9 %copy-start.4 = (s32[4096]{0:T(1024)S(1)}, s32[4096]{0:T(1024)}, u32[]{:S(2)}) copy-start(s32[4096]{0:T(1024)} %param.20) | copy-start | bytes 49156
  0.7 14.7 %copy-start.3 = (f32[12]{0:T(128)S(1)}, f32[12]{0:T(128)}, u32[]{:S(2)}) copy-start(f32[12]{0:T(128)} %refs_4_.2) | copy-start | bytes 148
  0.7 14.7 %copy-start.2 = (s32[2]{0:T(128)S(1)}, s32[2]{0:T(128)}, u32[]{:S(2)}) copy-start(s32[2]{0:T(128)} %refs_3_.3) | copy-start | bytes 28
  3.1 15.5 %collective-permute-start = (f32[7,128,128]{2,1,0:T(8,128)}, f32[7,128,128]{2,1,0:T(8,128)S(1)}, u32[]{:S(2)}, u32[]{:S(2)}) collective-permute-start(f32[7,128,128]{2,1,0:T(8,128)} %get-tuple-element.15), channel_id=1, source_target_pairs={{0,1},{1,0},{2,3},{3,2},{4,5},{5,4},{6,7},{7,6},{8,9},{9,8},{10,11... | collective-permute-start | bytes 1376264 | tf_op jit(solution)/shard_map/ppermute | solution.py:371
  3.2 15.5 %collective-permute-start.1 = (f32[7,128,128]{2,1,0:T(8,128)S(1)}, f32[7,128,128]{2,1,0:T(8,128)S(1)}, u32[]{:S(2)}, u32[]{:S(2)}) collective-permute-start(f32[7,128,128]{2,1,0:T(8,128)S(1)} %get-tuple-element.16), channel_id=1, source_target_pairs={{1,2},{2,1},{3,4},{4,3},{5,6},{6,5},{7,8},{8,7},{9,10},{10,9},{11,... | collective-permute-start | bytes 1376264 | tf_op jit(solution)/shard_map/ppermute | solution.py:371
  18.8 20.0 %copy-start = (bf16[2,5,32,16,128]{4,3,2,1,0:T(8,128)(2,1)S(1)}, bf16[2,5,32,16,128]{4,3,2,1,0:T(8,128)(2,1)}, u32[]{:S(2)}) copy-start(bf16[2,5,32,16,128]{4,3,2,1,0:T(8,128)(2,1)} %param.15) | copy-start | bytes 3932164
  41.8 7.0 %collective-permute-start.2 = (f32[7,128,128]{2,1,0:T(8,128)S(1)}, f32[7,128,128]{2,1,0:T(8,128)S(1)}, u32[]{:S(2)}, u32[]{:S(2)}) collective-permute-start(f32[7,128,128]{2,1,0:T(8,128)S(1)} %get-tuple-element.22), channel_id=1, source_target_pairs={{0,1},{1,0},{2,3},{3,2},{4,5},{5,4},{6,7},{7,6},{8,9},{9,8},{10,11... | collective-permute-start | bytes 1376264 | tf_op jit(solution)/shard_map/ppermute | solution.py:371
  41.9 11.9 %collective-permute-start.3 = (f32[7,128,128]{2,1,0:T(8,128)S(1)}, f32[7,128,128]{2,1,0:T(8,128)S(1)}, u32[]{:S(2)}, u32[]{:S(2)}) collective-permute-start(f32[7,128,128]{2,1,0:T(8,128)S(1)} %get-tuple-element.23), channel_id=1, source_target_pairs={{1,2},{2,1},{3,4},{4,3},{5,6},{6,5},{7,8},{8,7},{9,10},{10,9},{11,... | collective-permute-start | bytes 1376264 | tf_op jit(solution)/shard_map/ppermute | solution.py:371

commit v5 on v4

--- a/solution.py
+++ b/solution.py
@@ -189,24 +189,34 @@
     lax.fori_loop(0, fields, step, 0)
 
 
+def load_of(field, source, at, held, sems):
+    return pltpu.make_async_copy(source.at[at], held.at[field], sems.at[field])
+
+
+def start_loads(members, nvars, ens, stat, held, sems):
+    for m in range(members):
+        load_of(m, ens, m, held, sems).start()
+    for v in range(nvars):
+        load_of(members + v, stat, v, held, sems).start()
+
+
 def pack_kernel(dims, ens, stat, side_a, side_b, held, sems):
     members, nvars, levels, rows, cells, blocks, copies = dims
-    parts = [ens.at[m] for m in range(members)] + [stat.at[v] for v in range(nvars)]
-    loads = [pltpu.make_async_copy(part, held.at[field], sems.at[field]) for field, part in enumerate(parts)]
-    for load in loads:
-        load.start()
-    for field, load in enumerate(loads):
-        load.wait()
+    start_loads(members, nvars, ens, stat, held, sems)
+    for field in range(members + nvars):
+        load_of(field, ens, 0, held, sems).wait()
         for begin, side in zip(begins(rows), (side_a, side_b)):
             for j in range(SWEEPS):
                 side[field, pl.ds(j * levels, levels), :] = held[field, pl.ds(begin + j, levels, stride=rows), :]
 
 
-def own_kernel(dims, powers, held, group, localize, static, out):
+def own_kernel(dims, powers, ens, stat, group, localize, static, out, held, sems):
     members, nvars, levels, rows, cells, blocks, copies = dims
     inside = neighbours()
+    start_loads(members, nvars, ens, stat, held, sems)
 
     def of_field(field):
+        load_of(field, ens, 0, held, sems).wait()
         planes = {x: held[field, pl.ds(x, levels, stride=rows), :] for x in range(rows)}
         rate = rate_of(field, members, group, localize, static)
         planes = spread_product(planes, rows, rate, inside, powers)
@@ -350,18 +360,20 @@
 def edge_kernel(dims, own, side_a, side_b, group, localize, static, hv_ens, hv_stat, after, sems):
     members, nvars, levels, rows, cells, blocks, copies = dims
 
-    writes = []
-    for field in range(members + nvars):
+    def write_of(field, out, at):
+        return pltpu.make_async_copy(after.at[field], out.at[at], sems.at[field])
+
+    def of_field(field, out, at):
         rate = rate_of(field, members, group, localize, static)
         planes = with_sides(dims, own, side_a, side_b, field, rate)
         for x in range(rows):
             after[field, pl.ds(x, levels, stride=rows), :] = planes[x]
-        out = hv_ens.at[field] if field < members else hv_stat.at[field - members]
-        write = pltpu.make_async_copy(after.at[field], out, sems.at[field])
-        write.start()
-        writes.append(write)
-    for write in writes:
-        write.wait()
+        write_of(field, out, at).start()
+
+    each_field(members, lambda m: of_field(m, hv_ens, m))
+    each_field(nvars, lambda v: of_field(members + v, hv_stat, v))
+    each_field(members, lambda m: write_of(m, hv_ens, m).wait())
+    each_field(nvars, lambda v: write_of(members + v, hv_stat, v).wait())
 
 
 def exchange(side_a, side_b):
@@ -387,7 +399,7 @@
         in_specs=[VMEM] * len(ins) + [HBM] * len(far) + [SMEM] * len(scalars),
         out_specs=tuple([out_spec] * len(outs)),
         scratch_shapes=list(scratch),
-        compiler_params=pltpu.CompilerParams(vmem_limit_bytes=40 * 1024 * 1024),
+        compiler_params=pltpu.CompilerParams(vmem_limit_bytes=16 * 1024 * 1024),
         cost_estimate=pl.CostEstimate(flops=cost * 10, bytes_accessed=cost, transcendentals=0),
         name=kernel.__name__,
     )(*ins, *far, *scalars)
@@ -424,7 +436,7 @@
     whole = (fields, plane, cells)
     powers = y_powers(cells)
     copying = [pltpu.SemaphoreType.DMA((fields,))]
-    side_a, side_b, held = call(pack_kernel, dims, [strip, strip, whole], [], [ens, stat], [], copying)
+    side_a, side_b = call(pack_kernel, dims, [strip, strip], [], [ens, stat], [], [pltpu.VMEM(whole, jnp.float32)] + copying)
     side_a, side_b = exchange(side_a, side_b)
 
     scale = jnp.concatenate([jnp.ones((members, levels), jnp.float32), static_scale[0]])
@@ -438,7 +450,7 @@
     key, frac, weight = (x.reshape(-1, cells) for x in (key, frac, weight))
 
     table_rows = nvars * plane + BLOCK
-    (own,) = call(own_kernel, dims, [whole], [powers, held], [], rates)
+    own, held = call(own_kernel, dims, [whole, whole], [powers], [ens, stat], rates, copying)
     (seen,) = call(
         forward_kernel,
         dims,

time: 58.7 us -> 56.3 us (0.959)
  other arithmetic: 6.44 us -> 5.1 us
  Pallas kernels: 21.6 us -> 20.7 us
    pallas_call x6, Pallas kernels: 21.6 us -> 20.7 us  [call(): pl.pallas_call(body, out_shape=tuple((jax.ShapeDtypeStruct(shape, jnp.flo...]
    sort x1, other arithmetic: 5.72 us -> 4.98 us  [per_device(): lax.sort((key, obs_frac, weight), num_keys=1, is_stable=False)]
    reduce_sum x1, other arithmetic: 0.71 us -> 0.11 us  [per_device(): jnp.sum(jnp.where(obs_kind[:, None] == kind_ids[None, :], obs_precision[N...]
  transfers between devices with their start and end apart: 4 -> 4, of which waited for: 1 -> 1; matrix products, arithmetic and copies ran while one was open for 11% -> 9% of each run, Pallas kernels for 12% -> 14%
where the time goes in v5:
time: 56.3 us; the launch traced here: 56.1 us
  Pallas kernels  20.7 us (37%)
  blocking collectives  15.2 us (27%)
  starting transfers between devices  8.5 us (15%)
  other arithmetic  5.1 us (9%)
  waiting for transfers between devices  4.95 us (9%)
  between operations  1.55 us (3%)
    pallas_call x6, Pallas kernels, call(): pl.pallas_call(body, out_shape=tuple((jax.ShapeDtypeStruct(shape, jnp.flo...  20.7 us
    all_to_all x1, blocking collectives, per_device(): parts = lax.all_to_all(seen, 'grp', 0, 0)  15.2 us
    ppermute x2, starting transfers between devices, exchange(): lax.ppermute(side_b, 'tile', pairs_b)  8.33 us
    sort x1, other arithmetic, per_device(): lax.sort((key, obs_frac, weight), num_keys=1, is_stable=False)  4.98 us
    ppermute x2, waiting for transfers between devices, exchange(): lax.ppermute(side_b, 'tile', pairs_b)  4.95 us
  transfers between devices with their start and end apart: 4, of which 1 were waited for; matrix products, arithmetic and copies ran while one was open for 9% of the time, Pallas kernels for 14%

profile of v5, /device:TPU:2, one launch (start us, length us, event | category | flops | bytes accessed | tf_op | source)
XLA Modules:
  0.0 56.1 jit_solution(8955613419149459460)
XLA Ops:
  0.6 0.0 copy-start.1
  0.6 0.0 copy-start.8
  0.7 0.0 copy-start.9
  0.7 0.0 copy-start.7
  0.7 0.0 copy-start.5
  0.7 0.0 copy-start.4
  0.7 0.0 copy-start.6
  0.7 0.0 copy-start.3
  0.7 0.0 copy-start.2
  0.7 1.6 %pack_kernel.1 = (f32[7,128,128]{2,1,0:T(8,128)S(1)}, f32[7,128,128]{2,1,0:T(8,128)S(1)}) custom-call(f32[2,512,128]{2,1,0:T(8,128)} %bitcast.22, f32[5,512,128]{2,1,0:T(8,128)} %bitcast.20), custom_call_target="tpu_custom_call" | custom-call | flops 20000000 | bytes 2000000 | tf_op jit(solution)/shard_map/pack_kernel/pallas_call | solution.py:396
  2.4 0.1 collective-permute-start
  2.5 5.0 %collective-permute-start.1 = (f32[7,128,128]{2,1,0:T(8,128)S(1)}, f32[7,128,128]{2,1,0:T(8,128)S(1)}, u32[]{:S(2)}, u32[]{:S(2)}) collective-permute-start(f32[7,128,128]{2,1,0:T(8,128)S(1)} %get-tuple-element.17), channel_id=1, source_target_pairs={{1,2},{2,1},{3,4},{4,3},{5,6},{6,5},{7,8},{8,7},{9,10},{10,9},{11,... | collective-permute-start | bytes 1376264 | tf_op jit(solution)/shard_map/ppermute | solution.py:383
  8.1 0.0 copy-done.8
  8.1 0.0 copy-done.9
  8.2 0.0 copy-done.7
  8.2 0.1 select_reduce_fusion
  8.3 0.0 copy-done.5
  8.3 0.0 copy-done.4
  8.3 0.0 copy-done.6
  8.3 5.0 %sort.21 = (s32[4096]{0:T(1024)S(1)}, f32[4096]{0:T(1024)S(1)}, f32[4096]{0:T(1024)S(1)}) sort(s32[4096]{0:T(1024)S(1)} %multiply_add_fusion, f32[4096]{0:T(1024)S(1)} %copy-done.6, f32[4096]{0:T(1024)S(1)} %select_reduce_fusion), dimensions={0}, to_apply=%region_1.2 | sort | flops 49152 | bytes 98304 | tf_op jit(solution)/shard_map/sort | solution.py:449
  13.3 0.0 copy-done.1
  13.3 0.0 copy-done.3
  13.3 0.0 copy-done.2
  13.3 4.3 %own_kernel.1 = (f32[7,512,128]{2,1,0:T(8,128)S(1)}, f32[7,512,128]{2,1,0:T(8,128)S(1)}) custom-call(bf16[256,512]{1,0:T(8,128)(2,1)S(1)} %copy-done.1, f32[2,512,128]{2,1,0:T(8,128)} %bitcast.23, f32[5,512,128]{2,1,0:T(8,128)} %bitcast.21, s32[2]{0:T(128)S(1)} %copy-done.2, f32[12]{0:T(128)S(1)} %copy-done.3, f32[1]{0:T(128)S(6)} %copy.18.refs_5_.refs_10_.refs_7_), custom_call_target="tpu_custom_call" | custom-call | flops 20000000 | bytes 2000000 | tf_op jit(solution)/shard_map/own_kernel/pallas_call | solution.py:396
  17.6 0.0 collective-permute-done.refs_2_
  17.6 0.0 collective-permute-done.1.refs_3_
  17.6 0.1 broadcast_in_dim.10.refs_1_.refs_5_.refs_3_
  17.7 0.0 copy-start
  17.7 4.8 %forward_kernel.1 = f32[8,32,128]{2,1,0:T(8,128)S(1)} custom-call(f32[7,512,128]{2,1,0:T(8,128)S(1)} %get-tuple-element.15.refs_0_, f32[7,32,128]{2,1,0:T(8,128)S(1)} %broadcast_in_dim.10.refs_1_.refs_5_.refs_3_, f32[7,128,128]{2,1,0:T(8,128)S(1)} %collective-permute-done.refs_2_, f32[7,128,128]{2,1,0:T(8,128)S(1)} %collective-permute-done.1.refs_3_, ...), custom_call_target="tpu_custom_call" | custom-call | flops 20000000 | bytes 2000000 | tf_op jit(solution)/shard_map/forward_kernel/pallas_call | solution.py:396
  22.6 15.2 %all_to_all.5.refs_0_ = f32[8,32,128]{2,1,0:T(8,128)S(1)} all-to-all(f32[8,32,128]{2,1,0:T(8,128)S(1)} %forward_kernel.1), channel_id=1, replica_groups=mesh['grp'=8,'tile'=16] {'grp'}, dimensions={0} | all-to-all | bytes 262144 | tf_op jit(solution)/shard_map/all_to_all | solution.py:468
  37.8 0.0 copy-done
  37.8 3.0 %scatter_kernel.1 = (f32[2,512,128]{2,1,0:T(8,128)S(1)}, f32[7,128,128]{2,1,0:T(8,128)S(1)}, f32[7,128,128]{2,1,0:T(8,128)S(1)}, f32[2816,128]{1,0:T(8,128)S(1)}) custom-call(f32[8,32,128]{2,1,0:T(8,128)S(1)} %all_to_all.5.refs_0_, s32[32,128]{1,0:T(8,128)S(1)} %bitcast.15, f32[32,128]{1,0:T(8,128)S(1)} %bitcast.18, f32[32,128]{1,0:T(8,128)S(1)} %bitcast.19, ...), custom_call_target="tpu_custom_call" | custom-call | flops 20000000 | bytes 2000000 | tf_op jit(solution)/shard_map/scatter_kernel/pallas_call | solution.py:396
  40.7 0.1 collective-permute-start.2
  40.8 3.3 %collective-permute-start.3 = (f32[7,128,128]{2,1,0:T(8,128)S(1)}, f32[7,128,128]{2,1,0:T(8,128)S(1)}, u32[]{:S(2)}, u32[]{:S(2)}) collective-permute-start(f32[7,128,128]{2,1,0:T(8,128)S(1)} %get-tuple-element.25), channel_id=1, source_target_pairs={{1,2},{2,1},{3,4},{4,3},{5,6},{6,5},{7,8},{8,7},{9,10},{10,9},{11,... | collective-permute-start | bytes 1376264 | tf_op jit(solution)/shard_map/ppermute | solution.py:383
  44.2 3.6 %local_kernel.1.refs_0_ = f32[7,512,128]{2,1,0:T(8,128)S(1)} custom-call(bf16[256,512]{1,0:T(8,128)(2,1)S(1)} %copy-done.1, f32[2,512,128]{2,1,0:T(8,128)S(1)} %get-tuple-element.21.refs_1_, f32[2816,128]{1,0:T(8,128)S(1)} %get-tuple-element.22.refs_2_, f32[7,32,128]{2,1,0:T(8,128)S(1)} %broadcast_in_dim.10.refs_1_.refs_5_.refs_3_, ...), custom_call_target="tpu_custom_call" | custom-call | flops 20000000 | bytes 2000000 | tf_op jit(solution)/shard_map/local_kernel/pallas_call | solution.py:396
  47.8 0.0 collective-permute-done.2.refs_1_
  47.8 4.9 %collective-permute-done.3.refs_2_ = f32[7,128,128]{2,1,0:T(8,128)S(1)} collective-permute-done((f32[7,128,128]{2,1,0:T(8,128)S(1)}, f32[7,128,128]{2,1,0:T(8,128)S(1)}, u32[]{:S(2)}, u32[]{:S(2)}) %collective-permute-start.3) | collective-permute-done | bytes 458784 | tf_op jit(solution)/shard_map/ppermute | solution.py:383
  52.7 3.3 %edge_kernel.1 = (f32[2,512,128]{2,1,0:T(8,128)}, f32[5,512,128]{2,1,0:T(8,128)}) custom-call(f32[7,512,128]{2,1,0:T(8,128)S(1)} %local_kernel.1.refs_0_, f32[7,128,128]{2,1,0:T(8,128)S(1)} %collective-permute-done.2.refs_1_, f32[7,128,128]{2,1,0:T(8,128)S(1)} %collective-permute-done.3.refs_2_, s32[2]{0:T(128)S(1)} %copy-done.2, f32[12]{0:T(128)S(1)} %copy-done.3, ...), custom_call_target="tpu_custom_call" | custom-call | flops 20000000 | bytes 2000000 | tf_op jit(solution)/shard_map/edge_kernel/pallas_call | solution.py:396
  (3 shorter events, 0.0 us)
Async XLA Ops:
  0.6 12.7 %copy-start.1 = (bf16[256,512]{1,0:T(8,128)(2,1)S(1)}, bf16[256,512]{1,0:T(8,128)(2,1)}, u32[]{:S(2)}) copy-start(bf16[256,512]{1,0:T(8,128)(2,1)} %constant.8.clone.refs_0_) | copy-start | bytes 786436
  0.6 7.5 %copy-start.8 = (f32[1,5,32]{2,0,1:T(1,128)S(1)}, f32[1,5,32]{2,0,1:T(1,128)}, u32[]{:S(2)}) copy-start(f32[1,5,32]{2,0,1:T(1,128)} %param.19) | copy-start | bytes 1924
  0.7 7.5 %copy-start.9 = (f32[8]{0:T(128)S(1)}, f32[8]{0:T(128)}, u32[]{:S(2)}) copy-start(f32[8]{0:T(128)} %param.24) | copy-start | bytes 100
  0.7 7.5 %copy-start.7 = (s32[4096]{0:T(1024)S(1)}, s32[4096]{0:T(1024)}, u32[]{:S(2)}) copy-start(s32[4096]{0:T(1024)} %param.23) | copy-start | bytes 49156
  0.7 7.6 %copy-start.5 = (s32[4096]{0:T(1024)S(1)}, s32[4096]{0:T(1024)}, u32[]{:S(2)}) copy-start(s32[4096]{0:T(1024)} %param.22) | copy-start | bytes 49156
  0.7 7.6 %copy-start.4 = (s32[4096]{0:T(1024)S(1)}, s32[4096]{0:T(1024)}, u32[]{:S(2)}) copy-start(s32[4096]{0:T(1024)} %param.20) | copy-start | bytes 49156
  0.7 7.6 %copy-start.6 = (f32[4096]{0:T(1024)S(1)}, f32[4096]{0:T(1024)}, u32[]{:S(2)}) copy-start(f32[4096]{0:T(1024)} %param.21) | copy-start | bytes 49156
  0.7 12.6 %copy-start.3 = (f32[12]{0:T(128)S(1)}, f32[12]{0:T(128)}, u32[]{:S(2)}) copy-start(f32[12]{0:T(128)} %refs_4_.3) | copy-start | bytes 148
  0.7 12.6 %copy-start.2 = (s32[2]{0:T(128)S(1)}, s32[2]{0:T(128)}, u32[]{:S(2)}) copy-start(s32[2]{0:T(128)} %refs_3_.3) | copy-start | bytes 28
  2.4 15.2 %collective-permute-start = (f32[7,128,128]{2,1,0:T(8,128)S(1)}, f32[7,128,128]{2,1,0:T(8,128)S(1)}, u32[]{:S(2)}, u32[]{:S(2)}) collective-permute-start(f32[7,128,128]{2,1,0:T(8,128)S(1)} %get-tuple-element.16), channel_id=1, source_target_pairs={{0,1},{1,0},{2,3},{3,2},{4,5},{5,4},{6,7},{7,6},{8,9},{9,8},{10,11... | collective-permute-start | bytes 1376264 | tf_op jit(solution)/shard_map/ppermute | solution.py:383
  2.5 15.2 %collective-permute-start.1 = (f32[7,128,128]{2,1,0:T(8,128)S(1)}, f32[7,128,128]{2,1,0:T(8,128)S(1)}, u32[]{:S(2)}, u32[]{:S(2)}) collective-permute-start(f32[7,128,128]{2,1,0:T(8,128)S(1)} %get-tuple-element.17), channel_id=1, source_target_pairs={{1,2},{2,1},{3,4},{4,3},{5,6},{6,5},{7,8},{8,7},{9,10},{10,9},{11,... | collective-permute-start | bytes 1376264 | tf_op jit(solution)/shard_map/ppermute | solution.py:383
  17.7 20.0 %copy-start = (bf16[2,5,32,16,128]{4,3,2,1,0:T(8,128)(2,1)S(1)}, bf16[2,5,32,16,128]{4,3,2,1,0:T(8,128)(2,1)}, u32[]{:S(2)}) copy-start(bf16[2,5,32,16,128]{4,3,2,1,0:T(8,128)(2,1)} %param.15) | copy-start | bytes 3932164
  40.7 7.0 %collective-permute-start.2 = (f32[7,128,128]{2,1,0:T(8,128)S(1)}, f32[7,128,128]{2,1,0:T(8,128)S(1)}, u32[]{:S(2)}, u32[]{:S(2)}) collective-permute-start(f32[7,128,128]{2,1,0:T(8,128)S(1)} %get-tuple-element.24), channel_id=1, source_target_pairs={{0,1},{1,0},{2,3},{3,2},{4,5},{5,4},{6,7},{7,6},{8,9},{9,8},{10,11... | collective-permute-start | bytes 1376264 | tf_op jit(solution)/shard_map/ppermute | solution.py:383
  40.8 11.9 %collective-permute-start.3 = (f32[7,128,128]{2,1,0:T(8,128)S(1)}, f32[7,128,128]{2,1,0:T(8,128)S(1)}, u32[]{:S(2)}, u32[]{:S(2)}) collective-permute-start(f32[7,128,128]{2,1,0:T(8,128)S(1)} %get-tuple-element.25), channel_id=1, source_target_pairs={{1,2},{2,1},{3,4},{4,3},{5,6},{6,5},{7,8},{8,7},{9,10},{10,9},{11,... | collective-permute-start | bytes 1376264 | tf_op jit(solution)/shard_map/ppermute | solution.py:383

commit v6 on v5

--- a/solution.py
+++ b/solution.py
@@ -201,7 +201,7 @@
 
 
 def pack_kernel(dims, ens, stat, side_a, side_b, held, sems):
-    members, nvars, levels, rows, cells, blocks, copies = dims
+    members, nvars, levels, rows, cells, blocks = dims
     start_loads(members, nvars, ens, stat, held, sems)
     for field in range(members + nvars):
         load_of(field, ens, 0, held, sems).wait()
@@ -211,7 +211,7 @@
 
 
 def own_kernel(dims, powers, ens, stat, group, localize, static, out, held, sems):
-    members, nvars, levels, rows, cells, blocks, copies = dims
+    members, nvars, levels, rows, cells, blocks = dims
     inside = neighbours()
     start_loads(members, nvars, ens, stat, held, sems)
 
@@ -227,7 +227,7 @@
 
 
 def with_sides(dims, own, side_a, side_b, field, rate):
-    members, nvars, levels, rows, cells, blocks, copies = dims
+    members, nvars, levels, rows, cells, blocks = dims
     lower, upper = sides_of(side_a, side_b, field, levels)
     lower = spread_rolled({j - SWEEPS: lower[j] for j in range(SWEEPS)}, 0, SWEEPS - 1, rows, rate, (1.0, 1.0))
     upper = spread_rolled({rows + j: upper[j] for j in range(SWEEPS)}, rows - SWEEPS, rows - 1, rows, rate, (1.0, 1.0))
@@ -241,7 +241,7 @@
 
 
 def forward_kernel(dims, own, scale, side_a, side_b, key, frac, perturb_far, bound, group, localize, static, out, smooth, table, perturb, sem):
-    members, nvars, levels, rows, cells, blocks, copies = dims
+    members, nvars, levels, rows, cells, blocks = dims
     shift = cells.bit_length() - 1
     load = pltpu.make_async_copy(perturb_far, perturb, sem)
     load.start()
@@ -280,26 +280,21 @@
     def visit(block, start):
         seen = seen_in(block, start)
         for part in range(parts):
-            out[0, pl.ds(block * parts + part, 1), :] = seen[:, part * lanes : (part + 1) * lanes]
+            out[pl.ds(block * parts + part, 1), :] = seen[:, part * lanes : (part + 1) * lanes]
 
     def visit_again(block, start):
         seen = seen_in(block, start)
         for part in range(parts):
             at = pl.ds(block * parts + part, 1)
-            out[0, at, :] = out[0, at, :] + seen[:, part * lanes : (part + 1) * lanes]
+            out[at, :] = out[at, :] + seen[:, part * lanes : (part + 1) * lanes]
 
     every_window(bound, blocks, cells, visit, visit_again)
-    for copy in range(1, copies):
-        out[copy] = out[0]
-
-
-def scatter_kernel(dims, parts, key, frac, weight, perturb, scale, bound, source, side_a, side_b, gradient, valued):
-    members, nvars, levels, rows, cells, blocks, copies = dims
+
+
+def scatter_kernel(dims, seen, others, key, frac, weight, perturb, scale, bound, source, side_a, side_b, gradient, valued):
+    members, nvars, levels, rows, cells, blocks = dims
     shift = cells.bit_length() - 1
-    seen = parts[0]
-    for copy in range(1, copies):
-        seen = seen + parts[copy]
-    valued[...] = seen * weight[...]
+    valued[...] = (seen[...] + others[...]) * weight[...]
     gradient[...] = jnp.zeros(gradient.shape, jnp.float32)
 
     def add_block(block, start):
@@ -335,7 +330,7 @@
 
 
 def local_kernel(dims, powers, source, gradient, scale, held, group, localize, static, out):
-    members, nvars, levels, rows, cells, blocks, copies = dims
+    members, nvars, levels, rows, cells, blocks = dims
     inside = neighbours()
     plane = levels * rows
 
@@ -358,7 +353,7 @@
 
 
 def edge_kernel(dims, own, side_a, side_b, group, localize, static, hv_ens, hv_stat, after, sems):
-    members, nvars, levels, rows, cells, blocks, copies = dims
+    members, nvars, levels, rows, cells, blocks = dims
 
     def write_of(field, out, at):
         return pltpu.make_async_copy(after.at[field], out.at[at], sems.at[field])
@@ -381,6 +376,16 @@
     pairs_a = [(i, i ^ 1) for i in range(count)]
     pairs_b = [(i, ((i + 1) ^ 1) - 1) for i in range(1, count - 1)]
     return lax.ppermute(side_a, "tile", pairs_a), lax.ppermute(side_b, "tile", pairs_b)
+
+
+def halved_sums(value):
+    count = lax.axis_size("grp")
+    others = None
+    for turn in (2, 6, 1) if count == 8 else [1 << bit for bit in range(count.bit_length() - 1)]:
+        if others is not None:
+            value = value + others
+        others = lax.ppermute(value, "grp", [(i, i ^ turn) for i in range(count)])
+    return value, others
 
 
 VMEM = pl.BlockSpec(memory_space=pltpu.VMEM)
@@ -422,9 +427,8 @@
     members, levels, rows, cells = ens_control.shape
     nvars = static_control.shape[1]
     fields = members + nvars
-    copies = lax.axis_size("grp")
     blocks = obs_index.shape[0] // BLOCK
-    dims = (members, nvars, levels, rows, cells, blocks, copies)
+    dims = (members, nvars, levels, rows, cells, blocks)
     plane = levels * rows
     strip = (fields, SWEEPS * levels, cells)
 
@@ -454,7 +458,7 @@
     (seen,) = call(
         forward_kernel,
         dims,
-        [(copies,) + key.shape],
+        [key.shape],
         [own, scale, side_a, side_b, key, frac],
         [perturb],
         [key] + rates,
@@ -465,12 +469,12 @@
             pltpu.SemaphoreType.DMA(()),
         ],
     )
-    parts = lax.all_to_all(seen, "grp", 0, 0)
+    seen, others = halved_sums(seen)
     source, side_a, side_b, gradient = call(
         scatter_kernel,
         dims,
         [(members, plane, cells), strip, strip, (table_rows, cells)],
-        [parts, key, frac, weight, perturb, scale],
+        [seen, others, key, frac, weight, perturb, scale],
         [],
         [key],
         [pltpu.VMEM(key.shape, jnp.float32)],

time: 56.3 us -> 56.2 us (level)
  the two profiles are of different devices: /device:TPU:2 before, /device:TPU:6 now
where the time goes in v6:
time: 56.2 us; the launch traced here: 56 us
  Pallas kernels  20.7 us (37%)
  starting transfers between devices  15.4 us (27%)
  waiting for transfers between devices  13.2 us (23%)
  other arithmetic  5.1 us (9%)
  between operations  1.56 us (3%)
    pallas_call x6, Pallas kernels, call(): pl.pallas_call(body, out_shape=tuple((jax.ShapeDtypeStruct(shape, jnp.flo...  20.7 us
    ppermute x2, starting transfers between devices, exchange(): lax.ppermute(side_b, 'tile', pairs_b)  8.03 us
    ppermute x3, waiting for transfers between devices, halved_sums(): others = lax.ppermute(value, 'grp', [(i, i ^ turn) for i in range(count)])  7.66 us
    ppermute x3, starting transfers between devices, halved_sums(): others = lax.ppermute(value, 'grp', [(i, i ^ turn) for i in range(count)])  7.17 us
    ppermute x2, waiting for transfers between devices, exchange(): lax.ppermute(side_b, 'tile', pairs_b)  5.53 us
    sort x1, other arithmetic, per_device(): lax.sort((key, obs_frac, weight), num_keys=1, is_stable=False)  4.98 us
  transfers between devices with their start and end apart: 7, of which 4 were waited for; matrix products, arithmetic and copies ran while one was open for 9% of the time, Pallas kernels for 14%

profile of v6, /device:TPU:6, one launch (start us, length us, event | category | flops | bytes accessed | tf_op | source)
XLA Modules:
  0.0 56.0 jit_solution(17855592145396537976)
XLA Ops:
  0.6 0.0 copy-start.1
  0.6 0.0 copy-start.8
  0.7 0.0 copy-start.9
  0.7 0.0 copy-start.7
  0.7 0.0 copy-start.5
  0.7 0.0 copy-start.4
  0.7 0.0 copy-start.6
  0.7 0.0 copy-start.3
  0.7 0.0 copy-start.2
  0.7 1.6 %pack_kernel.1 = (f32[7,128,128]{2,1,0:T(8,128)S(1)}, f32[7,128,128]{2,1,0:T(8,128)S(1)}) custom-call(f32[2,512,128]{2,1,0:T(8,128)} %bitcast.22, f32[5,512,128]{2,1,0:T(8,128)} %bitcast.20), custom_call_target="tpu_custom_call" | custom-call | flops 20000000 | bytes 2000000 | tf_op jit(solution)/shard_map/pack_kernel/pallas_call | solution.py:401
  2.4 0.1 collective-permute-start
  2.5 5.3 %collective-permute-start.1 = (f32[7,128,128]{2,1,0:T(8,128)S(1)}, f32[7,128,128]{2,1,0:T(8,128)S(1)}, u32[]{:S(2)}, u32[]{:S(2)}) collective-permute-start(f32[7,128,128]{2,1,0:T(8,128)S(1)} %get-tuple-element.17), channel_id=1, source_target_pairs={{1,2},{2,1},{3,4},{4,3},{5,6},{6,5},{7,8},{8,7},{9,10},{10,9},{11,... | collective-permute-start | bytes 1376264 | tf_op jit(solution)/shard_map/ppermute | solution.py:378
  8.4 0.0 copy-done.8
  8.4 0.0 copy-done.9
  8.4 0.0 copy-done.7
  8.5 0.1 select_reduce_fusion
  8.6 0.0 copy-done.5
  8.6 0.0 copy-done.4
  8.6 0.0 copy-done.6
  8.6 5.0 %sort.21 = (s32[4096]{0:T(1024)S(1)}, f32[4096]{0:T(1024)S(1)}, f32[4096]{0:T(1024)S(1)}) sort(s32[4096]{0:T(1024)S(1)} %multiply_add_fusion, f32[4096]{0:T(1024)S(1)} %copy-done.6, f32[4096]{0:T(1024)S(1)} %select_reduce_fusion), dimensions={0}, to_apply=%region_1.2 | sort | flops 49152 | bytes 98304 | tf_op jit(solution)/shard_map/sort | solution.py:453
  13.6 0.0 copy-done.1
  13.6 0.0 copy-done.3
  13.6 0.0 copy-done.2
  13.6 4.3 %own_kernel.1 = (f32[7,512,128]{2,1,0:T(8,128)S(1)}, f32[7,512,128]{2,1,0:T(8,128)S(1)}) custom-call(bf16[256,512]{1,0:T(8,128)(2,1)S(1)} %copy-done.1, f32[2,512,128]{2,1,0:T(8,128)} %bitcast.23, f32[5,512,128]{2,1,0:T(8,128)} %bitcast.21, s32[2]{0:T(128)S(1)} %copy-done.2, f32[12]{0:T(128)S(1)} %copy-done.3, f32[1]{0:T(128)S(6)} %copy.18.refs_5_.refs_10_.refs_7_), custom_call_target="tpu_custom_call" | custom-call | flops 20000000 | bytes 2000000 | tf_op jit(solution)/shard_map/own_kernel/pallas_call | solution.py:401
  17.9 0.0 collective-permute-done.refs_2_
  17.9 0.0 collective-permute-done.1.refs_3_
  17.9 0.1 broadcast_in_dim.10.refs_1_.refs_6_.refs_3_
  18.0 0.0 copy-start
  18.0 4.8 %forward_kernel.1 = f32[32,128]{1,0:T(8,128)S(1)} custom-call(f32[7,512,128]{2,1,0:T(8,128)S(1)} %get-tuple-element.15.refs_0_, f32[7,32,128]{2,1,0:T(8,128)S(1)} %broadcast_in_dim.10.refs_1_.refs_6_.refs_3_, f32[7,128,128]{2,1,0:T(8,128)S(1)} %collective-permute-done.refs_2_, f32[7,128,128]{2,1,0:T(8,128)S(1)} %collective-permute-done.1.refs_3_, ...), custom_call_target="tpu_custom_call" | custom-call | flops 20000000 | bytes 2000000 | tf_op jit(solution)/shard_map/forward_kernel/pallas_call | solution.py:401
  22.9 2.0 %collective-permute-start.2 = (f32[32,128]{1,0:T(8,128)S(1)}, f32[32,128]{1,0:T(8,128)S(1)}, u32[]{:S(2)}, u32[]{:S(2)}) collective-permute-start(f32[32,128]{1,0:T(8,128)S(1)} %forward_kernel.1), channel_id=1, source_target_pairs={{0,32},{16,48},{32,0},{48,16},{64,96},{80,112},{96,64},{112,80},{1... | collective-permute-start | bytes 49160 | tf_op jit(solution)/shard_map/ppermute | solution.py:387
  24.9 1.8 %collective-permute-done.2 = f32[32,128]{1,0:T(8,128)S(1)} collective-permute-done((f32[32,128]{1,0:T(8,128)S(1)}, f32[32,128]{1,0:T(8,128)S(1)}, u32[]{:S(2)}, u32[]{:S(2)}) %collective-permute-start.2) | collective-permute-done | bytes 16416 | tf_op jit(solution)/shard_map/ppermute | solution.py:387
  26.7 4.1 %collective-permute-start.3 = (f32[32,128]{1,0:T(8,128)S(1)}, f32[32,128]{1,0:T(8,128)S(1)}, u32[]{:S(2)}, u32[]{:S(2)}) collective-permute-start(f32[32,128]{1,0:T(8,128)S(1)} %add.12), channel_id=1, source_target_pairs={{0,96},{16,112},{32,64},{48,80},{64,32},{80,48},{96,0},{112,16},{1... | collective-permute-start | bytes 49160 | tf_op jit(solution)/shard_map/ppermute | solution.py:387
  30.7 1.7 %collective-permute-done.3 = f32[32,128]{1,0:T(8,128)S(1)} collective-permute-done((f32[32,128]{1,0:T(8,128)S(1)}, f32[32,128]{1,0:T(8,128)S(1)}, u32[]{:S(2)}, u32[]{:S(2)}) %collective-permute-start.3) | collective-permute-done | bytes 16416 | tf_op jit(solution)/shard_map/ppermute | solution.py:387
  32.5 1.1 %collective-permute-start.4 = (f32[32,128]{1,0:T(8,128)S(1)}, f32[32,128]{1,0:T(8,128)S(1)}, u32[]{:S(2)}, u32[]{:S(2)}) collective-permute-start(f32[32,128]{1,0:T(8,128)S(1)} %add.13.refs_0_), channel_id=1, source_target_pairs={{0,16},{16,0},{32,48},{48,32},{64,80},{80,64},{96,112},{112,96},{1... | collective-permute-start | bytes 49160 | tf_op jit(solution)/shard_map/ppermute | solution.py:387
  33.6 4.1 %collective-permute-done.4.refs_1_ = f32[32,128]{1,0:T(8,128)S(1)} collective-permute-done((f32[32,128]{1,0:T(8,128)S(1)}, f32[32,128]{1,0:T(8,128)S(1)}, u32[]{:S(2)}, u32[]{:S(2)}) %collective-permute-start.4) | collective-permute-done | bytes 16416 | tf_op jit(solution)/shard_map/ppermute | solution.py:387
  37.7 0.0 copy-done
  37.7 3.0 %scatter_kernel.1 = (f32[2,512,128]{2,1,0:T(8,128)S(1)}, f32[7,128,128]{2,1,0:T(8,128)S(1)}, f32[7,128,128]{2,1,0:T(8,128)S(1)}, f32[2816,128]{1,0:T(8,128)S(1)}) custom-call(f32[32,128]{1,0:T(8,128)S(1)} %add.13.refs_0_, f32[32,128]{1,0:T(8,128)S(1)} %collective-permute-done.4.refs_1_, s32[32,128]{1,0:T(8,128)S(1)} %bitcast.15, f32[32,128]{1,0:T(8,128)S(1)} %bitcast.18, ...), custom_call_target="tpu_custom_call" | custom-call | flops 20000000 | bytes 2000000 | tf_op jit(solution)/shard_map/scatter_kernel/pallas_call | solution.py:401
  40.7 0.1 collective-permute-start.5
  40.8 2.8 %collective-permute-start.6 = (f32[7,128,128]{2,1,0:T(8,128)S(1)}, f32[7,128,128]{2,1,0:T(8,128)S(1)}, u32[]{:S(2)}, u32[]{:S(2)}) collective-permute-start(f32[7,128,128]{2,1,0:T(8,128)S(1)} %get-tuple-element.25), channel_id=1, source_target_pairs={{1,2},{2,1},{3,4},{4,3},{5,6},{6,5},{7,8},{8,7},{9,10},{10,9},{11,... | collective-permute-start | bytes 1376264 | tf_op jit(solution)/shard_map/ppermute | solution.py:378
  43.5 3.6 %local_kernel.1.refs_0_ = f32[7,512,128]{2,1,0:T(8,128)S(1)} custom-call(bf16[256,512]{1,0:T(8,128)(2,1)S(1)} %copy-done.1, f32[2,512,128]{2,1,0:T(8,128)S(1)} %get-tuple-element.21.refs_1_, f32[2816,128]{1,0:T(8,128)S(1)} %get-tuple-element.22.refs_2_, f32[7,32,128]{2,1,0:T(8,128)S(1)} %broadcast_in_dim.10.refs_1_.refs_6_.refs_3_, ...), custom_call_target="tpu_custom_call" | custom-call | flops 20000000 | bytes 2000000 | tf_op jit(solution)/shard_map/local_kernel/pallas_call | solution.py:401
  47.2 0.0 collective-permute-done.5.refs_1_
  47.2 5.5 %collective-permute-done.6.refs_2_ = f32[7,128,128]{2,1,0:T(8,128)S(1)} collective-permute-done((f32[7,128,128]{2,1,0:T(8,128)S(1)}, f32[7,128,128]{2,1,0:T(8,128)S(1)}, u32[]{:S(2)}, u32[]{:S(2)}) %collective-permute-start.6) | collective-permute-done | bytes 458784 | tf_op jit(solution)/shard_map/ppermute | solution.py:378
  52.7 3.3 %edge_kernel.1 = (f32[2,512,128]{2,1,0:T(8,128)}, f32[5,512,128]{2,1,0:T(8,128)}) custom-call(f32[7,512,128]{2,1,0:T(8,128)S(1)} %local_kernel.1.refs_0_, f32[7,128,128]{2,1,0:T(8,128)S(1)} %collective-permute-done.5.refs_1_, f32[7,128,128]{2,1,0:T(8,128)S(1)} %collective-permute-done.6.refs_2_, s32[2]{0:T(128)S(1)} %copy-done.2, f32[12]{0:T(128)S(1)} %copy-done.3, ...), custom_call_target="tpu_custom_call" | custom-call | flops 20000000 | bytes 2000000 | tf_op jit(solution)/shard_map/edge_kernel/pallas_call | solution.py:401
  (5 shorter events, 0.0 us)
Async XLA Ops:
  0.6 13.0 %copy-start.1 = (bf16[256,512]{1,0:T(8,128)(2,1)S(1)}, bf16[256,512]{1,0:T(8,128)(2,1)}, u32[]{:S(2)}) copy-start(bf16[256,512]{1,0:T(8,128)(2,1)} %constant.8.clone.refs_0_) | copy-start | bytes 786436
  0.6 7.8 %copy-start.8 = (f32[1,5,32]{2,0,1:T(1,128)S(1)}, f32[1,5,32]{2,0,1:T(1,128)}, u32[]{:S(2)}) copy-start(f32[1,5,32]{2,0,1:T(1,128)} %param.19) | copy-start | bytes 1924
  0.7 7.8 %copy-start.9 = (f32[8]{0:T(128)S(1)}, f32[8]{0:T(128)}, u32[]{:S(2)}) copy-start(f32[8]{0:T(128)} %param.24) | copy-start | bytes 100
  0.7 7.8 %copy-start.7 = (s32[4096]{0:T(1024)S(1)}, s32[4096]{0:T(1024)}, u32[]{:S(2)}) copy-start(s32[4096]{0:T(1024)} %param.23) | copy-start | bytes 49156
  0.7 7.9 %copy-start.5 = (s32[4096]{0:T(1024)S(1)}, s32[4096]{0:T(1024)}, u32[]{:S(2)}) copy-start(s32[4096]{0:T(1024)} %param.22) | copy-start | bytes 49156
  0.7 7.9 %copy-start.4 = (s32[4096]{0:T(1024)S(1)}, s32[4096]{0:T(1024)}, u32[]{:S(2)}) copy-start(s32[4096]{0:T(1024)} %param.20) | copy-start | bytes 49156
  0.7 7.9 %copy-start.6 = (f32[4096]{0:T(1024)S(1)}, f32[4096]{0:T(1024)}, u32[]{:S(2)}) copy-start(f32[4096]{0:T(1024)} %param.21) | copy-start | bytes 49156
  0.7 12.9 %copy-start.3 = (f32[12]{0:T(128)S(1)}, f32[12]{0:T(128)}, u32[]{:S(2)}) copy-start(f32[12]{0:T(128)} %refs_4_.3) | copy-start | bytes 148
  0.7 12.9 %copy-start.2 = (s32[2]{0:T(128)S(1)}, s32[2]{0:T(128)}, u32[]{:S(2)}) copy-start(s32[2]{0:T(128)} %refs_3_.3) | copy-start | bytes 28
  2.4 15.5 %collective-permute-start = (f32[7,128,128]{2,1,0:T(8,128)S(1)}, f32[7,128,128]{2,1,0:T(8,128)S(1)}, u32[]{:S(2)}, u32[]{:S(2)}) collective-permute-start(f32[7,128,128]{2,1,0:T(8,128)S(1)} %get-tuple-element.16), channel_id=1, source_target_pairs={{0,1},{1,0},{2,3},{3,2},{4,5},{5,4},{6,7},{7,6},{8,9},{9,8},{10,11... | collective-permute-start | bytes 1376264 | tf_op jit(solution)/shard_map/ppermute | solution.py:378
  2.5 15.4 %collective-permute-start.1 = (f32[7,128,128]{2,1,0:T(8,128)S(1)}, f32[7,128,128]{2,1,0:T(8,128)S(1)}, u32[]{:S(2)}, u32[]{:S(2)}) collective-permute-start(f32[7,128,128]{2,1,0:T(8,128)S(1)} %get-tuple-element.17), channel_id=1, source_target_pairs={{1,2},{2,1},{3,4},{4,3},{5,6},{6,5},{7,8},{8,7},{9,10},{10,9},{11,... | collective-permute-start | bytes 1376264 | tf_op jit(solution)/shard_map/ppermute | solution.py:378
  18.0 19.7 %copy-start = (bf16[2,5,32,16,128]{4,3,2,1,0:T(8,128)(2,1)S(1)}, bf16[2,5,32,16,128]{4,3,2,1,0:T(8,128)(2,1)}, u32[]{:S(2)}) copy-start(bf16[2,5,32,16,128]{4,3,2,1,0:T(8,128)(2,1)} %param.15) | copy-start | bytes 3932164
  22.9 3.8 %collective-permute-start.2 = (f32[32,128]{1,0:T(8,128)S(1)}, f32[32,128]{1,0:T(8,128)S(1)}, u32[]{:S(2)}, u32[]{:S(2)}) collective-permute-start(f32[32,128]{1,0:T(8,128)S(1)} %forward_kernel.1), channel_id=1, source_target_pairs={{0,32},{16,48},{32,0},{48,16},{64,96},{80,112},{96,64},{112,80},{1... | collective-permute-start | bytes 49160 | tf_op jit(solution)/shard_map/ppermute | solution.py:387
  26.7 5.8 %collective-permute-start.3 = (f32[32,128]{1,0:T(8,128)S(1)}, f32[32,128]{1,0:T(8,128)S(1)}, u32[]{:S(2)}, u32[]{:S(2)}) collective-permute-start(f32[32,128]{1,0:T(8,128)S(1)} %add.12), channel_id=1, source_target_pairs={{0,96},{16,112},{32,64},{48,80},{64,32},{80,48},{96,0},{112,16},{1... | collective-permute-start | bytes 49160 | tf_op jit(solution)/shard_map/ppermute | solution.py:387
  32.5 5.2 %collective-permute-start.4 = (f32[32,128]{1,0:T(8,128)S(1)}, f32[32,128]{1,0:T(8,128)S(1)}, u32[]{:S(2)}, u32[]{:S(2)}) collective-permute-start(f32[32,128]{1,0:T(8,128)S(1)} %add.13.refs_0_), channel_id=1, source_target_pairs={{0,16},{16,0},{32,48},{48,32},{64,80},{80,64},{96,112},{112,96},{1... | collective-permute-start | bytes 49160 | tf_op jit(solution)/shard_map/ppermute | solution.py:387
  40.7 6.5 %collective-permute-start.5 = (f32[7,128,128]{2,1,0:T(8,128)S(1)}, f32[7,128,128]{2,1,0:T(8,128)S(1)}, u32[]{:S(2)}, u32[]{:S(2)}) collective-permute-start(f32[7,128,128]{2,1,0:T(8,128)S(1)} %get-tuple-element.24), channel_id=1, source_target_pairs={{0,1},{1,0},{2,3},{3,2},{4,5},{5,4},{6,7},{7,6},{8,9},{9,8},{10,11... | collective-permute-start | bytes 1376264 | tf_op jit(solution)/shard_map/ppermute | solution.py:378
  40.8 11.9 %collective-permute-start.6 = (f32[7,128,128]{2,1,0:T(8,128)S(1)}, f32[7,128,128]{2,1,0:T(8,128)S(1)}, u32[]{:S(2)}, u32[]{:S(2)}) collective-permute-start(f32[7,128,128]{2,1,0:T(8,128)S(1)} %get-tuple-element.25), channel_id=1, source_target_pairs={{1,2},{2,1},{3,4},{4,3},{5,6},{6,5},{7,8},{8,7},{9,10},{10,9},{11,... | collective-permute-start | bytes 1376264 | tf_op jit(solution)/shard_map/ppermute | solution.py:378

commit v7 on v6

--- a/solution.py
+++ b/solution.py
@@ -291,10 +291,10 @@
     every_window(bound, blocks, cells, visit, visit_again)
 
 
-def scatter_kernel(dims, seen, others, key, frac, weight, perturb, scale, bound, source, side_a, side_b, gradient, valued):
+def scatter_kernel(dims, seen, key, frac, weight, perturb, scale, bound, source, side_a, side_b, gradient, valued):
     members, nvars, levels, rows, cells, blocks = dims
     shift = cells.bit_length() - 1
-    valued[...] = (seen[...] + others[...]) * weight[...]
+    valued[...] = seen[...] * weight[...]
     gradient[...] = jnp.zeros(gradient.shape, jnp.float32)
 
     def add_block(block, start):
@@ -378,14 +378,17 @@
     return lax.ppermute(side_a, "tile", pairs_a), lax.ppermute(side_b, "tile", pairs_b)
 
 
-def halved_sums(value):
-    count = lax.axis_size("grp")
-    others = None
+def summed(value):
+    count, tiles = lax.axis_size("grp"), lax.axis_size("tile")
+    odd = lax.axis_index("tile") % 2 == 1
+    other = lax.ppermute(value, "tile", [(t - 1, t) for t in range(1, tiles, 2)])
+    both = jnp.concatenate([value, other])
     for turn in (2, 6, 1) if count == 8 else [1 << bit for bit in range(count.bit_length() - 1)]:
-        if others is not None:
-            value = value + others
-        others = lax.ppermute(value, "grp", [(i, i ^ turn) for i in range(count)])
-    return value, others
+        pairs = [(g * tiles + t, (g ^ turn) * tiles + t) for g in range(count) for t in range(1, tiles, 2)]
+        both = both + lax.ppermute(both, ("grp", "tile"), pairs)
+    mine, theirs = both[: value.shape[0]], both[value.shape[0] :]
+    back = lax.ppermute(theirs, "tile", [(t, t - 1) for t in range(1, tiles, 2)])
+    return jnp.where(odd, mine, back)
 
 
 VMEM = pl.BlockSpec(memory_space=pltpu.VMEM)
@@ -469,12 +472,12 @@
             pltpu.SemaphoreType.DMA(()),
         ],
     )
-    seen, others = halved_sums(seen)
+    seen = summed(seen)
     source, side_a, side_b, gradient = call(
         scatter_kernel,
         dims,
         [(members, plane, cells), strip, strip, (table_rows, cells)],
-        [seen, others, key, frac, weight, perturb, scale],
+        [seen, key, frac, weight, perturb, scale],
         [],
         [key],
         [pltpu.VMEM(key.shape, jnp.float32)],

time: 56.2 us -> 73.4 us (1.31)
  waiting for transfers between devices: 13.2 us -> 22.7 us
  local copies, waits for them, and re-layouts: 0.14 us -> 6.96 us
  starting transfers between devices: 15.4 us -> 13.5 us
  other arithmetic: 5.1 us -> 6.46 us
  Pallas kernels: 20.7 us -> 21.5 us
    ppermute x3 -> x5, waiting for transfers between devices: 7.66 us -> 17.8 us  [the longest x1 17 us: summed(): lax.ppermute(theirs, 'tile', [(t, t - 1) for t in range(1, tiles, 2)])]
    unnamed x21 -> x41, local copies, waits for them, and re-layouts: 0.05 us -> 6.26 us
    ppermute x3 -> x5, starting transfers between devices: 7.17 us -> 4.55 us  [the longest x3 1.98 us: summed(): both = both + lax.ppermute(both, ('grp', 'tile'), pairs)]
    pallas_call x6, Pallas kernels: 20.7 us -> 21.5 us  [call(): pl.pallas_call(body, out_shape=tuple((jax.ShapeDtypeStruct(shape, jnp.flo...]
    select_n x0 -> x1, other arithmetic: none -> 0.74 us  [summed(): return jnp.where(odd, mine, back)]
  transfers between devices with their start and end apart: 7 -> 9, of which waited for: 4 -> 3; matrix products, arithmetic and copies ran while one was open for 9% -> 8% of each run, Pallas kernels for 14% -> 11%
where the time goes in v7:
time: 73.4 us; the launch traced here: 72.9 us
  waiting for transfers between devices  22.7 us (31%)
  Pallas kernels  21.5 us (29%)
  starting transfers between devices  13.5 us (18%)
  local copies, waits for them, and re-layouts  6.96 us (9%)
  other arithmetic  6.46 us (9%)
  between operations  1.68 us (2%)
    pallas_call x6, Pallas kernels, call(): pl.pallas_call(body, out_shape=tuple((jax.ShapeDtypeStruct(shape, jnp.flo...  21.5 us
    ppermute x1, waiting for transfers between devices, summed(): lax.ppermute(theirs, 'tile', [(t, t - 1) for t in range(1, tiles, 2)])  17 us
    ppermute x2, starting transfers between devices, exchange(): lax.ppermute(side_b, 'tile', pairs_b)  8.65 us
    unnamed x41, local copies, waits for them, and re-layouts  6.26 us
    sort x1, other arithmetic, per_device(): lax.sort((key, obs_frac, weight), num_keys=1, is_stable=False)  5.58 us
    ppermute x2, waiting for transfers between devices, exchange(): lax.ppermute(side_b, 'tile', pairs_b)  4.88 us
    ppermute x3, starting transfers between devices, summed(): both = both + lax.ppermute(both, ('grp', 'tile'), pairs)  1.98 us
  transfers between devices with their start and end apart: 9, of which 3 were waited for; matrix products, arithmetic and copies ran while one was open for 8% of the time, Pallas kernels for 11%

profile of v7, /device:TPU:6, one launch (start us, length us, event | category | flops | bytes accessed | tf_op | source)
XLA Modules:
  0.0 72.9 jit_solution(9879847533802815676)
XLA Ops:
  0.6 0.0 copy-start.1
  0.7 0.0 copy-start.10
  0.7 0.0 copy-start.7
  0.7 2.6 %pack_kernel.1 = (f32[7,128,128]{2,1,0:T(8,128)}, f32[7,128,128]{2,1,0:T(8,128)}) custom-call(f32[2,512,128]{2,1,0:T(8,128)} %bitcast.22, f32[5,512,128]{2,1,0:T(8,128)} %bitcast.20), custom_call_target="tpu_custom_call" | custom-call | flops 20000000 | bytes 2000000 | tf_op jit(solution)/shard_map/pack_kernel/pallas_call | solution.py:404
  3.3 0.1 collective-permute-start
  3.4 5.3 %collective-permute-start.1 = (f32[7,128,128]{2,1,0:T(8,128)}, f32[7,128,128]{2,1,0:T(8,128)S(1)}, u32[]{:S(2)}, u32[]{:S(2)}) collective-permute-start(f32[7,128,128]{2,1,0:T(8,128)} %get-tuple-element.17), channel_id=1, source_target_pairs={{1,2},{2,1},{3,4},{4,3},{5,6},{6,5},{7,8},{8,7},{9,10},{10,9},{11,... | collective-permute-start | bytes 1376264 | tf_op jit(solution)/shard_map/ppermute | solution.py:378
  9.4 0.1 select_reduce_fusion
  9.5 0.0 copy-done.16
  9.5 5.6 %sort.21 = (s32[4096]{0:T(1024)S(1)}, f32[4096]{0:T(1024)S(1)}, f32[4096]{0:T(1024)}) sort(s32[4096]{0:T(1024)S(1)} %multiply_add_fusion, f32[4096]{0:T(1024)S(1)} %copy-done.16, f32[4096]{0:T(1024)S(1)} %select_reduce_fusion), dimensions={0}, to_apply=%region_1.2 | sort | flops 49152 | bytes 98304 | tf_op jit(solution)/shard_map/sort | solution.py:456
  15.1 0.0 copy-done.7
  15.1 4.3 %own_kernel.1 = (f32[7,512,128]{2,1,0:T(8,128)S(1)}, f32[7,512,128]{2,1,0:T(8,128)S(1)}) custom-call(bf16[256,512]{1,0:T(8,128)(2,1)S(1)} %copy-done.1, f32[2,512,128]{2,1,0:T(8,128)} %bitcast.23, f32[5,512,128]{2,1,0:T(8,128)} %bitcast.21, s32[2]{0:T(128)S(1)} %copy-done.7, f32[12]{0:T(128)S(1)} %copy-done.10, f32[1]{0:T(128)S(6)} %copy.18.refs_5_.refs_10_.refs_7_), custom_call_target="tpu_custom_call" | custom-call | flops 20000000 | bytes 2000000 | tf_op jit(solution)/shard_map/own_kernel/pallas_call | solution.py:404
  19.4 0.0 collective-permute-done.refs_2_
  19.4 0.0 copy-start.2
  19.4 0.8 %copy-done.2 = f32[7,128,128]{2,1,0:T(8,128)} copy-done((f32[7,128,128]{2,1,0:T(8,128)}, f32[7,128,128]{2,1,0:T(8,128)S(1)}, u32[]{:S(2)}) %copy-start.2) | copy-done | bytes 458776
  20.2 0.0 collective-permute-done.1.refs_3_
  20.2 0.8 %copy-done.4 = f32[7,128,128]{2,1,0:T(8,128)} copy-done((f32[7,128,128]{2,1,0:T(8,128)}, f32[7,128,128]{2,1,0:T(8,128)S(1)}, u32[]{:S(2)}) %copy-start.4) | copy-done | bytes 458776
  21.0 0.1 broadcast_in_dim.10.refs_1_.refs_5_.refs_3_
  21.0 0.0 copy-start.3
  21.1 1.0 %copy-done.3 = f32[7,128,128]{2,1,0:T(8,128)S(1)} copy-done((f32[7,128,128]{2,1,0:T(8,128)S(1)}, f32[7,128,128]{2,1,0:T(8,128)}, u32[]{:S(2)}) %copy-start.3) | copy-done | bytes 458776
  22.1 1.0 %copy-done.5 = f32[7,128,128]{2,1,0:T(8,128)S(1)} copy-done((f32[7,128,128]{2,1,0:T(8,128)S(1)}, f32[7,128,128]{2,1,0:T(8,128)}, u32[]{:S(2)}) %copy-start.5) | copy-done | bytes 458776
  23.1 0.7 copy-done.8
  23.8 0.7 copy-done.11
  24.4 4.8 %forward_kernel.1 = f32[32,128]{1,0:T(8,128)S(1)} custom-call(f32[7,512,128]{2,1,0:T(8,128)S(1)} %get-tuple-element.15.refs_0_, f32[7,32,128]{2,1,0:T(8,128)S(1)} %broadcast_in_dim.10.refs_1_.refs_5_.refs_3_, f32[7,128,128]{2,1,0:T(8,128)S(1)} %copy-done.3, f32[7,128,128]{2,1,0:T(8,128)S(1)} %copy-done.5, s32[32,128]{1,0:T(8,128)S(1)} %bitcast.13, ...), custom_call_target="tpu_custom_call" | custom-call | flops 20000000 | bytes 2000000 | tf_op jit(solution)/shard_map/forward_kernel/pallas_call | solution.py:404
  29.2 1.3 %collective-permute-start.2 = (f32[32,128]{1,0:T(8,128)S(1)}, f32[32,128]{1,0:T(8,128)S(1)}, u32[]{:S(2)}, u32[]{:S(2)}) collective-permute-start(f32[32,128]{1,0:T(8,128)S(1)} %forward_kernel.1), channel_id=1, source_target_pairs={{0,1},{2,3},{4,5},{6,7},{8,9},{10,11},{12,13},{14,15},{16,17},{18,... | collective-permute-start | bytes 49160 | tf_op jit(solution)/shard_map/ppermute | solution.py:384
  30.5 0.8 %collective-permute-done.2 = f32[32,128]{1,0:T(8,128)S(1)} collective-permute-done((f32[32,128]{1,0:T(8,128)S(1)}, f32[32,128]{1,0:T(8,128)S(1)}, u32[]{:S(2)}, u32[]{:S(2)}) %collective-permute-start.2) | collective-permute-done | bytes 16416 | tf_op jit(solution)/shard_map/ppermute | solution.py:384
  31.3 0.7 collective-permute-start.3
  32.0 0.0 collective-permute-done.3
  32.0 0.7 collective-permute-start.4
  32.7 0.0 collective-permute-done.4
  32.7 0.7 collective-permute-start.5
  33.4 0.0 collective-permute-done.5
  33.4 0.0 copy-start.13
  33.4 0.6 copy-done.13
  34.0 0.6 slice.9
  34.6 1.3 %collective-permute-start.6 = (f32[32,128]{1,0:T(8,128)}, f32[32,128]{1,0:T(8,128)}, u32[]{:S(2)}, u32[]{:S(2)}) collective-permute-start(f32[32,128]{1,0:T(8,128)} %slice.9), channel_id=1, source_target_pairs={{1,0},{3,2},{5,4},{7,6},{9,8},{11,10},{13,12},{15,14},{17,16},{19,... | collective-permute-start | bytes 49160 | tf_op jit(solution)/shard_map/ppermute | solution.py:390
  35.9 0.0 copy-start.9
  36.0 0.0 copy-start.12
  36.0 17.0 %collective-permute-done.6 = f32[32,128]{1,0:T(8,128)} collective-permute-done((f32[32,128]{1,0:T(8,128)}, f32[32,128]{1,0:T(8,128)}, u32[]{:S(2)}, u32[]{:S(2)}) %collective-permute-start.6) | collective-permute-done | bytes 16416 | tf_op jit(solution)/shard_map/ppermute | solution.py:390
  53.0 0.7 %slice_select_fusion.refs_0_ = f32[32,128]{1,0:T(8,128)S(1)} fusion(f32[32,128]{1,0:T(8,128)} %collective-permute-done.6, f32[64,128]{1,0:T(8,128)} %copy-done.13, pred[]{:T(512)S(6)} %eq.18), kind=kLoop, calls=%fused_computation.3 | loop fusion | flops 4096 | bytes 49153 | tf_op jit(solution)/shard_map/jit(_where)/select_n | solution.py:391
  53.7 0.0 copy-done
  53.7 0.7 copy-done.6
  54.4 3.0 %scatter_kernel.1 = (f32[2,512,128]{2,1,0:T(8,128)S(1)}, f32[7,128,128]{2,1,0:T(8,128)S(1)}, f32[7,128,128]{2,1,0:T(8,128)S(1)}, f32[2816,128]{1,0:T(8,128)S(1)}) custom-call(f32[32,128]{1,0:T(8,128)S(1)} %slice_select_fusion.refs_0_, s32[32,128]{1,0:T(8,128)S(1)} %bitcast.15, f32[32,128]{1,0:T(8,128)S(1)} %bitcast.18, f32[32,128]{1,0:T(8,128)S(1)} %bitcast.19, ...), custom_call_target="tpu_custom_call" | custom-call | flops 20000000 | bytes 2000000 | tf_op jit(solution)/shard_map/scatter_kernel/pallas_call | solution.py:404
  57.4 0.2 collective-permute-start.7
  57.6 3.4 %collective-permute-start.8 = (f32[7,128,128]{2,1,0:T(8,128)S(1)}, f32[7,128,128]{2,1,0:T(8,128)S(1)}, u32[]{:S(2)}, u32[]{:S(2)}) collective-permute-start(f32[7,128,128]{2,1,0:T(8,128)S(1)} %get-tuple-element.25), channel_id=1, source_target_pairs={{1,2},{2,1},{3,4},{4,3},{5,6},{6,5},{7,8},{8,7},{9,10},{10,9},{11,... | collective-permute-start | bytes 1376264 | tf_op jit(solution)/shard_map/ppermute | solution.py:378
  61.0 3.6 %local_kernel.1.refs_0_ = f32[7,512,128]{2,1,0:T(8,128)S(1)} custom-call(bf16[256,512]{1,0:T(8,128)(2,1)S(1)} %copy-done.1, f32[2,512,128]{2,1,0:T(8,128)S(1)} %get-tuple-element.21.refs_1_, f32[2816,128]{1,0:T(8,128)S(1)} %get-tuple-element.22.refs_2_, f32[7,32,128]{2,1,0:T(8,128)S(1)} %broadcast_in_dim.10.refs_1_.refs_5_.refs_3_, ...), custom_call_target="tpu_custom_call" | custom-call | flops 20000000 | bytes 2000000 | tf_op jit(solution)/shard_map/local_kernel/pallas_call | solution.py:404
  64.7 0.0 collective-permute-done.7.refs_1_
  64.7 4.9 %collective-permute-done.8.refs_2_ = f32[7,128,128]{2,1,0:T(8,128)S(1)} collective-permute-done((f32[7,128,128]{2,1,0:T(8,128)S(1)}, f32[7,128,128]{2,1,0:T(8,128)S(1)}, u32[]{:S(2)}, u32[]{:S(2)}) %collective-permute-start.8) | collective-permute-done | bytes 458784 | tf_op jit(solution)/shard_map/ppermute | solution.py:378
  69.5 3.3 %edge_kernel.1 = (f32[2,512,128]{2,1,0:T(8,128)}, f32[5,512,128]{2,1,0:T(8,128)}) custom-call(f32[7,512,128]{2,1,0:T(8,128)S(1)} %local_kernel.1.refs_0_, f32[7,128,128]{2,1,0:T(8,128)S(1)} %collective-permute-done.7.refs_1_, f32[7,128,128]{2,1,0:T(8,128)S(1)} %collective-permute-done.8.refs_2_, s32[2]{0:T(128)S(1)} %copy-done.9, f32[12]{0:T(128)S(1)} %copy-done.12, ...), custom_call_target="tpu_custom_call" | custom-call | flops 20000000 | bytes 2000000 | tf_op jit(solution)/shard_map/edge_kernel/pallas_call | solution.py:404
  (28 shorter events, 0.1 us)
Async XLA Ops:
  0.6 14.5 %copy-start.1 = (bf16[256,512]{1,0:T(8,128)(2,1)S(1)}, bf16[256,512]{1,0:T(8,128)(2,1)}, u32[]{:S(2)}) copy-start(bf16[256,512]{1,0:T(8,128)(2,1)} %constant.26.clone.refs_0_) | copy-start | bytes 786436
  0.6 8.7 %copy-start.18 = (f32[1,5,32]{2,0,1:T(1,128)S(1)}, f32[1,5,32]{2,0,1:T(1,128)}, u32[]{:S(2)}) copy-start(f32[1,5,32]{2,0,1:T(1,128)} %param.19) | copy-start | bytes 1924
  0.7 8.7 %copy-start.19 = (f32[8]{0:T(128)S(1)}, f32[8]{0:T(128)}, u32[]{:S(2)}) copy-start(f32[8]{0:T(128)} %param.24) | copy-start | bytes 100
  0.7 8.7 %copy-start.17 = (s32[4096]{0:T(1024)S(1)}, s32[4096]{0:T(1024)}, u32[]{:S(2)}) copy-start(s32[4096]{0:T(1024)} %param.23) | copy-start | bytes 49156
  0.7 8.8 %copy-start.15 = (s32[4096]{0:T(1024)S(1)}, s32[4096]{0:T(1024)}, u32[]{:S(2)}) copy-start(s32[4096]{0:T(1024)} %param.22) | copy-start | bytes 49156
  0.7 8.8 %copy-start.14 = (s32[4096]{0:T(1024)S(1)}, s32[4096]{0:T(1024)}, u32[]{:S(2)}) copy-start(s32[4096]{0:T(1024)} %param.20) | copy-start | bytes 49156
  0.7 8.8 %copy-start.16 = (f32[4096]{0:T(1024)S(1)}, f32[4096]{0:T(1024)}, u32[]{:S(2)}) copy-start(f32[4096]{0:T(1024)} %param.21) | copy-start | bytes 49156
  0.7 14.4 %copy-start.10 = (f32[12]{0:T(128)S(1)}, f32[12]{0:T(128)}, u32[]{:S(2)}) copy-start(f32[12]{0:T(128)} %refs_4_.3) | copy-start | bytes 148
  0.7 14.4 %copy-start.7 = (s32[2]{0:T(128)S(1)}, s32[2]{0:T(128)}, u32[]{:S(2)}) copy-start(s32[2]{0:T(128)} %refs_3_.3) | copy-start | bytes 28
  3.3 16.1 %collective-permute-start = (f32[7,128,128]{2,1,0:T(8,128)}, f32[7,128,128]{2,1,0:T(8,128)S(1)}, u32[]{:S(2)}, u32[]{:S(2)}) collective-permute-start(f32[7,128,128]{2,1,0:T(8,128)} %get-tuple-element.16), channel_id=1, source_target_pairs={{0,1},{1,0},{2,3},{3,2},{4,5},{5,4},{6,7},{7,6},{8,9},{9,8},{10,11... | collective-permute-start | bytes 1376264 | tf_op jit(solution)/shard_map/ppermute | solution.py:378
  3.4 16.8 %collective-permute-start.1 = (f32[7,128,128]{2,1,0:T(8,128)}, f32[7,128,128]{2,1,0:T(8,128)S(1)}, u32[]{:S(2)}, u32[]{:S(2)}) collective-permute-start(f32[7,128,128]{2,1,0:T(8,128)} %get-tuple-element.17), channel_id=1, source_target_pairs={{1,2},{2,1},{3,4},{4,3},{5,6},{6,5},{7,8},{8,7},{9,10},{10,9},{11,... | collective-permute-start | bytes 1376264 | tf_op jit(solution)/shard_map/ppermute | solution.py:378
  19.4 0.8 %copy-start.2 = (f32[7,128,128]{2,1,0:T(8,128)}, f32[7,128,128]{2,1,0:T(8,128)S(1)}, u32[]{:S(2)}) copy-start(f32[7,128,128]{2,1,0:T(8,128)S(1)} %collective-permute-done.refs_2_) | copy-start | bytes 1376260
  20.2 0.8 %copy-start.4 = (f32[7,128,128]{2,1,0:T(8,128)}, f32[7,128,128]{2,1,0:T(8,128)S(1)}, u32[]{:S(2)}) copy-start(f32[7,128,128]{2,1,0:T(8,128)S(1)} %collective-permute-done.1.refs_3_) | copy-start | bytes 1376260
  21.0 1.0 %copy-start.3 = (f32[7,128,128]{2,1,0:T(8,128)S(1)}, f32[7,128,128]{2,1,0:T(8,128)}, u32[]{:S(2)}) copy-start(f32[7,128,128]{2,1,0:T(8,128)} %copy-done.2) | copy-start | bytes 1376260
  22.1 1.0 %copy-start.5 = (f32[7,128,128]{2,1,0:T(8,128)S(1)}, f32[7,128,128]{2,1,0:T(8,128)}, u32[]{:S(2)}) copy-start(f32[7,128,128]{2,1,0:T(8,128)} %copy-done.4) | copy-start | bytes 1376260
  23.1 0.7 copy-start.8
  23.7 0.7 copy-start.11
  24.4 29.3 %copy-start = (bf16[2,5,32,16,128]{4,3,2,1,0:T(8,128)(2,1)S(1)}, bf16[2,5,32,16,128]{4,3,2,1,0:T(8,128)(2,1)}, u32[]{:S(2)}) copy-start(bf16[2,5,32,16,128]{4,3,2,1,0:T(8,128)(2,1)} %param.15) | copy-start | bytes 3932164
  29.2 2.1 %collective-permute-start.2 = (f32[32,128]{1,0:T(8,128)S(1)}, f32[32,128]{1,0:T(8,128)S(1)}, u32[]{:S(2)}, u32[]{:S(2)}) collective-permute-start(f32[32,128]{1,0:T(8,128)S(1)} %forward_kernel.1), channel_id=1, source_target_pairs={{0,1},{2,3},{4,5},{6,7},{8,9},{10,11},{12,13},{14,15},{16,17},{18,... | collective-permute-start | bytes 49160 | tf_op jit(solution)/shard_map/ppermute | solution.py:384
  31.3 0.7 collective-permute-start.3
  32.0 0.7 collective-permute-start.4
  32.7 0.7 collective-permute-start.5
  33.4 0.6 copy-start.13
  34.6 18.3 %collective-permute-start.6 = (f32[32,128]{1,0:T(8,128)}, f32[32,128]{1,0:T(8,128)}, u32[]{:S(2)}, u32[]{:S(2)}) collective-permute-start(f32[32,128]{1,0:T(8,128)} %slice.9), channel_id=1, source_target_pairs={{1,0},{3,2},{5,4},{7,6},{9,8},{11,10},{13,12},{15,14},{17,16},{19,... | collective-permute-start | bytes 49160 | tf_op jit(solution)/shard_map/ppermute | solution.py:390
  35.9 25.1 %copy-start.9 = (s32[2]{0:T(128)S(1)}, s32[2]{0:T(128)}, u32[]{:S(2)}) copy-start(s32[2]{0:T(128)} %refs_3_.3) | copy-start | bytes 28
  36.0 25.1 %copy-start.12 = (f32[12]{0:T(128)S(1)}, f32[12]{0:T(128)}, u32[]{:S(2)}) copy-start(f32[12]{0:T(128)} %refs_4_.3) | copy-start | bytes 148
  53.7 0.7 copy-start.6
  57.4 7.2 %collective-permute-start.7 = (f32[7,128,128]{2,1,0:T(8,128)S(1)}, f32[7,128,128]{2,1,0:T(8,128)S(1)}, u32[]{:S(2)}, u32[]{:S(2)}) collective-permute-start(f32[7,128,128]{2,1,0:T(8,128)S(1)} %get-tuple-element.24), channel_id=1, source_target_pairs={{0,1},{1,0},{2,3},{3,2},{4,5},{5,4},{6,7},{7,6},{8,9},{9,8},{10,11... | collective-permute-start | bytes 1376264 | tf_op jit(solution)/shard_map/ppermute | solution.py:378
  57.6 11.9 %collective-permute-start.8 = (f32[7,128,128]{2,1,0:T(8,128)S(1)}, f32[7,128,128]{2,1,0:T(8,128)S(1)}, u32[]{:S(2)}, u32[]{:S(2)}) collective-permute-start(f32[7,128,128]{2,1,0:T(8,128)S(1)} %get-tuple-element.25), channel_id=1, source_target_pairs={{1,2},{2,1},{3,4},{4,3},{5,6},{6,5},{7,8},{8,7},{9,10},{10,9},{11,... | collective-permute-start | bytes 1376264 | tf_op jit(solution)/shard_map/ppermute | solution.py:378

commit v8 on v6

--- a/solution.py
+++ b/solution.py
@@ -124,10 +124,11 @@
 
 def sides_of(side_a, side_b, field, levels):
     even = is_even()
+    below, above = neighbours()
     lower, upper = [], []
     for j in range(SWEEPS):
         a = side_a[field, pl.ds(j * levels, levels), :]
-        b = side_b[field, pl.ds(j * levels, levels), :]
+        b = side_b[field, pl.ds(j * levels, levels), :] * (below * above)
         lower.append(jnp.where(even, b, a))
         upper.append(jnp.where(even, a, b))
     return lower, upper
@@ -374,7 +375,7 @@
 def exchange(side_a, side_b):
     count = lax.axis_size("tile")
     pairs_a = [(i, i ^ 1) for i in range(count)]
-    pairs_b = [(i, ((i + 1) ^ 1) - 1) for i in range(1, count - 1)]
+    pairs_b = [(i, (((i + 1) ^ 1) - 1) % count) for i in range(count)]
     return lax.ppermute(side_a, "tile", pairs_a), lax.ppermute(side_b, "tile", pairs_b)
 
 

time: 56.2 us -> 53.3 us (0.948); the launches traced: 56 us -> 52.4 us
  starting transfers between devices: 15.4 us -> 11.5 us
    ppermute x2, starting transfers between devices: 8.03 us -> 4.18 us  [exchange(): lax.ppermute(side_b, 'tile', pairs_b)]
  transfers between devices with their start and end apart: 7 -> 7, of which waited for: 4 -> 4; matrix products, arithmetic and copies ran while one was open for 9% -> 10% of each run, Pallas kernels for 14% -> 15%
where the time goes in v8:
time: 53.3 us; the launch traced here: 52.4 us
  Pallas kernels  20.7 us (39%)
  waiting for transfers between devices  13.4 us (25%)
  starting transfers between devices  11.5 us (22%)
  other arithmetic  5.1 us (10%)
  between operations  1.55 us (3%)
    pallas_call x6, Pallas kernels, call(): pl.pallas_call(body, out_shape=tuple((jax.ShapeDtypeStruct(shape, jnp.flo...  20.7 us
    ppermute x3, waiting for transfers between devices, halved_sums(): others = lax.ppermute(value, 'grp', [(i, i ^ turn) for i in range(count)])  7.68 us
    ppermute x3, starting transfers between devices, halved_sums(): others = lax.ppermute(value, 'grp', [(i, i ^ turn) for i in range(count)])  7.15 us
    ppermute x2, waiting for transfers between devices, exchange(): lax.ppermute(side_b, 'tile', pairs_b)  5.69 us
    sort x1, other arithmetic, per_device(): lax.sort((key, obs_frac, weight), num_keys=1, is_stable=False)  4.98 us
    ppermute x2, starting transfers between devices, exchange(): lax.ppermute(side_b, 'tile', pairs_b)  4.18 us
  transfers between devices with their start and end apart: 7, of which 4 were waited for; matrix products, arithmetic and copies ran while one was open for 10% of the time, Pallas kernels for 15%

profile of v8, /device:TPU:6, one launch (start us, length us, event | category | flops | bytes accessed | tf_op | source)
XLA Modules:
  0.0 52.4 jit_solution(16245140912048744686)
XLA Ops:
  0.6 0.0 copy-start.1
  0.6 0.0 copy-start.8
  0.7 0.0 copy-start.9
  0.7 0.0 copy-start.7
  0.7 0.0 copy-start.5
  0.7 0.0 copy-start.4
  0.7 0.0 copy-start.6
  0.7 0.0 copy-start.3
  0.7 0.0 copy-start.2
  0.7 1.6 %pack_kernel.1 = (f32[7,128,128]{2,1,0:T(8,128)S(1)}, f32[7,128,128]{2,1,0:T(8,128)S(1)}) custom-call(f32[2,512,128]{2,1,0:T(8,128)} %bitcast.22, f32[5,512,128]{2,1,0:T(8,128)} %bitcast.20), custom_call_target="tpu_custom_call" | custom-call | flops 20000000 | bytes 2000000 | tf_op jit(solution)/shard_map/pack_kernel/pallas_call | solution.py:402
  2.4 0.1 collective-permute-start
  2.5 3.4 %collective-permute-start.1 = (f32[7,128,128]{2,1,0:T(8,128)S(1)}, f32[7,128,128]{2,1,0:T(8,128)S(1)}, u32[]{:S(2)}, u32[]{:S(2)}) collective-permute-start(f32[7,128,128]{2,1,0:T(8,128)S(1)} %get-tuple-element.17), channel_id=1, source_target_pairs={{0,15},{1,2},{2,1},{3,4},{4,3},{5,6},{6,5},{7,8},{8,7},{9,10},{10,... | collective-permute-start | bytes 1376264 | tf_op jit(solution)/shard_map/ppermute | solution.py:379
  6.5 0.0 copy-done.8
  6.5 0.0 copy-done.9
  6.5 0.0 copy-done.7
  6.6 0.1 select_reduce_fusion
  6.7 0.0 copy-done.5
  6.7 0.0 copy-done.4
  6.7 0.0 copy-done.6
  6.7 5.0 %sort.21 = (s32[4096]{0:T(1024)S(1)}, f32[4096]{0:T(1024)S(1)}, f32[4096]{0:T(1024)S(1)}) sort(s32[4096]{0:T(1024)S(1)} %multiply_add_fusion, f32[4096]{0:T(1024)S(1)} %copy-done.6, f32[4096]{0:T(1024)S(1)} %select_reduce_fusion), dimensions={0}, to_apply=%region_1.2 | sort | flops 49152 | bytes 98304 | tf_op jit(solution)/shard_map/sort | solution.py:454
  11.7 0.0 copy-done.1
  11.7 0.0 copy-done.3
  11.7 0.0 copy-done.2
  11.7 4.3 %own_kernel.1 = (f32[7,512,128]{2,1,0:T(8,128)S(1)}, f32[7,512,128]{2,1,0:T(8,128)S(1)}) custom-call(bf16[256,512]{1,0:T(8,128)(2,1)S(1)} %copy-done.1, f32[2,512,128]{2,1,0:T(8,128)} %bitcast.23, f32[5,512,128]{2,1,0:T(8,128)} %bitcast.21, s32[2]{0:T(128)S(1)} %copy-done.2, f32[12]{0:T(128)S(1)} %copy-done.3, f32[1]{0:T(128)S(6)} %copy.18.refs_5_.refs_10_.refs_7_), custom_call_target="tpu_custom_call" | custom-call | flops 20000000 | bytes 2000000 | tf_op jit(solution)/shard_map/own_kernel/pallas_call | solution.py:402
  16.0 0.0 collective-permute-done.refs_2_
  16.0 0.0 collective-permute-done.1.refs_3_
  16.0 0.1 broadcast_in_dim.10.refs_1_.refs_6_.refs_3_
  16.1 0.0 copy-start
  16.1 4.8 %forward_kernel.1 = f32[32,128]{1,0:T(8,128)S(1)} custom-call(f32[7,512,128]{2,1,0:T(8,128)S(1)} %get-tuple-element.15.refs_0_, f32[7,32,128]{2,1,0:T(8,128)S(1)} %broadcast_in_dim.10.refs_1_.refs_6_.refs_3_, f32[7,128,128]{2,1,0:T(8,128)S(1)} %collective-permute-done.refs_2_, f32[7,128,128]{2,1,0:T(8,128)S(1)} %collective-permute-done.1.refs_3_, ...), custom_call_target="tpu_custom_call" | custom-call | flops 20000000 | bytes 2000000 | tf_op jit(solution)/shard_map/forward_kernel/pallas_call | solution.py:402
  21.0 2.0 %collective-permute-start.2 = (f32[32,128]{1,0:T(8,128)S(1)}, f32[32,128]{1,0:T(8,128)S(1)}, u32[]{:S(2)}, u32[]{:S(2)}) collective-permute-start(f32[32,128]{1,0:T(8,128)S(1)} %forward_kernel.1), channel_id=1, source_target_pairs={{0,32},{16,48},{32,0},{48,16},{64,96},{80,112},{96,64},{112,80},{1... | collective-permute-start | bytes 49160 | tf_op jit(solution)/shard_map/ppermute | solution.py:388
  23.0 1.8 %collective-permute-done.2 = f32[32,128]{1,0:T(8,128)S(1)} collective-permute-done((f32[32,128]{1,0:T(8,128)S(1)}, f32[32,128]{1,0:T(8,128)S(1)}, u32[]{:S(2)}, u32[]{:S(2)}) %collective-permute-start.2) | collective-permute-done | bytes 16416 | tf_op jit(solution)/shard_map/ppermute | solution.py:388
  24.8 4.0 %collective-permute-start.3 = (f32[32,128]{1,0:T(8,128)S(1)}, f32[32,128]{1,0:T(8,128)S(1)}, u32[]{:S(2)}, u32[]{:S(2)}) collective-permute-start(f32[32,128]{1,0:T(8,128)S(1)} %add.12), channel_id=1, source_target_pairs={{0,96},{16,112},{32,64},{48,80},{64,32},{80,48},{96,0},{112,16},{1... | collective-permute-start | bytes 49160 | tf_op jit(solution)/shard_map/ppermute | solution.py:388
  28.8 1.7 %collective-permute-done.3 = f32[32,128]{1,0:T(8,128)S(1)} collective-permute-done((f32[32,128]{1,0:T(8,128)S(1)}, f32[32,128]{1,0:T(8,128)S(1)}, u32[]{:S(2)}, u32[]{:S(2)}) %collective-permute-start.3) | collective-permute-done | bytes 16416 | tf_op jit(solution)/shard_map/ppermute | solution.py:388
  30.6 1.1 %collective-permute-start.4 = (f32[32,128]{1,0:T(8,128)S(1)}, f32[32,128]{1,0:T(8,128)S(1)}, u32[]{:S(2)}, u32[]{:S(2)}) collective-permute-start(f32[32,128]{1,0:T(8,128)S(1)} %add.13.refs_0_), channel_id=1, source_target_pairs={{0,16},{16,0},{32,48},{48,32},{64,80},{80,64},{96,112},{112,96},{1... | collective-permute-start | bytes 49160 | tf_op jit(solution)/shard_map/ppermute | solution.py:388
  31.7 4.1 %collective-permute-done.4.refs_1_ = f32[32,128]{1,0:T(8,128)S(1)} collective-permute-done((f32[32,128]{1,0:T(8,128)S(1)}, f32[32,128]{1,0:T(8,128)S(1)}, u32[]{:S(2)}, u32[]{:S(2)}) %collective-permute-start.4) | collective-permute-done | bytes 16416 | tf_op jit(solution)/shard_map/ppermute | solution.py:388
  35.8 0.0 copy-done
  35.8 3.0 %scatter_kernel.1 = (f32[2,512,128]{2,1,0:T(8,128)S(1)}, f32[7,128,128]{2,1,0:T(8,128)S(1)}, f32[7,128,128]{2,1,0:T(8,128)S(1)}, f32[2816,128]{1,0:T(8,128)S(1)}) custom-call(f32[32,128]{1,0:T(8,128)S(1)} %add.13.refs_0_, f32[32,128]{1,0:T(8,128)S(1)} %collective-permute-done.4.refs_1_, s32[32,128]{1,0:T(8,128)S(1)} %bitcast.15, f32[32,128]{1,0:T(8,128)S(1)} %bitcast.18, ...), custom_call_target="tpu_custom_call" | custom-call | flops 20000000 | bytes 2000000 | tf_op jit(solution)/shard_map/scatter_kernel/pallas_call | solution.py:402
  38.8 0.1 collective-permute-start.5
  38.9 0.8 %collective-permute-start.6 = (f32[7,128,128]{2,1,0:T(8,128)S(1)}, f32[7,128,128]{2,1,0:T(8,128)S(1)}, u32[]{:S(2)}, u32[]{:S(2)}) collective-permute-start(f32[7,128,128]{2,1,0:T(8,128)S(1)} %get-tuple-element.25), channel_id=1, source_target_pairs={{0,15},{1,2},{2,1},{3,4},{4,3},{5,6},{6,5},{7,8},{8,7},{9,10},{10,... | collective-permute-start | bytes 1376264 | tf_op jit(solution)/shard_map/ppermute | solution.py:379
  39.7 3.6 %local_kernel.1.refs_0_ = f32[7,512,128]{2,1,0:T(8,128)S(1)} custom-call(bf16[256,512]{1,0:T(8,128)(2,1)S(1)} %copy-done.1, f32[2,512,128]{2,1,0:T(8,128)S(1)} %get-tuple-element.21.refs_1_, f32[2816,128]{1,0:T(8,128)S(1)} %get-tuple-element.22.refs_2_, f32[7,32,128]{2,1,0:T(8,128)S(1)} %broadcast_in_dim.10.refs_1_.refs_6_.refs_3_, ...), custom_call_target="tpu_custom_call" | custom-call | flops 20000000 | bytes 2000000 | tf_op jit(solution)/shard_map/local_kernel/pallas_call | solution.py:402
  43.3 0.0 collective-permute-done.5.refs_1_
  43.3 5.7 %collective-permute-done.6.refs_2_ = f32[7,128,128]{2,1,0:T(8,128)S(1)} collective-permute-done((f32[7,128,128]{2,1,0:T(8,128)S(1)}, f32[7,128,128]{2,1,0:T(8,128)S(1)}, u32[]{:S(2)}, u32[]{:S(2)}) %collective-permute-start.6) | collective-permute-done | bytes 458784 | tf_op jit(solution)/shard_map/ppermute | solution.py:379
  49.0 3.3 %edge_kernel.1 = (f32[2,512,128]{2,1,0:T(8,128)}, f32[5,512,128]{2,1,0:T(8,128)}) custom-call(f32[7,512,128]{2,1,0:T(8,128)S(1)} %local_kernel.1.refs_0_, f32[7,128,128]{2,1,0:T(8,128)S(1)} %collective-permute-done.5.refs_1_, f32[7,128,128]{2,1,0:T(8,128)S(1)} %collective-permute-done.6.refs_2_, s32[2]{0:T(128)S(1)} %copy-done.2, f32[12]{0:T(128)S(1)} %copy-done.3, ...), custom_call_target="tpu_custom_call" | custom-call | flops 20000000 | bytes 2000000 | tf_op jit(solution)/shard_map/edge_kernel/pallas_call | solution.py:402
  (5 shorter events, 0.0 us)
Async XLA Ops:
  0.6 11.1 %copy-start.1 = (bf16[256,512]{1,0:T(8,128)(2,1)S(1)}, bf16[256,512]{1,0:T(8,128)(2,1)}, u32[]{:S(2)}) copy-start(bf16[256,512]{1,0:T(8,128)(2,1)} %constant.8.clone.refs_0_) | copy-start | bytes 786436
  0.6 5.9 %copy-start.8 = (f32[1,5,32]{2,0,1:T(1,128)S(1)}, f32[1,5,32]{2,0,1:T(1,128)}, u32[]{:S(2)}) copy-start(f32[1,5,32]{2,0,1:T(1,128)} %param.19) | copy-start | bytes 1924
  0.7 5.9 %copy-start.9 = (f32[8]{0:T(128)S(1)}, f32[8]{0:T(128)}, u32[]{:S(2)}) copy-start(f32[8]{0:T(128)} %param.24) | copy-start | bytes 100
  0.7 5.9 %copy-start.7 = (s32[4096]{0:T(1024)S(1)}, s32[4096]{0:T(1024)}, u32[]{:S(2)}) copy-start(s32[4096]{0:T(1024)} %param.23) | copy-start | bytes 49156
  0.7 6.0 %copy-start.5 = (s32[4096]{0:T(1024)S(1)}, s32[4096]{0:T(1024)}, u32[]{:S(2)}) copy-start(s32[4096]{0:T(1024)} %param.22) | copy-start | bytes 49156
  0.7 6.0 %copy-start.4 = (s32[4096]{0:T(1024)S(1)}, s32[4096]{0:T(1024)}, u32[]{:S(2)}) copy-start(s32[4096]{0:T(1024)} %param.20) | copy-start | bytes 49156
  0.7 6.0 %copy-start.6 = (f32[4096]{0:T(1024)S(1)}, f32[4096]{0:T(1024)}, u32[]{:S(2)}) copy-start(f32[4096]{0:T(1024)} %param.21) | copy-start | bytes 49156
  0.7 11.0 %copy-start.3 = (f32[12]{0:T(128)S(1)}, f32[12]{0:T(128)}, u32[]{:S(2)}) copy-start(f32[12]{0:T(128)} %refs_4_.3) | copy-start | bytes 148
  0.7 11.0 %copy-start.2 = (s32[2]{0:T(128)S(1)}, s32[2]{0:T(128)}, u32[]{:S(2)}) copy-start(s32[2]{0:T(128)} %refs_3_.3) | copy-start | bytes 28
  2.4 13.6 %collective-permute-start = (f32[7,128,128]{2,1,0:T(8,128)S(1)}, f32[7,128,128]{2,1,0:T(8,128)S(1)}, u32[]{:S(2)}, u32[]{:S(2)}) collective-permute-start(f32[7,128,128]{2,1,0:T(8,128)S(1)} %get-tuple-element.16), channel_id=1, source_target_pairs={{0,1},{1,0},{2,3},{3,2},{4,5},{5,4},{6,7},{7,6},{8,9},{9,8},{10,11... | collective-permute-start | bytes 1376264 | tf_op jit(solution)/shard_map/ppermute | solution.py:379
  2.5 13.6 %collective-permute-start.1 = (f32[7,128,128]{2,1,0:T(8,128)S(1)}, f32[7,128,128]{2,1,0:T(8,128)S(1)}, u32[]{:S(2)}, u32[]{:S(2)}) collective-permute-start(f32[7,128,128]{2,1,0:T(8,128)S(1)} %get-tuple-element.17), channel_id=1, source_target_pairs={{0,15},{1,2},{2,1},{3,4},{4,3},{5,6},{6,5},{7,8},{8,7},{9,10},{10,... | collective-permute-start | bytes 1376264 | tf_op jit(solution)/shard_map/ppermute | solution.py:379
  16.1 19.7 %copy-start = (bf16[2,5,32,16,128]{4,3,2,1,0:T(8,128)(2,1)S(1)}, bf16[2,5,32,16,128]{4,3,2,1,0:T(8,128)(2,1)}, u32[]{:S(2)}) copy-start(bf16[2,5,32,16,128]{4,3,2,1,0:T(8,128)(2,1)} %param.15) | copy-start | bytes 3932164
  21.0 3.8 %collective-permute-start.2 = (f32[32,128]{1,0:T(8,128)S(1)}, f32[32,128]{1,0:T(8,128)S(1)}, u32[]{:S(2)}, u32[]{:S(2)}) collective-permute-start(f32[32,128]{1,0:T(8,128)S(1)} %forward_kernel.1), channel_id=1, source_target_pairs={{0,32},{16,48},{32,0},{48,16},{64,96},{80,112},{96,64},{112,80},{1... | collective-permute-start | bytes 49160 | tf_op jit(solution)/shard_map/ppermute | solution.py:388
  24.8 5.8 %collective-permute-start.3 = (f32[32,128]{1,0:T(8,128)S(1)}, f32[32,128]{1,0:T(8,128)S(1)}, u32[]{:S(2)}, u32[]{:S(2)}) collective-permute-start(f32[32,128]{1,0:T(8,128)S(1)} %add.12), channel_id=1, source_target_pairs={{0,96},{16,112},{32,64},{48,80},{64,32},{80,48},{96,0},{112,16},{1... | collective-permute-start | bytes 49160 | tf_op jit(solution)/shard_map/ppermute | solution.py:388
  30.6 5.2 %collective-permute-start.4 = (f32[32,128]{1,0:T(8,128)S(1)}, f32[32,128]{1,0:T(8,128)S(1)}, u32[]{:S(2)}, u32[]{:S(2)}) collective-permute-start(f32[32,128]{1,0:T(8,128)S(1)} %add.13.refs_0_), channel_id=1, source_target_pairs={{0,16},{16,0},{32,48},{48,32},{64,80},{80,64},{96,112},{112,96},{1... | collective-permute-start | bytes 49160 | tf_op jit(solution)/shard_map/ppermute | solution.py:388
  38.8 4.5 %collective-permute-start.5 = (f32[7,128,128]{2,1,0:T(8,128)S(1)}, f32[7,128,128]{2,1,0:T(8,128)S(1)}, u32[]{:S(2)}, u32[]{:S(2)}) collective-permute-start(f32[7,128,128]{2,1,0:T(8,128)S(1)} %get-tuple-element.24), channel_id=1, source_target_pairs={{0,1},{1,0},{2,3},{3,2},{4,5},{5,4},{6,7},{7,6},{8,9},{9,8},{10,11... | collective-permute-start | bytes 1376264 | tf_op jit(solution)/shard_map/ppermute | solution.py:379
  38.9 10.1 %collective-permute-start.6 = (f32[7,128,128]{2,1,0:T(8,128)S(1)}, f32[7,128,128]{2,1,0:T(8,128)S(1)}, u32[]{:S(2)}, u32[]{:S(2)}) collective-permute-start(f32[7,128,128]{2,1,0:T(8,128)S(1)} %get-tuple-element.25), channel_id=1, source_target_pairs={{0,15},{1,2},{2,1},{3,4},{4,3},{5,6},{6,5},{7,8},{8,7},{9,10},{10,... | collective-permute-start | bytes 1376264 | tf_op jit(solution)/shard_map/ppermute | solution.py:379

commit v9 on v8

--- a/solution.py
+++ b/solution.py
@@ -122,16 +122,32 @@
     return jnp.where(even, rows - SWEEPS, 0), jnp.where(even, 0, rows - SWEEPS)
 
 
-def sides_of(side_a, side_b, field, levels):
-    even = is_even()
+def part_of_side(side, field, rate, levels, rows, upper, counts):
+    planes = {}
+    for away in range(1, SWEEPS + 1):
+        j = jnp.where(upper, away - 1, SWEEPS - away)
+        planes[-away] = side[field, pl.ds(pl.multiple_of(j * levels, levels), levels), :]
+    parts = spread_rolled(planes, 0, SWEEPS - 1, rows, rate, (1.0, 1.0))
+    return [part if counts is None else part * counts for part in (parts[depth] for depth in range(SWEEPS))]
+
+
+def add_near(into, field, side, rate, levels, rows, scale=None):
+    upper = is_even()
+    for depth, part in enumerate(part_of_side(side, field, rate, levels, rows, upper, None)):
+        if scale is not None:
+            part = part * scale[field]
+        at = pl.ds(jnp.where(upper, rows - 1 - depth, depth), levels, stride=rows)
+        into[field, at, :] = into[field, at, :] + part
+
+
+def add_far(into, field, side, rate, levels, rows, scale=None):
+    upper = jnp.logical_not(is_even())
     below, above = neighbours()
-    lower, upper = [], []
-    for j in range(SWEEPS):
-        a = side_a[field, pl.ds(j * levels, levels), :]
-        b = side_b[field, pl.ds(j * levels, levels), :] * (below * above)
-        lower.append(jnp.where(even, b, a))
-        upper.append(jnp.where(even, a, b))
-    return lower, upper
+    for depth, part in enumerate(part_of_side(side, field, rate, levels, rows, upper, below * above)):
+        if scale is not None:
+            part = part * scale[field]
+        at = pl.ds(jnp.where(upper, rows - 1 - depth, depth), levels, stride=rows)
+        into[field, at, :] = into[field, at, :] + part
 
 
 def block_of(ref, block):
@@ -211,37 +227,27 @@
                 side[field, pl.ds(j * levels, levels), :] = held[field, pl.ds(begin + j, levels, stride=rows), :]
 
 
-def own_kernel(dims, powers, ens, stat, group, localize, static, out, held, sems):
+def own_kernel(dims, powers, held, scale, side_a, layer, index, kind, group, localize, static, precision, out, key, weight):
     members, nvars, levels, rows, cells, blocks = dims
     inside = neighbours()
-    start_loads(members, nvars, ens, stat, held, sems)
 
     def of_field(field):
-        load_of(field, ens, 0, held, sems).wait()
         planes = {x: held[field, pl.ds(x, levels, stride=rows), :] for x in range(rows)}
         rate = rate_of(field, members, group, localize, static)
         planes = spread_product(planes, rows, rate, inside, powers)
         for x in range(rows):
-            out[field, pl.ds(x * levels, levels), :] = planes[x]
+            out[field, pl.ds(x, levels, stride=rows), :] = planes[x] * scale[field]
+        add_near(out, field, side_a, rate, levels, rows, scale)
 
     each_field(members + nvars, of_field)
-
-
-def with_sides(dims, own, side_a, side_b, field, rate):
-    members, nvars, levels, rows, cells, blocks = dims
-    lower, upper = sides_of(side_a, side_b, field, levels)
-    lower = spread_rolled({j - SWEEPS: lower[j] for j in range(SWEEPS)}, 0, SWEEPS - 1, rows, rate, (1.0, 1.0))
-    upper = spread_rolled({rows + j: upper[j] for j in range(SWEEPS)}, rows - SWEEPS, rows - 1, rows, rate, (1.0, 1.0))
-    planes = {}
-    for x in range(rows):
-        planes[x] = own[field, pl.ds(x * levels, levels), :]
-        for extra in (lower, upper):
-            if x in extra:
-                planes[x] = planes[x] + extra[x]
-    return planes
-
-
-def forward_kernel(dims, own, scale, side_a, side_b, key, frac, perturb_far, bound, group, localize, static, out, smooth, table, perturb, sem):
+    key[...] = layer[...] * (rows * cells) + index[...]
+    total = jnp.zeros(kind.shape, jnp.float32)
+    for k in range(precision.shape[0]):
+        total = jnp.where(kind[...] == k, precision[k], total)
+    weight[...] = total
+
+
+def forward_kernel(dims, own, scale, side_b, key, frac, perturb_far, bound, group, localize, static, out, smooth, table, perturb, sem):
     members, nvars, levels, rows, cells, blocks = dims
     shift = cells.bit_length() - 1
     load = pltpu.make_async_copy(perturb_far, perturb, sem)
@@ -249,9 +255,8 @@
 
     def of_field(field):
         rate = rate_of(field, members, group, localize, static)
-        planes = with_sides(dims, own, side_a, side_b, field, rate)
-        for x in range(rows):
-            smooth[field, pl.ds(x, levels, stride=rows), :] = planes[x] * scale[field]
+        smooth[field] = own[field]
+        add_far(smooth, field, side_b, rate, levels, rows, scale)
 
     each_field(members + nvars, of_field)
     load.wait()
@@ -292,10 +297,14 @@
     every_window(bound, blocks, cells, visit, visit_again)
 
 
-def scatter_kernel(dims, seen, others, key, frac, weight, perturb, scale, bound, source, side_a, side_b, gradient, valued):
+def scatter_kernel(dims, key, frac, weight, perturb, scale, *refs):
     members, nvars, levels, rows, cells, blocks = dims
+    *seen, bound, source, side_a, side_b, gradient, valued = refs
     shift = cells.bit_length() - 1
-    valued[...] = (seen[...] + others[...]) * weight[...]
+    total = seen[0][...]
+    for part in seen[1:]:
+        total = total + part[...]
+    valued[...] = total * weight[...]
     gradient[...] = jnp.zeros(gradient.shape, jnp.float32)
 
     def add_block(block, start):
@@ -330,16 +339,20 @@
                 side[field, pl.ds(j * levels, levels), :] = strip
 
 
-def local_kernel(dims, powers, source, gradient, scale, held, group, localize, static, out):
+def local_kernel(dims, powers, source, gradient, scale, side_a, ens, stat, group, localize, static, out, held, sems):
     members, nvars, levels, rows, cells, blocks = dims
     inside = neighbours()
     plane = levels * rows
+    start_loads(members, nvars, ens, stat, held, sems)
 
     def of_field(field, planes):
         rate = rate_of(field, members, group, localize, static)
         planes = spread_product(planes, rows, rate, inside, powers)
+        load_of(field, ens, 0, held, sems).wait()
         for x in range(rows):
-            out[field, pl.ds(x * levels, levels), :] = held[field, pl.ds(x, levels, stride=rows), :] + planes[x]
+            at = pl.ds(x, levels, stride=rows)
+            out[field, at, :] = held[field, at, :] + planes[x]
+        add_near(out, field, side_a, rate, levels, rows)
 
     def of_member(m):
         of_field(m, {x: source[m, pl.ds(x, levels, stride=rows), :] for x in range(rows)})
@@ -353,7 +366,7 @@
     each_field(nvars, of_group)
 
 
-def edge_kernel(dims, own, side_a, side_b, group, localize, static, hv_ens, hv_stat, after, sems):
+def edge_kernel(dims, own, side_b, group, localize, static, hv_ens, hv_stat, after, sems):
     members, nvars, levels, rows, cells, blocks = dims
 
     def write_of(field, out, at):
@@ -361,9 +374,8 @@
 
     def of_field(field, out, at):
         rate = rate_of(field, members, group, localize, static)
-        planes = with_sides(dims, own, side_a, side_b, field, rate)
-        for x in range(rows):
-            after[field, pl.ds(x, levels, stride=rows), :] = planes[x]
+        after[field] = own[field]
+        add_far(after, field, side_b, rate, levels, rows)
         write_of(field, out, at).start()
 
     each_field(members, lambda m: of_field(m, hv_ens, m))
@@ -379,14 +391,11 @@
     return lax.ppermute(side_a, "tile", pairs_a), lax.ppermute(side_b, "tile", pairs_b)
 
 
-def halved_sums(value):
+def summands(value):
     count = lax.axis_size("grp")
-    others = None
-    for turn in (2, 6, 1) if count == 8 else [1 << bit for bit in range(count.bit_length() - 1)]:
-        if others is not None:
-            value = value + others
-        others = lax.ppermute(value, "grp", [(i, i ^ turn) for i in range(count)])
-    return value, others
+    value = value + lax.ppermute(value, "grp", [(i, i ^ 1) for i in range(count)])
+    turns = [2, 6, 4] if count == 8 else list(range(2, count, 2))
+    return [value] + [lax.ppermute(value, "grp", [(i, i ^ turn) for i in range(count)]) for turn in turns]
 
 
 VMEM = pl.BlockSpec(memory_space=pltpu.VMEM)
@@ -394,14 +403,14 @@
 HBM = pl.BlockSpec(memory_space=pltpu.HBM)
 
 
-def call(kernel, dims, outs, ins, far=(), scalars=(), scratch=(), out_spec=VMEM, cost=2_000_000):
+def call(kernel, dims, outs, ins, far=(), scalars=(), scratch=(), out_spec=VMEM, kinds=None, cost=2_000_000):
     def body(*refs):
         kernel(dims, *refs)
 
     far = [pltpu.with_memory_space_constraint(x, pltpu.HBM) for x in far]
     return pl.pallas_call(
         body,
-        out_shape=tuple(jax.ShapeDtypeStruct(shape, jnp.float32) for shape in outs),
+        out_shape=tuple(jax.ShapeDtypeStruct(tuple(shape), kind) for shape, kind in zip(outs, kinds or [jnp.float32] * len(outs))),
         in_specs=[VMEM] * len(ins) + [HBM] * len(far) + [SMEM] * len(scalars),
         out_specs=tuple([out_spec] * len(outs)),
         scratch_shapes=list(scratch),
@@ -439,28 +448,33 @@
     rates = [member_group, localize_rate, static_rate]
 
     whole = (fields, plane, cells)
+    key_shape = (obs_index.shape[0] // cells, cells)
     powers = y_powers(cells)
     copying = [pltpu.SemaphoreType.DMA((fields,))]
-    side_a, side_b = call(pack_kernel, dims, [strip, strip], [], [ens, stat], [], [pltpu.VMEM(whole, jnp.float32)] + copying)
+    side_a, side_b, held = call(pack_kernel, dims, [strip, strip, whole], [], [ens, stat], [], copying)
     side_a, side_b = exchange(side_a, side_b)
 
     scale = jnp.concatenate([jnp.ones((members, levels), jnp.float32), static_scale[0]])
     scale = jnp.broadcast_to(scale[:, :, None], (fields, levels, cells))
-    kind_ids = jnp.arange(obs_precision.shape[0], dtype=jnp.int32)
-    weight = jnp.sum(
-        jnp.where(obs_kind[:, None] == kind_ids[None, :], obs_precision[None, :], 0.0), axis=1
+    layer, index, kind = (x.reshape(-1, cells) for x in (obs_layer, obs_index, obs_kind))
+    own, key, weight = call(
+        own_kernel,
+        dims,
+        [whole, key_shape, key_shape],
+        [powers, held, scale, side_a, layer, index, kind],
+        [],
+        rates + [obs_precision],
+        kinds=[jnp.float32, jnp.int32, jnp.float32],
     )
-    key = obs_layer * (rows * cells) + obs_index
-    key, frac, weight = lax.sort((key, obs_frac, weight), num_keys=1, is_stable=False)
-    key, frac, weight = (x.reshape(-1, cells) for x in (key, frac, weight))
+    key, frac, weight = lax.sort((key.reshape(-1), obs_frac, weight.reshape(-1)), num_keys=1, is_stable=False)
+    key, frac, weight = (x.reshape(key_shape) for x in (key, frac, weight))
 
     table_rows = nvars * plane + BLOCK
-    own, held = call(own_kernel, dims, [whole, whole], [powers], [ens, stat], rates, copying)
     (seen,) = call(
         forward_kernel,
         dims,
         [key.shape],
-        [own, scale, side_a, side_b, key, frac],
+        [own, scale, side_b, key, frac],
         [perturb],
         [key] + rates,
         [
@@ -470,23 +484,23 @@
             pltpu.SemaphoreType.DMA(()),
         ],
     )
-    seen, others = halved_sums(seen)
+    seen = summands(seen)
     source, side_a, side_b, gradient = call(
         scatter_kernel,
         dims,
         [(members, plane, cells), strip, strip, (table_rows, cells)],
-        [seen, others, key, frac, weight, perturb, scale],
+        [key, frac, weight, perturb, scale] + seen,
         [],
         [key],
         [pltpu.VMEM(key.shape, jnp.float32)],
     )
     side_a, side_b = exchange(side_a, side_b)
-    (own,) = call(local_kernel, dims, [whole], [powers, source, gradient, scale, held], [], rates)
+    (own,) = call(local_kernel, dims, [whole], [powers, source, gradient, scale, side_a], [ens, stat], rates, [pltpu.VMEM(whole, jnp.float32)] + copying)
     hv_ens, hv_stat = call(
         edge_kernel,
         dims,
         [(members, plane, cells), (nvars, plane, cells)],
-        [own, side_a, side_b],
+        [own, side_b],
         [],
         rates,
         [pltpu.VMEM(whole, jnp.float32), pltpu.SemaphoreType.DMA((fields,))],

time: 53.3 us -> 52.4 us (0.983)
  waiting for transfers between devices: 13.4 us -> 10.1 us
  Pallas kernels: 20.7 us -> 23.9 us
  starting transfers between devices: 11.5 us -> 10.8 us
    ppermute x2, waiting for transfers between devices: 5.69 us -> 1.4 us  [exchange(): lax.ppermute(side_b, 'tile', pairs_b)]
    pallas_call x6, Pallas kernels: 20.7 us -> 23.9 us  [call(): pl.pallas_call(body, out_shape=tuple((jax.ShapeDtypeStruct(tuple(shape),...]
    ppermute x3 -> x4, starting transfers between devices: 7.15 us -> 6.11 us  [the longest x3 4.91 us: summands(): lax.ppermute(value, 'grp', [(i, i ^ turn) for i in range(count)])]
    ppermute x2, waiting for transfers between devices: 0.01 us -> 0.69 us  [exchange(): lax.ppermute(side_a, 'tile', pairs_a)]
    ppermute x3 -> x4, waiting for transfers between devices: 7.68 us -> 8.04 us  [the longest x1 4.12 us: summands(): lax.ppermute(value, 'grp', [(i, i ^ 1) for i in range(count)])]
  transfers between devices with their start and end apart: 7 -> 8, of which waited for: 4 -> 5; matrix products, arithmetic and copies ran while one was open for 10% -> 10% of each run, Pallas kernels for 15% -> 22%
where the time goes in v9:
time: 52.4 us; the launch traced here: 51.4 us
  Pallas kernels  23.9 us (46%)
  starting transfers between devices  10.8 us (21%)
  waiting for transfers between devices  10.1 us (19%)
  other arithmetic  4.99 us (10%)
  between operations  1.53 us (3%)
    pallas_call x6, Pallas kernels, call(): pl.pallas_call(body, out_shape=tuple((jax.ShapeDtypeStruct(tuple(shape),...  23.9 us
    sort x1, other arithmetic, per_device(): lax.sort((key.reshape(-1), obs_frac, weight.reshape(-1)), num_keys=1, is_...  4.98 us
    ppermute x3, starting transfers between devices, summands(): lax.ppermute(value, 'grp', [(i, i ^ turn) for i in range(count)])  4.91 us
    ppermute x2, starting transfers between devices, exchange(): lax.ppermute(side_b, 'tile', pairs_b)  4.5 us
    ppermute x1, waiting for transfers between devices, summands(): lax.ppermute(value, 'grp', [(i, i ^ 1) for i in range(count)])  4.12 us
    ppermute x3, waiting for transfers between devices, summands(): lax.ppermute(value, 'grp', [(i, i ^ turn) for i in range(count)])  3.92 us
    ppermute x2, waiting for transfers between devices, exchange(): lax.ppermute(side_b, 'tile', pairs_b)  1.4 us
    ppermute x1, starting transfers between devices, summands(): lax.ppermute(value, 'grp', [(i, i ^ 1) for i in range(count)])  1.2 us
  transfers between devices with their start and end apart: 8, of which 5 were waited for; matrix products, arithmetic and copies ran while one was open for 10% of the time, Pallas kernels for 22%

profile of v9, /device:TPU:6, one launch (start us, length us, event | category | flops | bytes accessed | tf_op | source)
XLA Modules:
  0.0 51.4 jit_solution(17409782890520932365)
XLA Ops:
  0.6 0.0 copy-start.1
  0.6 0.0 copy-start.9
  0.7 0.0 copy-start.6
  0.7 0.0 copy-start.5
  0.7 0.0 copy-start.7
  0.7 0.0 copy-start.4
  0.7 0.0 copy-start.2
  0.7 0.0 copy-start.3
  0.7 1.6 %pack_kernel.1 = (f32[7,128,128]{2,1,0:T(8,128)S(1)}, f32[7,128,128]{2,1,0:T(8,128)S(1)}, f32[7,512,128]{2,1,0:T(8,128)S(1)}) custom-call(f32[2,512,128]{2,1,0:T(8,128)} %bitcast.32, f32[5,512,128]{2,1,0:T(8,128)} %bitcast.30), custom_call_target="tpu_custom_call" | custom-call | flops 20000000 | bytes 2000000 | tf_op jit(solution)/shard_map/pack_kernel/pallas_call | solution.py:411
  2.4 0.0 copy-start.8
  2.4 0.1 collective-permute-start
  2.5 3.4 %collective-permute-start.1 = (f32[7,128,128]{2,1,0:T(8,128)S(1)}, f32[7,128,128]{2,1,0:T(8,128)S(1)}, u32[]{:S(2)}, u32[]{:S(2)}) collective-permute-start(f32[7,128,128]{2,1,0:T(8,128)S(1)} %get-tuple-element.25), channel_id=1, source_target_pairs={{0,15},{1,2},{2,1},{3,4},{4,3},{5,6},{6,5},{7,8},{8,7},{9,10},{10,... | collective-permute-start | bytes 1376264 | tf_op jit(solution)/shard_map/ppermute | solution.py:391
  6.5 0.0 copy-done.9
  6.5 0.0 collective-permute-done.refs_3_
  6.5 0.1 broadcast_in_dim.2.refs_2_.refs_1_.refs_4_.refs_3_
  6.6 0.0 copy-done.1
  6.6 0.0 copy-done.6
  6.7 0.0 copy-done.5
  6.7 0.0 copy-done.7
  6.7 0.0 copy-done.4
  6.7 0.0 copy-done.2
  6.7 0.0 copy-done.3
  6.7 4.2 %own_kernel.1 = (f32[7,512,128]{2,1,0:T(8,128)S(1)}, s32[32,128]{1,0:T(8,128)S(1)}, f32[32,128]{1,0:T(8,128)S(1)}) custom-call(bf16[256,512]{1,0:T(8,128)(2,1)S(1)} %copy-done.1, f32[7,512,128]{2,1,0:T(8,128)S(1)} %get-tuple-element.17.refs_1_, f32[7,32,128]{2,1,0:T(8,128)S(1)} %broadcast_in_dim.2.refs_2_.refs_1_.refs_4_.refs_3_, ...), custom_call_target="tpu_custom_call" | custom-call | flops 20000000 | bytes 2000000 | tf_op jit(solution)/shard_map/own_kernel/pallas_call | solution.py:411
  10.9 0.0 copy-done.8
  10.9 5.0 %sort.21 = (s32[4096]{0:T(1024)S(1)}, f32[4096]{0:T(1024)S(1)}, f32[4096]{0:T(1024)S(1)}) sort(s32[4096]{0:T(1024)S(1)} %bitcast.28, f32[4096]{0:T(1024)S(1)} %copy-done.8, f32[4096]{0:T(1024)S(1)} %bitcast.29), dimensions={0}, to_apply=%region_0.0 | sort | flops 49152 | bytes 98304 | tf_op jit(solution)/shard_map/sort | solution.py:469
  15.9 0.0 collective-permute-done.1.refs_2_
  15.9 0.0 copy-start
  15.9 4.8 %forward_kernel.1 = f32[32,128]{1,0:T(8,128)S(1)} custom-call(f32[7,512,128]{2,1,0:T(8,128)S(1)} %get-tuple-element.24.refs_0_, f32[7,32,128]{2,1,0:T(8,128)S(1)} %broadcast_in_dim.2.refs_2_.refs_1_.refs_4_.refs_3_, f32[7,128,128]{2,1,0:T(8,128)S(1)} %collective-permute-done.1.refs_2_, s32[32,128]{1,0:T(8,128)S(1)} %bitcast.18, f32[32,128]{1,0:T(8,128)S(1)} %bitcast.22, ...), custom_call_target="tpu_custom_call" | custom-call | flops 20000000 | bytes 2000000 | tf_op jit(solution)/shard_map/forward_kernel/pallas_call | solution.py:411
  20.8 1.2 %collective-permute-start.2 = (f32[32,128]{1,0:T(8,128)S(1)}, f32[32,128]{1,0:T(8,128)S(1)}, u32[]{:S(2)}, u32[]{:S(2)}) collective-permute-start(f32[32,128]{1,0:T(8,128)S(1)} %forward_kernel.1), channel_id=1, source_target_pairs={{0,16},{16,0},{32,48},{48,32},{64,80},{80,64},{96,112},{112,96},{1... | collective-permute-start | bytes 49160 | tf_op jit(solution)/shard_map/ppermute | solution.py:396
  22.0 4.1 %collective-permute-done.2 = f32[32,128]{1,0:T(8,128)S(1)} collective-permute-done((f32[32,128]{1,0:T(8,128)S(1)}, f32[32,128]{1,0:T(8,128)S(1)}, u32[]{:S(2)}, u32[]{:S(2)}) %collective-permute-start.2) | collective-permute-done | bytes 16416 | tf_op jit(solution)/shard_map/ppermute | solution.py:396
  26.1 3.9 %collective-permute-start.5 = (f32[32,128]{1,0:T(8,128)S(1)}, f32[32,128]{1,0:T(8,128)S(1)}, u32[]{:S(2)}, u32[]{:S(2)}) collective-permute-start(f32[32,128]{1,0:T(8,128)S(1)} %add.5.refs_5_), channel_id=1, source_target_pairs={{0,64},{16,80},{32,96},{48,112},{64,0},{80,16},{96,32},{112,48},{1... | collective-permute-start | bytes 49160 | tf_op jit(solution)/shard_map/ppermute | solution.py:398
  30.0 0.7 %collective-permute-start.4 = (f32[32,128]{1,0:T(8,128)S(1)}, f32[32,128]{1,0:T(8,128)S(1)}, u32[]{:S(2)}, u32[]{:S(2)}) collective-permute-start(f32[32,128]{1,0:T(8,128)S(1)} %add.5.refs_5_), channel_id=1, source_target_pairs={{0,96},{16,112},{32,64},{48,80},{64,32},{80,48},{96,0},{112,16},{1... | collective-permute-start | bytes 49160 | tf_op jit(solution)/shard_map/ppermute | solution.py:398
  30.7 0.3 collective-permute-start.3
  31.0 0.7 %collective-permute-done.5.refs_8_ = f32[32,128]{1,0:T(8,128)S(1)} collective-permute-done((f32[32,128]{1,0:T(8,128)S(1)}, f32[32,128]{1,0:T(8,128)S(1)}, u32[]{:S(2)}, u32[]{:S(2)}) %collective-permute-start.5) | collective-permute-done | bytes 16416 | tf_op jit(solution)/shard_map/ppermute | solution.py:398
  31.7 3.2 %collective-permute-done.4.refs_7_ = f32[32,128]{1,0:T(8,128)S(1)} collective-permute-done((f32[32,128]{1,0:T(8,128)S(1)}, f32[32,128]{1,0:T(8,128)S(1)}, u32[]{:S(2)}, u32[]{:S(2)}) %collective-permute-start.4) | collective-permute-done | bytes 16416 | tf_op jit(solution)/shard_map/ppermute | solution.py:398
  34.9 0.0 collective-permute-done.3.refs_6_
  34.9 0.0 copy-done
  34.9 3.0 %scatter_kernel.1 = (f32[2,512,128]{2,1,0:T(8,128)S(1)}, f32[7,128,128]{2,1,0:T(8,128)S(1)}, f32[7,128,128]{2,1,0:T(8,128)S(1)}, f32[2816,128]{1,0:T(8,128)S(1)}) custom-call(s32[32,128]{1,0:T(8,128)S(1)} %bitcast.20, f32[32,128]{1,0:T(8,128)S(1)} %bitcast.23, f32[32,128]{1,0:T(8,128)S(1)} %bitcast.27, bf16[2,5,512,128]{3,2,1,0:T(8,128)(2,1)S(1)} %bitcast.17, ...), custom_call_target="tpu_custom_call" | custom-call | flops 20000000 | bytes 2000000 | tf_op jit(solution)/shard_map/scatter_kernel/pallas_call | solution.py:411
  37.9 0.1 collective-permute-start.6
  38.0 1.1 %collective-permute-start.7 = (f32[7,128,128]{2,1,0:T(8,128)S(1)}, f32[7,128,128]{2,1,0:T(8,128)S(1)}, u32[]{:S(2)}, u32[]{:S(2)}) collective-permute-start(f32[7,128,128]{2,1,0:T(8,128)S(1)} %get-tuple-element.29), channel_id=1, source_target_pairs={{0,15},{1,2},{2,1},{3,4},{4,3},{5,6},{6,5},{7,8},{8,7},{9,10},{10,... | collective-permute-start | bytes 1376264 | tf_op jit(solution)/shard_map/ppermute | solution.py:391
  39.1 0.7 %collective-permute-done.6.refs_4_ = f32[7,128,128]{2,1,0:T(8,128)S(1)} collective-permute-done((f32[7,128,128]{2,1,0:T(8,128)S(1)}, f32[7,128,128]{2,1,0:T(8,128)S(1)}, u32[]{:S(2)}, u32[]{:S(2)}) %collective-permute-start.6) | collective-permute-done | bytes 458784 | tf_op jit(solution)/shard_map/ppermute | solution.py:391
  39.8 6.9 %local_kernel.1.refs_0_ = f32[7,512,128]{2,1,0:T(8,128)S(1)} custom-call(bf16[256,512]{1,0:T(8,128)(2,1)S(1)} %copy-done.1, f32[2,512,128]{2,1,0:T(8,128)S(1)} %get-tuple-element.26.refs_1_, f32[2816,128]{1,0:T(8,128)S(1)} %get-tuple-element.27.refs_2_, f32[7,32,128]{2,1,0:T(8,128)S(1)} %broadcast_in_dim.2.refs_2_.refs_1_.refs_4_.refs_3_, ...), custom_call_target="tpu_custom_call" | custom-call | flops 20000000 | bytes 2000000 | tf_op jit(solution)/shard_map/local_kernel/pallas_call | solution.py:411
  46.7 1.4 %collective-permute-done.7.refs_1_ = f32[7,128,128]{2,1,0:T(8,128)S(1)} collective-permute-done((f32[7,128,128]{2,1,0:T(8,128)S(1)}, f32[7,128,128]{2,1,0:T(8,128)S(1)}, u32[]{:S(2)}, u32[]{:S(2)}) %collective-permute-start.7) | collective-permute-done | bytes 458784 | tf_op jit(solution)/shard_map/ppermute | solution.py:391
  48.1 3.3 %edge_kernel.1 = (f32[2,512,128]{2,1,0:T(8,128)}, f32[5,512,128]{2,1,0:T(8,128)}) custom-call(f32[7,512,128]{2,1,0:T(8,128)S(1)} %local_kernel.1.refs_0_, f32[7,128,128]{2,1,0:T(8,128)S(1)} %collective-permute-done.7.refs_1_, s32[2]{0:T(128)S(1)} %copy-done.5, f32[12]{0:T(128)S(1)} %copy-done.6, f32[1]{0:T(128)S(6)} %copy.18.refs_9_.refs_4_), custom_call_target="tpu_custom_call" | custom-call | flops 20000000 | bytes 2000000 | tf_op jit(solution)/shard_map/edge_kernel/pallas_call | solution.py:411
  (3 shorter events, 0.0 us)
Async XLA Ops:
  0.6 6.0 %copy-start.1 = (bf16[256,512]{1,0:T(8,128)(2,1)S(1)}, bf16[256,512]{1,0:T(8,128)(2,1)}, u32[]{:S(2)}) copy-start(bf16[256,512]{1,0:T(8,128)(2,1)} %constant.4.clone.refs_0_) | copy-start | bytes 786436
  0.6 5.9 %copy-start.9 = (f32[1,5,32]{2,0,1:T(1,128)S(1)}, f32[1,5,32]{2,0,1:T(1,128)}, u32[]{:S(2)}) copy-start(f32[1,5,32]{2,0,1:T(1,128)} %param.19) | copy-start | bytes 1924
  0.7 6.0 %copy-start.6 = (f32[12]{0:T(128)S(1)}, f32[12]{0:T(128)}, u32[]{:S(2)}) copy-start(f32[12]{0:T(128)} %refs_3_.1) | copy-start | bytes 148
  0.7 6.0 %copy-start.5 = (s32[2]{0:T(128)S(1)}, s32[2]{0:T(128)}, u32[]{:S(2)}) copy-start(s32[2]{0:T(128)} %refs_2_.1) | copy-start | bytes 28
  0.7 6.0 %copy-start.7 = (f32[8]{0:T(128)S(1)}, f32[8]{0:T(128)}, u32[]{:S(2)}) copy-start(f32[8]{0:T(128)} %refs_10_.1) | copy-start | bytes 100
  0.7 6.0 %copy-start.4 = (s32[4096]{0:T(1024)S(1)}, s32[4096]{0:T(1024)}, u32[]{:S(2)}) copy-start(s32[4096]{0:T(1024)} %param.23) | copy-start | bytes 49156
  0.7 6.0 %copy-start.2 = (s32[4096]{0:T(1024)S(1)}, s32[4096]{0:T(1024)}, u32[]{:S(2)}) copy-start(s32[4096]{0:T(1024)} %param.22) | copy-start | bytes 49156
  0.7 6.0 %copy-start.3 = (s32[4096]{0:T(1024)S(1)}, s32[4096]{0:T(1024)}, u32[]{:S(2)}) copy-start(s32[4096]{0:T(1024)} %param.20) | copy-start | bytes 49156
  2.4 8.6 %copy-start.8 = (f32[4096]{0:T(1024)S(1)}, f32[4096]{0:T(1024)}, u32[]{:S(2)}) copy-start(f32[4096]{0:T(1024)} %param.21) | copy-start | bytes 49156
  2.4 4.2 %collective-permute-start = (f32[7,128,128]{2,1,0:T(8,128)S(1)}, f32[7,128,128]{2,1,0:T(8,128)S(1)}, u32[]{:S(2)}, u32[]{:S(2)}) collective-permute-start(f32[7,128,128]{2,1,0:T(8,128)S(1)} %get-tuple-element.18), channel_id=1, source_target_pairs={{0,1},{1,0},{2,3},{3,2},{4,5},{5,4},{6,7},{7,6},{8,9},{9,8},{10,11... | collective-permute-start | bytes 1376264 | tf_op jit(solution)/shard_map/ppermute | solution.py:391
  2.5 13.4 %collective-permute-start.1 = (f32[7,128,128]{2,1,0:T(8,128)S(1)}, f32[7,128,128]{2,1,0:T(8,128)S(1)}, u32[]{:S(2)}, u32[]{:S(2)}) collective-permute-start(f32[7,128,128]{2,1,0:T(8,128)S(1)} %get-tuple-element.25), channel_id=1, source_target_pairs={{0,15},{1,2},{2,1},{3,4},{4,3},{5,6},{6,5},{7,8},{8,7},{9,10},{10,... | collective-permute-start | bytes 1376264 | tf_op jit(solution)/shard_map/ppermute | solution.py:391
  15.9 19.0 %copy-start = (bf16[2,5,32,16,128]{4,3,2,1,0:T(8,128)(2,1)S(1)}, bf16[2,5,32,16,128]{4,3,2,1,0:T(8,128)(2,1)}, u32[]{:S(2)}) copy-start(bf16[2,5,32,16,128]{4,3,2,1,0:T(8,128)(2,1)} %param.15) | copy-start | bytes 3932164
  20.8 5.3 %collective-permute-start.2 = (f32[32,128]{1,0:T(8,128)S(1)}, f32[32,128]{1,0:T(8,128)S(1)}, u32[]{:S(2)}, u32[]{:S(2)}) collective-permute-start(f32[32,128]{1,0:T(8,128)S(1)} %forward_kernel.1), channel_id=1, source_target_pairs={{0,16},{16,0},{32,48},{48,32},{64,80},{80,64},{96,112},{112,96},{1... | collective-permute-start | bytes 49160 | tf_op jit(solution)/shard_map/ppermute | solution.py:396
  26.1 5.6 %collective-permute-start.5 = (f32[32,128]{1,0:T(8,128)S(1)}, f32[32,128]{1,0:T(8,128)S(1)}, u32[]{:S(2)}, u32[]{:S(2)}) collective-permute-start(f32[32,128]{1,0:T(8,128)S(1)} %add.5.refs_5_), channel_id=1, source_target_pairs={{0,64},{16,80},{32,96},{48,112},{64,0},{80,16},{96,32},{112,48},{1... | collective-permute-start | bytes 49160 | tf_op jit(solution)/shard_map/ppermute | solution.py:398
  30.0 4.9 %collective-permute-start.4 = (f32[32,128]{1,0:T(8,128)S(1)}, f32[32,128]{1,0:T(8,128)S(1)}, u32[]{:S(2)}, u32[]{:S(2)}) collective-permute-start(f32[32,128]{1,0:T(8,128)S(1)} %add.5.refs_5_), channel_id=1, source_target_pairs={{0,96},{16,112},{32,64},{48,80},{64,32},{80,48},{96,0},{112,16},{1... | collective-permute-start | bytes 49160 | tf_op jit(solution)/shard_map/ppermute | solution.py:398
  30.7 4.2 %collective-permute-start.3 = (f32[32,128]{1,0:T(8,128)S(1)}, f32[32,128]{1,0:T(8,128)S(1)}, u32[]{:S(2)}, u32[]{:S(2)}) collective-permute-start(f32[32,128]{1,0:T(8,128)S(1)} %add.5.refs_5_), channel_id=1, source_target_pairs={{0,32},{16,48},{32,0},{48,16},{64,96},{80,112},{96,64},{112,80},{1... | collective-permute-start | bytes 49160 | tf_op jit(solution)/shard_map/ppermute | solution.py:398
  37.9 1.9 %collective-permute-start.6 = (f32[7,128,128]{2,1,0:T(8,128)S(1)}, f32[7,128,128]{2,1,0:T(8,128)S(1)}, u32[]{:S(2)}, u32[]{:S(2)}) collective-permute-start(f32[7,128,128]{2,1,0:T(8,128)S(1)} %get-tuple-element.28), channel_id=1, source_target_pairs={{0,1},{1,0},{2,3},{3,2},{4,5},{5,4},{6,7},{7,6},{8,9},{9,8},{10,11... | collective-permute-start | bytes 1376264 | tf_op jit(solution)/shard_map/ppermute | solution.py:391
  38.0 10.1 %collective-permute-start.7 = (f32[7,128,128]{2,1,0:T(8,128)S(1)}, f32[7,128,128]{2,1,0:T(8,128)S(1)}, u32[]{:S(2)}, u32[]{:S(2)}) collective-permute-start(f32[7,128,128]{2,1,0:T(8,128)S(1)} %get-tuple-element.29), channel_id=1, source_target_pairs={{0,15},{1,2},{2,1},{3,4},{4,3},{5,6},{6,5},{7,8},{8,7},{9,10},{10,... | collective-permute-start | bytes 1376264 | tf_op jit(solution)/shard_map/ppermute | solution.py:391

commit v10 on v9

--- a/solution.py
+++ b/solution.py
@@ -14,7 +14,9 @@
 
 
 def along_x(planes, wanted, rows, rate, inside):
-    factors = [(1.0 - 4.0 * rate, rate)] + [((1.0 - 4.0 * rate) * side, rate * side) for side in inside]
+    factors = [(1.0 - 4.0 * rate, rate)] * 3
+    if inside is not None:
+        factors[1:] = [((1.0 - 4.0 * rate) * side, rate * side) for side in inside]
     result = {}
     for x in wanted:
         keep, share = factors[1 if x < 0 else 2 if x >= rows else 0]
@@ -107,6 +109,10 @@
     return jnp.where(field < members, localize[group[member]], static[0])
 
 
+def rates_of(fields, members, group, localize, static):
+    return [rate_of(field, members, group, localize, static) for field in range(fields)]
+
+
 def neighbours():
     tile = lax.axis_index("tile")
     last = lax.axis_size("tile") - 1
@@ -122,32 +128,44 @@
     return jnp.where(even, rows - SWEEPS, 0), jnp.where(even, 0, rows - SWEEPS)
 
 
-def part_of_side(side, field, rate, levels, rows, upper, counts):
-    planes = {}
-    for away in range(1, SWEEPS + 1):
-        j = jnp.where(upper, away - 1, SWEEPS - away)
-        planes[-away] = side[field, pl.ds(pl.multiple_of(j * levels, levels), levels), :]
-    parts = spread_rolled(planes, 0, SWEEPS - 1, rows, rate, (1.0, 1.0))
-    return [part if counts is None else part * counts for part in (parts[depth] for depth in range(SWEEPS))]
-
-
-def add_near(into, field, side, rate, levels, rows, scale=None):
+BATCH = 4
+
+
+def add_side(side, upper, rates, shape, visit, counts=None):
+    levels, rows, cells = shape
+    for first in range(0, len(rates), BATCH):
+        fields = range(first, min(first + BATCH, len(rates)))
+        rate = jnp.concatenate([jnp.full((levels, cells), rates[field], jnp.float32) for field in fields], axis=0)
+        planes = {}
+        for away in range(1, SWEEPS + 1):
+            j = jnp.where(upper, away - 1, SWEEPS - away)
+            planes[-away] = side[j, first * levels : (first + len(fields)) * levels, :]
+        parts = spread_rolled(planes, 0, SWEEPS - 1, rows, rate, None)
+        for at, field in enumerate(fields):
+            for depth in range(SWEEPS):
+                part = parts[depth][at * levels : (at + 1) * levels]
+                visit(field, depth, part if counts is None else part * counts)
+
+
+def adder(into, upper, shape, scale=None):
+    levels, rows, cells = shape
+
+    def visit(field, depth, part):
+        at = pl.ds(jnp.where(upper, rows - 1 - depth, depth), levels, stride=rows)
+        into[field, at, :] = into[field, at, :] + (part if scale is None else part * scale[field])
+
+    return visit
+
+
+def add_near(into, side, rates, shape, scale=None):
     upper = is_even()
-    for depth, part in enumerate(part_of_side(side, field, rate, levels, rows, upper, None)):
-        if scale is not None:
-            part = part * scale[field]
-        at = pl.ds(jnp.where(upper, rows - 1 - depth, depth), levels, stride=rows)
-        into[field, at, :] = into[field, at, :] + part
-
-
-def add_far(into, field, side, rate, levels, rows, scale=None):
+    add_side(side, upper, rates, shape, adder(into, upper, shape, scale))
+
+
+def add_far(into, side, rates, shape, scale=None):
     upper = jnp.logical_not(is_even())
     below, above = neighbours()
-    for depth, part in enumerate(part_of_side(side, field, rate, levels, rows, upper, below * above)):
-        if scale is not None:
-            part = part * scale[field]
-        at = pl.ds(jnp.where(upper, rows - 1 - depth, depth), levels, stride=rows)
-        into[field, at, :] = into[field, at, :] + part
+    add_side(side, upper, rates, shape, adder(into, upper, shape, scale), below * above)
 
 
 def block_of(ref, block):
@@ -224,7 +242,7 @@
         load_of(field, ens, 0, held, sems).wait()
         for begin, side in zip(begins(rows), (side_a, side_b)):
             for j in range(SWEEPS):
-                side[field, pl.ds(j * levels, levels), :] = held[field, pl.ds(begin + j, levels, stride=rows), :]
+                side[j, pl.ds(field * levels, levels), :] = held[field, pl.ds(begin + j, levels, stride=rows), :]
 
 
 def own_kernel(dims, powers, held, scale, side_a, layer, index, kind, group, localize, static, precision, out, key, weight):
@@ -237,9 +255,10 @@
         planes = spread_product(planes, rows, rate, inside, powers)
         for x in range(rows):
             out[field, pl.ds(x, levels, stride=rows), :] = planes[x] * scale[field]
-        add_near(out, field, side_a, rate, levels, rows, scale)
 
     each_field(members + nvars, of_field)
+    rates = rates_of(members + nvars, members, group, localize, static)
+    add_near(out, side_a, rates, (levels, rows, cells), scale)
     key[...] = layer[...] * (rows * cells) + index[...]
     total = jnp.zeros(kind.shape, jnp.float32)
     for k in range(precision.shape[0]):
@@ -253,12 +272,9 @@
     load = pltpu.make_async_copy(perturb_far, perturb, sem)
     load.start()
 
-    def of_field(field):
-        rate = rate_of(field, members, group, localize, static)
-        smooth[field] = own[field]
-        add_far(smooth, field, side_b, rate, levels, rows, scale)
-
-    each_field(members + nvars, of_field)
+    smooth[...] = own[...]
+    rates = rates_of(members + nvars, members, group, localize, static)
+    add_far(smooth, side_b, rates, (levels, rows, cells), scale)
     load.wait()
     plane = levels * rows
     for v in range(nvars):
@@ -336,7 +352,7 @@
                 else:
                     at = (field - members) * plane + begin + j
                     strip = gradient[pl.ds(at, levels, stride=rows), :] * scale[field]
-                side[field, pl.ds(j * levels, levels), :] = strip
+                side[j, pl.ds(field * levels, levels), :] = strip
 
 
 def local_kernel(dims, powers, source, gradient, scale, side_a, ens, stat, group, localize, static, out, held, sems):
@@ -352,7 +368,6 @@
         for x in range(rows):
             at = pl.ds(x, levels, stride=rows)
             out[field, at, :] = held[field, at, :] + planes[x]
-        add_near(out, field, side_a, rate, levels, rows)
 
     def of_member(m):
         of_field(m, {x: source[m, pl.ds(x, levels, stride=rows), :] for x in range(rows)})
@@ -364,24 +379,32 @@
 
     each_field(members, of_member)
     each_field(nvars, of_group)
+    rates = rates_of(members + nvars, members, group, localize, static)
+    add_near(out, side_a, rates, (levels, rows, cells))
 
 
 def edge_kernel(dims, own, side_b, group, localize, static, hv_ens, hv_stat, after, sems):
     members, nvars, levels, rows, cells, blocks = dims
 
-    def write_of(field, out, at):
-        return pltpu.make_async_copy(after.at[field], out.at[at], sems.at[field])
-
-    def of_field(field, out, at):
-        rate = rate_of(field, members, group, localize, static)
-        after[field] = own[field]
-        add_far(after, field, side_b, rate, levels, rows)
-        write_of(field, out, at).start()
-
-    each_field(members, lambda m: of_field(m, hv_ens, m))
-    each_field(nvars, lambda v: of_field(members + v, hv_stat, v))
-    each_field(members, lambda m: write_of(m, hv_ens, m).wait())
-    each_field(nvars, lambda v: write_of(members + v, hv_stat, v).wait())
+    writes = []
+    rates = rates_of(members + nvars, members, group, localize, static)
+    upper = jnp.logical_not(is_even())
+    add = adder(after, upper, (levels, rows, cells))
+    below, above = neighbours()
+
+    def visit(field, depth, part):
+        if depth == 0:
+            after[field] = own[field]
+        add(field, depth, part)
+        if depth == SWEEPS - 1:
+            out = hv_ens.at[field] if field < members else hv_stat.at[field - members]
+            write = pltpu.make_async_copy(after.at[field], out, sems.at[field])
+            write.start()
+            writes.append(write)
+
+    add_side(side_b, upper, rates, (levels, rows, cells), visit, below * above)
+    for write in writes:
+        write.wait()
 
 
 def exchange(side_a, side_b):
@@ -440,7 +463,7 @@
     blocks = obs_index.shape[0] // BLOCK
     dims = (members, nvars, levels, rows, cells, blocks)
     plane = levels * rows
-    strip = (fields, SWEEPS * levels, cells)
+    strip = (SWEEPS, fields * levels, cells)
 
     ens = ens_control.reshape(members, plane, cells)
     stat = static_control.reshape(nvars, plane, cells)

time: 52.4 us -> 52.5 us (level)
  Pallas kernels: 23.9 us -> 22.6 us
  waiting for transfers between devices: 10.1 us -> 11.3 us
    pallas_call x6, Pallas kernels: 23.9 us -> 22.6 us  [call(): pl.pallas_call(body, out_shape=tuple((jax.ShapeDtypeStruct(tuple(shape),...]
    ppermute x2, waiting for transfers between devices: 1.4 us -> 2.53 us  [exchange(): lax.ppermute(side_b, 'tile', pairs_b)]
  transfers between devices with their start and end apart: 8 -> 8, of which waited for: 5 -> 5; matrix products, arithmetic and copies ran while one was open for 10% -> 10% of each run, Pallas kernels for 22% -> 21%
where the time goes in v10:
time: 52.5 us; the launch traced here: 51.5 us
  Pallas kernels  22.6 us (43%)
  waiting for transfers between devices  11.3 us (22%)
  starting transfers between devices  10.7 us (20%)
  other arithmetic  4.99 us (10%)
  between operations  1.69 us (3%)
    pallas_call x6, Pallas kernels, call(): pl.pallas_call(body, out_shape=tuple((jax.ShapeDtypeStruct(tuple(shape),...  22.6 us
    sort x1, other arithmetic, per_device(): lax.sort((key.reshape(-1), obs_frac, weight.reshape(-1)), num_keys=1, is_...  4.98 us
    ppermute x3, starting transfers between devices, summands(): lax.ppermute(value, 'grp', [(i, i ^ turn) for i in range(count)])  4.9 us
    ppermute x2, starting transfers between devices, exchange(): lax.ppermute(side_b, 'tile', pairs_b)  4.48 us
    ppermute x1, waiting for transfers between devices, summands(): lax.ppermute(value, 'grp', [(i, i ^ 1) for i in range(count)])  4.13 us
    ppermute x3, waiting for transfers between devices, summands(): lax.ppermute(value, 'grp', [(i, i ^ turn) for i in range(count)])  3.93 us
    ppermute x2, waiting for transfers between devices, exchange(): lax.ppermute(side_b, 'tile', pairs_b)  2.53 us
    ppermute x1, starting transfers between devices, summands(): lax.ppermute(value, 'grp', [(i, i ^ 1) for i in range(count)])  1.2 us
  transfers between devices with their start and end apart: 8, of which 5 were waited for; matrix products, arithmetic and copies ran while one was open for 10% of the time, Pallas kernels for 21%

profile of v10, /device:TPU:6, one launch (start us, length us, event | category | flops | bytes accessed | tf_op | source)
XLA Modules:
  0.0 51.5 jit_solution(7188817097360889549)
XLA Ops:
  0.6 0.0 copy-start.1
  0.6 0.0 copy-start.9
  0.7 0.0 copy-start.6
  0.7 0.0 copy-start.5
  0.7 0.0 copy-start.7
  0.7 0.0 copy-start.4
  0.7 0.0 copy-start.2
  0.7 0.0 copy-start.3
  0.7 1.6 %pack_kernel.1 = (f32[4,224,128]{2,1,0:T(8,128)S(1)}, f32[4,224,128]{2,1,0:T(8,128)S(1)}, f32[7,512,128]{2,1,0:T(8,128)S(1)}) custom-call(f32[2,512,128]{2,1,0:T(8,128)} %bitcast.32, f32[5,512,128]{2,1,0:T(8,128)} %bitcast.30), custom_call_target="tpu_custom_call" | custom-call | flops 20000000 | bytes 2000000 | tf_op jit(solution)/shard_map/pack_kernel/pallas_call | solution.py:434
  2.4 0.0 copy-start.8
  2.4 0.1 collective-permute-start
  2.5 3.4 %collective-permute-start.1 = (f32[4,224,128]{2,1,0:T(8,128)S(1)}, f32[4,224,128]{2,1,0:T(8,128)S(1)}, u32[]{:S(2)}, u32[]{:S(2)}) collective-permute-start(f32[4,224,128]{2,1,0:T(8,128)S(1)} %get-tuple-element.25), channel_id=1, source_target_pairs={{0,15},{1,2},{2,1},{3,4},{4,3},{5,6},{6,5},{7,8},{8,7},{9,10},{10,... | collective-permute-start | bytes 1376264 | tf_op jit(solution)/shard_map/ppermute | solution.py:414
  6.5 0.0 copy-done.9
  6.5 0.0 collective-permute-done.refs_3_
  6.5 0.1 broadcast_in_dim.2.refs_2_.refs_1_.refs_4_.refs_3_
  6.6 0.0 copy-done.1
  6.6 0.0 copy-done.6
  6.7 0.0 copy-done.5
  6.7 0.0 copy-done.7
  6.7 0.0 copy-done.4
  6.7 0.0 copy-done.2
  6.7 0.0 copy-done.3
  6.7 4.6 %own_kernel.1 = (f32[7,512,128]{2,1,0:T(8,128)S(1)}, s32[32,128]{1,0:T(8,128)S(1)}, f32[32,128]{1,0:T(8,128)S(1)}) custom-call(bf16[256,512]{1,0:T(8,128)(2,1)S(1)} %copy-done.1, f32[7,512,128]{2,1,0:T(8,128)S(1)} %get-tuple-element.17.refs_1_, f32[7,32,128]{2,1,0:T(8,128)S(1)} %broadcast_in_dim.2.refs_2_.refs_1_.refs_4_.refs_3_, ...), custom_call_target="tpu_custom_call" | custom-call | flops 20000000 | bytes 2000000 | tf_op jit(solution)/shard_map/own_kernel/pallas_call | solution.py:434
  11.3 0.0 copy-done.8
  11.4 5.0 %sort.21 = (s32[4096]{0:T(1024)S(1)}, f32[4096]{0:T(1024)S(1)}, f32[4096]{0:T(1024)S(1)}) sort(s32[4096]{0:T(1024)S(1)} %bitcast.28, f32[4096]{0:T(1024)S(1)} %copy-done.8, f32[4096]{0:T(1024)S(1)} %bitcast.29), dimensions={0}, to_apply=%region_0.0 | sort | flops 49152 | bytes 98304 | tf_op jit(solution)/shard_map/sort | solution.py:492
  16.3 0.0 collective-permute-done.1.refs_2_
  16.3 0.0 copy-start
  16.4 5.0 %forward_kernel.1 = f32[32,128]{1,0:T(8,128)S(1)} custom-call(f32[7,512,128]{2,1,0:T(8,128)S(1)} %get-tuple-element.24.refs_0_, f32[7,32,128]{2,1,0:T(8,128)S(1)} %broadcast_in_dim.2.refs_2_.refs_1_.refs_4_.refs_3_, f32[4,224,128]{2,1,0:T(8,128)S(1)} %collective-permute-done.1.refs_2_, s32[32,128]{1,0:T(8,128)S(1)} %bitcast.18, f32[32,128]{1,0:T(8,128)S(1)} %bitcast.22, ...), custom_call_target="tpu_custom_call" | custom-call | flops 20000000 | bytes 2000000 | tf_op jit(solution)/shard_map/forward_kernel/pallas_call | solution.py:434
  21.4 1.2 %collective-permute-start.2 = (f32[32,128]{1,0:T(8,128)S(1)}, f32[32,128]{1,0:T(8,128)S(1)}, u32[]{:S(2)}, u32[]{:S(2)}) collective-permute-start(f32[32,128]{1,0:T(8,128)S(1)} %forward_kernel.1), channel_id=1, source_target_pairs={{0,16},{16,0},{32,48},{48,32},{64,80},{80,64},{96,112},{112,96},{1... | collective-permute-start | bytes 49160 | tf_op jit(solution)/shard_map/ppermute | solution.py:419
  22.6 4.1 %collective-permute-done.2 = f32[32,128]{1,0:T(8,128)S(1)} collective-permute-done((f32[32,128]{1,0:T(8,128)S(1)}, f32[32,128]{1,0:T(8,128)S(1)}, u32[]{:S(2)}, u32[]{:S(2)}) %collective-permute-start.2) | collective-permute-done | bytes 16416 | tf_op jit(solution)/shard_map/ppermute | solution.py:419
  26.7 3.9 %collective-permute-start.5 = (f32[32,128]{1,0:T(8,128)S(1)}, f32[32,128]{1,0:T(8,128)S(1)}, u32[]{:S(2)}, u32[]{:S(2)}) collective-permute-start(f32[32,128]{1,0:T(8,128)S(1)} %add.5.refs_5_), channel_id=1, source_target_pairs={{0,64},{16,80},{32,96},{48,112},{64,0},{80,16},{96,32},{112,48},{1... | collective-permute-start | bytes 49160 | tf_op jit(solution)/shard_map/ppermute | solution.py:421
  30.6 0.7 %collective-permute-start.4 = (f32[32,128]{1,0:T(8,128)S(1)}, f32[32,128]{1,0:T(8,128)S(1)}, u32[]{:S(2)}, u32[]{:S(2)}) collective-permute-start(f32[32,128]{1,0:T(8,128)S(1)} %add.5.refs_5_), channel_id=1, source_target_pairs={{0,96},{16,112},{32,64},{48,80},{64,32},{80,48},{96,0},{112,16},{1... | collective-permute-start | bytes 49160 | tf_op jit(solution)/shard_map/ppermute | solution.py:421
  31.3 0.3 collective-permute-start.3
  31.6 0.7 %collective-permute-done.5.refs_8_ = f32[32,128]{1,0:T(8,128)S(1)} collective-permute-done((f32[32,128]{1,0:T(8,128)S(1)}, f32[32,128]{1,0:T(8,128)S(1)}, u32[]{:S(2)}, u32[]{:S(2)}) %collective-permute-start.5) | collective-permute-done | bytes 16416 | tf_op jit(solution)/shard_map/ppermute | solution.py:421
  32.3 3.2 %collective-permute-done.4.refs_7_ = f32[32,128]{1,0:T(8,128)S(1)} collective-permute-done((f32[32,128]{1,0:T(8,128)S(1)}, f32[32,128]{1,0:T(8,128)S(1)}, u32[]{:S(2)}, u32[]{:S(2)}) %collective-permute-start.4) | collective-permute-done | bytes 16416 | tf_op jit(solution)/shard_map/ppermute | solution.py:421
  35.6 0.0 collective-permute-done.3.refs_6_
  35.6 0.0 copy-done
  35.6 3.0 %scatter_kernel.1 = (f32[2,512,128]{2,1,0:T(8,128)S(1)}, f32[4,224,128]{2,1,0:T(8,128)S(1)}, f32[4,224,128]{2,1,0:T(8,128)S(1)}, f32[2816,128]{1,0:T(8,128)S(1)}) custom-call(s32[32,128]{1,0:T(8,128)S(1)} %bitcast.20, f32[32,128]{1,0:T(8,128)S(1)} %bitcast.23, f32[32,128]{1,0:T(8,128)S(1)} %bitcast.27, bf16[2,5,512,128]{3,2,1,0:T(8,128)(2,1)S(1)} %bitcast.17, ...), custom_call_target="tpu_custom_call" | custom-call | flops 20000000 | bytes 2000000 | tf_op jit(solution)/shard_map/scatter_kernel/pallas_call | solution.py:434
  38.5 0.1 collective-permute-start.6
  38.6 1.1 %collective-permute-start.7 = (f32[4,224,128]{2,1,0:T(8,128)S(1)}, f32[4,224,128]{2,1,0:T(8,128)S(1)}, u32[]{:S(2)}, u32[]{:S(2)}) collective-permute-start(f32[4,224,128]{2,1,0:T(8,128)S(1)} %get-tuple-element.29), channel_id=1, source_target_pairs={{0,15},{1,2},{2,1},{3,4},{4,3},{5,6},{6,5},{7,8},{8,7},{9,10},{10,... | collective-permute-start | bytes 1376264 | tf_op jit(solution)/shard_map/ppermute | solution.py:414
  39.7 0.7 %collective-permute-done.6.refs_4_ = f32[4,224,128]{2,1,0:T(8,128)S(1)} collective-permute-done((f32[4,224,128]{2,1,0:T(8,128)S(1)}, f32[4,224,128]{2,1,0:T(8,128)S(1)}, u32[]{:S(2)}, u32[]{:S(2)}) %collective-permute-start.6) | collective-permute-done | bytes 458784 | tf_op jit(solution)/shard_map/ppermute | solution.py:414
  40.4 5.9 %local_kernel.1.refs_0_ = f32[7,512,128]{2,1,0:T(8,128)S(1)} custom-call(bf16[256,512]{1,0:T(8,128)(2,1)S(1)} %copy-done.1, f32[2,512,128]{2,1,0:T(8,128)S(1)} %get-tuple-element.26.refs_1_, f32[2816,128]{1,0:T(8,128)S(1)} %get-tuple-element.27.refs_2_, f32[7,32,128]{2,1,0:T(8,128)S(1)} %broadcast_in_dim.2.refs_2_.refs_1_.refs_4_.refs_3_, ...), custom_call_target="tpu_custom_call" | custom-call | flops 20000000 | bytes 2000000 | tf_op jit(solution)/shard_map/local_kernel/pallas_call | solution.py:434
  46.4 2.5 %collective-permute-done.7.refs_1_ = f32[4,224,128]{2,1,0:T(8,128)S(1)} collective-permute-done((f32[4,224,128]{2,1,0:T(8,128)S(1)}, f32[4,224,128]{2,1,0:T(8,128)S(1)}, u32[]{:S(2)}, u32[]{:S(2)}) %collective-permute-start.7) | collective-permute-done | bytes 458784 | tf_op jit(solution)/shard_map/ppermute | solution.py:414
  48.9 2.4 %edge_kernel.1 = (f32[2,512,128]{2,1,0:T(8,128)}, f32[5,512,128]{2,1,0:T(8,128)}) custom-call(f32[7,512,128]{2,1,0:T(8,128)S(1)} %local_kernel.1.refs_0_, f32[4,224,128]{2,1,0:T(8,128)S(1)} %collective-permute-done.7.refs_1_, s32[2]{0:T(128)S(1)} %copy-done.5, f32[12]{0:T(128)S(1)} %copy-done.6, f32[1]{0:T(128)S(6)} %copy.18.refs_9_.refs_4_), custom_call_target="tpu_custom_call" | custom-call | flops 20000000 | bytes 2000000 | tf_op jit(solution)/shard_map/edge_kernel/pallas_call | solution.py:434
  (3 shorter events, 0.0 us)
Async XLA Ops:
  0.6 6.0 %copy-start.1 = (bf16[256,512]{1,0:T(8,128)(2,1)S(1)}, bf16[256,512]{1,0:T(8,128)(2,1)}, u32[]{:S(2)}) copy-start(bf16[256,512]{1,0:T(8,128)(2,1)} %constant.4.clone.refs_0_) | copy-start | bytes 786436
  0.6 5.9 %copy-start.9 = (f32[1,5,32]{2,0,1:T(1,128)S(1)}, f32[1,5,32]{2,0,1:T(1,128)}, u32[]{:S(2)}) copy-start(f32[1,5,32]{2,0,1:T(1,128)} %param.19) | copy-start | bytes 1924
  0.7 6.0 %copy-start.6 = (f32[12]{0:T(128)S(1)}, f32[12]{0:T(128)}, u32[]{:S(2)}) copy-start(f32[12]{0:T(128)} %refs_3_.1) | copy-start | bytes 148
  0.7 6.0 %copy-start.5 = (s32[2]{0:T(128)S(1)}, s32[2]{0:T(128)}, u32[]{:S(2)}) copy-start(s32[2]{0:T(128)} %refs_2_.1) | copy-start | bytes 28
  0.7 6.0 %copy-start.7 = (f32[8]{0:T(128)S(1)}, f32[8]{0:T(128)}, u32[]{:S(2)}) copy-start(f32[8]{0:T(128)} %refs_10_.1) | copy-start | bytes 100
  0.7 6.0 %copy-start.4 = (s32[4096]{0:T(1024)S(1)}, s32[4096]{0:T(1024)}, u32[]{:S(2)}) copy-start(s32[4096]{0:T(1024)} %param.23) | copy-start | bytes 49156
  0.7 6.0 %copy-start.2 = (s32[4096]{0:T(1024)S(1)}, s32[4096]{0:T(1024)}, u32[]{:S(2)}) copy-start(s32[4096]{0:T(1024)} %param.22) | copy-start | bytes 49156
  0.7 6.0 %copy-start.3 = (s32[4096]{0:T(1024)S(1)}, s32[4096]{0:T(1024)}, u32[]{:S(2)}) copy-start(s32[4096]{0:T(1024)} %param.20) | copy-start | bytes 49156
  2.4 9.0 %copy-start.8 = (f32[4096]{0:T(1024)S(1)}, f32[4096]{0:T(1024)}, u32[]{:S(2)}) copy-start(f32[4096]{0:T(1024)} %param.21) | copy-start | bytes 49156
  2.4 4.2 %collective-permute-start = (f32[4,224,128]{2,1,0:T(8,128)S(1)}, f32[4,224,128]{2,1,0:T(8,128)S(1)}, u32[]{:S(2)}, u32[]{:S(2)}) collective-permute-start(f32[4,224,128]{2,1,0:T(8,128)S(1)} %get-tuple-element.18), channel_id=1, source_target_pairs={{0,1},{1,0},{2,3},{3,2},{4,5},{5,4},{6,7},{7,6},{8,9},{9,8},{10,11... | collective-permute-start | bytes 1376264 | tf_op jit(solution)/shard_map/ppermute | solution.py:414
  2.5 13.9 %collective-permute-start.1 = (f32[4,224,128]{2,1,0:T(8,128)S(1)}, f32[4,224,128]{2,1,0:T(8,128)S(1)}, u32[]{:S(2)}, u32[]{:S(2)}) collective-permute-start(f32[4,224,128]{2,1,0:T(8,128)S(1)} %get-tuple-element.25), channel_id=1, source_target_pairs={{0,15},{1,2},{2,1},{3,4},{4,3},{5,6},{6,5},{7,8},{8,7},{9,10},{10,... | collective-permute-start | bytes 1376264 | tf_op jit(solution)/shard_map/ppermute | solution.py:414
  16.3 19.2 %copy-start = (bf16[2,5,32,16,128]{4,3,2,1,0:T(8,128)(2,1)S(1)}, bf16[2,5,32,16,128]{4,3,2,1,0:T(8,128)(2,1)}, u32[]{:S(2)}) copy-start(bf16[2,5,32,16,128]{4,3,2,1,0:T(8,128)(2,1)} %param.15) | copy-start | bytes 3932164
  21.4 5.3 %collective-permute-start.2 = (f32[32,128]{1,0:T(8,128)S(1)}, f32[32,128]{1,0:T(8,128)S(1)}, u32[]{:S(2)}, u32[]{:S(2)}) collective-permute-start(f32[32,128]{1,0:T(8,128)S(1)} %forward_kernel.1), channel_id=1, source_target_pairs={{0,16},{16,0},{32,48},{48,32},{64,80},{80,64},{96,112},{112,96},{1... | collective-permute-start | bytes 49160 | tf_op jit(solution)/shard_map/ppermute | solution.py:419
  26.7 5.6 %collective-permute-start.5 = (f32[32,128]{1,0:T(8,128)S(1)}, f32[32,128]{1,0:T(8,128)S(1)}, u32[]{:S(2)}, u32[]{:S(2)}) collective-permute-start(f32[32,128]{1,0:T(8,128)S(1)} %add.5.refs_5_), channel_id=1, source_target_pairs={{0,64},{16,80},{32,96},{48,112},{64,0},{80,16},{96,32},{112,48},{1... | collective-permute-start | bytes 49160 | tf_op jit(solution)/shard_map/ppermute | solution.py:421
  30.6 4.9 %collective-permute-start.4 = (f32[32,128]{1,0:T(8,128)S(1)}, f32[32,128]{1,0:T(8,128)S(1)}, u32[]{:S(2)}, u32[]{:S(2)}) collective-permute-start(f32[32,128]{1,0:T(8,128)S(1)} %add.5.refs_5_), channel_id=1, source_target_pairs={{0,96},{16,112},{32,64},{48,80},{64,32},{80,48},{96,0},{112,16},{1... | collective-permute-start | bytes 49160 | tf_op jit(solution)/shard_map/ppermute | solution.py:421
  31.3 4.2 %collective-permute-start.3 = (f32[32,128]{1,0:T(8,128)S(1)}, f32[32,128]{1,0:T(8,128)S(1)}, u32[]{:S(2)}, u32[]{:S(2)}) collective-permute-start(f32[32,128]{1,0:T(8,128)S(1)} %add.5.refs_5_), channel_id=1, source_target_pairs={{0,32},{16,48},{32,0},{48,16},{64,96},{80,112},{96,64},{112,80},{1... | collective-permute-start | bytes 49160 | tf_op jit(solution)/shard_map/ppermute | solution.py:421
  38.5 1.9 %collective-permute-start.6 = (f32[4,224,128]{2,1,0:T(8,128)S(1)}, f32[4,224,128]{2,1,0:T(8,128)S(1)}, u32[]{:S(2)}, u32[]{:S(2)}) collective-permute-start(f32[4,224,128]{2,1,0:T(8,128)S(1)} %get-tuple-element.28), channel_id=1, source_target_pairs={{0,1},{1,0},{2,3},{3,2},{4,5},{5,4},{6,7},{7,6},{8,9},{9,8},{10,11... | collective-permute-start | bytes 1376264 | tf_op jit(solution)/shard_map/ppermute | solution.py:414
  38.6 10.3 %collective-permute-start.7 = (f32[4,224,128]{2,1,0:T(8,128)S(1)}, f32[4,224,128]{2,1,0:T(8,128)S(1)}, u32[]{:S(2)}, u32[]{:S(2)}) collective-permute-start(f32[4,224,128]{2,1,0:T(8,128)S(1)} %get-tuple-element.29), channel_id=1, source_target_pairs={{0,15},{1,2},{2,1},{3,4},{4,3},{5,6},{6,5},{7,8},{8,7},{9,10},{10,... | collective-permute-start | bytes 1376264 | tf_op jit(solution)/shard_map/ppermute | solution.py:414

commit v11 on v10

--- a/solution.py
+++ b/solution.py
@@ -182,9 +182,9 @@
 
 
 def chosen_rows(key, start, shift):
-    row = (key >> shift) - start
-    spot = lax.broadcasted_iota(jnp.int32, (BLOCK, key.shape[1]), 0)
-    return jnp.where(spot == row, 1.0, 0.0).astype(jnp.bfloat16)
+    row = ((key >> shift) - start).astype(jnp.int16)
+    spot = lax.broadcasted_iota(jnp.int16, (BLOCK, key.shape[1]), 0)
+    return jnp.where(spot == row, jnp.bfloat16(1), jnp.bfloat16(0))
 
 
 def window_of(bound, block, cells):
@@ -216,12 +216,12 @@
         lax.fori_loop(0, blocks, of_block, 0)
 
 
-def each_field(fields, visit):
+def each_field(fields, visit, unroll=1):
     def step(field, carry):
         visit(field)
         return carry
 
-    lax.fori_loop(0, fields, step, 0)
+    lax.fori_loop(0, fields, step, 0, unroll=unroll)
 
 
 def load_of(field, source, at, held, sems):
@@ -256,7 +256,7 @@
         for x in range(rows):
             out[field, pl.ds(x, levels, stride=rows), :] = planes[x] * scale[field]
 
-    each_field(members + nvars, of_field)
+    each_field(members + nvars, of_field, members + nvars)
     rates = rates_of(members + nvars, members, group, localize, static)
     add_near(out, side_a, rates, (levels, rows, cells), scale)
     key[...] = layer[...] * (rows * cells) + index[...]
@@ -269,17 +269,18 @@
 def forward_kernel(dims, own, scale, side_b, key, frac, perturb_far, bound, group, localize, static, out, smooth, table, perturb, sem):
     members, nvars, levels, rows, cells, blocks = dims
     shift = cells.bit_length() - 1
-    load = pltpu.make_async_copy(perturb_far, perturb, sem)
-    load.start()
+    loads = [pltpu.make_async_copy(perturb_far.at[m, v], perturb.at[m, v], sem.at[m, v]) for v in range(nvars) for m in range(members)]
+    for load in loads:
+        load.start()
 
     smooth[...] = own[...]
     rates = rates_of(members + nvars, members, group, localize, static)
     add_far(smooth, side_b, rates, (levels, rows, cells), scale)
-    load.wait()
     plane = levels * rows
     for v in range(nvars):
         total = smooth[members + v]
         for m in range(members):
+            loads[v * members + m].wait()
             total = total + perturb[m, v].astype(jnp.float32) * smooth[m]
         high, low = halves(total)
         table[v * plane : (v + 1) * plane, :cells] = high
@@ -504,7 +505,7 @@
             pltpu.VMEM(whole, jnp.float32),
             pltpu.VMEM((table_rows, 2 * cells), jnp.bfloat16),
             pltpu.VMEM(perturb.shape, perturb.dtype),
-            pltpu.SemaphoreType.DMA(()),
+            pltpu.SemaphoreType.DMA((members, nvars)),
         ],
     )
     seen = summands(seen)

time: 52.5 us -> 51.4 us (0.979)
  Pallas kernels: 22.6 us -> 21.8 us
    pallas_call x6, Pallas kernels: 22.6 us -> 21.8 us  [call(): pl.pallas_call(body, out_shape=tuple((jax.ShapeDtypeStruct(tuple(shape),...]
where the time goes in v11:
time: 51.4 us; the launch traced here: 50.5 us
  Pallas kernels  21.8 us (42%)
  waiting for transfers between devices  11.1 us (22%)
  starting transfers between devices  10.7 us (21%)
  other arithmetic  4.99 us (10%)
  between operations  1.69 us (3%)
    pallas_call x6, Pallas kernels, call(): pl.pallas_call(body, out_shape=tuple((jax.ShapeDtypeStruct(tuple(shape),...  21.8 us
    sort x1, other arithmetic, per_device(): lax.sort((key.reshape(-1), obs_frac, weight.reshape(-1)), num_keys=1, is_...  4.98 us
    ppermute x3, starting transfers between devices, summands(): lax.ppermute(value, 'grp', [(i, i ^ turn) for i in range(count)])  4.9 us
    ppermute x2, starting transfers between devices, exchange(): lax.ppermute(side_b, 'tile', pairs_b)  4.48 us
    ppermute x1, waiting for transfers between devices, summands(): lax.ppermute(value, 'grp', [(i, i ^ 1) for i in range(count)])  4.13 us
    ppermute x3, waiting for transfers between devices, summands(): lax.ppermute(value, 'grp', [(i, i ^ turn) for i in range(count)])  3.92 us
    ppermute x2, waiting for transfers between devices, exchange(): lax.ppermute(side_b, 'tile', pairs_b)  2.35 us
    ppermute x1, starting transfers between devices, summands(): lax.ppermute(value, 'grp', [(i, i ^ 1) for i in range(count)])  1.19 us
  transfers between devices with their start and end apart: 8, of which 5 were waited for; matrix products, arithmetic and copies ran while one was open for 10% of the time, Pallas kernels for 21%

profile of v11, /device:TPU:6, one launch (start us, length us, event | category | flops | bytes accessed | tf_op | source)
XLA Modules:
  0.0 50.5 jit_solution(16850838580138646860)
XLA Ops:
  0.6 0.0 copy-start.1
  0.6 0.0 copy-start.9
  0.7 0.0 copy-start.6
  0.7 0.0 copy-start.5
  0.7 0.0 copy-start.7
  0.7 0.0 copy-start.4
  0.7 0.0 copy-start.2
  0.7 0.0 copy-start.3
  0.7 1.6 %pack_kernel.1 = (f32[4,224,128]{2,1,0:T(8,128)S(1)}, f32[4,224,128]{2,1,0:T(8,128)S(1)}, f32[7,512,128]{2,1,0:T(8,128)S(1)}) custom-call(f32[2,512,128]{2,1,0:T(8,128)} %bitcast.32, f32[5,512,128]{2,1,0:T(8,128)} %bitcast.30), custom_call_target="tpu_custom_call" | custom-call | flops 20000000 | bytes 2000000 | tf_op jit(solution)/shard_map/pack_kernel/pallas_call | solution.py:435
  2.4 0.0 copy-start.8
  2.4 0.1 collective-permute-start
  2.5 3.4 %collective-permute-start.1 = (f32[4,224,128]{2,1,0:T(8,128)S(1)}, f32[4,224,128]{2,1,0:T(8,128)S(1)}, u32[]{:S(2)}, u32[]{:S(2)}) collective-permute-start(f32[4,224,128]{2,1,0:T(8,128)S(1)} %get-tuple-element.25), channel_id=1, source_target_pairs={{0,15},{1,2},{2,1},{3,4},{4,3},{5,6},{6,5},{7,8},{8,7},{9,10},{10,... | collective-permute-start | bytes 1376264 | tf_op jit(solution)/shard_map/ppermute | solution.py:415
  6.5 0.0 copy-done.9
  6.5 0.0 collective-permute-done.refs_3_
  6.5 0.1 broadcast_in_dim.2.refs_2_.refs_1_.refs_4_.refs_3_
  6.6 0.0 copy-done.1
  6.6 0.0 copy-done.6
  6.7 0.0 copy-done.5
  6.7 0.0 copy-done.7
  6.7 0.0 copy-done.4
  6.7 0.0 copy-done.2
  6.7 0.0 copy-done.3
  6.7 4.4 %own_kernel.1 = (f32[7,512,128]{2,1,0:T(8,128)S(1)}, s32[32,128]{1,0:T(8,128)S(1)}, f32[32,128]{1,0:T(8,128)S(1)}) custom-call(bf16[256,512]{1,0:T(8,128)(2,1)S(1)} %copy-done.1, f32[7,512,128]{2,1,0:T(8,128)S(1)} %get-tuple-element.17.refs_1_, f32[7,32,128]{2,1,0:T(8,128)S(1)} %broadcast_in_dim.2.refs_2_.refs_1_.refs_4_.refs_3_, ...), custom_call_target="tpu_custom_call" | custom-call | flops 20000000 | bytes 2000000 | tf_op jit(solution)/shard_map/own_kernel/pallas_call | solution.py:435
  11.2 0.0 copy-done.8
  11.2 5.0 %sort.21 = (s32[4096]{0:T(1024)S(1)}, f32[4096]{0:T(1024)S(1)}, f32[4096]{0:T(1024)S(1)}) sort(s32[4096]{0:T(1024)S(1)} %bitcast.28, f32[4096]{0:T(1024)S(1)} %copy-done.8, f32[4096]{0:T(1024)S(1)} %bitcast.29), dimensions={0}, to_apply=%region_0.0 | sort | flops 49152 | bytes 98304 | tf_op jit(solution)/shard_map/sort | solution.py:493
  16.1 0.0 collective-permute-done.1.refs_2_
  16.2 0.0 copy-start
  16.2 4.4 %forward_kernel.1 = f32[32,128]{1,0:T(8,128)S(1)} custom-call(f32[7,512,128]{2,1,0:T(8,128)S(1)} %get-tuple-element.24.refs_0_, f32[7,32,128]{2,1,0:T(8,128)S(1)} %broadcast_in_dim.2.refs_2_.refs_1_.refs_4_.refs_3_, f32[4,224,128]{2,1,0:T(8,128)S(1)} %collective-permute-done.1.refs_2_, s32[32,128]{1,0:T(8,128)S(1)} %bitcast.18, f32[32,128]{1,0:T(8,128)S(1)} %bitcast.22, ...), custom_call_target="tpu_custom_call" | custom-call | flops 20000000 | bytes 2000000 | tf_op jit(solution)/shard_map/forward_kernel/pallas_call | solution.py:435
  20.6 1.2 %collective-permute-start.2 = (f32[32,128]{1,0:T(8,128)S(1)}, f32[32,128]{1,0:T(8,128)S(1)}, u32[]{:S(2)}, u32[]{:S(2)}) collective-permute-start(f32[32,128]{1,0:T(8,128)S(1)} %forward_kernel.1), channel_id=1, source_target_pairs={{0,16},{16,0},{32,48},{48,32},{64,80},{80,64},{96,112},{112,96},{1... | collective-permute-start | bytes 49160 | tf_op jit(solution)/shard_map/ppermute | solution.py:420
  21.8 4.1 %collective-permute-done.2 = f32[32,128]{1,0:T(8,128)S(1)} collective-permute-done((f32[32,128]{1,0:T(8,128)S(1)}, f32[32,128]{1,0:T(8,128)S(1)}, u32[]{:S(2)}, u32[]{:S(2)}) %collective-permute-start.2) | collective-permute-done | bytes 16416 | tf_op jit(solution)/shard_map/ppermute | solution.py:420
  25.9 3.9 %collective-permute-start.5 = (f32[32,128]{1,0:T(8,128)S(1)}, f32[32,128]{1,0:T(8,128)S(1)}, u32[]{:S(2)}, u32[]{:S(2)}) collective-permute-start(f32[32,128]{1,0:T(8,128)S(1)} %add.5.refs_5_), channel_id=1, source_target_pairs={{0,64},{16,80},{32,96},{48,112},{64,0},{80,16},{96,32},{112,48},{1... | collective-permute-start | bytes 49160 | tf_op jit(solution)/shard_map/ppermute | solution.py:422
  29.8 0.7 %collective-permute-start.4 = (f32[32,128]{1,0:T(8,128)S(1)}, f32[32,128]{1,0:T(8,128)S(1)}, u32[]{:S(2)}, u32[]{:S(2)}) collective-permute-start(f32[32,128]{1,0:T(8,128)S(1)} %add.5.refs_5_), channel_id=1, source_target_pairs={{0,96},{16,112},{32,64},{48,80},{64,32},{80,48},{96,0},{112,16},{1... | collective-permute-start | bytes 49160 | tf_op jit(solution)/shard_map/ppermute | solution.py:422
  30.5 0.3 collective-permute-start.3
  30.8 0.7 %collective-permute-done.5.refs_8_ = f32[32,128]{1,0:T(8,128)S(1)} collective-permute-done((f32[32,128]{1,0:T(8,128)S(1)}, f32[32,128]{1,0:T(8,128)S(1)}, u32[]{:S(2)}, u32[]{:S(2)}) %collective-permute-start.5) | collective-permute-done | bytes 16416 | tf_op jit(solution)/shard_map/ppermute | solution.py:422
  31.5 3.2 %collective-permute-done.4.refs_7_ = f32[32,128]{1,0:T(8,128)S(1)} collective-permute-done((f32[32,128]{1,0:T(8,128)S(1)}, f32[32,128]{1,0:T(8,128)S(1)}, u32[]{:S(2)}, u32[]{:S(2)}) %collective-permute-start.4) | collective-permute-done | bytes 16416 | tf_op jit(solution)/shard_map/ppermute | solution.py:422
  34.7 0.0 collective-permute-done.3.refs_6_
  34.7 0.0 copy-done
  34.7 3.0 %scatter_kernel.1 = (f32[2,512,128]{2,1,0:T(8,128)S(1)}, f32[4,224,128]{2,1,0:T(8,128)S(1)}, f32[4,224,128]{2,1,0:T(8,128)S(1)}, f32[2816,128]{1,0:T(8,128)S(1)}) custom-call(s32[32,128]{1,0:T(8,128)S(1)} %bitcast.20, f32[32,128]{1,0:T(8,128)S(1)} %bitcast.23, f32[32,128]{1,0:T(8,128)S(1)} %bitcast.27, bf16[2,5,512,128]{3,2,1,0:T(8,128)(2,1)S(1)} %bitcast.17, ...), custom_call_target="tpu_custom_call" | custom-call | flops 20000000 | bytes 2000000 | tf_op jit(solution)/shard_map/scatter_kernel/pallas_call | solution.py:435
  37.7 0.1 collective-permute-start.6
  37.8 1.1 %collective-permute-start.7 = (f32[4,224,128]{2,1,0:T(8,128)S(1)}, f32[4,224,128]{2,1,0:T(8,128)S(1)}, u32[]{:S(2)}, u32[]{:S(2)}) collective-permute-start(f32[4,224,128]{2,1,0:T(8,128)S(1)} %get-tuple-element.29), channel_id=1, source_target_pairs={{0,15},{1,2},{2,1},{3,4},{4,3},{5,6},{6,5},{7,8},{8,7},{9,10},{10,... | collective-permute-start | bytes 1376264 | tf_op jit(solution)/shard_map/ppermute | solution.py:415
  38.9 0.7 %collective-permute-done.6.refs_4_ = f32[4,224,128]{2,1,0:T(8,128)S(1)} collective-permute-done((f32[4,224,128]{2,1,0:T(8,128)S(1)}, f32[4,224,128]{2,1,0:T(8,128)S(1)}, u32[]{:S(2)}, u32[]{:S(2)}) %collective-permute-start.6) | collective-permute-done | bytes 458784 | tf_op jit(solution)/shard_map/ppermute | solution.py:415
  39.6 5.9 %local_kernel.1.refs_0_ = f32[7,512,128]{2,1,0:T(8,128)S(1)} custom-call(bf16[256,512]{1,0:T(8,128)(2,1)S(1)} %copy-done.1, f32[2,512,128]{2,1,0:T(8,128)S(1)} %get-tuple-element.26.refs_1_, f32[2816,128]{1,0:T(8,128)S(1)} %get-tuple-element.27.refs_2_, f32[7,32,128]{2,1,0:T(8,128)S(1)} %broadcast_in_dim.2.refs_2_.refs_1_.refs_4_.refs_3_, ...), custom_call_target="tpu_custom_call" | custom-call | flops 20000000 | bytes 2000000 | tf_op jit(solution)/shard_map/local_kernel/pallas_call | solution.py:435
  45.6 2.3 %collective-permute-done.7.refs_1_ = f32[4,224,128]{2,1,0:T(8,128)S(1)} collective-permute-done((f32[4,224,128]{2,1,0:T(8,128)S(1)}, f32[4,224,128]{2,1,0:T(8,128)S(1)}, u32[]{:S(2)}, u32[]{:S(2)}) %collective-permute-start.7) | collective-permute-done | bytes 458784 | tf_op jit(solution)/shard_map/ppermute | solution.py:415
  47.9 2.4 %edge_kernel.1 = (f32[2,512,128]{2,1,0:T(8,128)}, f32[5,512,128]{2,1,0:T(8,128)}) custom-call(f32[7,512,128]{2,1,0:T(8,128)S(1)} %local_kernel.1.refs_0_, f32[4,224,128]{2,1,0:T(8,128)S(1)} %collective-permute-done.7.refs_1_, s32[2]{0:T(128)S(1)} %copy-done.5, f32[12]{0:T(128)S(1)} %copy-done.6, f32[1]{0:T(128)S(6)} %copy.18.refs_9_.refs_4_), custom_call_target="tpu_custom_call" | custom-call | flops 20000000 | bytes 2000000 | tf_op jit(solution)/shard_map/edge_kernel/pallas_call | solution.py:435
  (3 shorter events, 0.0 us)
Async XLA Ops:
  0.6 6.0 %copy-start.1 = (bf16[256,512]{1,0:T(8,128)(2,1)S(1)}, bf16[256,512]{1,0:T(8,128)(2,1)}, u32[]{:S(2)}) copy-start(bf16[256,512]{1,0:T(8,128)(2,1)} %constant.4.clone.refs_0_) | copy-start | bytes 786436
  0.6 5.9 %copy-start.9 = (f32[1,5,32]{2,0,1:T(1,128)S(1)}, f32[1,5,32]{2,0,1:T(1,128)}, u32[]{:S(2)}) copy-start(f32[1,5,32]{2,0,1:T(1,128)} %param.19) | copy-start | bytes 1924
  0.7 6.0 %copy-start.6 = (f32[12]{0:T(128)S(1)}, f32[12]{0:T(128)}, u32[]{:S(2)}) copy-start(f32[12]{0:T(128)} %refs_3_.1) | copy-start | bytes 148
  0.7 6.0 %copy-start.5 = (s32[2]{0:T(128)S(1)}, s32[2]{0:T(128)}, u32[]{:S(2)}) copy-start(s32[2]{0:T(128)} %refs_2_.1) | copy-start | bytes 28
  0.7 6.0 %copy-start.7 = (f32[8]{0:T(128)S(1)}, f32[8]{0:T(128)}, u32[]{:S(2)}) copy-start(f32[8]{0:T(128)} %refs_10_.1) | copy-start | bytes 100
  0.7 6.0 %copy-start.4 = (s32[4096]{0:T(1024)S(1)}, s32[4096]{0:T(1024)}, u32[]{:S(2)}) copy-start(s32[4096]{0:T(1024)} %param.23) | copy-start | bytes 49156
  0.7 6.0 %copy-start.2 = (s32[4096]{0:T(1024)S(1)}, s32[4096]{0:T(1024)}, u32[]{:S(2)}) copy-start(s32[4096]{0:T(1024)} %param.22) | copy-start | bytes 49156
  0.7 6.0 %copy-start.3 = (s32[4096]{0:T(1024)S(1)}, s32[4096]{0:T(1024)}, u32[]{:S(2)}) copy-start(s32[4096]{0:T(1024)} %param.20) | copy-start | bytes 49156
  2.4 8.8 %copy-start.8 = (f32[4096]{0:T(1024)S(1)}, f32[4096]{0:T(1024)}, u32[]{:S(2)}) copy-start(f32[4096]{0:T(1024)} %param.21) | copy-start | bytes 49156
  2.4 4.2 %collective-permute-start = (f32[4,224,128]{2,1,0:T(8,128)S(1)}, f32[4,224,128]{2,1,0:T(8,128)S(1)}, u32[]{:S(2)}, u32[]{:S(2)}) collective-permute-start(f32[4,224,128]{2,1,0:T(8,128)S(1)} %get-tuple-element.18), channel_id=1, source_target_pairs={{0,1},{1,0},{2,3},{3,2},{4,5},{5,4},{6,7},{7,6},{8,9},{9,8},{10,11... | collective-permute-start | bytes 1376264 | tf_op jit(solution)/shard_map/ppermute | solution.py:415
  2.5 13.7 %collective-permute-start.1 = (f32[4,224,128]{2,1,0:T(8,128)S(1)}, f32[4,224,128]{2,1,0:T(8,128)S(1)}, u32[]{:S(2)}, u32[]{:S(2)}) collective-permute-start(f32[4,224,128]{2,1,0:T(8,128)S(1)} %get-tuple-element.25), channel_id=1, source_target_pairs={{0,15},{1,2},{2,1},{3,4},{4,3},{5,6},{6,5},{7,8},{8,7},{9,10},{10,... | collective-permute-start | bytes 1376264 | tf_op jit(solution)/shard_map/ppermute | solution.py:415
  16.2 18.6 %copy-start = (bf16[2,5,32,16,128]{4,3,2,1,0:T(8,128)(2,1)S(1)}, bf16[2,5,32,16,128]{4,3,2,1,0:T(8,128)(2,1)}, u32[]{:S(2)}) copy-start(bf16[2,5,32,16,128]{4,3,2,1,0:T(8,128)(2,1)} %param.15) | copy-start | bytes 3932164
  20.6 5.3 %collective-permute-start.2 = (f32[32,128]{1,0:T(8,128)S(1)}, f32[32,128]{1,0:T(8,128)S(1)}, u32[]{:S(2)}, u32[]{:S(2)}) collective-permute-start(f32[32,128]{1,0:T(8,128)S(1)} %forward_kernel.1), channel_id=1, source_target_pairs={{0,16},{16,0},{32,48},{48,32},{64,80},{80,64},{96,112},{112,96},{1... | collective-permute-start | bytes 49160 | tf_op jit(solution)/shard_map/ppermute | solution.py:420
  25.9 5.6 %collective-permute-start.5 = (f32[32,128]{1,0:T(8,128)S(1)}, f32[32,128]{1,0:T(8,128)S(1)}, u32[]{:S(2)}, u32[]{:S(2)}) collective-permute-start(f32[32,128]{1,0:T(8,128)S(1)} %add.5.refs_5_), channel_id=1, source_target_pairs={{0,64},{16,80},{32,96},{48,112},{64,0},{80,16},{96,32},{112,48},{1... | collective-permute-start | bytes 49160 | tf_op jit(solution)/shard_map/ppermute | solution.py:422
  29.8 4.9 %collective-permute-start.4 = (f32[32,128]{1,0:T(8,128)S(1)}, f32[32,128]{1,0:T(8,128)S(1)}, u32[]{:S(2)}, u32[]{:S(2)}) collective-permute-start(f32[32,128]{1,0:T(8,128)S(1)} %add.5.refs_5_), channel_id=1, source_target_pairs={{0,96},{16,112},{32,64},{48,80},{64,32},{80,48},{96,0},{112,16},{1... | collective-permute-start | bytes 49160 | tf_op jit(solution)/shard_map/ppermute | solution.py:422
  30.5 4.2 %collective-permute-start.3 = (f32[32,128]{1,0:T(8,128)S(1)}, f32[32,128]{1,0:T(8,128)S(1)}, u32[]{:S(2)}, u32[]{:S(2)}) collective-permute-start(f32[32,128]{1,0:T(8,128)S(1)} %add.5.refs_5_), channel_id=1, source_target_pairs={{0,32},{16,48},{32,0},{48,16},{64,96},{80,112},{96,64},{112,80},{1... | collective-permute-start | bytes 49160 | tf_op jit(solution)/shard_map/ppermute | solution.py:422
  37.7 1.9 %collective-permute-start.6 = (f32[4,224,128]{2,1,0:T(8,128)S(1)}, f32[4,224,128]{2,1,0:T(8,128)S(1)}, u32[]{:S(2)}, u32[]{:S(2)}) collective-permute-start(f32[4,224,128]{2,1,0:T(8,128)S(1)} %get-tuple-element.28), channel_id=1, source_target_pairs={{0,1},{1,0},{2,3},{3,2},{4,5},{5,4},{6,7},{7,6},{8,9},{9,8},{10,11... | collective-permute-start | bytes 1376264 | tf_op jit(solution)/shard_map/ppermute | solution.py:415
  37.8 10.1 %collective-permute-start.7 = (f32[4,224,128]{2,1,0:T(8,128)S(1)}, f32[4,224,128]{2,1,0:T(8,128)S(1)}, u32[]{:S(2)}, u32[]{:S(2)}) collective-permute-start(f32[4,224,128]{2,1,0:T(8,128)S(1)} %get-tuple-element.29), channel_id=1, source_target_pairs={{0,15},{1,2},{2,1},{3,4},{4,3},{5,6},{6,5},{7,8},{8,7},{9,10},{10,... | collective-permute-start | bytes 1376264 | tf_op jit(solution)/shard_map/ppermute | solution.py:415

commit v12 on v11

--- a/solution.py
+++ b/solution.py
@@ -78,14 +78,14 @@
 
 def y_powers(cells):
     once = np.eye(cells, k=1) + np.eye(cells, k=-1)
-    row = np.concatenate([np.linalg.matrix_power(once, j) for j in range(1, SWEEPS + 1)], axis=1)
-    return jnp.asarray(np.concatenate([row, row], axis=0), jnp.bfloat16)
+    row = [math.comb(SWEEPS, j) * np.linalg.matrix_power(once, j) for j in range(1, SWEEPS + 1)]
+    return jnp.asarray(np.concatenate([np.concatenate(row, axis=1)] * 2, axis=0), jnp.bfloat16)
 
 
 GROUP = 8
 
 
-def spread_product(planes, rows, rate, inside, powers):
+def spread_product(planes, rows, rate, inside, powers, scale=None):
     levels, cells = planes[0].shape
     terms = [{} for j in range(SWEEPS)]
     for first in range(0, rows, GROUP):
@@ -94,14 +94,22 @@
         for at in range(GROUP):
             for j in range(SWEEPS):
                 terms[j][first + at] = product[at * levels : (at + 1) * levels, j * cells : (j + 1) * cells]
+    own = jnp.broadcast_to(1.0 / jnp.full((8, cells), rate, jnp.float32) - 4.0, (levels // 8, 8, cells)).reshape(levels, cells)
     result = planes
     for j in range(1, SWEEPS + 1):
         left = SWEEPS - j
-        result = along_x(result, range(-left, rows + left), rows, rate, inside)
-        factor = binomial(j, rate)
-        for x in range(rows):
-            result[x] = result[x] + factor * terms[j - 1][x]
-    return result
+        before, result = result, {}
+        for x in range(-left, rows + left):
+            total = terms[j - 1].get(x)
+            for near in (x - 1, x + 1):
+                if near in before:
+                    total = before[near] if total is None else total + before[near]
+            if x in before:
+                total = own * before[x] if total is None else total + own * before[x]
+            if total is not None:
+                result[x] = total * inside[0] if x < 0 else total * inside[1] if x >= rows else total
+    fourth = rate * rate * (rate * rate)
+    return {x: value * (fourth if scale is None else fourth * scale) for x, value in result.items()}
 
 
 def rate_of(field, members, group, localize, static):
@@ -128,13 +136,11 @@
     return jnp.where(even, rows - SWEEPS, 0), jnp.where(even, 0, rows - SWEEPS)
 
 
-BATCH = 4
-
-
-def add_side(side, upper, rates, shape, visit, counts=None):
+def add_side(side, upper, rates, shape, visit, counts=None, batch=None):
     levels, rows, cells = shape
-    for first in range(0, len(rates), BATCH):
-        fields = range(first, min(first + BATCH, len(rates)))
+    batch = batch or len(rates)
+    for first in range(0, len(rates), batch):
+        fields = range(first, min(first + batch, len(rates)))
         rate = jnp.concatenate([jnp.full((levels, cells), rates[field], jnp.float32) for field in fields], axis=0)
         planes = {}
         for away in range(1, SWEEPS + 1):
@@ -252,9 +258,9 @@
     def of_field(field):
         planes = {x: held[field, pl.ds(x, levels, stride=rows), :] for x in range(rows)}
         rate = rate_of(field, members, group, localize, static)
-        planes = spread_product(planes, rows, rate, inside, powers)
+        planes = spread_product(planes, rows, rate, inside, powers, scale[field])
         for x in range(rows):
-            out[field, pl.ds(x, levels, stride=rows), :] = planes[x] * scale[field]
+            out[field, pl.ds(x, levels, stride=rows), :] = planes[x]
 
     each_field(members + nvars, of_field, members + nvars)
     rates = rates_of(members + nvars, members, group, localize, static)
@@ -403,7 +409,7 @@
             write.start()
             writes.append(write)
 
-    add_side(side_b, upper, rates, (levels, rows, cells), visit, below * above)
+    add_side(side_b, upper, rates, (levels, rows, cells), visit, below * above, 4)
     for write in writes:
         write.wait()
 

time: 51.4 us -> 50.7 us (0.986)
  Pallas kernels: 21.8 us -> 20.8 us
    pallas_call x6, Pallas kernels: 21.8 us -> 20.8 us  [call(): pl.pallas_call(body, out_shape=tuple((jax.ShapeDtypeStruct(tuple(shape),...]
  transfers between devices with their start and end apart: 8 -> 8, of which waited for: 5 -> 5; matrix products, arithmetic and copies ran while one was open for 10% -> 10% of each run, Pallas kernels for 21% -> 19%
where the time goes in v12:
time: 50.7 us; the launch traced here: 49.7 us
  Pallas kernels  20.8 us (41%)
  waiting for transfers between devices  11.4 us (22%)
  starting transfers between devices  10.8 us (21%)
  other arithmetic  4.99 us (10%)
  between operations  1.69 us (3%)
    pallas_call x6, Pallas kernels, call(): pl.pallas_call(body, out_shape=tuple((jax.ShapeDtypeStruct(tuple(shape),...  20.8 us
    sort x1, other arithmetic, per_device(): lax.sort((key.reshape(-1), obs_frac, weight.reshape(-1)), num_keys=1, is_...  4.98 us
    ppermute x3, starting transfers between devices, summands(): lax.ppermute(value, 'grp', [(i, i ^ turn) for i in range(count)])  4.9 us
    ppermute x2, starting transfers between devices, exchange(): lax.ppermute(side_b, 'tile', pairs_b)  4.5 us
    ppermute x1, waiting for transfers between devices, summands(): lax.ppermute(value, 'grp', [(i, i ^ 1) for i in range(count)])  4.13 us
    ppermute x3, waiting for transfers between devices, summands(): lax.ppermute(value, 'grp', [(i, i ^ turn) for i in range(count)])  3.92 us
    ppermute x2, waiting for transfers between devices, exchange(): lax.ppermute(side_b, 'tile', pairs_b)  2.62 us
    ppermute x1, starting transfers between devices, summands(): lax.ppermute(value, 'grp', [(i, i ^ 1) for i in range(count)])  1.19 us
  transfers between devices with their start and end apart: 8, of which 5 were waited for; matrix products, arithmetic and copies ran while one was open for 10% of the time, Pallas kernels for 19%

profile of v12, /device:TPU:6, one launch (start us, length us, event | category | flops | bytes accessed | tf_op | source)
XLA Modules:
  0.0 49.7 jit_solution(16851058076625486958)
XLA Ops:
  0.6 0.0 copy-start.1
  0.6 0.0 copy-start.9
  0.7 0.0 copy-start.6
  0.7 0.0 copy-start.5
  0.7 0.0 copy-start.7
  0.7 0.0 copy-start.4
  0.7 0.0 copy-start.2
  0.7 0.0 copy-start.3
  0.7 1.6 %pack_kernel.1 = (f32[4,224,128]{2,1,0:T(8,128)S(1)}, f32[4,224,128]{2,1,0:T(8,128)S(1)}, f32[7,512,128]{2,1,0:T(8,128)S(1)}) custom-call(f32[2,512,128]{2,1,0:T(8,128)} %bitcast.32, f32[5,512,128]{2,1,0:T(8,128)} %bitcast.30), custom_call_target="tpu_custom_call" | custom-call | flops 20000000 | bytes 2000000 | tf_op jit(solution)/shard_map/pack_kernel/pallas_call | solution.py:441
  2.4 0.0 copy-start.8
  2.4 0.1 collective-permute-start
  2.5 3.4 %collective-permute-start.1 = (f32[4,224,128]{2,1,0:T(8,128)S(1)}, f32[4,224,128]{2,1,0:T(8,128)S(1)}, u32[]{:S(2)}, u32[]{:S(2)}) collective-permute-start(f32[4,224,128]{2,1,0:T(8,128)S(1)} %get-tuple-element.25), channel_id=1, source_target_pairs={{0,15},{1,2},{2,1},{3,4},{4,3},{5,6},{6,5},{7,8},{8,7},{9,10},{10,... | collective-permute-start | bytes 1376264 | tf_op jit(solution)/shard_map/ppermute | solution.py:421
  6.5 0.0 copy-done.9
  6.5 0.0 collective-permute-done.refs_3_
  6.5 0.1 broadcast_in_dim.2.refs_2_.refs_1_.refs_4_.refs_3_
  6.6 0.0 copy-done.1
  6.6 0.0 copy-done.6
  6.7 0.0 copy-done.5
  6.7 0.0 copy-done.7
  6.7 0.0 copy-done.4
  6.7 0.0 copy-done.2
  6.7 0.0 copy-done.3
  6.7 4.0 %own_kernel.1 = (f32[7,512,128]{2,1,0:T(8,128)S(1)}, s32[32,128]{1,0:T(8,128)S(1)}, f32[32,128]{1,0:T(8,128)S(1)}) custom-call(bf16[256,512]{1,0:T(8,128)(2,1)S(1)} %copy-done.1, f32[7,512,128]{2,1,0:T(8,128)S(1)} %get-tuple-element.17.refs_1_, f32[7,32,128]{2,1,0:T(8,128)S(1)} %broadcast_in_dim.2.refs_2_.refs_1_.refs_4_.refs_3_, ...), custom_call_target="tpu_custom_call" | custom-call | flops 20000000 | bytes 2000000 | tf_op jit(solution)/shard_map/own_kernel/pallas_call | solution.py:441
  10.7 0.0 copy-done.8
  10.7 5.0 %sort.21 = (s32[4096]{0:T(1024)S(1)}, f32[4096]{0:T(1024)S(1)}, f32[4096]{0:T(1024)S(1)}) sort(s32[4096]{0:T(1024)S(1)} %bitcast.28, f32[4096]{0:T(1024)S(1)} %copy-done.8, f32[4096]{0:T(1024)S(1)} %bitcast.29), dimensions={0}, to_apply=%region_0.0 | sort | flops 49152 | bytes 98304 | tf_op jit(solution)/shard_map/sort | solution.py:499
  15.7 0.0 collective-permute-done.1.refs_2_
  15.7 0.0 copy-start
  15.7 4.1 %forward_kernel.1 = f32[32,128]{1,0:T(8,128)S(1)} custom-call(f32[7,512,128]{2,1,0:T(8,128)S(1)} %get-tuple-element.24.refs_0_, f32[7,32,128]{2,1,0:T(8,128)S(1)} %broadcast_in_dim.2.refs_2_.refs_1_.refs_4_.refs_3_, f32[4,224,128]{2,1,0:T(8,128)S(1)} %collective-permute-done.1.refs_2_, s32[32,128]{1,0:T(8,128)S(1)} %bitcast.18, f32[32,128]{1,0:T(8,128)S(1)} %bitcast.22, ...), custom_call_target="tpu_custom_call" | custom-call | flops 20000000 | bytes 2000000 | tf_op jit(solution)/shard_map/forward_kernel/pallas_call | solution.py:441
  19.8 1.2 %collective-permute-start.2 = (f32[32,128]{1,0:T(8,128)S(1)}, f32[32,128]{1,0:T(8,128)S(1)}, u32[]{:S(2)}, u32[]{:S(2)}) collective-permute-start(f32[32,128]{1,0:T(8,128)S(1)} %forward_kernel.1), channel_id=1, source_target_pairs={{0,16},{16,0},{32,48},{48,32},{64,80},{80,64},{96,112},{112,96},{1... | collective-permute-start | bytes 49160 | tf_op jit(solution)/shard_map/ppermute | solution.py:426
  21.0 4.1 %collective-permute-done.2 = f32[32,128]{1,0:T(8,128)S(1)} collective-permute-done((f32[32,128]{1,0:T(8,128)S(1)}, f32[32,128]{1,0:T(8,128)S(1)}, u32[]{:S(2)}, u32[]{:S(2)}) %collective-permute-start.2) | collective-permute-done | bytes 16416 | tf_op jit(solution)/shard_map/ppermute | solution.py:426
  25.1 3.9 %collective-permute-start.5 = (f32[32,128]{1,0:T(8,128)S(1)}, f32[32,128]{1,0:T(8,128)S(1)}, u32[]{:S(2)}, u32[]{:S(2)}) collective-permute-start(f32[32,128]{1,0:T(8,128)S(1)} %add.5.refs_5_), channel_id=1, source_target_pairs={{0,64},{16,80},{32,96},{48,112},{64,0},{80,16},{96,32},{112,48},{1... | collective-permute-start | bytes 49160 | tf_op jit(solution)/shard_map/ppermute | solution.py:428
  29.0 0.7 %collective-permute-start.4 = (f32[32,128]{1,0:T(8,128)S(1)}, f32[32,128]{1,0:T(8,128)S(1)}, u32[]{:S(2)}, u32[]{:S(2)}) collective-permute-start(f32[32,128]{1,0:T(8,128)S(1)} %add.5.refs_5_), channel_id=1, source_target_pairs={{0,96},{16,112},{32,64},{48,80},{64,32},{80,48},{96,0},{112,16},{1... | collective-permute-start | bytes 49160 | tf_op jit(solution)/shard_map/ppermute | solution.py:428
  29.7 0.3 collective-permute-start.3
  30.0 0.7 %collective-permute-done.5.refs_8_ = f32[32,128]{1,0:T(8,128)S(1)} collective-permute-done((f32[32,128]{1,0:T(8,128)S(1)}, f32[32,128]{1,0:T(8,128)S(1)}, u32[]{:S(2)}, u32[]{:S(2)}) %collective-permute-start.5) | collective-permute-done | bytes 16416 | tf_op jit(solution)/shard_map/ppermute | solution.py:428
  30.7 3.2 %collective-permute-done.4.refs_7_ = f32[32,128]{1,0:T(8,128)S(1)} collective-permute-done((f32[32,128]{1,0:T(8,128)S(1)}, f32[32,128]{1,0:T(8,128)S(1)}, u32[]{:S(2)}, u32[]{:S(2)}) %collective-permute-start.4) | collective-permute-done | bytes 16416 | tf_op jit(solution)/shard_map/ppermute | solution.py:428
  33.9 0.0 collective-permute-done.3.refs_6_
  33.9 0.0 copy-done
  34.0 3.0 %scatter_kernel.1 = (f32[2,512,128]{2,1,0:T(8,128)S(1)}, f32[4,224,128]{2,1,0:T(8,128)S(1)}, f32[4,224,128]{2,1,0:T(8,128)S(1)}, f32[2816,128]{1,0:T(8,128)S(1)}) custom-call(s32[32,128]{1,0:T(8,128)S(1)} %bitcast.20, f32[32,128]{1,0:T(8,128)S(1)} %bitcast.23, f32[32,128]{1,0:T(8,128)S(1)} %bitcast.27, bf16[2,5,512,128]{3,2,1,0:T(8,128)(2,1)S(1)} %bitcast.17, ...), custom_call_target="tpu_custom_call" | custom-call | flops 20000000 | bytes 2000000 | tf_op jit(solution)/shard_map/scatter_kernel/pallas_call | solution.py:441
  36.9 0.1 collective-permute-start.6
  37.0 1.1 %collective-permute-start.7 = (f32[4,224,128]{2,1,0:T(8,128)S(1)}, f32[4,224,128]{2,1,0:T(8,128)S(1)}, u32[]{:S(2)}, u32[]{:S(2)}) collective-permute-start(f32[4,224,128]{2,1,0:T(8,128)S(1)} %get-tuple-element.29), channel_id=1, source_target_pairs={{0,15},{1,2},{2,1},{3,4},{4,3},{5,6},{6,5},{7,8},{8,7},{9,10},{10,... | collective-permute-start | bytes 1376264 | tf_op jit(solution)/shard_map/ppermute | solution.py:421
  38.2 0.7 %collective-permute-done.6.refs_4_ = f32[4,224,128]{2,1,0:T(8,128)S(1)} collective-permute-done((f32[4,224,128]{2,1,0:T(8,128)S(1)}, f32[4,224,128]{2,1,0:T(8,128)S(1)}, u32[]{:S(2)}, u32[]{:S(2)}) %collective-permute-start.6) | collective-permute-done | bytes 458784 | tf_op jit(solution)/shard_map/ppermute | solution.py:421
  38.8 5.7 %local_kernel.1.refs_0_ = f32[7,512,128]{2,1,0:T(8,128)S(1)} custom-call(bf16[256,512]{1,0:T(8,128)(2,1)S(1)} %copy-done.1, f32[2,512,128]{2,1,0:T(8,128)S(1)} %get-tuple-element.26.refs_1_, f32[2816,128]{1,0:T(8,128)S(1)} %get-tuple-element.27.refs_2_, f32[7,32,128]{2,1,0:T(8,128)S(1)} %broadcast_in_dim.2.refs_2_.refs_1_.refs_4_.refs_3_, ...), custom_call_target="tpu_custom_call" | custom-call | flops 20000000 | bytes 2000000 | tf_op jit(solution)/shard_map/local_kernel/pallas_call | solution.py:441
  44.5 2.6 %collective-permute-done.7.refs_1_ = f32[4,224,128]{2,1,0:T(8,128)S(1)} collective-permute-done((f32[4,224,128]{2,1,0:T(8,128)S(1)}, f32[4,224,128]{2,1,0:T(8,128)S(1)}, u32[]{:S(2)}, u32[]{:S(2)}) %collective-permute-start.7) | collective-permute-done | bytes 458784 | tf_op jit(solution)/shard_map/ppermute | solution.py:421
  47.1 2.4 %edge_kernel.1 = (f32[2,512,128]{2,1,0:T(8,128)}, f32[5,512,128]{2,1,0:T(8,128)}) custom-call(f32[7,512,128]{2,1,0:T(8,128)S(1)} %local_kernel.1.refs_0_, f32[4,224,128]{2,1,0:T(8,128)S(1)} %collective-permute-done.7.refs_1_, s32[2]{0:T(128)S(1)} %copy-done.5, f32[12]{0:T(128)S(1)} %copy-done.6, f32[1]{0:T(128)S(6)} %copy.18.refs_9_.refs_4_), custom_call_target="tpu_custom_call" | custom-call | flops 20000000 | bytes 2000000 | tf_op jit(solution)/shard_map/edge_kernel/pallas_call | solution.py:441
  (3 shorter events, 0.0 us)
Async XLA Ops:
  0.6 6.0 %copy-start.1 = (bf16[256,512]{1,0:T(8,128)(2,1)S(1)}, bf16[256,512]{1,0:T(8,128)(2,1)}, u32[]{:S(2)}) copy-start(bf16[256,512]{1,0:T(8,128)(2,1)} %constant.4.clone.refs_0_) | copy-start | bytes 786436
  0.6 5.9 %copy-start.9 = (f32[1,5,32]{2,0,1:T(1,128)S(1)}, f32[1,5,32]{2,0,1:T(1,128)}, u32[]{:S(2)}) copy-start(f32[1,5,32]{2,0,1:T(1,128)} %param.19) | copy-start | bytes 1924
  0.7 6.0 %copy-start.6 = (f32[12]{0:T(128)S(1)}, f32[12]{0:T(128)}, u32[]{:S(2)}) copy-start(f32[12]{0:T(128)} %refs_3_.1) | copy-start | bytes 148
  0.7 6.0 %copy-start.5 = (s32[2]{0:T(128)S(1)}, s32[2]{0:T(128)}, u32[]{:S(2)}) copy-start(s32[2]{0:T(128)} %refs_2_.1) | copy-start | bytes 28
  0.7 6.0 %copy-start.7 = (f32[8]{0:T(128)S(1)}, f32[8]{0:T(128)}, u32[]{:S(2)}) copy-start(f32[8]{0:T(128)} %refs_10_.1) | copy-start | bytes 100
  0.7 6.0 %copy-start.4 = (s32[4096]{0:T(1024)S(1)}, s32[4096]{0:T(1024)}, u32[]{:S(2)}) copy-start(s32[4096]{0:T(1024)} %param.23) | copy-start | bytes 49156
  0.7 6.0 %copy-start.2 = (s32[4096]{0:T(1024)S(1)}, s32[4096]{0:T(1024)}, u32[]{:S(2)}) copy-start(s32[4096]{0:T(1024)} %param.22) | copy-start | bytes 49156
  0.7 6.0 %copy-start.3 = (s32[4096]{0:T(1024)S(1)}, s32[4096]{0:T(1024)}, u32[]{:S(2)}) copy-start(s32[4096]{0:T(1024)} %param.20) | copy-start | bytes 49156
  2.4 8.3 %copy-start.8 = (f32[4096]{0:T(1024)S(1)}, f32[4096]{0:T(1024)}, u32[]{:S(2)}) copy-start(f32[4096]{0:T(1024)} %param.21) | copy-start | bytes 49156
  2.4 4.2 %collective-permute-start = (f32[4,224,128]{2,1,0:T(8,128)S(1)}, f32[4,224,128]{2,1,0:T(8,128)S(1)}, u32[]{:S(2)}, u32[]{:S(2)}) collective-permute-start(f32[4,224,128]{2,1,0:T(8,128)S(1)} %get-tuple-element.18), channel_id=1, source_target_pairs={{0,1},{1,0},{2,3},{3,2},{4,5},{5,4},{6,7},{7,6},{8,9},{9,8},{10,11... | collective-permute-start | bytes 1376264 | tf_op jit(solution)/shard_map/ppermute | solution.py:421
  2.5 13.2 %collective-permute-start.1 = (f32[4,224,128]{2,1,0:T(8,128)S(1)}, f32[4,224,128]{2,1,0:T(8,128)S(1)}, u32[]{:S(2)}, u32[]{:S(2)}) collective-permute-start(f32[4,224,128]{2,1,0:T(8,128)S(1)} %get-tuple-element.25), channel_id=1, source_target_pairs={{0,15},{1,2},{2,1},{3,4},{4,3},{5,6},{6,5},{7,8},{8,7},{9,10},{10,... | collective-permute-start | bytes 1376264 | tf_op jit(solution)/shard_map/ppermute | solution.py:421
  15.7 18.3 %copy-start = (bf16[2,5,32,16,128]{4,3,2,1,0:T(8,128)(2,1)S(1)}, bf16[2,5,32,16,128]{4,3,2,1,0:T(8,128)(2,1)}, u32[]{:S(2)}) copy-start(bf16[2,5,32,16,128]{4,3,2,1,0:T(8,128)(2,1)} %param.15) | copy-start | bytes 3932164
  19.8 5.3 %collective-permute-start.2 = (f32[32,128]{1,0:T(8,128)S(1)}, f32[32,128]{1,0:T(8,128)S(1)}, u32[]{:S(2)}, u32[]{:S(2)}) collective-permute-start(f32[32,128]{1,0:T(8,128)S(1)} %forward_kernel.1), channel_id=1, source_target_pairs={{0,16},{16,0},{32,48},{48,32},{64,80},{80,64},{96,112},{112,96},{1... | collective-permute-start | bytes 49160 | tf_op jit(solution)/shard_map/ppermute | solution.py:426
  25.1 5.6 %collective-permute-start.5 = (f32[32,128]{1,0:T(8,128)S(1)}, f32[32,128]{1,0:T(8,128)S(1)}, u32[]{:S(2)}, u32[]{:S(2)}) collective-permute-start(f32[32,128]{1,0:T(8,128)S(1)} %add.5.refs_5_), channel_id=1, source_target_pairs={{0,64},{16,80},{32,96},{48,112},{64,0},{80,16},{96,32},{112,48},{1... | collective-permute-start | bytes 49160 | tf_op jit(solution)/shard_map/ppermute | solution.py:428
  29.0 4.9 %collective-permute-start.4 = (f32[32,128]{1,0:T(8,128)S(1)}, f32[32,128]{1,0:T(8,128)S(1)}, u32[]{:S(2)}, u32[]{:S(2)}) collective-permute-start(f32[32,128]{1,0:T(8,128)S(1)} %add.5.refs_5_), channel_id=1, source_target_pairs={{0,96},{16,112},{32,64},{48,80},{64,32},{80,48},{96,0},{112,16},{1... | collective-permute-start | bytes 49160 | tf_op jit(solution)/shard_map/ppermute | solution.py:428
  29.7 4.2 %collective-permute-start.3 = (f32[32,128]{1,0:T(8,128)S(1)}, f32[32,128]{1,0:T(8,128)S(1)}, u32[]{:S(2)}, u32[]{:S(2)}) collective-permute-start(f32[32,128]{1,0:T(8,128)S(1)} %add.5.refs_5_), channel_id=1, source_target_pairs={{0,32},{16,48},{32,0},{48,16},{64,96},{80,112},{96,64},{112,80},{1... | collective-permute-start | bytes 49160 | tf_op jit(solution)/shard_map/ppermute | solution.py:428
  36.9 1.9 %collective-permute-start.6 = (f32[4,224,128]{2,1,0:T(8,128)S(1)}, f32[4,224,128]{2,1,0:T(8,128)S(1)}, u32[]{:S(2)}, u32[]{:S(2)}) collective-permute-start(f32[4,224,128]{2,1,0:T(8,128)S(1)} %get-tuple-element.28), channel_id=1, source_target_pairs={{0,1},{1,0},{2,3},{3,2},{4,5},{5,4},{6,7},{7,6},{8,9},{9,8},{10,11... | collective-permute-start | bytes 1376264 | tf_op jit(solution)/shard_map/ppermute | solution.py:421
  37.0 10.1 %collective-permute-start.7 = (f32[4,224,128]{2,1,0:T(8,128)S(1)}, f32[4,224,128]{2,1,0:T(8,128)S(1)}, u32[]{:S(2)}, u32[]{:S(2)}) collective-permute-start(f32[4,224,128]{2,1,0:T(8,128)S(1)} %get-tuple-element.29), channel_id=1, source_target_pairs={{0,15},{1,2},{2,1},{3,4},{4,3},{5,6},{6,5},{7,8},{8,7},{9,10},{10,... | collective-permute-start | bytes 1376264 | tf_op jit(solution)/shard_map/ppermute | solution.py:421

commit v13 on v12

--- a/solution.py
+++ b/solution.py
@@ -320,7 +320,17 @@
     every_window(bound, blocks, cells, visit, visit_again)
 
 
-def scatter_kernel(dims, key, frac, weight, perturb, scale, *refs):
+def ready_kernel(dims, key, frac, bound, chosen, spread_out):
+    members, nvars, levels, rows, cells, blocks = dims
+    shift = cells.bit_length() - 1
+    for block in range(blocks):
+        start, count = window_of(bound, block, cells)
+        keys = block_of(key, block)
+        chosen[block] = chosen_rows(keys, start, shift)
+        spread_out[block] = weights_of(keys, block_of(frac, block), cells)
+
+
+def scatter_kernel(dims, chosen, spread_out, key, frac, weight, perturb, scale, *refs):
     members, nvars, levels, rows, cells, blocks = dims
     *seen, bound, source, side_a, side_b, gradient, valued = refs
     shift = cells.bit_length() - 1
@@ -330,12 +340,10 @@
     valued[...] = total * weight[...]
     gradient[...] = jnp.zeros(gradient.shape, jnp.float32)
 
-    def add_block(block, start):
-        keys = block_of(key, block)
-        placed = weights_of(keys, block_of(frac, block), cells) * block_of(valued, block)
-        high, low = halves(placed)
+    def add_placed(block, start, taken, places):
+        high, low = halves(places * block_of(valued, block))
         both = lax.dot_general(
-            chosen_rows(keys, start, shift),
+            taken,
             jnp.concatenate([high, low], axis=0),
             (((1,), (1,)), ((), ())),
             preferred_element_type=jnp.float32,
@@ -343,7 +351,14 @@
         at = pl.ds(pl.multiple_of(start, ALIGN), BLOCK)
         gradient[at, :] = gradient[at, :] + (both[:, :cells] + both[:, cells:])
 
-    every_window(bound, blocks, cells, add_block, add_block)
+    def add_first(block, start):
+        add_placed(block, start, chosen[block], spread_out[block])
+
+    def add_further(block, start):
+        keys = block_of(key, block)
+        add_placed(block, start, chosen_rows(keys, start, shift), weights_of(keys, block_of(frac, block), cells))
+
+    every_window(bound, blocks, cells, add_first, add_further)
 
     plane = levels * rows
     for m in range(members):
@@ -515,11 +530,20 @@
         ],
     )
     seen = summands(seen)
+    chosen, spread_out = call(
+        ready_kernel,
+        dims,
+        [(blocks, BLOCK, BLOCK), (blocks, cells, BLOCK)],
+        [key, frac],
+        [],
+        [key],
+        kinds=[jnp.bfloat16, jnp.float32],
+    )
     source, side_a, side_b, gradient = call(
         scatter_kernel,
         dims,
         [(members, plane, cells), strip, strip, (table_rows, cells)],
-        [key, frac, weight, perturb, scale] + seen,
+        [chosen, spread_out, key, frac, weight, perturb, scale] + seen,
         [],
         [key],
         [pltpu.VMEM(key.shape, jnp.float32)],

time: 50.7 us -> 50.2 us (level)
  waiting for transfers between devices: 11.4 us -> 9.99 us
  Pallas kernels: 20.8 us -> 21.7 us
    ppermute x3, waiting for transfers between devices: 3.92 us -> 2.56 us  [summands(): lax.ppermute(value, 'grp', [(i, i ^ turn) for i in range(count)])]
    pallas_call x6 -> x7, Pallas kernels: 20.8 us -> 21.7 us  [call(): pl.pallas_call(body, out_shape=tuple((jax.ShapeDtypeStruct(tuple(shape),...]
  transfers between devices with their start and end apart: 8 -> 8, of which waited for: 5 -> 4; matrix products, arithmetic and copies ran while one was open for 10% -> 10% of each run, Pallas kernels for 19% -> 22%
where the time goes in v13:
time: 50.2 us; the launch traced here: 49.3 us
  Pallas kernels  21.7 us (43%)
  starting transfers between devices  10.8 us (22%)
  waiting for transfers between devices  9.99 us (20%)
  other arithmetic  4.99 us (10%)
  between operations  1.7 us (3%)
    pallas_call x7, Pallas kernels, call(): pl.pallas_call(body, out_shape=tuple((jax.ShapeDtypeStruct(tuple(shape),...  21.7 us
    sort x1, other arithmetic, per_device(): lax.sort((key.reshape(-1), obs_frac, weight.reshape(-1)), num_keys=1, is_...  4.98 us
    ppermute x3, starting transfers between devices, summands(): lax.ppermute(value, 'grp', [(i, i ^ turn) for i in range(count)])  4.9 us
    ppermute x2, starting transfers between devices, exchange(): lax.ppermute(side_b, 'tile', pairs_b)  4.51 us
    ppermute x1, waiting for transfers between devices, summands(): lax.ppermute(value, 'grp', [(i, i ^ 1) for i in range(count)])  4.13 us
    ppermute x2, waiting for transfers between devices, exchange(): lax.ppermute(side_b, 'tile', pairs_b)  2.63 us
    ppermute x3, waiting for transfers between devices, summands(): lax.ppermute(value, 'grp', [(i, i ^ turn) for i in range(count)])  2.56 us
    ppermute x1, starting transfers between devices, summands(): lax.ppermute(value, 'grp', [(i, i ^ 1) for i in range(count)])  1.19 us
  transfers between devices with their start and end apart: 8, of which 4 were waited for; matrix products, arithmetic and copies ran while one was open for 10% of the time, Pallas kernels for 22%

profile of v13, /device:TPU:6, one launch (start us, length us, event | category | flops | bytes accessed | tf_op | source)
XLA Modules:
  0.0 49.3 jit_solution(4993129576947349823)
XLA Ops:
  0.6 0.0 copy-start.1
  0.6 0.0 copy-start.9
  0.7 0.0 copy-start.6
  0.7 0.0 copy-start.5
  0.7 0.0 copy-start.7
  0.7 0.0 copy-start.4
  0.7 0.0 copy-start.2
  0.7 0.0 copy-start.3
  0.7 1.6 %pack_kernel.1 = (f32[4,224,128]{2,1,0:T(8,128)S(1)}, f32[4,224,128]{2,1,0:T(8,128)S(1)}, f32[7,512,128]{2,1,0:T(8,128)S(1)}) custom-call(f32[2,512,128]{2,1,0:T(8,128)} %bitcast.35, f32[5,512,128]{2,1,0:T(8,128)} %bitcast.33), custom_call_target="tpu_custom_call" | custom-call | flops 20000000 | bytes 2000000 | tf_op jit(solution)/shard_map/pack_kernel/pallas_call | solution.py:456
  2.4 0.0 copy-start.8
  2.4 0.1 collective-permute-start
  2.5 3.4 %collective-permute-start.1 = (f32[4,224,128]{2,1,0:T(8,128)S(1)}, f32[4,224,128]{2,1,0:T(8,128)S(1)}, u32[]{:S(2)}, u32[]{:S(2)}) collective-permute-start(f32[4,224,128]{2,1,0:T(8,128)S(1)} %get-tuple-element.29), channel_id=1, source_target_pairs={{0,15},{1,2},{2,1},{3,4},{4,3},{5,6},{6,5},{7,8},{8,7},{9,10},{10,... | collective-permute-start | bytes 1376264 | tf_op jit(solution)/shard_map/ppermute | solution.py:436
  6.5 0.0 copy-done.9
  6.5 0.0 collective-permute-done.refs_3_
  6.5 0.1 broadcast_in_dim.2.refs_2_.refs_1_.refs_6_.refs_3_
  6.6 0.0 copy-done.1
  6.6 0.0 copy-done.6
  6.7 0.0 copy-done.5
  6.7 0.0 copy-done.7
  6.7 0.0 copy-done.4
  6.7 0.0 copy-done.2
  6.7 0.0 copy-done.3
  6.7 4.0 %own_kernel.1 = (f32[7,512,128]{2,1,0:T(8,128)S(1)}, s32[32,128]{1,0:T(8,128)S(1)}, f32[32,128]{1,0:T(8,128)S(1)}) custom-call(bf16[256,512]{1,0:T(8,128)(2,1)S(1)} %copy-done.1, f32[7,512,128]{2,1,0:T(8,128)S(1)} %get-tuple-element.19.refs_1_, f32[7,32,128]{2,1,0:T(8,128)S(1)} %broadcast_in_dim.2.refs_2_.refs_1_.refs_6_.refs_3_, ...), custom_call_target="tpu_custom_call" | custom-call | flops 20000000 | bytes 2000000 | tf_op jit(solution)/shard_map/own_kernel/pallas_call | solution.py:456
  10.7 0.0 copy-done.8
  10.7 5.0 %sort.21 = (s32[4096]{0:T(1024)S(1)}, f32[4096]{0:T(1024)S(1)}, f32[4096]{0:T(1024)S(1)}) sort(s32[4096]{0:T(1024)S(1)} %bitcast.31, f32[4096]{0:T(1024)S(1)} %copy-done.8, f32[4096]{0:T(1024)S(1)} %bitcast.32), dimensions={0}, to_apply=%region_0.0 | sort | flops 49152 | bytes 98304 | tf_op jit(solution)/shard_map/sort | solution.py:514
  15.7 0.0 collective-permute-done.1.refs_2_
  15.7 0.0 copy-start
  15.7 4.1 %forward_kernel.1 = f32[32,128]{1,0:T(8,128)S(1)} custom-call(f32[7,512,128]{2,1,0:T(8,128)S(1)} %get-tuple-element.28.refs_0_, f32[7,32,128]{2,1,0:T(8,128)S(1)} %broadcast_in_dim.2.refs_2_.refs_1_.refs_6_.refs_3_, f32[4,224,128]{2,1,0:T(8,128)S(1)} %collective-permute-done.1.refs_2_, s32[32,128]{1,0:T(8,128)S(1)} %bitcast.18, f32[32,128]{1,0:T(8,128)S(1)} %bitcast.24, ...), custom_call_target="tpu_custom_call" | custom-call | flops 20000000 | bytes 2000000 | tf_op jit(solution)/shard_map/forward_kernel/pallas_call | solution.py:456
  19.8 1.2 %collective-permute-start.2 = (f32[32,128]{1,0:T(8,128)S(1)}, f32[32,128]{1,0:T(8,128)S(1)}, u32[]{:S(2)}, u32[]{:S(2)}) collective-permute-start(f32[32,128]{1,0:T(8,128)S(1)} %forward_kernel.1), channel_id=1, source_target_pairs={{0,16},{16,0},{32,48},{48,32},{64,80},{80,64},{96,112},{112,96},{1... | collective-permute-start | bytes 49160 | tf_op jit(solution)/shard_map/ppermute | solution.py:441
  21.0 4.1 %collective-permute-done.2 = f32[32,128]{1,0:T(8,128)S(1)} collective-permute-done((f32[32,128]{1,0:T(8,128)S(1)}, f32[32,128]{1,0:T(8,128)S(1)}, u32[]{:S(2)}, u32[]{:S(2)}) %collective-permute-start.2) | collective-permute-done | bytes 16416 | tf_op jit(solution)/shard_map/ppermute | solution.py:441
  25.1 3.9 %collective-permute-start.5 = (f32[32,128]{1,0:T(8,128)S(1)}, f32[32,128]{1,0:T(8,128)S(1)}, u32[]{:S(2)}, u32[]{:S(2)}) collective-permute-start(f32[32,128]{1,0:T(8,128)S(1)} %add.5.refs_7_), channel_id=1, source_target_pairs={{0,64},{16,80},{32,96},{48,112},{64,0},{80,16},{96,32},{112,48},{1... | collective-permute-start | bytes 49160 | tf_op jit(solution)/shard_map/ppermute | solution.py:443
  29.0 0.7 %collective-permute-start.4 = (f32[32,128]{1,0:T(8,128)S(1)}, f32[32,128]{1,0:T(8,128)S(1)}, u32[]{:S(2)}, u32[]{:S(2)}) collective-permute-start(f32[32,128]{1,0:T(8,128)S(1)} %add.5.refs_7_), channel_id=1, source_target_pairs={{0,96},{16,112},{32,64},{48,80},{64,32},{80,48},{96,0},{112,16},{1... | collective-permute-start | bytes 49160 | tf_op jit(solution)/shard_map/ppermute | solution.py:443
  29.7 0.3 collective-permute-start.3
  30.0 1.4 %ready_kernel.1 = (bf16[16,256,256]{2,1,0:T(8,128)(2,1)S(1)}, f32[16,128,256]{2,1,0:T(8,128)S(1)}) custom-call(s32[32,128]{1,0:T(8,128)S(1)} %bitcast.20, f32[32,128]{1,0:T(8,128)S(1)} %bitcast.25, s32[32,128]{1,0:T(8,128)S(1)} %bitcast.21), custom_call_target="tpu_custom_call" | custom-call | flops 20000000 | bytes 2000000 | tf_op jit(solution)/shard_map/ready_kernel/pallas_call | solution.py:456
  31.4 0.0 collective-permute-done.5.refs_10_
  31.4 2.6 %collective-permute-done.4.refs_9_ = f32[32,128]{1,0:T(8,128)S(1)} collective-permute-done((f32[32,128]{1,0:T(8,128)S(1)}, f32[32,128]{1,0:T(8,128)S(1)}, u32[]{:S(2)}, u32[]{:S(2)}) %collective-permute-start.4) | collective-permute-done | bytes 16416 | tf_op jit(solution)/shard_map/ppermute | solution.py:443
  33.9 0.0 collective-permute-done.3.refs_8_
  33.9 0.0 copy-done
  33.9 2.6 %scatter_kernel.1 = (f32[2,512,128]{2,1,0:T(8,128)S(1)}, f32[4,224,128]{2,1,0:T(8,128)S(1)}, f32[4,224,128]{2,1,0:T(8,128)S(1)}, f32[2816,128]{1,0:T(8,128)S(1)}) custom-call(bf16[16,256,256]{2,1,0:T(8,128)(2,1)S(1)} %get-tuple-element.25.refs_0_, f32[16,128,256]{2,1,0:T(8,128)S(1)} %get-tuple-element.26.refs_1_, s32[32,128]{1,0:T(8,128)S(1)} %bitcast.22, ...), custom_call_target="tpu_custom_call" | custom-call | flops 20000000 | bytes 2000000 | tf_op jit(solution)/shard_map/scatter_kernel/pallas_call | solution.py:456
  36.5 0.1 collective-permute-start.6
  36.6 1.1 %collective-permute-start.7 = (f32[4,224,128]{2,1,0:T(8,128)S(1)}, f32[4,224,128]{2,1,0:T(8,128)S(1)}, u32[]{:S(2)}, u32[]{:S(2)}) collective-permute-start(f32[4,224,128]{2,1,0:T(8,128)S(1)} %get-tuple-element.33), channel_id=1, source_target_pairs={{0,15},{1,2},{2,1},{3,4},{4,3},{5,6},{6,5},{7,8},{8,7},{9,10},{10,... | collective-permute-start | bytes 1376264 | tf_op jit(solution)/shard_map/ppermute | solution.py:436
  37.7 0.7 %collective-permute-done.6.refs_4_ = f32[4,224,128]{2,1,0:T(8,128)S(1)} collective-permute-done((f32[4,224,128]{2,1,0:T(8,128)S(1)}, f32[4,224,128]{2,1,0:T(8,128)S(1)}, u32[]{:S(2)}, u32[]{:S(2)}) %collective-permute-start.6) | collective-permute-done | bytes 458784 | tf_op jit(solution)/shard_map/ppermute | solution.py:436
  38.4 5.7 %local_kernel.1.refs_0_ = f32[7,512,128]{2,1,0:T(8,128)S(1)} custom-call(bf16[256,512]{1,0:T(8,128)(2,1)S(1)} %copy-done.1, f32[2,512,128]{2,1,0:T(8,128)S(1)} %get-tuple-element.30.refs_1_, f32[2816,128]{1,0:T(8,128)S(1)} %get-tuple-element.31.refs_2_, f32[7,32,128]{2,1,0:T(8,128)S(1)} %broadcast_in_dim.2.refs_2_.refs_1_.refs_6_.refs_3_, ...), custom_call_target="tpu_custom_call" | custom-call | flops 20000000 | bytes 2000000 | tf_op jit(solution)/shard_map/local_kernel/pallas_call | solution.py:456
  44.1 2.6 %collective-permute-done.7.refs_1_ = f32[4,224,128]{2,1,0:T(8,128)S(1)} collective-permute-done((f32[4,224,128]{2,1,0:T(8,128)S(1)}, f32[4,224,128]{2,1,0:T(8,128)S(1)}, u32[]{:S(2)}, u32[]{:S(2)}) %collective-permute-start.7) | collective-permute-done | bytes 458784 | tf_op jit(solution)/shard_map/ppermute | solution.py:436
  46.7 2.4 %edge_kernel.1 = (f32[2,512,128]{2,1,0:T(8,128)}, f32[5,512,128]{2,1,0:T(8,128)}) custom-call(f32[7,512,128]{2,1,0:T(8,128)S(1)} %local_kernel.1.refs_0_, f32[4,224,128]{2,1,0:T(8,128)S(1)} %collective-permute-done.7.refs_1_, s32[2]{0:T(128)S(1)} %copy-done.5, f32[12]{0:T(128)S(1)} %copy-done.6, f32[1]{0:T(128)S(6)} %copy.18.refs_9_.refs_4_), custom_call_target="tpu_custom_call" | custom-call | flops 20000000 | bytes 2000000 | tf_op jit(solution)/shard_map/edge_kernel/pallas_call | solution.py:456
  (3 shorter events, 0.0 us)
Async XLA Ops:
  0.6 6.0 %copy-start.1 = (bf16[256,512]{1,0:T(8,128)(2,1)S(1)}, bf16[256,512]{1,0:T(8,128)(2,1)}, u32[]{:S(2)}) copy-start(bf16[256,512]{1,0:T(8,128)(2,1)} %constant.4.clone.refs_0_) | copy-start | bytes 786436
  0.6 5.9 %copy-start.9 = (f32[1,5,32]{2,0,1:T(1,128)S(1)}, f32[1,5,32]{2,0,1:T(1,128)}, u32[]{:S(2)}) copy-start(f32[1,5,32]{2,0,1:T(1,128)} %param.19) | copy-start | bytes 1924
  0.7 6.0 %copy-start.6 = (f32[12]{0:T(128)S(1)}, f32[12]{0:T(128)}, u32[]{:S(2)}) copy-start(f32[12]{0:T(128)} %refs_3_.1) | copy-start | bytes 148
  0.7 6.0 %copy-start.5 = (s32[2]{0:T(128)S(1)}, s32[2]{0:T(128)}, u32[]{:S(2)}) copy-start(s32[2]{0:T(128)} %refs_2_.1) | copy-start | bytes 28
  0.7 6.0 %copy-start.7 = (f32[8]{0:T(128)S(1)}, f32[8]{0:T(128)}, u32[]{:S(2)}) copy-start(f32[8]{0:T(128)} %refs_10_.1) | copy-start | bytes 100
  0.7 6.0 %copy-start.4 = (s32[4096]{0:T(1024)S(1)}, s32[4096]{0:T(1024)}, u32[]{:S(2)}) copy-start(s32[4096]{0:T(1024)} %param.23) | copy-start | bytes 49156
  0.7 6.0 %copy-start.2 = (s32[4096]{0:T(1024)S(1)}, s32[4096]{0:T(1024)}, u32[]{:S(2)}) copy-start(s32[4096]{0:T(1024)} %param.22) | copy-start | bytes 49156
  0.7 6.0 %copy-start.3 = (s32[4096]{0:T(1024)S(1)}, s32[4096]{0:T(1024)}, u32[]{:S(2)}) copy-start(s32[4096]{0:T(1024)} %param.20) | copy-start | bytes 49156
  2.4 8.3 %copy-start.8 = (f32[4096]{0:T(1024)S(1)}, f32[4096]{0:T(1024)}, u32[]{:S(2)}) copy-start(f32[4096]{0:T(1024)} %param.21) | copy-start | bytes 49156
  2.4 4.2 %collective-permute-start = (f32[4,224,128]{2,1,0:T(8,128)S(1)}, f32[4,224,128]{2,1,0:T(8,128)S(1)}, u32[]{:S(2)}, u32[]{:S(2)}) collective-permute-start(f32[4,224,128]{2,1,0:T(8,128)S(1)} %get-tuple-element.20), channel_id=1, source_target_pairs={{0,1},{1,0},{2,3},{3,2},{4,5},{5,4},{6,7},{7,6},{8,9},{9,8},{10,11... | collective-permute-start | bytes 1376264 | tf_op jit(solution)/shard_map/ppermute | solution.py:436
  2.5 13.2 %collective-permute-start.1 = (f32[4,224,128]{2,1,0:T(8,128)S(1)}, f32[4,224,128]{2,1,0:T(8,128)S(1)}, u32[]{:S(2)}, u32[]{:S(2)}) collective-permute-start(f32[4,224,128]{2,1,0:T(8,128)S(1)} %get-tuple-element.29), channel_id=1, source_target_pairs={{0,15},{1,2},{2,1},{3,4},{4,3},{5,6},{6,5},{7,8},{8,7},{9,10},{10,... | collective-permute-start | bytes 1376264 | tf_op jit(solution)/shard_map/ppermute | solution.py:436
  15.7 18.3 %copy-start = (bf16[2,5,32,16,128]{4,3,2,1,0:T(8,128)(2,1)S(1)}, bf16[2,5,32,16,128]{4,3,2,1,0:T(8,128)(2,1)}, u32[]{:S(2)}) copy-start(bf16[2,5,32,16,128]{4,3,2,1,0:T(8,128)(2,1)} %param.15) | copy-start | bytes 3932164
  19.8 5.3 %collective-permute-start.2 = (f32[32,128]{1,0:T(8,128)S(1)}, f32[32,128]{1,0:T(8,128)S(1)}, u32[]{:S(2)}, u32[]{:S(2)}) collective-permute-start(f32[32,128]{1,0:T(8,128)S(1)} %forward_kernel.1), channel_id=1, source_target_pairs={{0,16},{16,0},{32,48},{48,32},{64,80},{80,64},{96,112},{112,96},{1... | collective-permute-start | bytes 49160 | tf_op jit(solution)/shard_map/ppermute | solution.py:441
  25.1 6.3 %collective-permute-start.5 = (f32[32,128]{1,0:T(8,128)S(1)}, f32[32,128]{1,0:T(8,128)S(1)}, u32[]{:S(2)}, u32[]{:S(2)}) collective-permute-start(f32[32,128]{1,0:T(8,128)S(1)} %add.5.refs_7_), channel_id=1, source_target_pairs={{0,64},{16,80},{32,96},{48,112},{64,0},{80,16},{96,32},{112,48},{1... | collective-permute-start | bytes 49160 | tf_op jit(solution)/shard_map/ppermute | solution.py:443
  29.0 4.9 %collective-permute-start.4 = (f32[32,128]{1,0:T(8,128)S(1)}, f32[32,128]{1,0:T(8,128)S(1)}, u32[]{:S(2)}, u32[]{:S(2)}) collective-permute-start(f32[32,128]{1,0:T(8,128)S(1)} %add.5.refs_7_), channel_id=1, source_target_pairs={{0,96},{16,112},{32,64},{48,80},{64,32},{80,48},{96,0},{112,16},{1... | collective-permute-start | bytes 49160 | tf_op jit(solution)/shard_map/ppermute | solution.py:443
  29.7 4.2 %collective-permute-start.3 = (f32[32,128]{1,0:T(8,128)S(1)}, f32[32,128]{1,0:T(8,128)S(1)}, u32[]{:S(2)}, u32[]{:S(2)}) collective-permute-start(f32[32,128]{1,0:T(8,128)S(1)} %add.5.refs_7_), channel_id=1, source_target_pairs={{0,32},{16,48},{32,0},{48,16},{64,96},{80,112},{96,64},{112,80},{1... | collective-permute-start | bytes 49160 | tf_op jit(solution)/shard_map/ppermute | solution.py:443
  36.5 1.9 %collective-permute-start.6 = (f32[4,224,128]{2,1,0:T(8,128)S(1)}, f32[4,224,128]{2,1,0:T(8,128)S(1)}, u32[]{:S(2)}, u32[]{:S(2)}) collective-permute-start(f32[4,224,128]{2,1,0:T(8,128)S(1)} %get-tuple-element.32), channel_id=1, source_target_pairs={{0,1},{1,0},{2,3},{3,2},{4,5},{5,4},{6,7},{7,6},{8,9},{9,8},{10,11... | collective-permute-start | bytes 1376264 | tf_op jit(solution)/shard_map/ppermute | solution.py:436
  36.6 10.1 %collective-permute-start.7 = (f32[4,224,128]{2,1,0:T(8,128)S(1)}, f32[4,224,128]{2,1,0:T(8,128)S(1)}, u32[]{:S(2)}, u32[]{:S(2)}) collective-permute-start(f32[4,224,128]{2,1,0:T(8,128)S(1)} %get-tuple-element.33), channel_id=1, source_target_pairs={{0,15},{1,2},{2,1},{3,4},{4,3},{5,6},{6,5},{7,8},{8,7},{9,10},{10,... | collective-permute-start | bytes 1376264 | tf_op jit(solution)/shard_map/ppermute | solution.py:436

commit v14 on v13

--- a/solution.py
+++ b/solution.py
@@ -320,7 +320,7 @@
     every_window(bound, blocks, cells, visit, visit_again)
 
 
-def ready_kernel(dims, key, frac, bound, chosen, spread_out):
+def ready_kernel(dims, key, frac, perturb, bound, chosen, spread_out, strips, wide):
     members, nvars, levels, rows, cells, blocks = dims
     shift = cells.bit_length() - 1
     for block in range(blocks):
@@ -328,11 +328,17 @@
         keys = block_of(key, block)
         chosen[block] = chosen_rows(keys, start, shift)
         spread_out[block] = weights_of(keys, block_of(frac, block), cells)
-
-
-def scatter_kernel(dims, chosen, spread_out, key, frac, weight, perturb, scale, *refs):
-    members, nvars, levels, rows, cells, blocks = dims
-    *seen, bound, source, side_a, side_b, gradient, valued = refs
+    for m in range(members):
+        for v in range(nvars):
+            wide[m, v] = perturb[m, v].astype(jnp.float32)
+            for number, begin in enumerate(begins(rows)):
+                for j in range(SWEEPS):
+                    strips[m, v, number * SWEEPS + j] = wide[m, v, pl.ds(begin + j, levels, stride=rows), :]
+
+
+def scatter_kernel(dims, chosen, spread_out, strips, key, frac, weight, scale, *refs):
+    members, nvars, levels, rows, cells, blocks = dims
+    *seen, bound, side_a, side_b, gradient, valued = refs
     shift = cells.bit_length() - 1
     total = seen[0][...]
     for part in seen[1:]:
@@ -361,27 +367,29 @@
     every_window(bound, blocks, cells, add_first, add_further)
 
     plane = levels * rows
+    for number, (begin, side) in enumerate(zip(begins(rows), (side_a, side_b))):
+        for j in range(SWEEPS):
+            near = [gradient[pl.ds(v * plane + begin + j, levels, stride=rows), :] for v in range(nvars)]
+            for m in range(members):
+                total = strips[m, 0, number * SWEEPS + j] * near[0]
+                for v in range(1, nvars):
+                    total = total + strips[m, v, number * SWEEPS + j] * near[v]
+                side[j, pl.ds(m * levels, levels), :] = total
+            for v in range(nvars):
+                field = members + v
+                side[j, pl.ds(field * levels, levels), :] = near[v] * scale[field]
+
+
+def local_kernel(dims, powers, gradient, scale, side_a, perturb, ens, stat, group, localize, static, out, held, source, sems):
+    members, nvars, levels, rows, cells, blocks = dims
+    inside = neighbours()
+    plane = levels * rows
+    start_loads(members, nvars, ens, stat, held, sems)
     for m in range(members):
         total = perturb[m, 0].astype(jnp.float32) * gradient[:plane, :]
         for v in range(1, nvars):
             total = total + perturb[m, v].astype(jnp.float32) * gradient[v * plane : (v + 1) * plane, :]
         source[m] = total
-    for begin, side in zip(begins(rows), (side_a, side_b)):
-        for field in range(members + nvars):
-            for j in range(SWEEPS):
-                if field < members:
-                    strip = source[field, pl.ds(begin + j, levels, stride=rows), :]
-                else:
-                    at = (field - members) * plane + begin + j
-                    strip = gradient[pl.ds(at, levels, stride=rows), :] * scale[field]
-                side[j, pl.ds(field * levels, levels), :] = strip
-
-
-def local_kernel(dims, powers, source, gradient, scale, side_a, ens, stat, group, localize, static, out, held, sems):
-    members, nvars, levels, rows, cells, blocks = dims
-    inside = neighbours()
-    plane = levels * rows
-    start_loads(members, nvars, ens, stat, held, sems)
 
     def of_field(field, planes):
         rate = rate_of(field, members, group, localize, static)
@@ -530,26 +538,28 @@
         ],
     )
     seen = summands(seen)
-    chosen, spread_out = call(
+    chosen, spread_out, strips = call(
         ready_kernel,
         dims,
-        [(blocks, BLOCK, BLOCK), (blocks, cells, BLOCK)],
-        [key, frac],
+        [(blocks, BLOCK, BLOCK), (blocks, cells, BLOCK), (members, nvars, 2 * SWEEPS, levels, cells)],
+        [key, frac, perturb],
         [],
         [key],
-        kinds=[jnp.bfloat16, jnp.float32],
-    )
-    source, side_a, side_b, gradient = call(
+        [pltpu.VMEM((members, nvars, plane, cells), jnp.float32)],
+        kinds=[jnp.bfloat16, jnp.float32, jnp.float32],
+    )
+    side_a, side_b, gradient = call(
         scatter_kernel,
         dims,
-        [(members, plane, cells), strip, strip, (table_rows, cells)],
-        [chosen, spread_out, key, frac, weight, perturb, scale] + seen,
+        [strip, strip, (table_rows, cells)],
+        [chosen, spread_out, strips, key, frac, weight, scale] + seen,
         [],
         [key],
         [pltpu.VMEM(key.shape, jnp.float32)],
     )
     side_a, side_b = exchange(side_a, side_b)
-    (own,) = call(local_kernel, dims, [whole], [powers, source, gradient, scale, side_a], [ens, stat], rates, [pltpu.VMEM(whole, jnp.float32)] + copying)
+    held_source = [pltpu.VMEM(whole, jnp.float32), pltpu.VMEM((members, plane, cells), jnp.float32)]
+    (own,) = call(local_kernel, dims, [whole], [powers, gradient, scale, side_a, perturb], [ens, stat], rates, held_source + copying)
     hv_ens, hv_stat = call(
         edge_kernel,
         dims,

time: 50.2 us -> 49.8 us (level)
  waiting for transfers between devices: 9.99 us -> 8.97 us
  Pallas kernels: 21.7 us -> 22.4 us
    ppermute x3, waiting for transfers between devices: 2.56 us -> 1.5 us  [summands(): lax.ppermute(value, 'grp', [(i, i ^ turn) for i in range(count)])]
    pallas_call x7, Pallas kernels: 21.7 us -> 22.4 us  [call(): pl.pallas_call(body, out_shape=tuple((jax.ShapeDtypeStruct(tuple(shape),...]
  transfers between devices with their start and end apart: 8 -> 8, of which waited for: 4 -> 4; matrix products, arithmetic and copies ran while one was open for 10% -> 10% of each run, Pallas kernels for 22% -> 25%
where the time goes in v14:
time: 49.8 us; the launch traced here: 48.9 us
  Pallas kernels  22.4 us (45%)
  starting transfers between devices  10.7 us (21%)
  waiting for transfers between devices  8.97 us (18%)
  other arithmetic  4.99 us (10%)
  between operations  1.7 us (3%)
    pallas_call x7, Pallas kernels, call(): pl.pallas_call(body, out_shape=tuple((jax.ShapeDtypeStruct(tuple(shape),...  22.4 us
    sort x1, other arithmetic, per_device(): lax.sort((key.reshape(-1), obs_frac, weight.reshape(-1)), num_keys=1, is_...  4.98 us
    ppermute x3, starting transfers between devices, summands(): lax.ppermute(value, 'grp', [(i, i ^ turn) for i in range(count)])  4.9 us
    ppermute x2, starting transfers between devices, exchange(): lax.ppermute(side_b, 'tile', pairs_b)  4.47 us
    ppermute x1, waiting for transfers between devices, summands(): lax.ppermute(value, 'grp', [(i, i ^ 1) for i in range(count)])  4.13 us
    ppermute x2, waiting for transfers between devices, exchange(): lax.ppermute(side_b, 'tile', pairs_b)  2.63 us
    ppermute x3, waiting for transfers between devices, summands(): lax.ppermute(value, 'grp', [(i, i ^ turn) for i in range(count)])  1.5 us
    ppermute x1, starting transfers between devices, summands(): lax.ppermute(value, 'grp', [(i, i ^ 1) for i in range(count)])  1.19 us
  transfers between devices with their start and end apart: 8, of which 4 were waited for; matrix products, arithmetic and copies ran while one was open for 10% of the time, Pallas kernels for 25%

profile of v14, /device:TPU:6, one launch (start us, length us, event | category | flops | bytes accessed | tf_op | source)
XLA Modules:
  0.0 48.9 jit_solution(12641130385799880179)
XLA Ops:
  0.6 0.0 copy-start.1
  0.6 0.0 copy-start.9
  0.7 0.0 copy-start.6
  0.7 0.0 copy-start.5
  0.7 0.0 copy-start.7
  0.7 0.0 copy-start.4
  0.7 0.0 copy-start.2
  0.7 0.0 copy-start.3
  0.7 1.6 %pack_kernel.1 = (f32[4,224,128]{2,1,0:T(8,128)S(1)}, f32[4,224,128]{2,1,0:T(8,128)S(1)}, f32[7,512,128]{2,1,0:T(8,128)S(1)}) custom-call(f32[2,512,128]{2,1,0:T(8,128)} %bitcast.36, f32[5,512,128]{2,1,0:T(8,128)} %bitcast.34), custom_call_target="tpu_custom_call" | custom-call | flops 20000000 | bytes 2000000 | tf_op jit(solution)/shard_map/pack_kernel/pallas_call | solution.py:464
  2.4 0.0 copy-start.8
  2.4 0.1 collective-permute-start
  2.5 3.4 %collective-permute-start.1 = (f32[4,224,128]{2,1,0:T(8,128)S(1)}, f32[4,224,128]{2,1,0:T(8,128)S(1)}, u32[]{:S(2)}, u32[]{:S(2)}) collective-permute-start(f32[4,224,128]{2,1,0:T(8,128)S(1)} %get-tuple-element.30), channel_id=1, source_target_pairs={{0,15},{1,2},{2,1},{3,4},{4,3},{5,6},{6,5},{7,8},{8,7},{9,10},{10,... | collective-permute-start | bytes 1376264 | tf_op jit(solution)/shard_map/ppermute | solution.py:444
  6.5 0.0 copy-done.9
  6.5 0.0 collective-permute-done.refs_3_
  6.5 0.1 broadcast_in_dim.2.refs_2_.refs_1_.refs_6_
  6.6 0.0 copy-done.1
  6.6 0.0 copy-done.6
  6.7 0.0 copy-done.5
  6.7 0.0 copy-done.7
  6.7 0.0 copy-done.4
  6.7 0.0 copy-done.2
  6.7 0.0 copy-done.3
  6.7 4.0 %own_kernel.1 = (f32[7,512,128]{2,1,0:T(8,128)S(1)}, s32[32,128]{1,0:T(8,128)S(1)}, f32[32,128]{1,0:T(8,128)S(1)}) custom-call(bf16[256,512]{1,0:T(8,128)(2,1)S(1)} %copy-done.1, f32[7,512,128]{2,1,0:T(8,128)S(1)} %get-tuple-element.19.refs_1_, f32[7,32,128]{2,1,0:T(8,128)S(1)} %broadcast_in_dim.2.refs_2_.refs_1_.refs_6_, ...), custom_call_target="tpu_custom_call" | custom-call | flops 20000000 | bytes 2000000 | tf_op jit(solution)/shard_map/own_kernel/pallas_call | solution.py:464
  10.7 0.0 copy-done.8
  10.7 5.0 %sort.21 = (s32[4096]{0:T(1024)S(1)}, f32[4096]{0:T(1024)S(1)}, f32[4096]{0:T(1024)S(1)}) sort(s32[4096]{0:T(1024)S(1)} %bitcast.32, f32[4096]{0:T(1024)S(1)} %copy-done.8, f32[4096]{0:T(1024)S(1)} %bitcast.33), dimensions={0}, to_apply=%region_0.0 | sort | flops 49152 | bytes 98304 | tf_op jit(solution)/shard_map/sort | solution.py:522
  15.7 0.0 collective-permute-done.1.refs_2_
  15.7 0.0 copy-start
  15.7 4.1 %forward_kernel.1 = f32[32,128]{1,0:T(8,128)S(1)} custom-call(f32[7,512,128]{2,1,0:T(8,128)S(1)} %get-tuple-element.29.refs_0_, f32[7,32,128]{2,1,0:T(8,128)S(1)} %broadcast_in_dim.2.refs_2_.refs_1_.refs_6_, f32[4,224,128]{2,1,0:T(8,128)S(1)} %collective-permute-done.1.refs_2_, s32[32,128]{1,0:T(8,128)S(1)} %bitcast.19, f32[32,128]{1,0:T(8,128)S(1)} %bitcast.25, ...), custom_call_target="tpu_custom_call" | custom-call | flops 20000000 | bytes 2000000 | tf_op jit(solution)/shard_map/forward_kernel/pallas_call | solution.py:464
  19.8 1.2 %collective-permute-start.2 = (f32[32,128]{1,0:T(8,128)S(1)}, f32[32,128]{1,0:T(8,128)S(1)}, u32[]{:S(2)}, u32[]{:S(2)}) collective-permute-start(f32[32,128]{1,0:T(8,128)S(1)} %forward_kernel.1), channel_id=1, source_target_pairs={{0,16},{16,0},{32,48},{48,32},{64,80},{80,64},{96,112},{112,96},{1... | collective-permute-start | bytes 49160 | tf_op jit(solution)/shard_map/ppermute | solution.py:449
  21.0 4.1 %collective-permute-done.2 = f32[32,128]{1,0:T(8,128)S(1)} collective-permute-done((f32[32,128]{1,0:T(8,128)S(1)}, f32[32,128]{1,0:T(8,128)S(1)}, u32[]{:S(2)}, u32[]{:S(2)}) %collective-permute-start.2) | collective-permute-done | bytes 16416 | tf_op jit(solution)/shard_map/ppermute | solution.py:449
  25.1 3.9 %collective-permute-start.5 = (f32[32,128]{1,0:T(8,128)S(1)}, f32[32,128]{1,0:T(8,128)S(1)}, u32[]{:S(2)}, u32[]{:S(2)}) collective-permute-start(f32[32,128]{1,0:T(8,128)S(1)} %add.5.refs_7_), channel_id=1, source_target_pairs={{0,64},{16,80},{32,96},{48,112},{64,0},{80,16},{96,32},{112,48},{1... | collective-permute-start | bytes 49160 | tf_op jit(solution)/shard_map/ppermute | solution.py:451
  29.0 0.7 %collective-permute-start.4 = (f32[32,128]{1,0:T(8,128)S(1)}, f32[32,128]{1,0:T(8,128)S(1)}, u32[]{:S(2)}, u32[]{:S(2)}) collective-permute-start(f32[32,128]{1,0:T(8,128)S(1)} %add.5.refs_7_), channel_id=1, source_target_pairs={{0,96},{16,112},{32,64},{48,80},{64,32},{80,48},{96,0},{112,16},{1... | collective-permute-start | bytes 49160 | tf_op jit(solution)/shard_map/ppermute | solution.py:451
  29.7 0.3 collective-permute-start.3
  30.0 0.0 copy-done
  30.0 2.4 %ready_kernel.1 = (bf16[16,256,256]{2,1,0:T(8,128)(2,1)S(1)}, f32[16,128,256]{2,1,0:T(8,128)S(1)}, f32[2,5,8,32,128]{4,3,2,1,0:T(8,128)S(1)}) custom-call(s32[32,128]{1,0:T(8,128)S(1)} %bitcast.21, f32[32,128]{1,0:T(8,128)S(1)} %bitcast.26, bf16[2,5,512,128]{3,2,1,0:T(8,128)(2,1)S(1)} %bitcast.17, s32[32,128]{1,0:T(8,128)S(1)} %bitcast.22), custom_call_target="tpu_custom_call" | custom-call | flops 20000000 | bytes 2000000 | tf_op jit(solution)/shard_map/ready_kernel/pallas_call | solution.py:464
  32.5 0.0 collective-permute-done.5.refs_10_
  32.5 1.5 %collective-permute-done.4.refs_9_ = f32[32,128]{1,0:T(8,128)S(1)} collective-permute-done((f32[32,128]{1,0:T(8,128)S(1)}, f32[32,128]{1,0:T(8,128)S(1)}, u32[]{:S(2)}, u32[]{:S(2)}) %collective-permute-start.4) | collective-permute-done | bytes 16416 | tf_op jit(solution)/shard_map/ppermute | solution.py:451
  34.0 0.0 collective-permute-done.3.refs_8_
  34.0 2.2 %scatter_kernel.1 = (f32[4,224,128]{2,1,0:T(8,128)S(1)}, f32[4,224,128]{2,1,0:T(8,128)S(1)}, f32[2816,128]{1,0:T(8,128)S(1)}) custom-call(bf16[16,256,256]{2,1,0:T(8,128)(2,1)S(1)} %get-tuple-element.25.refs_0_, f32[16,128,256]{2,1,0:T(8,128)S(1)} %get-tuple-element.26.refs_1_, f32[2,5,8,32,128]{4,3,2,1,0:T(8,128)S(1)} %get-tuple-element.27.refs_2_, ...), custom_call_target="tpu_custom_call" | custom-call | flops 20000000 | bytes 2000000 | tf_op jit(solution)/shard_map/scatter_kernel/pallas_call | solution.py:464
  36.1 0.1 collective-permute-start.6
  36.2 1.1 %collective-permute-start.7 = (f32[4,224,128]{2,1,0:T(8,128)S(1)}, f32[4,224,128]{2,1,0:T(8,128)S(1)}, u32[]{:S(2)}, u32[]{:S(2)}) collective-permute-start(f32[4,224,128]{2,1,0:T(8,128)S(1)} %get-tuple-element.33), channel_id=1, source_target_pairs={{0,15},{1,2},{2,1},{3,4},{4,3},{5,6},{6,5},{7,8},{8,7},{9,10},{10,... | collective-permute-start | bytes 1376264 | tf_op jit(solution)/shard_map/ppermute | solution.py:444
  37.3 0.7 %collective-permute-done.6.refs_3_ = f32[4,224,128]{2,1,0:T(8,128)S(1)} collective-permute-done((f32[4,224,128]{2,1,0:T(8,128)S(1)}, f32[4,224,128]{2,1,0:T(8,128)S(1)}, u32[]{:S(2)}, u32[]{:S(2)}) %collective-permute-start.6) | collective-permute-done | bytes 458784 | tf_op jit(solution)/shard_map/ppermute | solution.py:444
  38.0 5.7 %local_kernel.1.refs_0_ = f32[7,512,128]{2,1,0:T(8,128)S(1)} custom-call(bf16[256,512]{1,0:T(8,128)(2,1)S(1)} %copy-done.1, f32[2816,128]{1,0:T(8,128)S(1)} %get-tuple-element.31.refs_1_, f32[7,32,128]{2,1,0:T(8,128)S(1)} %broadcast_in_dim.2.refs_2_.refs_1_.refs_6_, f32[4,224,128]{2,1,0:T(8,128)S(1)} %collective-permute-done.6.refs_3_, ...), custom_call_target="tpu_custom_call" | custom-call | flops 20000000 | bytes 2000000 | tf_op jit(solution)/shard_map/local_kernel/pallas_call | solution.py:464
  43.7 2.6 %collective-permute-done.7.refs_1_ = f32[4,224,128]{2,1,0:T(8,128)S(1)} collective-permute-done((f32[4,224,128]{2,1,0:T(8,128)S(1)}, f32[4,224,128]{2,1,0:T(8,128)S(1)}, u32[]{:S(2)}, u32[]{:S(2)}) %collective-permute-start.7) | collective-permute-done | bytes 458784 | tf_op jit(solution)/shard_map/ppermute | solution.py:444
  46.3 2.4 %edge_kernel.1 = (f32[2,512,128]{2,1,0:T(8,128)}, f32[5,512,128]{2,1,0:T(8,128)}) custom-call(f32[7,512,128]{2,1,0:T(8,128)S(1)} %local_kernel.1.refs_0_, f32[4,224,128]{2,1,0:T(8,128)S(1)} %collective-permute-done.7.refs_1_, s32[2]{0:T(128)S(1)} %copy-done.5, f32[12]{0:T(128)S(1)} %copy-done.6, f32[1]{0:T(128)S(6)} %copy.18.refs_9_.refs_4_), custom_call_target="tpu_custom_call" | custom-call | flops 20000000 | bytes 2000000 | tf_op jit(solution)/shard_map/edge_kernel/pallas_call | solution.py:464
  (3 shorter events, 0.0 us)
Async XLA Ops:
  0.6 6.0 %copy-start.1 = (bf16[256,512]{1,0:T(8,128)(2,1)S(1)}, bf16[256,512]{1,0:T(8,128)(2,1)}, u32[]{:S(2)}) copy-start(bf16[256,512]{1,0:T(8,128)(2,1)} %constant.4.clone.refs_0_) | copy-start | bytes 786436
  0.6 5.9 %copy-start.9 = (f32[1,5,32]{2,0,1:T(1,128)S(1)}, f32[1,5,32]{2,0,1:T(1,128)}, u32[]{:S(2)}) copy-start(f32[1,5,32]{2,0,1:T(1,128)} %param.19) | copy-start | bytes 1924
  0.7 6.0 %copy-start.6 = (f32[12]{0:T(128)S(1)}, f32[12]{0:T(128)}, u32[]{:S(2)}) copy-start(f32[12]{0:T(128)} %refs_3_.1) | copy-start | bytes 148
  0.7 6.0 %copy-start.5 = (s32[2]{0:T(128)S(1)}, s32[2]{0:T(128)}, u32[]{:S(2)}) copy-start(s32[2]{0:T(128)} %refs_2_.1) | copy-start | bytes 28
  0.7 6.0 %copy-start.7 = (f32[8]{0:T(128)S(1)}, f32[8]{0:T(128)}, u32[]{:S(2)}) copy-start(f32[8]{0:T(128)} %refs_10_.1) | copy-start | bytes 100
  0.7 6.0 %copy-start.4 = (s32[4096]{0:T(1024)S(1)}, s32[4096]{0:T(1024)}, u32[]{:S(2)}) copy-start(s32[4096]{0:T(1024)} %param.23) | copy-start | bytes 49156
  0.7 6.0 %copy-start.2 = (s32[4096]{0:T(1024)S(1)}, s32[4096]{0:T(1024)}, u32[]{:S(2)}) copy-start(s32[4096]{0:T(1024)} %param.22) | copy-start | bytes 49156
  0.7 6.0 %copy-start.3 = (s32[4096]{0:T(1024)S(1)}, s32[4096]{0:T(1024)}, u32[]{:S(2)}) copy-start(s32[4096]{0:T(1024)} %param.20) | copy-start | bytes 49156
  2.4 8.3 %copy-start.8 = (f32[4096]{0:T(1024)S(1)}, f32[4096]{0:T(1024)}, u32[]{:S(2)}) copy-start(f32[4096]{0:T(1024)} %param.21) | copy-start | bytes 49156
  2.4 4.2 %collective-permute-start = (f32[4,224,128]{2,1,0:T(8,128)S(1)}, f32[4,224,128]{2,1,0:T(8,128)S(1)}, u32[]{:S(2)}, u32[]{:S(2)}) collective-permute-start(f32[4,224,128]{2,1,0:T(8,128)S(1)} %get-tuple-element.20), channel_id=1, source_target_pairs={{0,1},{1,0},{2,3},{3,2},{4,5},{5,4},{6,7},{7,6},{8,9},{9,8},{10,11... | collective-permute-start | bytes 1376264 | tf_op jit(solution)/shard_map/ppermute | solution.py:444
  2.5 13.2 %collective-permute-start.1 = (f32[4,224,128]{2,1,0:T(8,128)S(1)}, f32[4,224,128]{2,1,0:T(8,128)S(1)}, u32[]{:S(2)}, u32[]{:S(2)}) collective-permute-start(f32[4,224,128]{2,1,0:T(8,128)S(1)} %get-tuple-element.30), channel_id=1, source_target_pairs={{0,15},{1,2},{2,1},{3,4},{4,3},{5,6},{6,5},{7,8},{8,7},{9,10},{10,... | collective-permute-start | bytes 1376264 | tf_op jit(solution)/shard_map/ppermute | solution.py:444
  15.7 14.4 %copy-start = (bf16[2,5,32,16,128]{4,3,2,1,0:T(8,128)(2,1)S(1)}, bf16[2,5,32,16,128]{4,3,2,1,0:T(8,128)(2,1)}, u32[]{:S(2)}) copy-start(bf16[2,5,32,16,128]{4,3,2,1,0:T(8,128)(2,1)} %param.15) | copy-start | bytes 3932164
  19.8 5.3 %collective-permute-start.2 = (f32[32,128]{1,0:T(8,128)S(1)}, f32[32,128]{1,0:T(8,128)S(1)}, u32[]{:S(2)}, u32[]{:S(2)}) collective-permute-start(f32[32,128]{1,0:T(8,128)S(1)} %forward_kernel.1), channel_id=1, source_target_pairs={{0,16},{16,0},{32,48},{48,32},{64,80},{80,64},{96,112},{112,96},{1... | collective-permute-start | bytes 49160 | tf_op jit(solution)/shard_map/ppermute | solution.py:449
  25.1 7.3 %collective-permute-start.5 = (f32[32,128]{1,0:T(8,128)S(1)}, f32[32,128]{1,0:T(8,128)S(1)}, u32[]{:S(2)}, u32[]{:S(2)}) collective-permute-start(f32[32,128]{1,0:T(8,128)S(1)} %add.5.refs_7_), channel_id=1, source_target_pairs={{0,64},{16,80},{32,96},{48,112},{64,0},{80,16},{96,32},{112,48},{1... | collective-permute-start | bytes 49160 | tf_op jit(solution)/shard_map/ppermute | solution.py:451
  29.0 4.9 %collective-permute-start.4 = (f32[32,128]{1,0:T(8,128)S(1)}, f32[32,128]{1,0:T(8,128)S(1)}, u32[]{:S(2)}, u32[]{:S(2)}) collective-permute-start(f32[32,128]{1,0:T(8,128)S(1)} %add.5.refs_7_), channel_id=1, source_target_pairs={{0,96},{16,112},{32,64},{48,80},{64,32},{80,48},{96,0},{112,16},{1... | collective-permute-start | bytes 49160 | tf_op jit(solution)/shard_map/ppermute | solution.py:451
  29.7 4.2 %collective-permute-start.3 = (f32[32,128]{1,0:T(8,128)S(1)}, f32[32,128]{1,0:T(8,128)S(1)}, u32[]{:S(2)}, u32[]{:S(2)}) collective-permute-start(f32[32,128]{1,0:T(8,128)S(1)} %add.5.refs_7_), channel_id=1, source_target_pairs={{0,32},{16,48},{32,0},{48,16},{64,96},{80,112},{96,64},{112,80},{1... | collective-permute-start | bytes 49160 | tf_op jit(solution)/shard_map/ppermute | solution.py:451
  36.1 1.9 %collective-permute-start.6 = (f32[4,224,128]{2,1,0:T(8,128)S(1)}, f32[4,224,128]{2,1,0:T(8,128)S(1)}, u32[]{:S(2)}, u32[]{:S(2)}) collective-permute-start(f32[4,224,128]{2,1,0:T(8,128)S(1)} %get-tuple-element.32), channel_id=1, source_target_pairs={{0,1},{1,0},{2,3},{3,2},{4,5},{5,4},{6,7},{7,6},{8,9},{9,8},{10,11... | collective-permute-start | bytes 1376264 | tf_op jit(solution)/shard_map/ppermute | solution.py:444
  36.2 10.1 %collective-permute-start.7 = (f32[4,224,128]{2,1,0:T(8,128)S(1)}, f32[4,224,128]{2,1,0:T(8,128)S(1)}, u32[]{:S(2)}, u32[]{:S(2)}) collective-permute-start(f32[4,224,128]{2,1,0:T(8,128)S(1)} %get-tuple-element.33), channel_id=1, source_target_pairs={{0,15},{1,2},{2,1},{3,4},{4,3},{5,6},{6,5},{7,8},{8,7},{9,10},{10,... | collective-permute-start | bytes 1376264 | tf_op jit(solution)/shard_map/ppermute | solution.py:444

commit v15 on v14

--- a/solution.py
+++ b/solution.py
@@ -145,12 +145,12 @@
         planes = {}
         for away in range(1, SWEEPS + 1):
             j = jnp.where(upper, away - 1, SWEEPS - away)
-            planes[-away] = side[j, first * levels : (first + len(fields)) * levels, :]
+            plane = side[j, first * levels : (first + len(fields)) * levels, :]
+            planes[-away] = plane if counts is None else plane * counts
         parts = spread_rolled(planes, 0, SWEEPS - 1, rows, rate, None)
         for at, field in enumerate(fields):
             for depth in range(SWEEPS):
-                part = parts[depth][at * levels : (at + 1) * levels]
-                visit(field, depth, part if counts is None else part * counts)
+                visit(field, depth, parts[depth][at * levels : (at + 1) * levels])
 
 
 def adder(into, upper, shape, scale=None):
@@ -166,12 +166,6 @@
 def add_near(into, side, rates, shape, scale=None):
     upper = is_even()
     add_side(side, upper, rates, shape, adder(into, upper, shape, scale))
-
-
-def add_far(into, side, rates, shape, scale=None):
-    upper = jnp.logical_not(is_even())
-    below, above = neighbours()
-    add_side(side, upper, rates, shape, adder(into, upper, shape, scale), below * above)
 
 
 def block_of(ref, block):
@@ -279,9 +273,17 @@
     for load in loads:
         load.start()
 
-    smooth[...] = own[...]
     rates = rates_of(members + nvars, members, group, localize, static)
-    add_far(smooth, side_b, rates, (levels, rows, cells), scale)
+    upper = jnp.logical_not(is_even())
+    add = adder(smooth, upper, (levels, rows, cells), scale)
+    below, above = neighbours()
+
+    def far_part(field, depth, part):
+        if depth == 0:
+            smooth[field] = own[field]
+        add(field, depth, part)
+
+    add_side(side_b, upper, rates, (levels, rows, cells), far_part, below * above)
     plane = levels * rows
     for v in range(nvars):
         total = smooth[members + v]

time: 49.8 us -> 49.8 us (level)
  no operation moved by 1% of the time
where the time goes in v15:
time: 49.8 us; the launch traced here: 48.8 us
  Pallas kernels  22.3 us (45%)
  starting transfers between devices  10.8 us (22%)
  waiting for transfers between devices  8.91 us (18%)
  other arithmetic  4.99 us (10%)
  between operations  1.7 us (3%)
    pallas_call x7, Pallas kernels, call(): pl.pallas_call(body, out_shape=tuple((jax.ShapeDtypeStruct(tuple(shape),...  22.3 us
    sort x1, other arithmetic, per_device(): lax.sort((key.reshape(-1), obs_frac, weight.reshape(-1)), num_keys=1, is_...  4.98 us
    ppermute x3, starting transfers between devices, summands(): lax.ppermute(value, 'grp', [(i, i ^ turn) for i in range(count)])  4.9 us
    ppermute x2, starting transfers between devices, exchange(): lax.ppermute(side_b, 'tile', pairs_b)  4.54 us
    ppermute x1, waiting for transfers between devices, summands(): lax.ppermute(value, 'grp', [(i, i ^ 1) for i in range(count)])  4.13 us
    ppermute x2, waiting for transfers between devices, exchange(): lax.ppermute(side_b, 'tile', pairs_b)  2.63 us
    ppermute x3, waiting for transfers between devices, summands(): lax.ppermute(value, 'grp', [(i, i ^ turn) for i in range(count)])  1.5 us
    ppermute x1, starting transfers between devices, summands(): lax.ppermute(value, 'grp', [(i, i ^ 1) for i in range(count)])  1.19 us
  transfers between devices with their start and end apart: 8, of which 4 were waited for; matrix products, arithmetic and copies ran while one was open for 10% of the time, Pallas kernels for 25%

profile of v15, /device:TPU:6, one launch (start us, length us, event | category | flops | bytes accessed | tf_op | source)
XLA Modules:
  0.0 48.8 jit_solution(3926905967636640517)
XLA Ops:
  0.6 0.0 copy-start.1
  0.6 0.0 copy-start.9
  0.7 0.0 copy-start.6
  0.7 0.0 copy-start.5
  0.7 0.0 copy-start.7
  0.7 0.0 copy-start.4
  0.7 0.0 copy-start.2
  0.7 0.0 copy-start.3
  0.7 1.6 %pack_kernel.1 = (f32[4,224,128]{2,1,0:T(8,128)S(1)}, f32[4,224,128]{2,1,0:T(8,128)S(1)}, f32[7,512,128]{2,1,0:T(8,128)S(1)}) custom-call(f32[2,512,128]{2,1,0:T(8,128)} %bitcast.36, f32[5,512,128]{2,1,0:T(8,128)} %bitcast.34), custom_call_target="tpu_custom_call" | custom-call | flops 20000000 | bytes 2000000 | tf_op jit(solution)/shard_map/pack_kernel/pallas_call | solution.py:466
  2.4 0.0 copy-start.8
  2.4 0.1 collective-permute-start
  2.5 3.4 %collective-permute-start.1 = (f32[4,224,128]{2,1,0:T(8,128)S(1)}, f32[4,224,128]{2,1,0:T(8,128)S(1)}, u32[]{:S(2)}, u32[]{:S(2)}) collective-permute-start(f32[4,224,128]{2,1,0:T(8,128)S(1)} %get-tuple-element.30), channel_id=1, source_target_pairs={{0,15},{1,2},{2,1},{3,4},{4,3},{5,6},{6,5},{7,8},{8,7},{9,10},{10,... | collective-permute-start | bytes 1376264 | tf_op jit(solution)/shard_map/ppermute | solution.py:446
  6.5 0.0 copy-done.9
  6.5 0.0 collective-permute-done.refs_3_
  6.5 0.1 broadcast_in_dim.2.refs_2_.refs_1_.refs_6_
  6.6 0.0 copy-done.1
  6.6 0.0 copy-done.6
  6.7 0.0 copy-done.5
  6.7 0.0 copy-done.7
  6.7 0.0 copy-done.4
  6.7 0.0 copy-done.2
  6.7 0.0 copy-done.3
  6.7 4.0 %own_kernel.1 = (f32[7,512,128]{2,1,0:T(8,128)S(1)}, s32[32,128]{1,0:T(8,128)S(1)}, f32[32,128]{1,0:T(8,128)S(1)}) custom-call(bf16[256,512]{1,0:T(8,128)(2,1)S(1)} %copy-done.1, f32[7,512,128]{2,1,0:T(8,128)S(1)} %get-tuple-element.19.refs_1_, f32[7,32,128]{2,1,0:T(8,128)S(1)} %broadcast_in_dim.2.refs_2_.refs_1_.refs_6_, ...), custom_call_target="tpu_custom_call" | custom-call | flops 20000000 | bytes 2000000 | tf_op jit(solution)/shard_map/own_kernel/pallas_call | solution.py:466
  10.7 0.0 copy-done.8
  10.7 5.0 %sort.21 = (s32[4096]{0:T(1024)S(1)}, f32[4096]{0:T(1024)S(1)}, f32[4096]{0:T(1024)S(1)}) sort(s32[4096]{0:T(1024)S(1)} %bitcast.32, f32[4096]{0:T(1024)S(1)} %copy-done.8, f32[4096]{0:T(1024)S(1)} %bitcast.33), dimensions={0}, to_apply=%region_0.0 | sort | flops 49152 | bytes 98304 | tf_op jit(solution)/shard_map/sort | solution.py:524
  15.7 0.0 collective-permute-done.1.refs_2_
  15.7 0.0 copy-start
  15.7 4.0 %forward_kernel.1 = f32[32,128]{1,0:T(8,128)S(1)} custom-call(f32[7,512,128]{2,1,0:T(8,128)S(1)} %get-tuple-element.29.refs_0_, f32[7,32,128]{2,1,0:T(8,128)S(1)} %broadcast_in_dim.2.refs_2_.refs_1_.refs_6_, f32[4,224,128]{2,1,0:T(8,128)S(1)} %collective-permute-done.1.refs_2_, s32[32,128]{1,0:T(8,128)S(1)} %bitcast.19, f32[32,128]{1,0:T(8,128)S(1)} %bitcast.25, ...), custom_call_target="tpu_custom_call" | custom-call | flops 20000000 | bytes 2000000 | tf_op jit(solution)/shard_map/forward_kernel/pallas_call | solution.py:466
  19.7 1.2 %collective-permute-start.2 = (f32[32,128]{1,0:T(8,128)S(1)}, f32[32,128]{1,0:T(8,128)S(1)}, u32[]{:S(2)}, u32[]{:S(2)}) collective-permute-start(f32[32,128]{1,0:T(8,128)S(1)} %forward_kernel.1), channel_id=1, source_target_pairs={{0,16},{16,0},{32,48},{48,32},{64,80},{80,64},{96,112},{112,96},{1... | collective-permute-start | bytes 49160 | tf_op jit(solution)/shard_map/ppermute | solution.py:451
  20.9 4.1 %collective-permute-done.2 = f32[32,128]{1,0:T(8,128)S(1)} collective-permute-done((f32[32,128]{1,0:T(8,128)S(1)}, f32[32,128]{1,0:T(8,128)S(1)}, u32[]{:S(2)}, u32[]{:S(2)}) %collective-permute-start.2) | collective-permute-done | bytes 16416 | tf_op jit(solution)/shard_map/ppermute | solution.py:451
  25.1 3.9 %collective-permute-start.5 = (f32[32,128]{1,0:T(8,128)S(1)}, f32[32,128]{1,0:T(8,128)S(1)}, u32[]{:S(2)}, u32[]{:S(2)}) collective-permute-start(f32[32,128]{1,0:T(8,128)S(1)} %add.5.refs_7_), channel_id=1, source_target_pairs={{0,64},{16,80},{32,96},{48,112},{64,0},{80,16},{96,32},{112,48},{1... | collective-permute-start | bytes 49160 | tf_op jit(solution)/shard_map/ppermute | solution.py:453
  28.9 0.7 %collective-permute-start.4 = (f32[32,128]{1,0:T(8,128)S(1)}, f32[32,128]{1,0:T(8,128)S(1)}, u32[]{:S(2)}, u32[]{:S(2)}) collective-permute-start(f32[32,128]{1,0:T(8,128)S(1)} %add.5.refs_7_), channel_id=1, source_target_pairs={{0,96},{16,112},{32,64},{48,80},{64,32},{80,48},{96,0},{112,16},{1... | collective-permute-start | bytes 49160 | tf_op jit(solution)/shard_map/ppermute | solution.py:453
  29.7 0.3 collective-permute-start.3
  30.0 0.0 copy-done
  30.0 2.4 %ready_kernel.1 = (bf16[16,256,256]{2,1,0:T(8,128)(2,1)S(1)}, f32[16,128,256]{2,1,0:T(8,128)S(1)}, f32[2,5,8,32,128]{4,3,2,1,0:T(8,128)S(1)}) custom-call(s32[32,128]{1,0:T(8,128)S(1)} %bitcast.21, f32[32,128]{1,0:T(8,128)S(1)} %bitcast.26, bf16[2,5,512,128]{3,2,1,0:T(8,128)(2,1)S(1)} %bitcast.17, s32[32,128]{1,0:T(8,128)S(1)} %bitcast.22), custom_call_target="tpu_custom_call" | custom-call | flops 20000000 | bytes 2000000 | tf_op jit(solution)/shard_map/ready_kernel/pallas_call | solution.py:466
  32.4 0.0 collective-permute-done.5.refs_10_
  32.4 1.5 %collective-permute-done.4.refs_9_ = f32[32,128]{1,0:T(8,128)S(1)} collective-permute-done((f32[32,128]{1,0:T(8,128)S(1)}, f32[32,128]{1,0:T(8,128)S(1)}, u32[]{:S(2)}, u32[]{:S(2)}) %collective-permute-start.4) | collective-permute-done | bytes 16416 | tf_op jit(solution)/shard_map/ppermute | solution.py:453
  33.9 0.0 collective-permute-done.3.refs_8_
  33.9 2.2 %scatter_kernel.1 = (f32[4,224,128]{2,1,0:T(8,128)S(1)}, f32[4,224,128]{2,1,0:T(8,128)S(1)}, f32[2816,128]{1,0:T(8,128)S(1)}) custom-call(bf16[16,256,256]{2,1,0:T(8,128)(2,1)S(1)} %get-tuple-element.25.refs_0_, f32[16,128,256]{2,1,0:T(8,128)S(1)} %get-tuple-element.26.refs_1_, f32[2,5,8,32,128]{4,3,2,1,0:T(8,128)S(1)} %get-tuple-element.27.refs_2_, ...), custom_call_target="tpu_custom_call" | custom-call | flops 20000000 | bytes 2000000 | tf_op jit(solution)/shard_map/scatter_kernel/pallas_call | solution.py:466
  36.1 0.1 collective-permute-start.6
  36.2 1.2 %collective-permute-start.7 = (f32[4,224,128]{2,1,0:T(8,128)S(1)}, f32[4,224,128]{2,1,0:T(8,128)S(1)}, u32[]{:S(2)}, u32[]{:S(2)}) collective-permute-start(f32[4,224,128]{2,1,0:T(8,128)S(1)} %get-tuple-element.33), channel_id=1, source_target_pairs={{0,15},{1,2},{2,1},{3,4},{4,3},{5,6},{6,5},{7,8},{8,7},{9,10},{10,... | collective-permute-start | bytes 1376264 | tf_op jit(solution)/shard_map/ppermute | solution.py:446
  37.3 0.6 %collective-permute-done.6.refs_3_ = f32[4,224,128]{2,1,0:T(8,128)S(1)} collective-permute-done((f32[4,224,128]{2,1,0:T(8,128)S(1)}, f32[4,224,128]{2,1,0:T(8,128)S(1)}, u32[]{:S(2)}, u32[]{:S(2)}) %collective-permute-start.6) | collective-permute-done | bytes 458784 | tf_op jit(solution)/shard_map/ppermute | solution.py:446
  38.0 5.7 %local_kernel.1.refs_0_ = f32[7,512,128]{2,1,0:T(8,128)S(1)} custom-call(bf16[256,512]{1,0:T(8,128)(2,1)S(1)} %copy-done.1, f32[2816,128]{1,0:T(8,128)S(1)} %get-tuple-element.31.refs_1_, f32[7,32,128]{2,1,0:T(8,128)S(1)} %broadcast_in_dim.2.refs_2_.refs_1_.refs_6_, f32[4,224,128]{2,1,0:T(8,128)S(1)} %collective-permute-done.6.refs_3_, ...), custom_call_target="tpu_custom_call" | custom-call | flops 20000000 | bytes 2000000 | tf_op jit(solution)/shard_map/local_kernel/pallas_call | solution.py:466
  43.6 2.6 %collective-permute-done.7.refs_1_ = f32[4,224,128]{2,1,0:T(8,128)S(1)} collective-permute-done((f32[4,224,128]{2,1,0:T(8,128)S(1)}, f32[4,224,128]{2,1,0:T(8,128)S(1)}, u32[]{:S(2)}, u32[]{:S(2)}) %collective-permute-start.7) | collective-permute-done | bytes 458784 | tf_op jit(solution)/shard_map/ppermute | solution.py:446
  46.3 2.4 %edge_kernel.1 = (f32[2,512,128]{2,1,0:T(8,128)}, f32[5,512,128]{2,1,0:T(8,128)}) custom-call(f32[7,512,128]{2,1,0:T(8,128)S(1)} %local_kernel.1.refs_0_, f32[4,224,128]{2,1,0:T(8,128)S(1)} %collective-permute-done.7.refs_1_, s32[2]{0:T(128)S(1)} %copy-done.5, f32[12]{0:T(128)S(1)} %copy-done.6, f32[1]{0:T(128)S(6)} %copy.18.refs_9_.refs_4_), custom_call_target="tpu_custom_call" | custom-call | flops 20000000 | bytes 2000000 | tf_op jit(solution)/shard_map/edge_kernel/pallas_call | solution.py:466
  (3 shorter events, 0.0 us)
Async XLA Ops:
  0.6 6.0 %copy-start.1 = (bf16[256,512]{1,0:T(8,128)(2,1)S(1)}, bf16[256,512]{1,0:T(8,128)(2,1)}, u32[]{:S(2)}) copy-start(bf16[256,512]{1,0:T(8,128)(2,1)} %constant.4.clone.refs_0_) | copy-start | bytes 786436
  0.6 5.9 %copy-start.9 = (f32[1,5,32]{2,0,1:T(1,128)S(1)}, f32[1,5,32]{2,0,1:T(1,128)}, u32[]{:S(2)}) copy-start(f32[1,5,32]{2,0,1:T(1,128)} %param.19) | copy-start | bytes 1924
  0.7 6.0 %copy-start.6 = (f32[12]{0:T(128)S(1)}, f32[12]{0:T(128)}, u32[]{:S(2)}) copy-start(f32[12]{0:T(128)} %refs_3_.1) | copy-start | bytes 148
  0.7 6.0 %copy-start.5 = (s32[2]{0:T(128)S(1)}, s32[2]{0:T(128)}, u32[]{:S(2)}) copy-start(s32[2]{0:T(128)} %refs_2_.1) | copy-start | bytes 28
  0.7 6.0 %copy-start.7 = (f32[8]{0:T(128)S(1)}, f32[8]{0:T(128)}, u32[]{:S(2)}) copy-start(f32[8]{0:T(128)} %refs_10_.1) | copy-start | bytes 100
  0.7 6.0 %copy-start.4 = (s32[4096]{0:T(1024)S(1)}, s32[4096]{0:T(1024)}, u32[]{:S(2)}) copy-start(s32[4096]{0:T(1024)} %param.23) | copy-start | bytes 49156
  0.7 6.0 %copy-start.2 = (s32[4096]{0:T(1024)S(1)}, s32[4096]{0:T(1024)}, u32[]{:S(2)}) copy-start(s32[4096]{0:T(1024)} %param.22) | copy-start | bytes 49156
  0.7 6.0 %copy-start.3 = (s32[4096]{0:T(1024)S(1)}, s32[4096]{0:T(1024)}, u32[]{:S(2)}) copy-start(s32[4096]{0:T(1024)} %param.20) | copy-start | bytes 49156
  2.4 8.3 %copy-start.8 = (f32[4096]{0:T(1024)S(1)}, f32[4096]{0:T(1024)}, u32[]{:S(2)}) copy-start(f32[4096]{0:T(1024)} %param.21) | copy-start | bytes 49156
  2.4 4.2 %collective-permute-start = (f32[4,224,128]{2,1,0:T(8,128)S(1)}, f32[4,224,128]{2,1,0:T(8,128)S(1)}, u32[]{:S(2)}, u32[]{:S(2)}) collective-permute-start(f32[4,224,128]{2,1,0:T(8,128)S(1)} %get-tuple-element.20), channel_id=1, source_target_pairs={{0,1},{1,0},{2,3},{3,2},{4,5},{5,4},{6,7},{7,6},{8,9},{9,8},{10,11... | collective-permute-start | bytes 1376264 | tf_op jit(solution)/shard_map/ppermute | solution.py:446
  2.5 13.2 %collective-permute-start.1 = (f32[4,224,128]{2,1,0:T(8,128)S(1)}, f32[4,224,128]{2,1,0:T(8,128)S(1)}, u32[]{:S(2)}, u32[]{:S(2)}) collective-permute-start(f32[4,224,128]{2,1,0:T(8,128)S(1)} %get-tuple-element.30), channel_id=1, source_target_pairs={{0,15},{1,2},{2,1},{3,4},{4,3},{5,6},{6,5},{7,8},{8,7},{9,10},{10,... | collective-permute-start | bytes 1376264 | tf_op jit(solution)/shard_map/ppermute | solution.py:446
  15.7 14.3 %copy-start = (bf16[2,5,32,16,128]{4,3,2,1,0:T(8,128)(2,1)S(1)}, bf16[2,5,32,16,128]{4,3,2,1,0:T(8,128)(2,1)}, u32[]{:S(2)}) copy-start(bf16[2,5,32,16,128]{4,3,2,1,0:T(8,128)(2,1)} %param.15) | copy-start | bytes 3932164
  19.7 5.3 %collective-permute-start.2 = (f32[32,128]{1,0:T(8,128)S(1)}, f32[32,128]{1,0:T(8,128)S(1)}, u32[]{:S(2)}, u32[]{:S(2)}) collective-permute-start(f32[32,128]{1,0:T(8,128)S(1)} %forward_kernel.1), channel_id=1, source_target_pairs={{0,16},{16,0},{32,48},{48,32},{64,80},{80,64},{96,112},{112,96},{1... | collective-permute-start | bytes 49160 | tf_op jit(solution)/shard_map/ppermute | solution.py:451
  25.1 7.3 %collective-permute-start.5 = (f32[32,128]{1,0:T(8,128)S(1)}, f32[32,128]{1,0:T(8,128)S(1)}, u32[]{:S(2)}, u32[]{:S(2)}) collective-permute-start(f32[32,128]{1,0:T(8,128)S(1)} %add.5.refs_7_), channel_id=1, source_target_pairs={{0,64},{16,80},{32,96},{48,112},{64,0},{80,16},{96,32},{112,48},{1... | collective-permute-start | bytes 49160 | tf_op jit(solution)/shard_map/ppermute | solution.py:453
  28.9 4.9 %collective-permute-start.4 = (f32[32,128]{1,0:T(8,128)S(1)}, f32[32,128]{1,0:T(8,128)S(1)}, u32[]{:S(2)}, u32[]{:S(2)}) collective-permute-start(f32[32,128]{1,0:T(8,128)S(1)} %add.5.refs_7_), channel_id=1, source_target_pairs={{0,96},{16,112},{32,64},{48,80},{64,32},{80,48},{96,0},{112,16},{1... | collective-permute-start | bytes 49160 | tf_op jit(solution)/shard_map/ppermute | solution.py:453
  29.7 4.2 %collective-permute-start.3 = (f32[32,128]{1,0:T(8,128)S(1)}, f32[32,128]{1,0:T(8,128)S(1)}, u32[]{:S(2)}, u32[]{:S(2)}) collective-permute-start(f32[32,128]{1,0:T(8,128)S(1)} %add.5.refs_7_), channel_id=1, source_target_pairs={{0,32},{16,48},{32,0},{48,16},{64,96},{80,112},{96,64},{112,80},{1... | collective-permute-start | bytes 49160 | tf_op jit(solution)/shard_map/ppermute | solution.py:453
  36.1 1.9 %collective-permute-start.6 = (f32[4,224,128]{2,1,0:T(8,128)S(1)}, f32[4,224,128]{2,1,0:T(8,128)S(1)}, u32[]{:S(2)}, u32[]{:S(2)}) collective-permute-start(f32[4,224,128]{2,1,0:T(8,128)S(1)} %get-tuple-element.32), channel_id=1, source_target_pairs={{0,1},{1,0},{2,3},{3,2},{4,5},{5,4},{6,7},{7,6},{8,9},{9,8},{10,11... | collective-permute-start | bytes 1376264 | tf_op jit(solution)/shard_map/ppermute | solution.py:446
  36.2 10.1 %collective-permute-start.7 = (f32[4,224,128]{2,1,0:T(8,128)S(1)}, f32[4,224,128]{2,1,0:T(8,128)S(1)}, u32[]{:S(2)}, u32[]{:S(2)}) collective-permute-start(f32[4,224,128]{2,1,0:T(8,128)S(1)} %get-tuple-element.33), channel_id=1, source_target_pairs={{0,15},{1,2},{2,1},{3,4},{4,3},{5,6},{6,5},{7,8},{8,7},{9,10},{10,... | collective-permute-start | bytes 1376264 | tf_op jit(solution)/shard_map/ppermute | solution.py:446
